TPU v7x, 256 devices: a whole 4x4x8 slice. The times are simulated.
256 devices in a mesh: pool: 2 (over core), ep: 64 (over x_hi, z, y), tp: 2 (over x_lo).
Axes of the slice: x: 4 (x_hi: 2, x_lo: 2; x = x_hi * 2 + x_lo), y: 4, z: 8, core: 2. Of those that a mesh axis runs over, the one named last changes fastest.
Arguments:
- latent_pages: bfloat16 [16384, 16, 576], P(('pool', 'ep')), may hold values from -6.1 to 6.1
- page_table: int32 [4096, 4], P(('pool', 'ep')), may hold values from 0 to 127, as said below
- lengths: int32 [4096], P(('pool', 'ep')), may hold values from 1 to 63, as said below
- new_place: int32 [4096], P(('pool', 'ep')), may hold values from 0 to 2047, as said below
- queries: bfloat16 [4096, 64, 576], P(('pool', 'ep'), 'tp'), may hold values from -90 to 90
- fresh_latent: bfloat16 [4096, 576], P(('pool', 'ep')), may hold values from -6 to 6
- hidden_states: bfloat16 [4096, 3584], P(('pool', 'ep')), may hold values from -6 to 6
- routing: int32 [4096, 8], P(('pool', 'ep')), may hold values from 0 to 63, all different within a row; in each aligned block of 32 rows (0 to 31, 32 to 63, ...) at most 8 rows name the same one
- route_weight: float32 [4096, 8], P(('pool', 'ep')), may hold values from 0.05 to 0.5
- gate_value: bfloat16 [64, 3584, 1024], P('ep', None, ('pool', 'tp')), may hold values from -0.09375 to 0.09375
- gate_scale: bfloat16 [64, 28, 8], P('ep', None, ('pool', 'tp')), may hold values from 0.5 to 2
- up_value: bfloat16 [64, 3584, 1024], P('ep', None, ('pool', 'tp')), may hold values from -0.09375 to 0.09375
- up_scale: bfloat16 [64, 28, 8], P('ep', None, ('pool', 'tp')), may hold values from 0.5 to 2
- down_value: bfloat16 [64, 1024, 3584], P('ep', ('pool', 'tp')), may hold values from -0.1875 to 0.1875
- down_scale: bfloat16 [64, 8, 28], P('ep', ('pool', 'tp')), may hold values from 0.5 to 2
Outputs:
- new_cache: bfloat16 [4096, 64, 576], P(('pool', 'ep'))
- latent_attention_output: bfloat16 [4096, 64, 512], P(('pool', 'ep'), 'tp')
- expert_mix: bfloat16 [4096, 3584], P(('pool', 'ep'), 'tp')
Inputs may be any that keep to these rules, and one draw needn't show every extreme that they name: `page_table`: the rows of each device's 32 trajectories name every index of that device's 32 * 4 pages exactly once. `lengths`: no trajectory fills its cache; every device holds one trajectory of length 63. Within each group of 2048 trajectories along pool, new_place is a permutation; the new owner along ep is new_place // 32. Each device hands at most 1 trajectories to any one device, and exactly 1 to some device. `routing`: each token names 8 different experts; among the 32 rows of one device no expert is named more than 8 times, a bound that some block reaches.
All inputs are finite; a program needn't handle non-finite values.
Results may differ from a plain program's by a relative error of at most 0.0076.
Values may be sent and summed in bfloat16 or wider, within the bound.
No kernel may reach another device: no remote copies, remote signals or barrier semaphores. Data moves between devices by JAX's collectives and lax.ppermute only.
A program may use at most 128 MiB of HBM per device.

v0:
```python
import jax
import jax.numpy as jnp
from jax import lax
from jax.sharding import PartitionSpec as P

LATENT_WIDTH = 512
BLOCK = 128
MAXLEN = 64
LATENT = 576


score_scale = 192.0 ** (-0.5)


def dequant(value_rows, scales):
    scale_wide = jnp.repeat(jnp.repeat(scales.astype(jnp.float32), BLOCK, axis=0), BLOCK, axis=1)
    return (value_rows.astype(jnp.float32) * scale_wide).astype(jnp.bfloat16)


def slot_matrix(owners, groups, group_depth):
    owner_marks = (owners[:, None] == jnp.arange(groups, dtype=jnp.int32)[None, :]).astype(
        jnp.int32
    )
    before = jnp.cumsum(owner_marks, axis=0) - owner_marks
    group_rank = jnp.sum(before * owner_marks, axis=1)
    target = owners * group_depth + group_rank
    return target[:, None] == jnp.arange(groups * group_depth, dtype=jnp.int32)[None, :]


def migrate(latent_pages, page_table, lengths, new_place, fresh_latent):
    traj_count = lengths.shape[0]
    ep_size = lax.axis_size("ep")
    pair_cap = max(1, 2 * traj_count // ep_size)
    old_cache = latent_pages[page_table.reshape(-1)].reshape(traj_count, MAXLEN, LATENT)
    new_owner = new_place // traj_count
    new_slot = new_place % traj_count
    select = slot_matrix(new_owner, ep_size, pair_cap)
    pick_matrix = select.T.astype(jnp.bfloat16)
    filled = jnp.any(select, axis=0)
    labels_in = jnp.stack([new_slot, lengths], axis=1).astype(jnp.float32)
    labels_out = jnp.dot(select.T.astype(jnp.float32), labels_in, precision=lax.Precision.HIGHEST)
    labels_out = jnp.where(filled[:, None], labels_out, -1.0).astype(jnp.bfloat16)
    flat_cache = old_cache.reshape(traj_count, MAXLEN * LATENT)
    outgoing = jnp.dot(pick_matrix, flat_cache, preferred_element_type=jnp.float32).astype(
        jnp.bfloat16
    )
    arrived, arrived_labels = (
        lax.all_to_all(outgoing, "ep", split_axis=0, concat_axis=0, tiled=True),
        lax.all_to_all(labels_out, "ep", split_axis=0, concat_axis=0, tiled=True),
    )
    arrived_labels = arrived_labels.astype(jnp.float32)
    placing = arrived_labels[:, 0][None, :] == jnp.arange(traj_count, dtype=jnp.float32)[:, None]
    arrived_cache = jnp.dot(
        placing.astype(jnp.bfloat16), arrived, preferred_element_type=jnp.float32
    ).astype(jnp.bfloat16)
    arrived_cache = arrived_cache.reshape(traj_count, MAXLEN, LATENT)
    new_length = jnp.dot(
        placing.astype(jnp.float32), arrived_labels[:, 1], precision=lax.Precision.HIGHEST
    ).astype(jnp.int32)
    positions = jnp.arange(MAXLEN, dtype=jnp.int32)[None, :, None]
    fill_len = new_length[:, None, None]
    new_cache = jnp.where(
        positions < fill_len,
        arrived_cache,
        jnp.where(positions == fill_len, fresh_latent[:, None, :], jnp.zeros((), jnp.bfloat16)),
    )
    return (new_cache, new_length)


def attend(queries, compressed_latent_cache, length_now):
    scores = (
        jnp.einsum(
            "rhc,rtc->rht", queries, compressed_latent_cache, preferred_element_type=jnp.float32
        )
        * score_scale
    )
    positions = jnp.arange(compressed_latent_cache.shape[1], dtype=jnp.int32)
    valid = positions[None, None, :] <= length_now[:, None, None]
    scores = jnp.where(valid, scores, -jnp.inf)
    attention_weights = jax.nn.softmax(scores, axis=-1).astype(jnp.bfloat16)
    return jnp.einsum(
        "djm,dmc->djc",
        attention_weights,
        compressed_latent_cache[:, :, :LATENT_WIDTH],
        preferred_element_type=jnp.float32,
    ).astype(jnp.bfloat16)


def expert_rows(slot_rows, gate_w, up_w, down_w):
    gate_act = jnp.dot(slot_rows, gate_w, preferred_element_type=jnp.float32)
    up_act = jnp.dot(slot_rows, up_w, preferred_element_type=jnp.float32)
    hidden_act = (jax.nn.silu(gate_act) * up_act).astype(jnp.bfloat16)
    return jnp.dot(hidden_act, down_w, preferred_element_type=jnp.float32)


def mixture(
    hidden_states,
    routing,
    route_weight,
    gate_value,
    gate_scale,
    up_value,
    up_scale,
    down_value,
    down_scale,
):
    traj_count, top_count = routing.shape
    ep_size = lax.axis_size("ep")
    slot_cap = 2 * traj_count * top_count // ep_size
    select = slot_matrix(routing.reshape(-1), ep_size, slot_cap)
    per_token = select.reshape(traj_count, top_count, ep_size * slot_cap)
    pick_matrix = jnp.any(per_token, axis=1).T.astype(jnp.bfloat16)
    blend_matrix = jnp.sum(
        jnp.where(per_token, route_weight[:, :, None], jnp.zeros((), jnp.float32)), axis=1
    )
    outgoing = jnp.dot(pick_matrix, hidden_states, preferred_element_type=jnp.float32).astype(
        jnp.bfloat16
    )
    arrived = lax.all_to_all(outgoing, "ep", split_axis=0, concat_axis=0, tiled=True)
    gate_panel, up_panel, gate_block, up_block, down_panel, down_block = (
        lax.all_gather(gate_value, "pool", axis=2, tiled=True),
        lax.all_gather(up_value, "pool", axis=2, tiled=True),
        lax.all_gather(gate_scale, "pool", axis=2, tiled=True),
        lax.all_gather(up_scale, "pool", axis=2, tiled=True),
        lax.all_gather(down_value, "pool", axis=1, tiled=True),
        lax.all_gather(down_scale, "pool", axis=1, tiled=True),
    )
    partial_value = expert_rows(
        arrived,
        dequant(gate_panel[0], gate_block[0]),
        dequant(up_panel[0], up_block[0]),
        dequant(down_panel[0], down_block[0]),
    )
    share_width = partial_value.shape[1] // lax.axis_size("tp")
    summed = lax.psum(partial_value, "tp")
    own_part = lax.dynamic_slice_in_dim(summed, lax.axis_index("tp") * share_width, share_width, 1)
    returned = lax.all_to_all(
        own_part.astype(jnp.bfloat16), "ep", split_axis=0, concat_axis=0, tiled=True
    )
    mixed_out = jnp.dot(blend_matrix, returned.astype(jnp.float32), precision=lax.Precision.HIGHEST)
    return mixed_out.astype(jnp.bfloat16)


def on_device(
    latent_pages,
    page_table,
    lengths,
    new_place,
    queries,
    fresh_latent,
    hidden_states,
    routing,
    route_weight,
    gate_value,
    gate_scale,
    up_value,
    up_scale,
    down_value,
    down_scale,
):
    new_cache, new_length = migrate(latent_pages, page_table, lengths, new_place, fresh_latent)
    latent_attention_output = attend(queries, new_cache, new_length)
    expert_mix = mixture(
        hidden_states,
        routing,
        route_weight,
        gate_value,
        gate_scale,
        up_value,
        up_scale,
        down_value,
        down_scale,
    )
    return (new_cache, latent_attention_output, expert_mix)


def solution(mesh):
    placed = (
        P(("pool", "ep"), None, None),
        P(("pool", "ep"), None),
        P(("pool", "ep")),
        P(("pool", "ep")),
        P(("pool", "ep"), "tp", None),
        P(("pool", "ep"), None),
        P(("pool", "ep"), None),
        P(("pool", "ep"), None),
        P(("pool", "ep"), None),
        P("ep", None, ("pool", "tp")),
        P("ep", None, ("pool", "tp")),
        P("ep", None, ("pool", "tp")),
        P("ep", None, ("pool", "tp")),
        P("ep", ("pool", "tp"), None),
        P("ep", ("pool", "tp"), None),
    )
    return jax.shard_map(
        on_device,
        mesh=mesh,
        in_specs=placed,
        out_specs=(
            P(("pool", "ep"), None, None),
            P(("pool", "ep"), "tp", None),
            P(("pool", "ep"), "tp"),
        ),
        check_vma=False,
    )
```

profile of v0, /device:TPU:68, one launch (start us, length us, event | category | flops | bytes accessed | tf_op | source)
XLA Modules:
  0.0 435.1 jit_solution(742568508392097790)
XLA Ops:
  7.3 0.7 all-gather.4.cloned.1.call-update
  8.0 0.7 all-gather.6.cloned.1.call-update
  8.7 0.1 fusion.54
  8.9 0.2 select_reduce_fusion.1
  9.1 0.1 fusion.53
  9.2 0.2 fusion.36
  9.3 0.7 copy.68
  10.1 13.9 %all-to-all-start = ((bf16[64,1,2]{2,1,0:T(2,128)(2,1)}), bf16[64,1,2]{2,1,0:T(2,128)(2,1)S(1)}, u32[]{:S(2)}, u32[]{:S(2)}) async-start(bf16[64,1,2]{2,1,0:T(2,128)(2,1)} %copy.68), calls=%async_computation | async-start | bytes 65536 | tf_op jit(solution)/shard_map/all_to_all | solution.py:49
  24.0 0.1 copy.73
  24.0 0.1 eq.115
  24.1 0.1 eq.111
  24.2 0.6 reduce-window.6
  24.9 0.2 slice_reduce_fusion
  25.1 0.1 fusion.51
  25.2 0.1 reduce_sum.41
  25.3 0.2 fusion.47
  25.5 3.0 fusion.3
  28.6 3.0 all-to-all-done
  31.5 10.1 %all-to-all-start.2 = ((bf16[64,8,3584]{2,1,0:T(8,128)(2,1)}), bf16[64,8,3584]{2,1,0:T(8,128)(2,1)}, u32[]{:S(2)}, u32[]{:S(2)}) async-start(bf16[64,8,3584]{2,1,0:T(8,128)(2,1)} %fusion.3), calls=%async_computation.2 | async-start | bytes 7340032 | tf_op jit(solution)/shard_map/all_to_all | solution.py:119
  41.7 2.3 copy.82
  44.1 5.1 %copy.71 = bf16[128,16,576]{2,1,0:T(8,128)(2,1)} copy(bf16[128,16,576]{0,2,1:T(8,128)(2,1)} %param.15) | data formatting | bytes 4718592 | tf_op args[0]
  49.1 0.1 copy.70
  49.2 0.1 reshape.212
  49.3 4.1 gather_fusion
  53.5 5.6 %reshape_reshape.3 = bf16[32,36864]{1,0:T(8,128)(2,1)} reshape(bf16[128,16,576]{2,1,0:T(8,128)(2,1)} %gather_fusion) | data formatting | bytes 4718592 | tf_op jit(solution)/shard_map/reshape;reshape | solution.py:43
  59.1 5.3 %fusion.1 = bf16[64,1,36864]{2,0,1:T(8,128)(2,1)} fusion(bf16[32,36864]{1,0:T(8,128)(2,1)} %reshape_reshape.3, s32[32]{0:T(128)S(1)} %add.39), kind=kOutput, calls=%fused_computation.3 | convolution fusion | flops 153356288 | bytes 7078016 | tf_op jit(solution)/shard_map/dot_general | solution.py:44
  64.4 0.5 broadcast.143
  64.9 8.0 %reduce.2 = bf16[64,36864]{1,0:T(8,128)(2,1)} reduce(bf16[64,1,36864]{2,0,1:T(8,128)(2,1)} %fusion.1, bf16[]{:T(256)} %broadcast.143), dimensions={1}, to_apply=%copy.72.reduce_sub_computation | reduce | bytes 9437186 | tf_op jit(solution)/shard_map/all_to_all | solution.py:48
  73.0 8.3 %reshape.237 = bf16[64,2,18432]{2,1,0:T(2,128)(2,1)} reshape(bf16[64,36864]{1,0:T(8,128)(2,1)} %reduce.2) | data formatting | bytes 9437184
  81.3 1.8 all_gather.19
  83.1 0.1 copy.79
  83.2 1.8 all_gather.21
  85.0 0.1 copy.81
  85.1 2.0 all_gather.23
  87.1 0.1 copy.84
  87.2 0.1 broadcast_bitcast_fusion
  87.3 7.6 %reshape.220 = f32[3584,4,128]{2,1,0:T(4,128)} reshape(bf16[1,3584,512]{2,1,0:T(8,128)(2,1)} %all-gather.4.cloned.1.call-done) | data formatting | bytes 11010048 | tf_op jit(solution)/shard_map/convert_element_type | solution.py:17
  94.9 7.6 %reshape.222 = f32[3584,4,128]{2,1,0:T(4,128)} reshape(bf16[1,3584,512]{2,1,0:T(8,128)(2,1)} %all-gather.6.cloned.1.call-done) | data formatting | bytes 11010048 | tf_op jit(solution)/shard_map/convert_element_type | solution.py:17
  102.6 4.9 %fusion.2 = bf16[512,3584]{0,1:T(8,128)(2,1)} fusion(bf16[1,512,3584]{1,2,0:T(8,128)(2,1)} %all-gather.8.cloned.1.call-done, f32[512,28]{0,1:T(8,128)S(1)} %bitcast.105), kind=kLoop, calls=%fused_computation.6 | loop fusion | flops 5505024 | bytes 7397376 | tf_op jit(solution)/shard_map/convert_element_type | solution.py:17
  107.4 0.1 broadcast_in_dim.110
  107.6 9.1 %multiply_convert_fusion.1 = bf16[3584,4,128]{2,1,0:T(4,128)(2,1)} fusion(f32[3584,4,128]{2,1,0:T(4,128)S(1)} %copy-done.1, f32[3584,4]{1,0:T(8,128)S(1)} %bitcast.101), kind=kLoop, calls=%fused_computation.8 | loop fusion | flops 3670016 | bytes 11067392 | tf_op jit(solution)/shard_map/convert_element_type | solution.py:17
  116.7 0.1 broadcast_in_dim.112
  116.8 9.1 %multiply_convert_fusion = bf16[3584,4,128]{2,1,0:T(4,128)(2,1)} fusion(f32[3584,4,128]{2,1,0:T(4,128)S(1)} %bitcast.100, f32[3584,4]{1,0:T(8,128)S(1)} %bitcast.102), kind=kLoop, calls=%fused_computation.7 | loop fusion | flops 3670016 | bytes 11067392 | tf_op jit(solution)/shard_map/convert_element_type | solution.py:17
  126.0 13.0 %all-to-all-start.1 = ((bf16[64,2,18432]{2,1,0:T(2,128)(2,1)}), bf16[64,2,18432]{2,1,0:T(2,128)(2,1)}, u32[]{:S(2)}, u32[]{:S(2)}) async-start(bf16[64,2,18432]{2,1,0:T(2,128)(2,1)} %reshape.237), calls=%async_computation.1 | async-start | bytes 9437184 | tf_op jit(solution)/shard_map/all_to_all | solution.py:48
  139.0 5.2 %fusion.9 = f32[512,512]{1,0:T(8,128)S(1)} fusion(bf16[448,8,4,128]{3,2,1,0:T(4,128)(2,1)} %bitcast.103, bf16[64,8,3584]{2,1,0:T(8,128)(2,1)} %all-to-all-done.2), kind=kOutput, calls=%fused_computation.16 | convolution fusion | flops 1879048192 | bytes 8388608 | tf_op jit(solution)/shard_map/dot_general | solution.py:90
  144.2 11.2 %fusion.40 = f32[512,3584]{1,0:T(8,128)} fusion(bf16[512,3584]{0,1:T(8,128)(2,1)} %fusion.2, bf16[448,8,4,128]{3,2,1,0:T(4,128)(2,1)} %bitcast.104, bf16[64,8,3584]{2,1,0:T(8,128)(2,1)} %all-to-all-done.2, f32[512,512]{1,0:T(8,128)S(1)} %fusion.9), kind=kOutput, calls=%fused_computation.41 | convolution fusion | flops 3759669248 | bytes 19398656 | tf_op jit(solution)/shard_map/dot_general | solution.py:93
  155.4 211.2 %all-reduce.1 = bf16[512,3584]{1,0:T(8,128)(2,1)} all-reduce(f32[512,3584]{1,0:T(8,128)} %fusion.40), channel_id=1, replica_groups=mesh['pool'=2,'ep'=64,'tp'=2] {'tp'}, use_global_device_ids=true, to_apply=%region_10.11 | all-reduce | flops 1835008 | bytes 11010048 | tf_op jit(solution)/shard_map/psum | solution.py:135
  366.5 2.9 fusion.16
  369.4 9.7 %all-to-all-start.3 = ((bf16[64,8,1792]{2,1,0:T(8,128)(2,1)}), bf16[64,8,1792]{2,1,0:T(8,128)(2,1)S(1)}, u32[]{:S(2)}, u32[]{:S(2)}) async-start(bf16[64,8,1792]{2,1,0:T(8,128)(2,1)} %fusion.16), calls=%async_computation.3 | async-start | bytes 3670016 | tf_op jit(solution)/shard_map/all_to_all | solution.py:137
  379.2 0.1 copy.77
  379.3 0.2 select_reduce_fusion
  379.5 0.1 copy.69
  379.6 0.1 fusion.37
  379.7 0.1 iota_compare_fusion.3
  379.8 20.2 %reshape.238 = bf16[64,1,36864]{2,1,0:T(2,128)(2,1)} reshape(bf16[64,2,18432]{2,1,0:T(2,128)(2,1)} %all-to-all-done.1) | data formatting | bytes 9437184
  400.0 10.7 %convolution_convert_fusion.1 = bf16[32,36864]{1,0:T(8,128)(2,1)} fusion(bf16[64,1,36864]{2,1,0:T(2,128)(2,1)} %reshape.238, f32[64]{0:T(128)S(1)} %bitcast_convert_fusion), kind=kOutput, calls=%fused_computation.4 | convolution fusion | flops 152176640 | bytes 7078144 | tf_op jit(solution)/shard_map/dot_general | solution.py:53
  410.8 5.6 %reshape.213 = bf16[32,64,576]{2,1,0:T(8,128)(2,1)} reshape(bf16[32,36864]{1,0:T(8,128)(2,1)} %convolution_convert_fusion.1) | data formatting | bytes 4718592 | tf_op jit(solution)/shard_map/reshape | solution.py:56
  416.4 2.1 select_select_fusion
  418.5 1.5 copy-done.2
  420.0 0.9 fusion.34
  421.0 0.8 copy-done.3
  421.8 0.3 fusion.67
  422.1 4.8 %fusion.18 = bf16[32,32,512]{2,1,0:T(8,128)(2,1)} fusion(bf16[32,64,576]{2,1,0:T(8,128)(2,1)} %copy-done.2, f32[32,32]{1,0:T(8,128)S(1)} %fusion.67, f32[32,32,64]{2,1,0:T(8,128)} %copy-done.3), kind=kOutput, calls=%fused_computation.28 | convolution fusion | flops 67830848 | bytes 3674112 | tf_op jit(solution)/shard_map/djm,dmc->djc/dot_general | solution.py:81
  426.9 1.6 convolution_convert_fusion.3
  (61 shorter events, 0.4 us)
Async XLA Ops:
  7.2 412.9 %copy-start = (bf16[32,32,576]{2,1,0:T(8,128)(2,1)S(1)}, bf16[32,32,576]{2,1,0:T(8,128)(2,1)}, u32[]{:S(2)}) copy-start(bf16[32,32,576]{2,1,0:T(8,128)(2,1)} %param.19) | copy-start | bytes 3538948
  7.2 1.5 copy-start.10
  7.2 2.0 copy-start.11
  7.2 16.8 %copy-start.7 = (s32[32,8]{0,1:T(8,128)S(1)}, s32[32,8]{0,1:T(8,128)}, u32[]{:S(2)}) copy-start(s32[32,8]{0,1:T(8,128)} %param.22) | copy-start | bytes 3076
  7.2 18.3 %copy-start.5 = (bf16[32,3584]{1,0:T(8,128)(2,1)S(1)}, bf16[32,3584]{1,0:T(8,128)(2,1)}, u32[]{:S(2)}) copy-start(bf16[32,3584]{1,0:T(8,128)(2,1)} %param.21) | copy-start | bytes 688132
  7.2 80.1 %all-gather.4.cloned.1.call-start = ((), (), s32[]{:S(2)}) async-start(), calls=%async_computation.4 | async-start | bytes 5505024 | tf_op jit(solution)/shard_map/all_gather | solution.py:121
  8.0 87.0 %all-gather.6.cloned.1.call-start = ((), (), s32[]{:S(2)}) async-start(), calls=%async_computation.5 | async-start | bytes 5505024 | tf_op jit(solution)/shard_map/all_gather | solution.py:122
  10.1 21.4 %all-to-all-start = ((bf16[64,1,2]{2,1,0:T(2,128)(2,1)}), bf16[64,1,2]{2,1,0:T(2,128)(2,1)S(1)}, u32[]{:S(2)}, u32[]{:S(2)}) async-start(bf16[64,1,2]{2,1,0:T(2,128)(2,1)} %copy.68), calls=%async_computation | async-start | bytes 65536 | tf_op jit(solution)/shard_map/all_to_all | solution.py:49
  28.6 13.2 %copy-start.4 = (bf16[1,256,3584]{2,1,0:T(8,128)(2,1)S(1)}, bf16[1,256,3584]{2,1,0:T(8,128)(2,1)}, u32[]{:S(2)}) copy-start(bf16[1,256,3584]{2,1,0:T(8,128)(2,1)} %param.28) | copy-start | bytes 5505028
  31.5 94.4 %all-to-all-start.2 = ((bf16[64,8,3584]{2,1,0:T(8,128)(2,1)}), bf16[64,8,3584]{2,1,0:T(8,128)(2,1)}, u32[]{:S(2)}, u32[]{:S(2)}) async-start(bf16[64,8,3584]{2,1,0:T(8,128)(2,1)} %fusion.3), calls=%async_computation.2 | async-start | bytes 7340032 | tf_op jit(solution)/shard_map/all_to_all | solution.py:119
  41.7 60.9 %all-gather.8.cloned.1.call-start = ((), (), s32[]{:S(2)}) async-start(), calls=%async_computation.6 | async-start | bytes 5505024 | tf_op jit(solution)/shard_map/all_gather | solution.py:125
  44.0 5.1 %copy-start.9 = (s32[32,4]{0,1:T(4,128)S(1)}, s32[32,4]{0,1:T(4,128)}, u32[]{:S(2)}) copy-start(s32[32,4]{0,1:T(4,128)} %param.16) | copy-start | bytes 1540
  73.0 8.3 %copy-start.12 = (bf16[1,28,2]{1,2,0:T(2,128)(2,1)S(1)}, bf16[1,28,2]{1,2,0:T(2,128)(2,1)}, u32[]{:S(2)}) copy-start(bf16[1,28,2]{1,2,0:T(2,128)(2,1)} %param.25) | copy-start | bytes 340
  73.0 10.2 %copy-start.13 = (bf16[1,28,2]{1,2,0:T(2,128)(2,1)S(1)}, bf16[1,28,2]{1,2,0:T(2,128)(2,1)}, u32[]{:S(2)}) copy-start(bf16[1,28,2]{1,2,0:T(2,128)(2,1)} %param.27) | copy-start | bytes 340
  73.0 12.1 %copy-start.14 = (bf16[1,2,28]{2,1,0:T(2,128)(2,1)S(1)}, bf16[1,2,28]{2,1,0:T(2,128)(2,1)}, u32[]{:S(2)}) copy-start(bf16[1,2,28]{2,1,0:T(2,128)(2,1)} %param.29) | copy-start | bytes 340
  102.6 5.0 %copy-start.1 = (f32[3584,4,128]{2,1,0:T(4,128)S(1)}, f32[3584,4,128]{2,1,0:T(4,128)}, u32[]{:S(2)}) copy-start(f32[3584,4,128]{2,1,0:T(4,128)} %reshape.220) | copy-start | bytes 22020100
  107.5 9.3 %slice-start = ((s8[7340032]{0:T(1024)(128)(4,1)}), s8[4194304]{0:T(1024)(128)(4,1)S(1)}, s32[]{:S(2)}) async-start(s8[7340032]{0:T(1024)(128)(4,1)} %bitcast.99), calls=%async_computation.7 | async-start | bytes 8388608
  107.6 9.3 %slice-start.1 = ((s8[7340032]{0:T(1024)(128)(4,1)}), s8[3145728]{0:T(1024)(128)(4,1)S(1)}, s32[]{:S(2)}) async-start(s8[7340032]{0:T(1024)(128)(4,1)} %bitcast.99), calls=%async_computation.8 | async-start | bytes 6291456
  126.0 243.4 %all-to-all-start.1 = ((bf16[64,2,18432]{2,1,0:T(2,128)(2,1)}), bf16[64,2,18432]{2,1,0:T(2,128)(2,1)}, u32[]{:S(2)}, u32[]{:S(2)}) async-start(bf16[64,2,18432]{2,1,0:T(2,128)(2,1)} %reshape.237), calls=%async_computation.1 | async-start | bytes 9437184 | tf_op jit(solution)/shard_map/all_to_all | solution.py:48
  366.5 12.6 %copy-start.8 = (f32[32,8]{0,1:T(8,128)S(1)}, f32[32,8]{0,1:T(8,128)}, u32[]{:S(2)}) copy-start(f32[32,8]{0,1:T(8,128)} %param.23) | copy-start | bytes 3076
  369.4 57.5 %all-to-all-start.3 = ((bf16[64,8,1792]{2,1,0:T(8,128)(2,1)}), bf16[64,8,1792]{2,1,0:T(8,128)(2,1)S(1)}, u32[]{:S(2)}, u32[]{:S(2)}) async-start(bf16[64,8,1792]{2,1,0:T(8,128)(2,1)} %fusion.16), calls=%async_computation.3 | async-start | bytes 3670016 | tf_op jit(solution)/shard_map/all_to_all | solution.py:137
  410.8 5.6 %copy-start.6 = (bf16[32,576]{1,0:T(8,128)(2,1)S(1)}, bf16[32,576]{1,0:T(8,128)(2,1)}, u32[]{:S(2)}) copy-start(bf16[32,576]{1,0:T(8,128)(2,1)} %param.20) | copy-start | bytes 110596
  418.5 1.5 copy-start.2
  421.0 0.8 copy-start.3
Sparse Core Ops, SparseCore 0:
  9.8 19.8 all-gather.3
  31.5 18.9 all-gather.5
  52.3 18.9 all-gather.7
where the time goes:
time: 438 us; the launch traced here: 435 us
  blocking collectives  217 us (50%)
  local copies, waits for them, and re-layouts  74.5 us (17%)
  starting transfers between devices  46.9 us (11%)
  matrix products  43.3 us (10%)
  other arithmetic  35.4 us (8%)
  between operations  14.1 us (3%)
  waiting for transfers between devices  4.38 us (1%)
    psum x1, blocking collectives, mixture(): summed = lax.psum(partial_value, 'tp')  211 us
    unnamed x47, local copies, waits for them, and re-layouts  38.6 us
    convert_element_type x3, other arithmetic, dequant(): return (value_rows.astype(jnp.float32) * scale_wide).astype(jnp.bfloat16)  23.1 us
    convert_element_type x2, local copies, waits for them, and re-layouts, dequant(): return (value_rows.astype(jnp.float32) * scale_wide).astype(jnp.bfloat16)  15.2 us
    all_to_all x1, starting transfers between devices, migrate(): lax.all_to_all(labels_out, 'ep', split_axis=0, concat_axis=0, tiled=True)  13.9 us
    all_to_all x1, starting transfers between devices, migrate(): lax.all_to_all(outgoing, 'ep', split_axis=0, concat_axis=0, tiled=True)  13 us
    dot_general x1, matrix products, expert_rows(): return jnp.dot(hidden_act, down_w, preferred_element_type=jnp.float32)  11.2 us
    dot_general x1, matrix products, migrate(): jnp.dot(placing.astype(jnp.bfloat16), arrived, preferred_element_type=jnp...  10.7 us
  transfers between devices with their start and end apart: 7, of which 1 were waited for; matrix products, arithmetic and copies ran while one was open for 34% of the time, Pallas kernels for 0%

commit v1 on v0

v1 whole, which is shorter than its diff:
```python
import functools

import jax
import jax.numpy as jnp
from jax import lax
from jax.experimental import pallas as pl
from jax.experimental.pallas import tpu as pltpu
from jax.sharding import Mesh, PartitionSpec as P

F32, BF16, I32 = jnp.float32, jnp.bfloat16, jnp.int32
LATENT_WIDTH = 512
BLOCK = 128
MAXLEN = 64
LATENT = 576
LANES = 640
D = 3584
HALF_D = 1792
TRAJ = 32
CAP = 8
NZ, NY, NX = 8, 4, 2
EP = NZ * NY * NX
SCORE_SCALE = 192.0 ** (-0.5)
MB = 1024 * 1024

SMEM = pltpu.SMEM


def whole(shape):
    return pl.BlockSpec(shape, lambda *_: (0,) * len(shape))


def smem():
    return pl.BlockSpec(memory_space=SMEM)


def params(mb):
    return pltpu.CompilerParams(vmem_limit_bytes=mb * MB)


def cost(flops, nbytes):
    return pl.CostEstimate(flops=int(flops), bytes_accessed=int(nbytes), transcendentals=0)


def panel_kernel(tp_ref, gs, us, ds, gv, uv, dv, g_out, u_out, keep_out, send_out):
    step = pl.program_id(0)
    for a in range(2):
        for f in range(2):
            rows, cols = slice(a * BLOCK, (a + 1) * BLOCK), slice(f * BLOCK, (f + 1) * BLOCK)
            at = (step * 2 + a) * 2 + f
            g_out[rows, cols] = (gv[0, rows, cols].astype(F32) * gs[at]).astype(BF16)
            u_out[rows, cols] = (uv[0, rows, cols].astype(F32) * us[at]).astype(BF16)
    half = jnp.where(step < 7, tp_ref[0], 1 - tp_ref[0])
    column = half * 14 + jnp.where(step < 7, step, step - 7) * 2

    def down(out):
        for a in range(2):
            for f in range(2):
                rows, cols = slice(a * BLOCK, (a + 1) * BLOCK), slice(f * BLOCK, (f + 1) * BLOCK)
                out[rows, cols] = (
                    dv[0, rows, cols].astype(F32) * ds[a * 28 + column + f]
                ).astype(BF16)

    @pl.when(step < 7)
    def _():
        down(keep_out)

    @pl.when(step >= 7)
    def _():
        down(send_out)


def scale_panels(tp_index, gate_value, gate_scale, up_value, up_scale, down_value, down_scale):
    def flat(scale):
        return scale.astype(F32).reshape(-1)

    def down_at(i, t):
        return (0, 0, jnp.where(i < 7, t[0] * 7 + i, (1 - t[0]) * 7 + i - 7))

    return pl.pallas_call(
        panel_kernel,
        grid_spec=pltpu.PrefetchScalarGridSpec(
            num_scalar_prefetch=1,
            grid=(14,),
            in_specs=[
                smem(),
                smem(),
                smem(),
                pl.BlockSpec((1, 256, 256), lambda i, t: (0, i, 0)),
                pl.BlockSpec((1, 256, 256), lambda i, t: (0, i, 0)),
                pl.BlockSpec((1, 256, 256), down_at),
            ],
            out_specs=[
                pl.BlockSpec((256, 256), lambda i, t: (i, 0)),
                pl.BlockSpec((256, 256), lambda i, t: (i, 0)),
                pl.BlockSpec((256, 256), lambda i, t: (0, jnp.minimum(i, 6))),
                pl.BlockSpec((256, 256), lambda i, t: (0, jnp.maximum(i - 7, 0))),
            ],
        ),
        out_shape=[
            jax.ShapeDtypeStruct((D, 256), BF16),
            jax.ShapeDtypeStruct((D, 256), BF16),
            jax.ShapeDtypeStruct((256, HALF_D), BF16),
            jax.ShapeDtypeStruct((256, HALF_D), BF16),
        ],
        compiler_params=params(16),
        cost_estimate=cost(3e6, 11e6),
        name="scale_panels",
    )(
        tp_index,
        flat(gate_scale),
        flat(up_scale),
        flat(down_scale),
        gate_value,
        up_value,
        down_value,
    )


def named_by(routing, experts):
    marks = jnp.zeros((routing.shape[0], experts.shape[1]), F32)
    for k in range(routing.shape[1]):
        marks = marks + (routing[:, k : k + 1] == experts).astype(F32)
    return marks


def earlier(marks):
    n = marks.shape[0]
    lower = (
        lax.broadcasted_iota(I32, (n, n), 0) > lax.broadcasted_iota(I32, (n, n), 1)
    ).astype(BF16)
    return jnp.dot(lower, marks.astype(BF16), preferred_element_type=F32)


def pick_kernel(place_ref, *refs):
    blocks, outs = refs[:NZ], refs[NZ:]
    xh, z, y = place_ref[0], place_ref[1], place_ref[2]
    column = lax.broadcasted_iota(I32, (1, EP), 1)
    peer, slot = column >> 3, column & 7
    experts = (((peer >> 2) ^ xh) * NZ + z) * NY + (((peer & 3) + y) & 3)
    for b, block in enumerate(blocks):
        routing = block[:, D : D + 8].astype(F32).astype(I32)
        marks = named_by(routing, experts)
        chosen = jnp.where(earlier(marks) == slot.astype(F32), marks, 0.0).astype(BF16)
        rows = lax.dot_general(
            chosen,
            block[:, :D],
            (((0,), (0,)), ((), ())),
            preferred_element_type=F32,
        ).astype(BF16)
        for r, out in enumerate(outs):
            out[b * CAP : (b + 1) * CAP, :] = rows[r * CAP : (r + 1) * CAP, :]


def pick_rows(place, blocks):
    return pl.pallas_call(
        pick_kernel,
        in_specs=[smem()] + [pl.BlockSpec(memory_space=pltpu.VMEM)] * NZ,
        out_specs=[pl.BlockSpec(memory_space=pltpu.VMEM)] * 8,
        out_shape=[jax.ShapeDtypeStruct((NZ * CAP, D), BF16)] * 8,
        compiler_params=params(24),
        cost_estimate=cost(1e9, 6e6),
        name="pick_rows",
    )(place, *blocks)


def hidden_kernel(*refs):
    tokens, (g0, g1, u0, u1, out), (acc_g, acc_u) = refs[:8], refs[8:13], refs[13:]
    step = pl.program_id(0)

    @pl.when(step == 0)
    def _():
        acc_g[...] = jnp.zeros_like(acc_g)
        acc_u[...] = jnp.zeros_like(acc_u)

    x = jnp.concatenate([t[...] for t in tokens], axis=0)
    acc_g[:, :256] += jnp.dot(x, g0[...], preferred_element_type=F32)
    acc_u[:, :256] += jnp.dot(x, u0[...], preferred_element_type=F32)
    acc_g[:, 256:] += jnp.dot(x, g1[...], preferred_element_type=F32)
    acc_u[:, 256:] += jnp.dot(x, u1[...], preferred_element_type=F32)

    @pl.when(step == pl.num_programs(0) - 1)
    def _():
        g = acc_g[...]
        out[...] = (g / (1.0 + jnp.exp(-g)) * acc_u[...]).astype(BF16)


def hidden_units(tokens, g0, g1, u0, u1):
    depth = 512
    return pl.pallas_call(
        hidden_kernel,
        grid=(D // depth,),
        in_specs=[pl.BlockSpec((64, depth), lambda k: (0, k))] * 8
        + [pl.BlockSpec((depth, 256), lambda k: (k, 0))] * 4,
        out_specs=whole((512, 512)),
        out_shape=jax.ShapeDtypeStruct((512, 512), BF16),
        scratch_shapes=[pltpu.VMEM((512, 512), F32)] * 2,
        compiler_params=params(24),
        cost_estimate=cost(3.8e9, 12e6),
        name="hidden_units",
    )(*tokens, g0, g1, u0, u1)


def down_kernel(order_ref, h0, h1, w0, w1, w2, w3, out):
    h = jnp.concatenate([h0[...], h1[...]], axis=1)
    w = jnp.concatenate([w0[...], w1[...], w2[...], w3[...]], axis=0)
    rows = jnp.dot(h, w, preferred_element_type=F32)
    for group in range(EP):
        out[order_ref[group]] = rows[group * CAP : (group + 1) * CAP, :].astype(BF16)


def down_rows(order, h0, h1, weights):
    wide = 256
    return pl.pallas_call(
        down_kernel,
        grid=(HALF_D // wide,),
        in_specs=[smem(), whole((512, 512)), whole((512, 512))]
        + [pl.BlockSpec((256, wide), lambda i: (0, i))] * 4,
        out_specs=pl.BlockSpec((EP, CAP, wide), lambda i: (0, 0, i)),
        out_shape=jax.ShapeDtypeStruct((EP, CAP, HALF_D), BF16),
        compiler_params=params(24),
        cost_estimate=cost(1.9e9, 7e6),
        name="down_rows",
    )(order, h0, h1, *weights)


def blend_kernel(routing_ref, weight_ref, rows_ref, out):
    column = lax.broadcasted_iota(I32, (1, EP * CAP), 1)
    experts, slot = column >> 3, column & 7
    routing, weight = routing_ref[...], weight_ref[...]
    marks = jnp.zeros((TRAJ, EP * CAP), F32)
    share = jnp.zeros((TRAJ, EP * CAP), F32)
    for k in range(8):
        hit = routing[:, k : k + 1] == experts
        marks = marks + hit.astype(F32)
        share = share + jnp.where(hit, weight[:, k : k + 1], 0.0)
    share = jnp.where(earlier(marks) == slot.astype(F32), share, 0.0)
    high = share.astype(BF16)
    low = (share - high.astype(F32)).astype(BF16)
    rows = rows_ref[...].reshape(EP * CAP, rows_ref.shape[2])
    out[...] = (
        jnp.dot(high, rows, preferred_element_type=F32)
        + jnp.dot(low, rows, preferred_element_type=F32)
    ).astype(BF16)


def blend(routing, weight, rows):
    wide = 896
    return pl.pallas_call(
        blend_kernel,
        grid=(HALF_D // wide,),
        in_specs=[
            whole((TRAJ, 8)),
            whole((TRAJ, 8)),
            pl.BlockSpec((EP, CAP, wide), lambda i: (0, 0, i)),
        ],
        out_specs=pl.BlockSpec((TRAJ, wide), lambda i: (0, i)),
        out_shape=jax.ShapeDtypeStruct((TRAJ, HALF_D), BF16),
        compiler_params=params(16),
        cost_estimate=cost(1e8, 2e6),
        name="blend",
    )(routing, weight, rows)


def collect_kernel(index_ref, pages, out):
    lane = lax.broadcasted_iota(I32, (32, LANES - 512), 1)

    def body(j, carry):
        first, second = index_ref[j, 0], index_ref[j, 1]
        slot, length = index_ref[j, 2].astype(F32), index_ref[j, 3].astype(F32)
        out[j, 0:16, 0:LATENT] = pages[first]
        out[j, 16:32, 0:LATENT] = pages[second]
        label = jnp.where(lane[:, 64:] == 64, slot, length).astype(BF16)
        out[j, :, LATENT:LANES] = label
        return carry

    lax.fori_loop(0, EP, body, 0)


def collect(index, pages):
    return pl.pallas_call(
        collect_kernel,
        in_specs=[smem(), pl.BlockSpec(memory_space=pltpu.VMEM)],
        out_specs=pl.BlockSpec(memory_space=pltpu.VMEM),
        out_shape=jax.ShapeDtypeStruct((EP, 32, LANES), BF16),
        compiler_params=params(16),
        cost_estimate=cost(1e6, 6e6),
        name="collect",
    )(index, pages)


def compact_kernel(source_ref, arrived, out, sem):
    copies = [
        pltpu.make_async_copy(arrived.at[source_ref[s]], out.at[s], sem.at[s])
        for s in range(TRAJ)
    ]
    for copy in copies:
        copy.start()
    for copy in copies:
        copy.wait()


def compact(source, arrived):
    return pl.pallas_call(
        compact_kernel,
        in_specs=[smem(), pl.BlockSpec(memory_space=pl.ANY)],
        out_specs=pl.BlockSpec(memory_space=pl.ANY),
        out_shape=jax.ShapeDtypeStruct((TRAJ, 32, LANES), BF16),
        scratch_shapes=[pltpu.SemaphoreType.DMA((TRAJ,))],
        cost_estimate=cost(1e6, 3e6),
        name="compact",
    )(source, arrived)


ATTEND_STEP = 4


def attend_kernel(tp_ref, length_ref, mine, other, queries, fresh, cache_out, out):
    step = pl.program_id(0)
    first = tp_ref[0] == 0
    row = lax.broadcasted_iota(I32, (MAXLEN, LATENT), 0)
    column = lax.broadcasted_iota(I32, (TRAJ, MAXLEN), 1)
    for i in range(ATTEND_STEP):
        length = length_ref[step * ATTEND_STEP + i]
        a, b = mine[i, :, :LATENT], other[i, :, :LATENT]
        old = jnp.concatenate([jnp.where(first, a, b), jnp.where(first, b, a)], axis=0)
        new = jnp.broadcast_to(fresh[i], (MAXLEN, LATENT))
        cache = jnp.where(
            row < length,
            old.astype(F32),
            jnp.where(row == length, new.astype(F32), 0.0),
        ).astype(BF16)
        cache_out[i] = cache
        scores = lax.dot_general(
            queries[i], cache, (((1,), (1,)), ((), ())), preferred_element_type=F32
        )
        scores = jnp.where(column <= length, scores * SCORE_SCALE, -jnp.inf)
        top = jnp.max(scores, axis=1, keepdims=True)
        weight = jnp.exp(scores - top)
        weight = (weight / jnp.sum(weight, axis=1, keepdims=True)).astype(BF16)
        out[i] = jnp.dot(
            weight, cache[:, :LATENT_WIDTH], preferred_element_type=F32
        ).astype(BF16)


def attend(tp_index, length, mine, other, queries, fresh):
    n = ATTEND_STEP
    return pl.pallas_call(
        attend_kernel,
        grid=(TRAJ // n,),
        in_specs=[
            smem(),
            smem(),
            pl.BlockSpec((n, 32, LANES), lambda i: (i, 0, 0)),
            pl.BlockSpec((n, 32, LANES), lambda i: (i, 0, 0)),
            pl.BlockSpec((n, 32, LATENT), lambda i: (i, 0, 0)),
            pl.BlockSpec((n, 1, LATENT), lambda i: (i, 0, 0)),
        ],
        out_specs=[
            pl.BlockSpec((n, MAXLEN, LATENT), lambda i: (i, 0, 0)),
            pl.BlockSpec((n, 32, LATENT_WIDTH), lambda i: (i, 0, 0)),
        ],
        out_shape=[
            jax.ShapeDtypeStruct((TRAJ, MAXLEN, LATENT), BF16),
            jax.ShapeDtypeStruct((TRAJ, 32, LATENT_WIDTH), BF16),
        ],
        compiler_params=params(16),
        cost_estimate=cost(2e8, 8e6),
        name="attend",
    )(tp_index, length, mine, other, queries, fresh.reshape(TRAJ, 1, LATENT))


def swap(x, axis):
    return lax.ppermute(x, axis, [(0, 1), (1, 0)])


def z_shift(x, by):
    return lax.ppermute(x, "z", [(i, (i + by) % NZ) for i in range(NZ)])


def plane_shift(x, dx, dy):
    return lax.ppermute(
        x,
        ("xh", "y"),
        [
            (a * NY + b, ((a + dx) % NX) * NY + (b + dy) % NY)
            for a in range(NX)
            for b in range(NY)
        ],
    )


def on_device(
    latent_pages,
    page_table,
    lengths,
    new_place,
    queries,
    fresh_latent,
    hidden_states,
    routing,
    route_weight,
    gate_value,
    gate_scale,
    up_value,
    up_scale,
    down_value,
    down_scale,
):
    xh, z, y, tp = (lax.axis_index(name) for name in ("xh", "z", "y", "tp"))
    tp_index = tp.astype(I32).reshape(1)
    place = jnp.stack([xh, z, y]).astype(I32)

    own = jnp.concatenate(
        [hidden_states, jnp.pad(routing.astype(BF16), ((0, 0), (0, BLOCK - 8)))], axis=1
    )
    up_way, down_way = [own], [own]
    for step in range(4):
        up_way.append(z_shift(up_way[-1], 1))
        if step < 3:
            down_way.append(z_shift(down_way[-1], -1))
    blocks = up_way + down_way[1:]
    behind = [0, 1, 2, 3, 4, -1, -2, -3]

    owner, slot = new_place // TRAJ, new_place % TRAJ
    to_owner = owner[None, :] == jnp.arange(EP, dtype=I32)[:, None]
    mine = lax.dynamic_slice_in_dim(page_table, tp * 2, 2, 1)
    facts = jnp.concatenate([mine, slot[:, None] + 1, lengths[:, None]], axis=1)
    index = jnp.sum(jnp.where(to_owner[:, :, None], facts[None], 0), axis=1)
    index = index - jnp.array([0, 0, 1, 0], I32)[None, :]
    arrived = lax.all_to_all(
        collect(index, latent_pages), ("xh", "z", "y"), split_axis=0, concat_axis=0, tiled=True
    )

    gate, up, down_keep, down_send = scale_panels(
        tp_index, gate_value, gate_scale, up_value, up_scale, down_value, down_scale
    )
    gate_far, up_far = swap(gate, "pool"), swap(up, "pool")
    down_tp = swap(down_send, "tp")
    down_far, down_tp_far = swap(down_keep, "pool"), swap(down_tp, "pool")

    picked = pick_rows(place, blocks)
    tokens = [picked[0]] + [
        plane_shift(picked[dx * NY + dy], dx, dy)
        for dx in range(NX)
        for dy in range(NY)
        if dx or dy
    ]
    act = hidden_units(tokens, gate, gate_far, up, up_far)
    act_tp = swap(act, "tp")
    order = jnp.stack(
        [
            (((xh + dx) % NX) * NZ + (z - b) % NZ) * NY + (y - dy) % NY
            for dx in range(NX)
            for dy in range(NY)
            for b in behind
        ]
    ).astype(I32)
    out_rows = down_rows(order, act, act_tp, [down_keep, down_far, down_tp, down_tp_far])
    returned = lax.all_to_all(
        out_rows, ("xh", "z", "y"), split_axis=0, concat_axis=0, tiled=True
    )
    expert_mix = blend(routing, route_weight, returned)

    labels = arrived[:, 0, LATENT : LATENT + 2].astype(I32)
    taken = labels[:, 0][None, :] == jnp.arange(TRAJ, dtype=I32)[:, None]
    source = jnp.sum(jnp.where(taken, jnp.arange(EP, dtype=I32)[None, :], 0), axis=1)
    length = jnp.sum(jnp.where(taken, labels[:, 1][None, :], 0), axis=1)
    my_half = compact(source, arrived)
    other_half = swap(my_half, "tp")
    new_cache, attention = attend(tp_index, length, my_half, other_half, queries, fresh_latent)
    return new_cache, attention, expert_mix


def solution(mesh):
    grid = Mesh(mesh.devices.reshape(2, NX, NZ, NY, 2), ("pool", "xh", "z", "y", "tp"))
    ep = ("xh", "z", "y")
    rows = ("pool",) + ep
    placed = (
        P(rows, None, None),
        P(rows, None),
        P(rows),
        P(rows),
        P(rows, "tp", None),
        P(rows, None),
        P(rows, None),
        P(rows, None),
        P(rows, None),
        P(ep, None, ("pool", "tp")),
        P(ep, None, ("pool", "tp")),
        P(ep, None, ("pool", "tp")),
        P(ep, None, ("pool", "tp")),
        P(ep, ("pool", "tp"), None),
        P(ep, ("pool", "tp"), None),
    )
    return jax.shard_map(
        on_device,
        mesh=grid,
        in_specs=placed,
        out_specs=(P(rows, None, None), P(rows, "tp", None), P(rows, "tp")),
        check_vma=False,
    )
```

time: 438 us -> 308 us (0.70)
  blocking collectives: 217 us -> 0 us
  waiting for transfers between devices: 4.38 us -> 148 us
  Pallas kernels: 0 us -> 85.1 us
  local copies, waits for them, and re-layouts: 74.5 us -> 10.7 us
  matrix products: 43.3 us -> 0 us
  other arithmetic: 35.4 us -> 3.26 us
  between operations: 14.1 us -> 0.88 us
  starting transfers between devices: 46.9 us -> 58.8 us
    psum x1 -> x0, blocking collectives: 211 us -> none  [mixture(): summed = lax.psum(partial_value, 'tp')]
    ppermute x0 -> x21, waiting for transfers between devices: none -> 148 us  [the longest x7 70.8 us: z_shift(): return lax.ppermute(x, 'z', [(i, (i + by) % NZ) for i in range(NZ)])]
    pallas_call x0 -> x8, Pallas kernels: none -> 85.1 us  [the longest x1 41.9 us: compact(): pl.pallas_call(compact_kernel, in_specs=[smem(), pl.BlockSpec(memory_spac...]
    dot_general x10 -> x0, matrix products: 43.3 us -> none  [the longest x1 11.2 us: expert_rows(): return jnp.dot(hidden_act, down_w, preferred_element_type=jnp.float32)]
    ppermute x0 -> x21, starting transfers between devices: none -> 31.2 us  [the longest x7 17.2 us: plane_shift(): lax.ppermute(x, ('xh', 'y'), [(a * NY + b, (a + dx) % NX * NY + (b + dy)...]
    unnamed x47 -> x33, local copies, waits for them, and re-layouts: 38.6 us -> 9.69 us
    convert_element_type x8 -> x2, other arithmetic: 23.2 us -> 1.02 us  [the longest x1 1.02 us: on_device(): labels = arrived[:, 0, LATENT:LATENT + 2].astype(I32)]
    all_to_all x4 -> x2, starting transfers between devices: 46.7 us -> 27.5 us  [the longest x1 14.2 us: on_device(): lax.all_to_all(collect(index, latent_pages), ('xh', 'z', 'y'), split_axis...]
  transfers between devices with their start and end apart: 7 -> 23, of which waited for: 1 -> 13; matrix products, arithmetic and copies ran while one was open for 34% -> 1% of each run, Pallas kernels for 0% -> 22%
where the time goes in v1:
time: 308 us; the launch traced here: 306 us
  waiting for transfers between devices  148 us (48%)
  Pallas kernels  85.1 us (28%)
  starting transfers between devices  58.8 us (19%)
  local copies, waits for them, and re-layouts  10.7 us (3%)
  other arithmetic  3.26 us (1%)
    ppermute x7, waiting for transfers between devices, z_shift(): return lax.ppermute(x, 'z', [(i, (i + by) % NZ) for i in range(NZ)])  70.8 us
    pallas_call x1, Pallas kernels, compact(): pl.pallas_call(compact_kernel, in_specs=[smem(), pl.BlockSpec(memory_spac...  41.9 us
    ppermute x7, waiting for transfers between devices, swap(): return lax.ppermute(x, axis, [(0, 1), (1, 0)])  40 us
    ppermute x7, waiting for transfers between devices, plane_shift(): lax.ppermute(x, ('xh', 'y'), [(a * NY + b, (a + dx) % NX * NY + (b + dy)...  37 us
    ppermute x7, starting transfers between devices, plane_shift(): lax.ppermute(x, ('xh', 'y'), [(a * NY + b, (a + dx) % NX * NY + (b + dy)...  17.2 us
    all_to_all x1, starting transfers between devices, on_device(): lax.all_to_all(collect(index, latent_pages), ('xh', 'z', 'y'), split_axis...  14.2 us
    all_to_all x1, starting transfers between devices, on_device(): lax.all_to_all(out_rows, ('xh', 'z', 'y'), split_axis=0, concat_axis=0, t...  13.4 us
    pallas_call x1, Pallas kernels, attend(): pl.pallas_call(attend_kernel, grid=(TRAJ // n,), in_specs=[smem(), smem()...  12.9 us
  transfers between devices with their start and end apart: 23, of which 13 were waited for; matrix products, arithmetic and copies ran while one was open for 1% of the time, Pallas kernels for 22%

profile of v1, /device:TPU:68, one launch (start us, length us, event | category | flops | bytes accessed | tf_op | source)
XLA Modules:
  0.0 306.4 jit_solution(2877647233451633250)
XLA Ops:
  0.7 0.7 and_select_fusion.1
  1.3 0.1 iota_compare_fusion.2
  1.4 0.7 pad_add_fusion
  2.1 0.1 select_reduce_fusion
  2.2 0.1 copy.45
  2.3 3.9 %copy.47.pages = bf16[128,16,576]{2,1,0:T(8,128)(2,1)S(1)} copy(bf16[128,16,576]{0,2,1:T(8,128)(2,1)} %param.16) | data formatting | bytes 4718592 | tf_op args[0]
  6.2 3.3 %collect.1 = bf16[64,32,640]{2,1,0:T(8,128)(2,1)} custom-call(s32[64,4]{1,0:T(8,128)S(1)} %broadcast_add_fusion.index_ref, bf16[128,16,576]{2,1,0:T(8,128)(2,1)S(1)} %copy.47.pages), custom_call_target="tpu_custom_call" | custom-call | flops 1000000 | bytes 6000000 | tf_op jit(solution)/shard_map/collect/pallas_call | solution.py:280
  9.6 14.2 %all-to-all-start = ((bf16[64,32,640]{2,1,0:T(8,128)(2,1)}), bf16[64,32,640]{2,1,0:T(8,128)(2,1)}, u32[]{:S(2)}, u32[]{:S(2)}) async-start(bf16[64,32,640]{2,1,0:T(8,128)(2,1)} %collect.1), calls=%async_computation | async-start | bytes 5242880 | tf_op jit(solution)/shard_map/all_to_all | solution.py:430
  23.8 0.1 copy.50
  23.9 1.6 collective-permute-start.1
  25.5 0.5 collective-permute-start.5
  26.0 59.4 %collective-permute-done.1.refs_1_ = bf16[32,3712]{1,0:T(8,128)(2,1)S(1)} collective-permute-done((bf16[32,3712]{1,0:T(8,128)(2,1)S(1)}, bf16[32,3712]{1,0:T(8,128)(2,1)S(1)}, u32[]{:S(2)}, u32[]{:S(2)}) %collective-permute-start.1) | collective-permute-done | bytes 237600 | tf_op jit(solution)/shard_map/ppermute | solution.py:377
  85.4 1.5 collective-permute-start.2
  86.8 0.5 collective-permute-start.6
  87.4 5.3 %collective-permute-done.2.refs_2_ = bf16[32,3712]{1,0:T(8,128)(2,1)} collective-permute-done((bf16[32,3712]{1,0:T(8,128)(2,1)S(1)}, bf16[32,3712]{1,0:T(8,128)(2,1)}, u32[]{:S(2)}, u32[]{:S(2)}) %collective-permute-start.2) | collective-permute-done | bytes 237600 | tf_op jit(solution)/shard_map/ppermute | solution.py:377
  92.7 1.3 collective-permute-start.3
  93.9 0.1 copy.51
  94.1 0.1 reshape.62.gs
  94.2 0.1 copy.52
  94.3 0.1 reshape.64.us
  94.4 0.1 reshape.66.ds
  94.5 1.5 copy-done.4
  96.0 1.5 copy-done.5
  97.5 6.6 %scale_panels.1 = (bf16[3584,256]{1,0:T(8,128)(2,1)}, bf16[3584,256]{1,0:T(8,128)(2,1)}, bf16[256,1792]{1,0:T(8,128)(2,1)S(1)}, bf16[256,1792]{1,0:T(8,128)(2,1)}) custom-call(s32[1]{0:T(128)} %bitcast.tp_ref, f32[56]{0:T(128)S(1)} %reshape.62.gs, f32[56]{0:T(128)S(1)} %reshape.64.us, f32[56]{0:T(128)S(1)} %reshape.66.ds, ...), custom_call_target="tpu_custom_call" | custom-call | flops 3000000 | bytes 11000000 | tf_op jit(solution)/shard_map/scale_panels/pallas_call | solution.py:79
  104.0 1.2 collective-permute-start.19
  105.2 0.5 collective-permute-start.16
  105.7 0.8 collective-permute-start.7
  106.5 3.1 collective-permute-start.4
  109.6 0.1 pad_add_fusion.1.place_ref
  109.7 6.1 %collective-permute-done.7.refs_7_ = bf16[32,3712]{1,0:T(8,128)(2,1)} collective-permute-done((bf16[32,3712]{1,0:T(8,128)(2,1)}, bf16[32,3712]{1,0:T(8,128)(2,1)}, u32[]{:S(2)}, u32[]{:S(2)}) %collective-permute-start.7) | collective-permute-done | bytes 237600 | tf_op jit(solution)/shard_map/ppermute | solution.py:377
  115.8 4.1 %pick_rows.1 = (bf16[64,3584]{1,0:T(8,128)(2,1)S(1)}, bf16[64,3584]{1,0:T(8,128)(2,1)S(1)}, bf16[64,3584]{1,0:T(8,128)(2,1)S(1)}, bf16[64,3584]{1,0:T(8,128)(2,1...) custom-call(s32[3]{0:T(128)S(1)} %pad_add_fusion.1.place_ref, ...), custom_call_target="tpu_custom_call" | custom-call | flops 1000000000 | bytes 6000000 | tf_op jit(solution)/shard_map/pick_rows/pallas_call | solution.py:155
  119.8 3.2 %collective-permute-start.10 = (bf16[64,3584]{1,0:T(8,128)(2,1)S(1)}, bf16[64,3584]{1,0:T(8,128)(2,1)S(1)}, u32[]{:S(2)}, u32[]{:S(2)}) collective-permute-start(bf16[64,3584]{1,0:T(8,128)(2,1)S(1)} %get-tuple-element.22), channel_id=1, source_target_pairs={{0,6},{2,0},{4,2},{6,4},{64,70},{66,64},{68,66},{70,68},{1,7},{3,1... | collective-permute-start | bytes 1376264 | tf_op jit(solution)/shard_map/ppermute | solution.py:381
  123.0 1.7 collective-permute-done.19.w2
  124.7 3.0 collective-permute-start.12
  127.8 4.7 %collective-permute-done.10.refs_3_ = bf16[64,3584]{1,0:T(8,128)(2,1)S(1)} collective-permute-done((bf16[64,3584]{1,0:T(8,128)(2,1)S(1)}, bf16[64,3584]{1,0:T(8,128)(2,1)S(1)}, u32[]{:S(2)}, u32[]{:S(2)}) %collective-permute-start.10) | collective-permute-done | bytes 458784 | tf_op jit(solution)/shard_map/ppermute | solution.py:381
  132.5 2.1 collective-permute-start.13
  134.6 3.4 %collective-permute-done.11.refs_4_ = bf16[64,3584]{1,0:T(8,128)(2,1)S(1)} collective-permute-done((bf16[64,3584]{1,0:T(8,128)(2,1)S(1)}, bf16[64,3584]{1,0:T(8,128)(2,1)S(1)}, u32[]{:S(2)}, u32[]{:S(2)}) %collective-permute-start.11) | collective-permute-done | bytes 458784 | tf_op jit(solution)/shard_map/ppermute | solution.py:381
  138.0 4.6 %collective-permute-start.14 = (bf16[64,3584]{1,0:T(8,128)(2,1)S(1)}, bf16[64,3584]{1,0:T(8,128)(2,1)S(1)}, u32[]{:S(2)}, u32[]{:S(2)}) collective-permute-start(bf16[64,3584]{1,0:T(8,128)(2,1)S(1)} %get-tuple-element.26), channel_id=1, source_target_pairs={{0,70},{2,64},{4,66},{6,68},{64,6},{66,0},{68,2},{70,4},{1,71},{3,... | collective-permute-start | bytes 1376264 | tf_op jit(solution)/shard_map/ppermute | solution.py:381
  142.6 5.4 %collective-permute-done.12.refs_5_ = bf16[64,3584]{1,0:T(8,128)(2,1)S(1)} collective-permute-done((bf16[64,3584]{1,0:T(8,128)(2,1)S(1)}, bf16[64,3584]{1,0:T(8,128)(2,1)S(1)}, u32[]{:S(2)}, u32[]{:S(2)}) %collective-permute-start.12) | collective-permute-done | bytes 458784 | tf_op jit(solution)/shard_map/ppermute | solution.py:381
  148.0 1.4 collective-permute-start.8
  149.4 8.5 %collective-permute-done.13.refs_6_ = bf16[64,3584]{1,0:T(8,128)(2,1)S(1)} collective-permute-done((bf16[64,3584]{1,0:T(8,128)(2,1)S(1)}, bf16[64,3584]{1,0:T(8,128)(2,1)S(1)}, u32[]{:S(2)}, u32[]{:S(2)}) %collective-permute-start.13) | collective-permute-done | bytes 458784 | tf_op jit(solution)/shard_map/ppermute | solution.py:381
  157.9 2.8 collective-permute-start.9
  160.7 4.1 %collective-permute-done.14.refs_7_ = bf16[64,3584]{1,0:T(8,128)(2,1)S(1)} collective-permute-done((bf16[64,3584]{1,0:T(8,128)(2,1)S(1)}, bf16[64,3584]{1,0:T(8,128)(2,1)S(1)}, u32[]{:S(2)}, u32[]{:S(2)}) %collective-permute-start.14) | collective-permute-done | bytes 458784 | tf_op jit(solution)/shard_map/ppermute | solution.py:381
  164.8 1.3 collective-permute-done.8.refs_1_
  166.1 9.7 %collective-permute-done.9.refs_2_ = bf16[64,3584]{1,0:T(8,128)(2,1)S(1)} collective-permute-done((bf16[64,3584]{1,0:T(8,128)(2,1)S(1)}, bf16[64,3584]{1,0:T(8,128)(2,1)S(1)}, u32[]{:S(2)}, u32[]{:S(2)}) %collective-permute-start.9) | collective-permute-done | bytes 458784 | tf_op jit(solution)/shard_map/ppermute | solution.py:381
  175.8 8.1 %hidden_units.1.h0 = bf16[512,512]{1,0:T(8,128)(2,1)S(1)} custom-call(bf16[64,3584]{1,0:T(8,128)(2,1)S(1)} %get-tuple-element.19.refs_0_, bf16[64,3584]{1,0:T(8,128)(2,1)S(1)} %collective-permute-done.8.refs_1_, bf16[64,3584]{1,0:T(8,128)(2,1)S(1)} %collective-permute-done.9.refs_2_, bf16[64,3584]{1,0:T(8,128)(2,1)S(1)} %collective-permute-done.10.refs_3_, ...), custom_call_target="tpu_custom_call" | custom-call | flops 3800000000 | bytes 12000000 | tf_op jit(solution)/shard_map/hidden_units/pallas_call | solution.py:189
  183.9 2.1 collective-permute-start.17
  186.0 0.1 stack.271.order_ref
  186.2 11.8 %collective-permute-done.17.h1 = bf16[512,512]{1,0:T(8,128)(2,1)S(1)} collective-permute-done((bf16[512,512]{1,0:T(8,128)(2,1)S(1)}, bf16[512,512]{1,0:T(8,128)(2,1)S(1)}, u32[]{:S(2)}, u32[]{:S(2)}) %collective-permute-start.17) | collective-permute-done | bytes 524320 | tf_op jit(solution)/shard_map/ppermute | solution.py:373
  198.0 6.2 %down_rows.1 = bf16[64,8,1792]{2,1,0:T(8,128)(2,1)S(1)} custom-call(s32[64]{0:T(128)S(1)} %stack.271.order_ref, bf16[512,512]{1,0:T(8,128)(2,1)S(1)} %hidden_units.1.h0, bf16[512,512]{1,0:T(8,128)(2,1)S(1)} %collective-permute-done.17.h1, bf16[256,1792]{1,0:T(8,128)(2,1)S(1)} %get-tuple-element.29.w0, bf16[256,1792]{1,0:T(8,128)(2,1)} %collective-permute-done.18.w1, ...), custom_call_target="tpu_custom_call" | custom-call | flops 1900000000 | bytes 7000000 | tf_op jit(solution)/shard_map/down_rows/pallas_call | solution.py:213
  204.2 1.2 copy-done.2
  205.4 13.4 %all-to-all-start.1 = ((bf16[64,8,1792]{2,1,0:T(8,128)(2,1)}), bf16[64,8,1792]{2,1,0:T(8,128)(2,1)S(1)}, u32[]{:S(2)}, u32[]{:S(2)}) async-start(bf16[64,8,1792]{2,1,0:T(8,128)(2,1)} %copy-done.2), calls=%async_computation.1 | async-start | bytes 3670016 | tf_op jit(solution)/shard_map/all_to_all | solution.py:459
  218.8 1.0 slice_convert_fusion
  219.8 0.1 copy.48
  219.9 0.6 select_reduce_fusion.1
  220.5 41.9 %compact.1.mine = bf16[32,32,640]{2,1,0:T(8,128)(2,1)} custom-call(s32[32]{0:T(128)} %get-tuple-element.31.source_ref, bf16[64,32,640]{2,1,0:T(8,128)(2,1)} %all-to-all-done.arrived), custom_call_target="tpu_custom_call" | custom-call | flops 1000000 | bytes 3000000 | tf_op jit(solution)/shard_map/compact/pallas_call | solution.py:303
  262.5 0.9 collective-permute-start
  263.4 0.1 copy.53.routing_ref
  263.5 0.1 copy.54.weight_ref
  263.6 0.1 copy.49.fresh
  263.7 2.1 blend.1
  265.7 26.4 %collective-permute-done.other = bf16[32,32,640]{2,1,0:T(8,128)(2,1)} collective-permute-done((bf16[32,32,640]{2,1,0:T(8,128)(2,1)}, bf16[32,32,640]{2,1,0:T(8,128)(2,1)}, u32[]{:S(2)}, u32[]{:S(2)}) %collective-permute-start) | collective-permute-done | bytes 1310752 | tf_op jit(solution)/shard_map/ppermute | solution.py:373
  292.2 1.3 copy-done.6
  293.5 12.9 %attend.1 = (bf16[32,64,576]{2,1,0:T(8,128)(2,1)}, bf16[32,32,512]{2,1,0:T(8,128)(2,1)}) custom-call(s32[1]{0:T(128)} %bitcast.tp_ref, s32[32]{0:T(128)S(1)} %get-tuple-element.32.length_ref, bf16[32,32,640]{2,1,0:T(8,128)(2,1)S(1)} %copy-done.1, bf16[32,32,640]{2,1,0:T(8,128)(2,1)} %collective-permute-done.other, bf16[32,32,576]{2,1,0:T(8,128)(2,1)S(1)} %copy-done.6, ...), custom_call_target="tpu_custom_call" | custom-call | flops 200000000 | bytes 8000000 | tf_op jit(solution)/shard_map/attend/pallas_call | solution.py:347
  (45 shorter events, 0.1 us)
Async XLA Ops:
  0.6 0.8 copy-start
  2.3 3.9 %copy-start.11 = (s32[4]{0:T(128)S(1)}, s32[4]{0:T(128)}, u32[]{:S(2)}) copy-start(s32[4]{0:T(128)} %constant.516) | copy-start | bytes 52
  9.5 14.2 %copy-start.9 = (s32[32,8]{0,1:T(8,128)S(1)}, s32[32,8]{0,1:T(8,128)}, u32[]{:S(2)}) copy-start(s32[32,8]{0,1:T(8,128)} %param.23) | copy-start | bytes 3076
  9.5 14.3 %copy-start.7 = (bf16[32,3584]{1,0:T(8,128)(2,1)S(1)}, bf16[32,3584]{1,0:T(8,128)(2,1)}, u32[]{:S(2)}) copy-start(bf16[32,3584]{1,0:T(8,128)(2,1)} %param.22) | copy-start | bytes 688132
  9.5 84.4 %copy-start.12 = (bf16[1,28,2]{1,2,0:T(2,128)(2,1)S(1)}, bf16[1,28,2]{1,2,0:T(2,128)(2,1)}, u32[]{:S(2)}) copy-start(bf16[1,28,2]{1,2,0:T(2,128)(2,1)} %param.26) | copy-start | bytes 340
  9.5 84.6 %copy-start.13 = (bf16[1,28,2]{1,2,0:T(2,128)(2,1)S(1)}, bf16[1,28,2]{1,2,0:T(2,128)(2,1)}, u32[]{:S(2)}) copy-start(bf16[1,28,2]{1,2,0:T(2,128)(2,1)} %param.28) | copy-start | bytes 340
  9.5 84.8 %copy-start.14 = (bf16[1,2,28]{2,1,0:T(2,128)(2,1)S(1)}, bf16[1,2,28]{2,1,0:T(2,128)(2,1)}, u32[]{:S(2)}) copy-start(bf16[1,2,28]{2,1,0:T(2,128)(2,1)} %param.30) | copy-start | bytes 340
  9.6 84.9 %copy-start.3 = (bf16[1,3584,256]{2,1,0:T(8,128)(2,1)S(1)}, bf16[1,3584,256]{2,1,0:T(8,128)(2,1)}, u32[]{:S(2)}) copy-start(bf16[1,3584,256]{2,1,0:T(8,128)(2,1)} %gv.1) | copy-start | bytes 5505028
  9.6 195.9 %all-to-all-start = ((bf16[64,32,640]{2,1,0:T(8,128)(2,1)}), bf16[64,32,640]{2,1,0:T(8,128)(2,1)}, u32[]{:S(2)}, u32[]{:S(2)}) async-start(bf16[64,32,640]{2,1,0:T(8,128)(2,1)} %collect.1), calls=%async_computation | async-start | bytes 5242880 | tf_op jit(solution)/shard_map/all_to_all | solution.py:430
  23.9 61.5 %collective-permute-start.1 = (bf16[32,3712]{1,0:T(8,128)(2,1)S(1)}, bf16[32,3712]{1,0:T(8,128)(2,1)S(1)}, u32[]{:S(2)}, u32[]{:S(2)}) collective-permute-start(bf16[32,3712]{1,0:T(8,128)(2,1)S(1)} %fusion.1.refs_0_), channel_id=1, source_target_pairs={{0,8},{8,16},{16,24},{24,32},{32,40},{40,48},{48,56},{56,0},{1,9},... | collective-permute-start | bytes 712712 | tf_op jit(solution)/shard_map/ppermute | solution.py:377
  25.5 61.4 %collective-permute-start.5 = (bf16[32,3712]{1,0:T(8,128)(2,1)S(1)}, bf16[32,3712]{1,0:T(8,128)(2,1)S(1)}, u32[]{:S(2)}, u32[]{:S(2)}) collective-permute-start(bf16[32,3712]{1,0:T(8,128)(2,1)S(1)} %fusion.1.refs_0_), channel_id=1, source_target_pairs={{0,56},{8,0},{16,8},{24,16},{32,24},{40,32},{48,40},{56,48},{1,57}... | collective-permute-start | bytes 712712 | tf_op jit(solution)/shard_map/ppermute | solution.py:377
  85.4 7.3 %collective-permute-start.2 = (bf16[32,3712]{1,0:T(8,128)(2,1)S(1)}, bf16[32,3712]{1,0:T(8,128)(2,1)}, u32[]{:S(2)}, u32[]{:S(2)}) collective-permute-start(bf16[32,3712]{1,0:T(8,128)(2,1)S(1)} %collective-permute-done.1.refs_1_), channel_id=1, source_target_pairs={{0,8},{8,16},{16,24},{24,32},{32,40},{40,48},{48,56},{56,0},{1,9},... | collective-permute-start | bytes 712712 | tf_op jit(solution)/shard_map/ppermute | solution.py:377
  86.8 18.9 %collective-permute-start.6 = (bf16[32,3712]{1,0:T(8,128)(2,1)S(1)}, bf16[32,3712]{1,0:T(8,128)(2,1)}, u32[]{:S(2)}, u32[]{:S(2)}) collective-permute-start(bf16[32,3712]{1,0:T(8,128)(2,1)S(1)} %collective-permute-done.5.refs_5_), channel_id=1, source_target_pairs={{0,56},{8,0},{16,8},{24,16},{32,24},{40,32},{48,40},{56,48},{1,57}... | collective-permute-start | bytes 712712 | tf_op jit(solution)/shard_map/ppermute | solution.py:377
  92.7 13.8 %collective-permute-start.3 = (bf16[32,3712]{1,0:T(8,128)(2,1)}, bf16[32,3712]{1,0:T(8,128)(2,1)}, u32[]{:S(2)}, u32[]{:S(2)}) collective-permute-start(bf16[32,3712]{1,0:T(8,128)(2,1)} %collective-permute-done.2.refs_2_), channel_id=1, source_target_pairs={{0,8},{8,16},{16,24},{24,32},{32,40},{40,48},{48,56},{56,0},{1,9},... | collective-permute-start | bytes 712712 | tf_op jit(solution)/shard_map/ppermute | solution.py:377
  94.5 1.5 copy-start.4
  96.0 1.5 copy-start.5
  104.0 20.7 %collective-permute-start.19 = (bf16[256,1792]{1,0:T(8,128)(2,1)}, bf16[256,1792]{1,0:T(8,128)(2,1)}, u32[]{:S(2)}, u32[]{:S(2)}) collective-permute-start(bf16[256,1792]{1,0:T(8,128)(2,1)} %get-tuple-element.30), channel_id=1, source_target_pairs={{0,1},{1,0},{2,3},{3,2},{4,5},{5,4},{6,7},{7,6},{8,9},{9,8},{10,11... | collective-permute-start | bytes 2752520 | tf_op jit(solution)/shard_map/ppermute | solution.py:373
  105.2 70.5 %collective-permute-start.15 = (bf16[3584,256]{1,0:T(8,128)(2,1)}, bf16[3584,256]{1,0:T(8,128)(2,1)S(1)}, u32[]{:S(2)}, u32[]{:S(2)}) collective-permute-start(bf16[3584,256]{1,0:T(8,128)(2,1)} %get-tuple-element.27.refs_8_), channel_id=1, source_target_pairs={{0,128},{128,0},{1,129},{129,1},{2,130},{130,2},{3,131},{131,3},{4... | collective-permute-start | bytes 5505032 | tf_op jit(solution)/shard_map/ppermute | solution.py:373
  105.2 70.5 %collective-permute-start.16 = (bf16[3584,256]{1,0:T(8,128)(2,1)}, bf16[3584,256]{1,0:T(8,128)(2,1)}, u32[]{:S(2)}, u32[]{:S(2)}) collective-permute-start(bf16[3584,256]{1,0:T(8,128)(2,1)} %get-tuple-element.28.refs_10_), channel_id=1, source_target_pairs={{0,128},{128,0},{1,129},{129,1},{2,130},{130,2},{3,131},{131,3},{4... | collective-permute-start | bytes 5505032 | tf_op jit(solution)/shard_map/ppermute | solution.py:373
  105.7 10.0 %collective-permute-start.7 = (bf16[32,3712]{1,0:T(8,128)(2,1)}, bf16[32,3712]{1,0:T(8,128)(2,1)}, u32[]{:S(2)}, u32[]{:S(2)}) collective-permute-start(bf16[32,3712]{1,0:T(8,128)(2,1)} %collective-permute-done.6.refs_6_), channel_id=1, source_target_pairs={{0,56},{8,0},{16,8},{24,16},{32,24},{40,32},{48,40},{56,48},{1,57}... | collective-permute-start | bytes 712712 | tf_op jit(solution)/shard_map/ppermute | solution.py:377
  106.5 9.2 %collective-permute-start.4 = (bf16[32,3712]{1,0:T(8,128)(2,1)}, bf16[32,3712]{1,0:T(8,128)(2,1)}, u32[]{:S(2)}, u32[]{:S(2)}) collective-permute-start(bf16[32,3712]{1,0:T(8,128)(2,1)} %collective-permute-done.3.refs_3_), channel_id=1, source_target_pairs={{0,8},{8,16},{16,24},{24,32},{32,40},{40,48},{48,56},{56,0},{1,9},... | collective-permute-start | bytes 712712 | tf_op jit(solution)/shard_map/ppermute | solution.py:377
  119.8 12.6 %collective-permute-start.10 = (bf16[64,3584]{1,0:T(8,128)(2,1)S(1)}, bf16[64,3584]{1,0:T(8,128)(2,1)S(1)}, u32[]{:S(2)}, u32[]{:S(2)}) collective-permute-start(bf16[64,3584]{1,0:T(8,128)(2,1)S(1)} %get-tuple-element.22), channel_id=1, source_target_pairs={{0,6},{2,0},{4,2},{6,4},{64,70},{66,64},{68,66},{70,68},{1,7},{3,1... | collective-permute-start | bytes 1376264 | tf_op jit(solution)/shard_map/ppermute | solution.py:381
  123.0 15.0 %collective-permute-start.11 = (bf16[64,3584]{1,0:T(8,128)(2,1)S(1)}, bf16[64,3584]{1,0:T(8,128)(2,1)S(1)}, u32[]{:S(2)}, u32[]{:S(2)}) collective-permute-start(bf16[64,3584]{1,0:T(8,128)(2,1)S(1)} %get-tuple-element.23), channel_id=1, source_target_pairs={{0,64},{2,66},{4,68},{6,70},{64,0},{66,2},{68,4},{70,6},{1,65},{3,... | collective-permute-start | bytes 1376264 | tf_op jit(solution)/shard_map/ppermute | solution.py:381
  124.7 23.3 %collective-permute-start.12 = (bf16[64,3584]{1,0:T(8,128)(2,1)S(1)}, bf16[64,3584]{1,0:T(8,128)(2,1)S(1)}, u32[]{:S(2)}, u32[]{:S(2)}) collective-permute-start(bf16[64,3584]{1,0:T(8,128)(2,1)S(1)} %get-tuple-element.24), channel_id=1, source_target_pairs={{0,66},{2,68},{4,70},{6,64},{64,2},{66,4},{68,6},{70,0},{1,67},{3,... | collective-permute-start | bytes 1376264 | tf_op jit(solution)/shard_map/ppermute | solution.py:381
  132.5 25.4 %collective-permute-start.13 = (bf16[64,3584]{1,0:T(8,128)(2,1)S(1)}, bf16[64,3584]{1,0:T(8,128)(2,1)S(1)}, u32[]{:S(2)}, u32[]{:S(2)}) collective-permute-start(bf16[64,3584]{1,0:T(8,128)(2,1)S(1)} %get-tuple-element.25), channel_id=1, source_target_pairs={{0,68},{2,70},{4,64},{6,66},{64,4},{66,6},{68,0},{70,2},{1,69},{3,... | collective-permute-start | bytes 1376264 | tf_op jit(solution)/shard_map/ppermute | solution.py:381
  138.0 26.8 %collective-permute-start.14 = (bf16[64,3584]{1,0:T(8,128)(2,1)S(1)}, bf16[64,3584]{1,0:T(8,128)(2,1)S(1)}, u32[]{:S(2)}, u32[]{:S(2)}) collective-permute-start(bf16[64,3584]{1,0:T(8,128)(2,1)S(1)} %get-tuple-element.26), channel_id=1, source_target_pairs={{0,70},{2,64},{4,66},{6,68},{64,6},{66,0},{68,2},{70,4},{1,71},{3,... | collective-permute-start | bytes 1376264 | tf_op jit(solution)/shard_map/ppermute | solution.py:381
  148.0 18.1 %collective-permute-start.8 = (bf16[64,3584]{1,0:T(8,128)(2,1)S(1)}, bf16[64,3584]{1,0:T(8,128)(2,1)S(1)}, u32[]{:S(2)}, u32[]{:S(2)}) collective-permute-start(bf16[64,3584]{1,0:T(8,128)(2,1)S(1)} %get-tuple-element.20), channel_id=1, source_target_pairs={{0,2},{2,4},{4,6},{6,0},{64,66},{66,68},{68,70},{70,64},{1,3},{3,5... | collective-permute-start | bytes 1376264 | tf_op jit(solution)/shard_map/ppermute | solution.py:381
  157.9 17.9 %collective-permute-start.9 = (bf16[64,3584]{1,0:T(8,128)(2,1)S(1)}, bf16[64,3584]{1,0:T(8,128)(2,1)S(1)}, u32[]{:S(2)}, u32[]{:S(2)}) collective-permute-start(bf16[64,3584]{1,0:T(8,128)(2,1)S(1)} %get-tuple-element.21), channel_id=1, source_target_pairs={{0,4},{2,6},{4,0},{6,2},{64,68},{66,70},{68,64},{70,66},{1,5},{3,7... | collective-permute-start | bytes 1376264 | tf_op jit(solution)/shard_map/ppermute | solution.py:381
  164.8 21.4 %collective-permute-start.18 = (bf16[256,1792]{1,0:T(8,128)(2,1)S(1)}, bf16[256,1792]{1,0:T(8,128)(2,1)}, u32[]{:S(2)}, u32[]{:S(2)}) collective-permute-start(bf16[256,1792]{1,0:T(8,128)(2,1)S(1)} %get-tuple-element.29.w0), channel_id=1, source_target_pairs={{0,128},{128,0},{1,129},{129,1},{2,130},{130,2},{3,131},{131,3},{4... | collective-permute-start | bytes 2752520 | tf_op jit(solution)/shard_map/ppermute | solution.py:373
  166.1 20.1 %collective-permute-start.20 = (bf16[256,1792]{1,0:T(8,128)(2,1)}, bf16[256,1792]{1,0:T(8,128)(2,1)}, u32[]{:S(2)}, u32[]{:S(2)}) collective-permute-start(bf16[256,1792]{1,0:T(8,128)(2,1)} %collective-permute-done.19.w2), channel_id=1, source_target_pairs={{0,128},{128,0},{1,129},{129,1},{2,130},{130,2},{3,131},{131,3},{4... | collective-permute-start | bytes 2752520 | tf_op jit(solution)/shard_map/ppermute | solution.py:373
  183.9 14.1 %collective-permute-start.17 = (bf16[512,512]{1,0:T(8,128)(2,1)S(1)}, bf16[512,512]{1,0:T(8,128)(2,1)S(1)}, u32[]{:S(2)}, u32[]{:S(2)}) collective-permute-start(bf16[512,512]{1,0:T(8,128)(2,1)S(1)} %hidden_units.1.h0), channel_id=1, source_target_pairs={{0,1},{1,0},{2,3},{3,2},{4,5},{5,4},{6,7},{7,6},{8,9},{9,8},{10,11... | collective-permute-start | bytes 1572872 | tf_op jit(solution)/shard_map/ppermute | solution.py:373
  204.2 1.3 copy-start.2
  205.4 58.2 %all-to-all-start.1 = ((bf16[64,8,1792]{2,1,0:T(8,128)(2,1)}), bf16[64,8,1792]{2,1,0:T(8,128)(2,1)S(1)}, u32[]{:S(2)}, u32[]{:S(2)}) async-start(bf16[64,8,1792]{2,1,0:T(8,128)(2,1)} %copy-done.2), calls=%async_computation.1 | async-start | bytes 3670016 | tf_op jit(solution)/shard_map/all_to_all | solution.py:459
  220.5 43.0 %copy-start.10 = (f32[32,8]{0,1:T(8,128)S(1)}, f32[32,8]{0,1:T(8,128)}, u32[]{:S(2)}) copy-start(f32[32,8]{0,1:T(8,128)} %param.24) | copy-start | bytes 3076
  220.5 43.0 %copy-start.8 = (bf16[32,576]{1,0:T(8,128)(2,1)S(1)}, bf16[32,576]{1,0:T(8,128)(2,1)}, u32[]{:S(2)}) copy-start(bf16[32,576]{1,0:T(8,128)(2,1)} %param.21) | copy-start | bytes 110596
  262.5 29.7 %copy-start.1 = (bf16[32,32,640]{2,1,0:T(8,128)(2,1)S(1)}, bf16[32,32,640]{2,1,0:T(8,128)(2,1)}, u32[]{:S(2)}) copy-start(bf16[32,32,640]{2,1,0:T(8,128)(2,1)} %compact.1.mine) | copy-start | bytes 3932164
  262.5 29.7 %collective-permute-start = (bf16[32,32,640]{2,1,0:T(8,128)(2,1)}, bf16[32,32,640]{2,1,0:T(8,128)(2,1)}, u32[]{:S(2)}, u32[]{:S(2)}) collective-permute-start(bf16[32,32,640]{2,1,0:T(8,128)(2,1)} %compact.1.mine), channel_id=1, source_target_pairs={{0,1},{1,0},{2,3},{3,2},{4,5},{5,4},{6,7},{7,6},{8,9},{9,8},{10,11... | collective-permute-start | bytes 3932168 | tf_op jit(solution)/shard_map/ppermute | solution.py:373
  292.2 1.3 copy-start.6

commit v2 on v1

v2 whole, which is shorter than its diff:
```python
import jax
import jax.numpy as jnp
import numpy as np
from jax import lax
from jax.experimental import pallas as pl
from jax.experimental.pallas import tpu as pltpu
from jax.sharding import Mesh, PartitionSpec as P

F32, BF16, I32 = jnp.float32, jnp.bfloat16, jnp.int32
LATENT_WIDTH = 512
BLOCK = 128
MAXLEN = 64
LATENT = 576
LANES = 640
D = 3584
HALF_D = 1792
TRAJ = 32
CAP = 8
NZ, NY, NX = 8, 4, 2
EP = NZ * NY * NX
SCORE_SCALE = 192.0 ** (-0.5)
MB = 1024 * 1024

SMEM = pltpu.SMEM
PLANE_MAJOR = np.arange(EP, dtype=np.int32).reshape(NX, NZ, NY).transpose(0, 2, 1).reshape(-1)


def whole(shape):
    return pl.BlockSpec(shape, lambda *_: (0,) * len(shape))


def smem():
    return pl.BlockSpec(memory_space=SMEM)


def hbm(*arrays):
    kept = tuple(pltpu.with_memory_space_constraint(x, pltpu.HBM) for x in arrays)
    return kept if len(kept) > 1 else kept[0]


def in_hbm(shape):
    return jax.ShapeDtypeStruct(shape, BF16)


def params(mb):
    return pltpu.CompilerParams(vmem_limit_bytes=mb * MB)


def cost(flops, nbytes):
    return pl.CostEstimate(flops=int(flops), bytes_accessed=int(nbytes), transcendentals=0)


def scaled_blocks(out, value, scale_at):
    for a in range(2):
        for f in range(2):
            rows, cols = slice(a * BLOCK, (a + 1) * BLOCK), slice(f * BLOCK, (f + 1) * BLOCK)
            out[rows, cols] = (value[0, rows, cols].astype(F32) * scale_at(a, f)).astype(BF16)


def wide_kernel(late_ref, gs, us, gv, uv, g_out, u_out):
    step = pl.program_id(0)
    scaled_blocks(g_out, gv, lambda a, f: gs[(step * 2 + a) * 2 + f])
    scaled_blocks(u_out, uv, lambda a, f: us[(step * 2 + a) * 2 + f])


def scale_wide(late, gate_value, gate_scale, up_value, up_scale):
    value = pl.BlockSpec((1, 256, 256), lambda i: (0, i, 0))
    return pl.pallas_call(
        wide_kernel,
        grid=(14,),
        in_specs=[smem(), smem(), smem(), value, value],
        out_specs=[pl.BlockSpec((256, 256), lambda i: (i, 0))] * 2,
        out_shape=[in_hbm((D, 256))] * 2,
        compiler_params=params(16),
        cost_estimate=cost(2e6, 7e6),
        name="scale_wide",
    )(
        late,
        gate_scale.astype(F32).reshape(-1),
        up_scale.astype(F32).reshape(-1),
        *hbm(gate_value, up_value),
    )


def down_panel_kernel(tp_ref, ds, dv, keep_out, send_out):
    step = pl.program_id(0)
    half = jnp.where(step < 7, 1 - tp_ref[0], tp_ref[0])
    column = half * 14 + jnp.where(step < 7, step, step - 7) * 2

    @pl.when(step < 7)
    def _():
        scaled_blocks(send_out, dv, lambda a, f: ds[a * 28 + column + f])

    @pl.when(step >= 7)
    def _():
        scaled_blocks(keep_out, dv, lambda a, f: ds[a * 28 + column + f])


def scale_down(tp_index, down_value, down_scale):
    def value_at(i, t):
        return (0, 0, jnp.where(i < 7, (1 - t[0]) * 7 + i, t[0] * 7 + i - 7))

    return pl.pallas_call(
        down_panel_kernel,
        grid_spec=pltpu.PrefetchScalarGridSpec(
            num_scalar_prefetch=1,
            grid=(14,),
            in_specs=[smem(), pl.BlockSpec((1, 256, 256), value_at)],
            out_specs=[
                pl.BlockSpec((256, 256), lambda i, t: (0, jnp.maximum(i - 7, 0))),
                pl.BlockSpec((256, 256), lambda i, t: (0, jnp.minimum(i, 6))),
            ],
        ),
        out_shape=[in_hbm((256, HALF_D))] * 2,
        compiler_params=params(16),
        cost_estimate=cost(1e6, 4e6),
        name="scale_down",
    )(tp_index, down_scale.astype(F32).reshape(-1), hbm(down_value))


def named_by(routing, experts):
    marks = jnp.zeros((routing.shape[0], experts.shape[1]), F32)
    for k in range(routing.shape[1]):
        marks = marks + (routing[:, k : k + 1] == experts).astype(F32)
    return marks


def earlier(marks):
    n = marks.shape[0]
    lower = (
        lax.broadcasted_iota(I32, (n, n), 0) > lax.broadcasted_iota(I32, (n, n), 1)
    ).astype(BF16)
    return jnp.dot(lower, marks.astype(BF16), preferred_element_type=F32)


def pick_kernel(place_ref, *refs):
    names, blocks, outs, chosen_ref = refs[:NZ], refs[NZ : 2 * NZ], refs[2 * NZ : -1], refs[-1]

    @pl.when(pl.program_id(0) == 0)
    def _():
        xh, z, y = place_ref[0], place_ref[1], place_ref[2]
        column = lax.broadcasted_iota(I32, (1, EP), 1)
        peer, slot = column >> 3, column & 7
        experts = (((peer >> 2) ^ xh) * NZ + z) * NY + (((peer & 3) + y) & 3)
        for b, name in enumerate(names):
            marks = named_by(name[...].astype(F32).astype(I32)[:, :8], experts)
            chosen_ref[b] = jnp.where(earlier(marks) == slot.astype(F32), marks, 0.0).astype(BF16)

    for b, block in enumerate(blocks):
        rows = lax.dot_general(
            chosen_ref[b],
            block[...],
            (((0,), (0,)), ((), ())),
            preferred_element_type=F32,
        ).astype(BF16)
        for r, out in enumerate(outs):
            out[b * CAP : (b + 1) * CAP, :] = rows[r * CAP : (r + 1) * CAP, :]


def pick_rows(place, blocks):
    wide = 896
    return pl.pallas_call(
        pick_kernel,
        grid=(D // wide,),
        in_specs=[smem()]
        + [pl.BlockSpec((TRAJ, BLOCK), lambda i: (0, D // BLOCK))] * NZ
        + [pl.BlockSpec((TRAJ, wide), lambda i: (0, i))] * NZ,
        out_specs=[pl.BlockSpec((NZ * CAP, wide), lambda i: (0, i))] * 8,
        out_shape=[in_hbm((NZ * CAP, D))] * 8,
        scratch_shapes=[pltpu.VMEM((NZ, TRAJ, EP), BF16)],
        compiler_params=params(16),
        cost_estimate=cost(1e9, 6e6),
        name="pick_rows",
    )(place, *blocks, *blocks)


def hidden_kernel(*refs):
    tokens, (g0, g1, u0, u1, out), (acc_g, acc_u) = refs[:8], refs[8:13], refs[13:]
    step = pl.program_id(0)

    @pl.when(step == 0)
    def _():
        acc_g[...] = jnp.zeros_like(acc_g)
        acc_u[...] = jnp.zeros_like(acc_u)

    x = jnp.concatenate([t[...] for t in tokens], axis=0)
    acc_g[:, :256] += jnp.dot(x, g0[...], preferred_element_type=F32)
    acc_u[:, :256] += jnp.dot(x, u0[...], preferred_element_type=F32)
    acc_g[:, 256:] += jnp.dot(x, g1[...], preferred_element_type=F32)
    acc_u[:, 256:] += jnp.dot(x, u1[...], preferred_element_type=F32)

    @pl.when(step == pl.num_programs(0) - 1)
    def _():
        g = acc_g[...]
        out[...] = (g / (1.0 + jnp.exp(-g)) * acc_u[...]).astype(BF16)


def hidden_units(tokens, g0, g1, u0, u1):
    depth = 512
    return pl.pallas_call(
        hidden_kernel,
        grid=(D // depth,),
        in_specs=[pl.BlockSpec((64, depth), lambda k: (0, k))] * 8
        + [pl.BlockSpec((depth, 256), lambda k: (k, 0))] * 4,
        out_specs=whole((512, 512)),
        out_shape=jax.ShapeDtypeStruct((512, 512), BF16),
        scratch_shapes=[pltpu.VMEM((512, 512), F32)] * 2,
        compiler_params=params(24),
        cost_estimate=cost(3.8e9, 12e6),
        name="hidden_units",
    )(*tokens, g0, g1, u0, u1)


def down_kernel(order_ref, h0, h1, w0, w1, w2, w3, out):
    h = jnp.concatenate([h0[...], h1[...]], axis=1)
    w = jnp.concatenate([w0[...], w1[...], w2[...], w3[...]], axis=0)
    rows = jnp.dot(h, w, preferred_element_type=F32)
    for group in range(EP):
        out[order_ref[group]] = rows[group * CAP : (group + 1) * CAP, :].astype(BF16)


def down_rows(order, h0, h1, weights):
    wide = 256
    return pl.pallas_call(
        down_kernel,
        grid=(HALF_D // wide,),
        in_specs=[smem(), whole((512, 512)), whole((512, 512))]
        + [pl.BlockSpec((256, wide), lambda i: (0, i))] * 4,
        out_specs=pl.BlockSpec((EP, CAP, wide), lambda i: (0, 0, i)),
        out_shape=in_hbm((EP, CAP, HALF_D)),
        compiler_params=params(24),
        cost_estimate=cost(1.9e9, 7e6),
        name="down_rows",
    )(order, h0, h1, *weights)


def blend_kernel(routing_ref, weight_ref, rows_ref, out):
    column = lax.broadcasted_iota(I32, (1, EP * CAP), 1)
    experts, slot = column >> 3, column & 7
    routing, weight = routing_ref[...], weight_ref[...]
    marks = jnp.zeros((TRAJ, EP * CAP), F32)
    share = jnp.zeros((TRAJ, EP * CAP), F32)
    for k in range(8):
        hit = routing[:, k : k + 1] == experts
        marks = marks + hit.astype(F32)
        share = share + jnp.where(hit, weight[:, k : k + 1], 0.0)
    share = jnp.where(earlier(marks) == slot.astype(F32), share, 0.0)
    high = share.astype(BF16)
    low = (share - high.astype(F32)).astype(BF16)
    rows = rows_ref[...].reshape(EP * CAP, rows_ref.shape[2])
    out[...] = (
        jnp.dot(high, rows, preferred_element_type=F32)
        + jnp.dot(low, rows, preferred_element_type=F32)
    ).astype(BF16)


def blend(routing, weight, rows):
    wide = 896
    return pl.pallas_call(
        blend_kernel,
        grid=(HALF_D // wide,),
        in_specs=[
            whole((TRAJ, 8)),
            whole((TRAJ, 8)),
            pl.BlockSpec((EP, CAP, wide), lambda i: (0, 0, i)),
        ],
        out_specs=pl.BlockSpec((TRAJ, wide), lambda i: (0, i)),
        out_shape=jax.ShapeDtypeStruct((TRAJ, HALF_D), BF16),
        compiler_params=params(16),
        cost_estimate=cost(1e8, 2e6),
        name="blend",
    )(routing, weight, rows)


def collect_kernel(index_ref, pages, out):
    step = pl.program_id(0)
    lane = lax.broadcasted_iota(I32, (32, LANES - LATENT), 1)
    for i in range(8):
        j = step * 8 + i
        out[i, 0:16, 0:LATENT] = pages[index_ref[j, 0]]
        out[i, 16:32, 0:LATENT] = pages[index_ref[j, 1]]
        slot, length = index_ref[j, 2].astype(F32), index_ref[j, 3].astype(F32)
        out[i, :, LATENT:LANES] = jnp.where(lane == 0, slot, length).astype(BF16)


def collect(index, pages):
    return pl.pallas_call(
        collect_kernel,
        grid=(EP // 8,),
        in_specs=[smem(), whole(pages.shape)],
        out_specs=pl.BlockSpec((8, 32, LANES), lambda i: (i, 0, 0)),
        out_shape=in_hbm((EP, 32, LANES)),
        compiler_params=params(16),
        cost_estimate=cost(1e6, 6e6),
        name="collect",
    )(index, pages)


def regroup_kernel(midway, out):
    out[0] = midway[:, 0]


def regroup(midway):
    return pl.pallas_call(
        regroup_kernel,
        grid=(8,),
        in_specs=[pl.BlockSpec((8, 1, 32, LANES), lambda i: (0, i, 0, 0))],
        out_specs=pl.BlockSpec((1, 8, 32, LANES), lambda i: (i, 0, 0, 0)),
        out_shape=in_hbm((8, 8, 32, LANES)),
        compiler_params=params(8),
        cost_estimate=cost(1e6, 6e6),
        name="regroup",
    )(midway)


def compact_kernel(source_ref, arrived, out):
    step = pl.program_id(0)
    for i in range(8):
        out[i] = arrived[source_ref[step * 8 + i]]


def compact(source, arrived):
    return pl.pallas_call(
        compact_kernel,
        grid=(TRAJ // 8,),
        in_specs=[smem(), whole(arrived.shape)],
        out_specs=pl.BlockSpec((8, 32, LANES), lambda i: (i, 0, 0)),
        out_shape=in_hbm((TRAJ, 32, LANES)),
        compiler_params=params(16),
        cost_estimate=cost(1e6, 4e6),
        name="compact",
    )(source, arrived)


ATTEND_STEP = 8


def attend_kernel(tp_ref, length_ref, mine, other, queries, fresh, cache_out, out):
    step = pl.program_id(0)
    first = tp_ref[0] == 0
    row = lax.broadcasted_iota(I32, (MAXLEN, LATENT), 0).astype(F32).astype(BF16)
    column = lax.broadcasted_iota(I32, (TRAJ, MAXLEN), 1)
    scores = []
    for i in range(ATTEND_STEP):
        length = length_ref[step * ATTEND_STEP + i]
        edge = length.astype(F32).astype(BF16)
        a, b = mine[i, :, :LATENT], other[i, :, :LATENT]
        old = jnp.concatenate([jnp.where(first, a, b), jnp.where(first, b, a)], axis=0)
        new = jnp.broadcast_to(fresh[i], (MAXLEN, LATENT))
        zero = jnp.zeros((), BF16)
        cache = jnp.where(row < edge, old, jnp.where(row == edge, new, zero))
        cache_out[i] = cache
        score = lax.dot_general(
            queries[i], cache, (((1,), (1,)), ((), ())), preferred_element_type=F32
        )
        scores.append(jnp.where(column <= length, score * SCORE_SCALE, -jnp.inf))
    scores = jnp.concatenate(scores, axis=0)
    top = jnp.max(scores, axis=1, keepdims=True)
    weight = jnp.exp(scores - top)
    weight = (weight * (1.0 / jnp.sum(weight, axis=1, keepdims=True))).astype(BF16)
    for i in range(ATTEND_STEP):
        out[i] = jnp.dot(
            weight[i * TRAJ : (i + 1) * TRAJ],
            cache_out[i, :, :LATENT_WIDTH],
            preferred_element_type=F32,
        ).astype(BF16)


def attend(tp_index, length, mine, other, queries, fresh):
    n = ATTEND_STEP
    return pl.pallas_call(
        attend_kernel,
        grid=(TRAJ // n,),
        in_specs=[
            smem(),
            smem(),
            pl.BlockSpec((n, 32, LANES), lambda i: (i, 0, 0)),
            pl.BlockSpec((n, 32, LANES), lambda i: (i, 0, 0)),
            pl.BlockSpec((n, 32, LATENT), lambda i: (i, 0, 0)),
            pl.BlockSpec((n, 1, LATENT), lambda i: (i, 0, 0)),
        ],
        out_specs=[
            pl.BlockSpec((n, MAXLEN, LATENT), lambda i: (i, 0, 0)),
            pl.BlockSpec((n, 32, LATENT_WIDTH), lambda i: (i, 0, 0)),
        ],
        out_shape=[
            jax.ShapeDtypeStruct((TRAJ, MAXLEN, LATENT), BF16),
            jax.ShapeDtypeStruct((TRAJ, 32, LATENT_WIDTH), BF16),
        ],
        compiler_params=params(24),
        cost_estimate=cost(2e8, 8e6),
        name="attend",
    )(tp_index, length, mine, other, hbm(queries), fresh.reshape(TRAJ, 1, LATENT))


def swap(x, axis):
    return lax.ppermute(x, axis, [(0, 1), (1, 0)])


def z_shift(x, by):
    return lax.ppermute(x, "z", [(i, (i + by) % NZ) for i in range(NZ)])


def plane_shift(x, dx, dy):
    return lax.ppermute(
        x,
        ("xh", "y"),
        [
            (a * NY + b, ((a + dx) % NX) * NY + (b + dy) % NY)
            for a in range(NX)
            for b in range(NY)
        ],
    )


def on_device(
    latent_pages,
    page_table,
    lengths,
    new_place,
    queries,
    fresh_latent,
    hidden_states,
    routing,
    route_weight,
    gate_value,
    gate_scale,
    up_value,
    up_scale,
    down_value,
    down_scale,
):
    xh, z, y, tp = (lax.axis_index(name) for name in ("xh", "z", "y", "tp"))
    tp_index = tp.astype(I32).reshape(1)
    place = jnp.stack([xh, z, y]).astype(I32)

    own = jnp.concatenate(
        [hidden_states, jnp.pad(routing.astype(BF16), ((0, 0), (0, BLOCK - 8)))], axis=1
    )
    up_way, down_way = [own, z_shift(own, 1)], [own, z_shift(own, -1)]
    down_keep, down_send = scale_down(tp_index, down_value, down_scale)

    owner, slot = new_place // TRAJ, new_place % TRAJ
    to_owner = owner[None, :] == jnp.asarray(PLANE_MAJOR)[:, None]
    mine = lax.dynamic_slice_in_dim(page_table, tp * 2, 2, 1)
    facts = jnp.concatenate([mine, slot[:, None] + 1, lengths[:, None]], axis=1)
    index = jnp.sum(jnp.where(to_owner[:, :, None], facts[None], 0), axis=1)
    index = index - (jnp.arange(4) == 2).astype(I32)[None, :]
    leaving = collect(index, latent_pages).reshape(8, 8, 32, LANES)
    leaving, up_way[1], down_way[1], down_send = lax.optimization_barrier(
        (leaving, up_way[1], down_way[1], down_send)
    )
    down_tp = swap(down_send, "tp")
    midway = lax.all_to_all(leaving, ("xh", "y"), split_axis=0, concat_axis=0, tiled=True)

    gate, up = scale_wide(tp_index, gate_value, gate_scale, up_value, up_scale)
    gate_far, up_far = swap(gate, "pool"), swap(up, "pool")
    down_far = swap(down_keep, "pool")
    for step in range(1, 4):
        up_way.append(z_shift(up_way[-1], 1))
        if step < 3:
            down_way.append(z_shift(down_way[-1], -1))
    behind = np.array([0, 1, 2, 3, 4, -1, -2, -3], np.int32)

    place, gate_far, up_far, down_far = lax.optimization_barrier(
        (place, gate_far, up_far, down_far)
    )
    picked = pick_rows(place, up_way + down_way[1:])
    tokens = [picked[0]] + [
        plane_shift(picked[dx * NY + dy], dx, dy)
        for dx in range(NX)
        for dy in range(NY)
        if dx or dy
    ]

    midway, tokens[1], tokens[2], tokens[3] = lax.optimization_barrier(
        (midway, tokens[1], tokens[2], tokens[3])
    )
    arrived = lax.all_to_all(regroup(midway), "z", split_axis=0, concat_axis=0, tiled=True)
    down_tp_far = swap(down_tp, "pool")

    act = hidden_units(tokens, gate, gate_far, up, up_far)
    act_tp = swap(act, "tp")
    group = jnp.arange(EP, dtype=I32)
    order = (
        ((xh + (group >> 5)) % NX) * NZ + (z - jnp.tile(jnp.asarray(behind), 8)) % NZ
    ) * NY + (y - (group >> 3)) % NY
    out_rows = down_rows(order, act, act_tp, [down_keep, down_far, down_tp, down_tp_far])
    arrived, out_rows = lax.optimization_barrier((arrived, out_rows))
    returned = lax.all_to_all(
        out_rows, ("xh", "z", "y"), split_axis=0, concat_axis=0, tiled=True
    )
    expert_mix = blend(routing, route_weight, returned)

    arrived = arrived.reshape(EP, 32, LANES)
    labels = arrived[:, 0, LATENT : LATENT + 2].astype(I32)
    taken = labels[:, 0][None, :] == jnp.arange(TRAJ, dtype=I32)[:, None]
    source = jnp.sum(jnp.where(taken, jnp.arange(EP, dtype=I32)[None, :], 0), axis=1)
    length = jnp.sum(jnp.where(taken, labels[:, 1][None, :], 0), axis=1)
    my_half = compact(source, arrived)
    other_half = swap(my_half, "tp")
    new_cache, attention = attend(tp_index, length, my_half, other_half, queries, fresh_latent)
    return new_cache, attention, expert_mix


def solution(mesh):
    grid = Mesh(mesh.devices.reshape(2, NX, NZ, NY, 2), ("pool", "xh", "z", "y", "tp"))
    ep = ("xh", "z", "y")
    rows = ("pool",) + ep
    placed = (
        P(rows, None, None),
        P(rows, None),
        P(rows),
        P(rows),
        P(rows, "tp", None),
        P(rows, None),
        P(rows, None),
        P(rows, None),
        P(rows, None),
        P(ep, None, ("pool", "tp")),
        P(ep, None, ("pool", "tp")),
        P(ep, None, ("pool", "tp")),
        P(ep, None, ("pool", "tp")),
        P(ep, ("pool", "tp"), None),
        P(ep, ("pool", "tp"), None),
    )
    return jax.shard_map(
        on_device,
        mesh=grid,
        in_specs=placed,
        out_specs=(P(rows, None, None), P(rows, "tp", None), P(rows, "tp")),
        check_vma=False,
    )
```

time: 308 us -> 284 us (0.922)
  Pallas kernels: 85.1 us -> 52.4 us
  waiting for transfers between devices: 148 us -> 134 us
  local copies, waits for them, and re-layouts: 10.7 us -> 22.8 us
  starting transfers between devices: 58.8 us -> 69.5 us
    ppermute x7, waiting for transfers between devices: 70.8 us -> 14.2 us  [z_shift(): return lax.ppermute(x, 'z', [(i, (i + by) % NZ) for i in range(NZ)])]
    pallas_call x4 -> x6, Pallas kernels: 55.8 us -> 28.4 us  [the longest x1 9.31 us: scale_wide(): pl.pallas_call(wide_kernel, grid=(14,), in_specs=[smem(), smem(), smem(),...]
    ppermute x7, waiting for transfers between devices: 40 us -> 66.7 us  [swap(): return lax.ppermute(x, axis, [(0, 1), (1, 0)])]
    ppermute x7, waiting for transfers between devices: 37 us -> 53.1 us  [plane_shift(): lax.ppermute(x, ('xh', 'y'), [(a * NY + b, (a + dx) % NX * NY + (b + dy)...]
    unnamed x33 -> x61, local copies, waits for them, and re-layouts: 9.69 us -> 20.6 us
    pallas_call x1, Pallas kernels: 12.9 us -> 5.02 us  [attend(): pl.pallas_call(attend_kernel, grid=(TRAJ // n,), in_specs=[smem(), smem()...]
    all_to_all x1, starting transfers between devices: 13.4 us -> 19.8 us  [on_device(): lax.all_to_all(out_rows, ('xh', 'z', 'y'), split_axis=0, concat_axis=0, t...]
    all_to_all x1 -> x2, starting transfers between devices: 14.2 us -> 17.8 us  [the longest x1 10.3 us: on_device(): lax.all_to_all(regroup(midway), 'z', split_axis=0, concat_axis=0, tiled=T...]
  transfers between devices with their start and end apart: 23 -> 24, of which waited for: 13 -> 13; matrix products, arithmetic and copies ran while one was open for 1% -> 2% of each run, Pallas kernels for 22% -> 17%
where the time goes in v2:
time: 284 us; the launch traced here: 282 us
  waiting for transfers between devices  134 us (47%)
  starting transfers between devices  69.5 us (24%)
  Pallas kernels  52.4 us (18%)
  local copies, waits for them, and re-layouts  22.8 us (8%)
    ppermute x7, waiting for transfers between devices, swap(): return lax.ppermute(x, axis, [(0, 1), (1, 0)])  66.7 us
    ppermute x7, waiting for transfers between devices, plane_shift(): lax.ppermute(x, ('xh', 'y'), [(a * NY + b, (a + dx) % NX * NY + (b + dy)...  53.1 us
    unnamed x61, local copies, waits for them, and re-layouts  20.6 us
    all_to_all x1, starting transfers between devices, on_device(): lax.all_to_all(out_rows, ('xh', 'z', 'y'), split_axis=0, concat_axis=0, t...  19.8 us
    ppermute x7, starting transfers between devices, plane_shift(): lax.ppermute(x, ('xh', 'y'), [(a * NY + b, (a + dx) % NX * NY + (b + dy)...  15.5 us
    ppermute x7, waiting for transfers between devices, z_shift(): return lax.ppermute(x, 'z', [(i, (i + by) % NZ) for i in range(NZ)])  14.2 us
    ppermute x7, starting transfers between devices, z_shift(): return lax.ppermute(x, 'z', [(i, (i + by) % NZ) for i in range(NZ)])  12.1 us
    all_to_all x1, starting transfers between devices, on_device(): lax.all_to_all(regroup(midway), 'z', split_axis=0, concat_axis=0, tiled=T...  10.3 us
  transfers between devices with their start and end apart: 24, of which 13 were waited for; matrix products, arithmetic and copies ran while one was open for 2% of the time, Pallas kernels for 17%

profile of v2, /device:TPU:68, one launch (start us, length us, event | category | flops | bytes accessed | tf_op | source)
XLA Modules:
  0.0 281.8 jit_solution(16506790968886915514)
XLA Ops:
  0.6 0.7 convert_element_type.22
  1.4 1.0 fusion.1.refs_0_.refs_8_
  2.4 2.0 collective-permute-start
  4.5 0.8 copy.50
  5.4 0.8 copy.51
  6.3 9.3 %scale_wide.1 = (bf16[3584,256]{1,0:T(8,128)(2,1)}, bf16[3584,256]{1,0:T(8,128)(2,1)}) custom-call(s32[1]{0:T(128)} %bitcast.tp_ref.late_ref, f32[56]{0:T(128)S(1)} %reshape.87.gs, f32[56]{0:T(128)S(1)} %reshape.89.us, bf16[1,3584,256]{2,1,0:T(8,128)(2,1)} %gv.1, bf16[1,3584,256]{2,1,0:T(8,128)(2,1)} %uv.1), custom_call_target="tpu_custom_call" | custom-call | flops 2000000 | bytes 7000000 | tf_op jit(solution)/shard_map/scale_wide/pallas_call | solution.py:68
  15.6 0.5 collective-permute-start.3
  16.5 3.9 %copy.48.pages = bf16[128,16,576]{2,1,0:T(8,128)(2,1)S(1)} copy(bf16[128,16,576]{0,2,1:T(8,128)(2,1)} %param.17) | data formatting | bytes 4718592 | tf_op args[0]
  20.4 7.2 %scale_down.1 = (bf16[256,1792]{1,0:T(8,128)(2,1)S(1)}, bf16[256,1792]{1,0:T(8,128)(2,1)S(1)}) custom-call(s32[1]{0:T(128)} %bitcast.tp_ref.late_ref, f32[56]{0:T(128)S(1)} %reshape.85.ds, bf16[1,256,3584]{2,1,0:T(8,128)(2,1)} %dv.1), custom_call_target="tpu_custom_call" | custom-call | flops 1000000 | bytes 4000000 | tf_op jit(solution)/shard_map/scale_down/pallas_call | solution.py:103
  27.6 0.9 copy-done.5
  28.6 0.9 copy-done.7
  29.5 4.5 %collect.1 = bf16[64,32,640]{2,1,0:T(8,128)(2,1)} custom-call(s32[64,4]{1,0:T(8,128)S(1)} %broadcast_subtract_fusion.index_ref, bf16[128,16,576]{2,1,0:T(8,128)(2,1)S(1)} %copy.48.pages), custom_call_target="tpu_custom_call" | custom-call | flops 1000000 | bytes 6000000 | tf_op jit(solution)/shard_map/collect/pallas_call | solution.py:287
  34.0 7.4 %all-to-all-start = ((bf16[8,8,32,640]{3,2,1,0:T(8,128)(2,1)}), bf16[8,8,32,640]{3,2,1,0:T(8,128)(2,1)S(1)}, u32[]{:S(2)}, u32[]{:S(2)}) async-start(bf16[8,8,32,640]{3,2,1,0:T(8,128)(2,1)} %bitcast.3), calls=%async_computation | async-start | bytes 5242880 | tf_op jit(solution)/shard_map/all_to_all | solution.py:454
  41.4 3.0 %collective-permute-start.5 = (bf16[32,3712]{1,0:T(8,128)(2,1)S(1)}, bf16[32,3712]{1,0:T(8,128)(2,1)S(1)}, u32[]{:S(2)}, u32[]{:S(2)}) collective-permute-start(bf16[32,3712]{1,0:T(8,128)(2,1)S(1)} %collective-permute-done.refs_1_.refs_9_), channel_id=1, source_target_pairs={{0,8},{8,16},{16,24},{24,32},{32,40},{40,48},{48,56},{56,0},{1,9},... | collective-permute-start | bytes 712712 | tf_op jit(solution)/shard_map/ppermute | solution.py:401
  44.5 5.7 %collective-permute-done.5.refs_2_.refs_10_ = bf16[32,3712]{1,0:T(8,128)(2,1)S(1)} collective-permute-done((bf16[32,3712]{1,0:T(8,128)(2,1)S(1)}, bf16[32,3712]{1,0:T(8,128)(2,1)S(1)}, u32[]{:S(2)}, u32[]{:S(2)}) %collective-permute-start.5) | collective-permute-done | bytes 237600 | tf_op jit(solution)/shard_map/ppermute | solution.py:401
  50.2 3.2 %collective-permute-start.6 = (bf16[32,3712]{1,0:T(8,128)(2,1)S(1)}, bf16[32,3712]{1,0:T(8,128)(2,1)}, u32[]{:S(2)}, u32[]{:S(2)}) collective-permute-start(bf16[32,3712]{1,0:T(8,128)(2,1)S(1)} %collective-permute-done.5.refs_2_.refs_10_), channel_id=1, source_target_pairs={{0,8},{8,16},{16,24},{24,32},{32,40},{40,48},{48,56},{56,0},{1,9},... | collective-permute-start | bytes 712712 | tf_op jit(solution)/shard_map/ppermute | solution.py:401
  53.4 0.7 copy-done.3
  54.1 4.2 %collective-permute-done.6.refs_3_.refs_11_ = bf16[32,3712]{1,0:T(8,128)(2,1)} collective-permute-done((bf16[32,3712]{1,0:T(8,128)(2,1)S(1)}, bf16[32,3712]{1,0:T(8,128)(2,1)}, u32[]{:S(2)}, u32[]{:S(2)}) %collective-permute-start.6) | collective-permute-done | bytes 237600 | tf_op jit(solution)/shard_map/ppermute | solution.py:401
  58.3 3.7 %collective-permute-start.7 = (bf16[32,3712]{1,0:T(8,128)(2,1)}, bf16[32,3712]{1,0:T(8,128)(2,1)}, u32[]{:S(2)}, u32[]{:S(2)}) collective-permute-start(bf16[32,3712]{1,0:T(8,128)(2,1)} %collective-permute-done.6.refs_3_.refs_11_), channel_id=1, source_target_pairs={{0,8},{8,16},{16,24},{24,32},{32,40},{40,48},{48,56},{56,0},{1,9},... | collective-permute-start | bytes 712712 | tf_op jit(solution)/shard_map/ppermute | solution.py:401
  62.1 1.4 collective-permute-done.9.refs_7_.refs_15_
  63.5 2.9 %collective-permute-done.7.refs_4_.refs_12_ = bf16[32,3712]{1,0:T(8,128)(2,1)} collective-permute-done((bf16[32,3712]{1,0:T(8,128)(2,1)}, bf16[32,3712]{1,0:T(8,128)(2,1)}, u32[]{:S(2)}, u32[]{:S(2)}) %collective-permute-start.7) | collective-permute-done | bytes 237600 | tf_op jit(solution)/shard_map/ppermute | solution.py:401
  66.4 0.9 copy-done.4
  67.3 4.6 %pick_rows.1 = (bf16[64,3584]{1,0:T(8,128)(2,1)S(1)}, bf16[64,3584]{1,0:T(8,128)(2,1)S(1)}, bf16[64,3584]{1,0:T(8,128)(2,1)S(1)}, bf16[64,3584]{1,0:T(8,128)(2,1...) custom-call(s32[3]{0:T(128)S(1)} %pad_add_fusion.1.place_ref, ...), custom_call_target="tpu_custom_call" | custom-call | flops 1000000000 | bytes 6000000 | tf_op jit(solution)/shard_map/pick_rows/pallas_call | solution.py:162
  71.9 0.8 copy-done.9
  72.7 0.8 copy-done.11
  73.5 0.8 copy-done.12
  74.3 0.8 copy-done.15
  75.1 0.8 copy-done.18
  75.8 1.5 collective-permute-start.10
  77.3 2.7 collective-permute-start.11
  80.0 1.5 collective-permute-start.12
  81.4 8.2 %collective-permute-done.10.refs_1_ = bf16[64,3584]{1,0:T(8,128)(2,1)S(1)} collective-permute-done((bf16[64,3584]{1,0:T(8,128)(2,1)S(1)}, bf16[64,3584]{1,0:T(8,128)(2,1)S(1)}, u32[]{:S(2)}, u32[]{:S(2)}) %collective-permute-start.10) | collective-permute-done | bytes 458784 | tf_op jit(solution)/shard_map/ppermute | solution.py:405
  89.6 0.8 copy-done.13
  90.4 8.1 %collective-permute-done.11.refs_2_ = bf16[64,3584]{1,0:T(8,128)(2,1)S(1)} collective-permute-done((bf16[64,3584]{1,0:T(8,128)(2,1)S(1)}, bf16[64,3584]{1,0:T(8,128)(2,1)S(1)}, u32[]{:S(2)}, u32[]{:S(2)}) %collective-permute-start.11) | collective-permute-done | bytes 458784 | tf_op jit(solution)/shard_map/ppermute | solution.py:405
  98.5 0.8 copy-done.16
  99.3 0.8 copy-done.19
  100.1 0.6 regroup.1
  100.7 1.5 copy-done.1
  102.2 10.3 %all-to-all-start.1 = ((bf16[8,8,32,640]{3,2,1,0:T(8,128)(2,1)}), bf16[8,8,32,640]{3,2,1,0:T(8,128)(2,1)S(1)}, u32[]{:S(2)}, u32[]{:S(2)}) async-start(bf16[8,8,32,640]{3,2,1,0:T(8,128)(2,1)} %copy-done.1), calls=%async_computation.1 | async-start | bytes 5242880 | tf_op jit(solution)/shard_map/all_to_all | solution.py:479
  112.5 1.2 collective-permute-start.18
  113.7 3.6 %collective-permute-start.14 = (bf16[64,3584]{1,0:T(8,128)(2,1)}, bf16[64,3584]{1,0:T(8,128)(2,1)S(1)}, u32[]{:S(2)}, u32[]{:S(2)}) collective-permute-start(bf16[64,3584]{1,0:T(8,128)(2,1)} %copy-done.15), channel_id=1, source_target_pairs={{0,66},{2,68},{4,70},{6,64},{64,2},{66,4},{68,6},{70,0},{1,67},{3,... | collective-permute-start | bytes 1376264 | tf_op jit(solution)/shard_map/ppermute | solution.py:405
  117.3 1.8 collective-permute-start.15
  119.1 4.5 %collective-permute-start.16 = (bf16[64,3584]{1,0:T(8,128)(2,1)}, bf16[64,3584]{1,0:T(8,128)(2,1)S(1)}, u32[]{:S(2)}, u32[]{:S(2)}) collective-permute-start(bf16[64,3584]{1,0:T(8,128)(2,1)} %copy-done.11), channel_id=1, source_target_pairs={{0,70},{2,64},{4,66},{6,68},{64,6},{66,0},{68,2},{70,4},{1,71},{3,... | collective-permute-start | bytes 1376264 | tf_op jit(solution)/shard_map/ppermute | solution.py:405
  123.6 12.3 %collective-permute-done.18.w2 = bf16[256,1792]{1,0:T(8,128)(2,1)} collective-permute-done((bf16[256,1792]{1,0:T(8,128)(2,1)S(1)}, bf16[256,1792]{1,0:T(8,128)(2,1)}, u32[]{:S(2)}, u32[]{:S(2)}) %collective-permute-start.18) | collective-permute-done | bytes 917536 | tf_op jit(solution)/shard_map/ppermute | solution.py:397
  135.9 8.8 %collective-permute-done.13.refs_4_ = bf16[64,3584]{1,0:T(8,128)(2,1)S(1)} collective-permute-done((bf16[64,3584]{1,0:T(8,128)(2,1)}, bf16[64,3584]{1,0:T(8,128)(2,1)S(1)}, u32[]{:S(2)}, u32[]{:S(2)}) %collective-permute-start.13) | collective-permute-done | bytes 458784 | tf_op jit(solution)/shard_map/ppermute | solution.py:405
  144.7 14.7 %collective-permute-done.14.refs_5_ = bf16[64,3584]{1,0:T(8,128)(2,1)S(1)} collective-permute-done((bf16[64,3584]{1,0:T(8,128)(2,1)}, bf16[64,3584]{1,0:T(8,128)(2,1)S(1)}, u32[]{:S(2)}, u32[]{:S(2)}) %collective-permute-start.14) | collective-permute-done | bytes 458784 | tf_op jit(solution)/shard_map/ppermute | solution.py:405
  159.4 7.1 %collective-permute-done.15.refs_6_ = bf16[64,3584]{1,0:T(8,128)(2,1)S(1)} collective-permute-done((bf16[64,3584]{1,0:T(8,128)(2,1)}, bf16[64,3584]{1,0:T(8,128)(2,1)S(1)}, u32[]{:S(2)}, u32[]{:S(2)}) %collective-permute-start.15) | collective-permute-done | bytes 458784 | tf_op jit(solution)/shard_map/ppermute | solution.py:405
  166.6 6.2 %collective-permute-done.16.refs_7_ = bf16[64,3584]{1,0:T(8,128)(2,1)S(1)} collective-permute-done((bf16[64,3584]{1,0:T(8,128)(2,1)}, bf16[64,3584]{1,0:T(8,128)(2,1)S(1)}, u32[]{:S(2)}, u32[]{:S(2)}) %collective-permute-start.16) | collective-permute-done | bytes 458784 | tf_op jit(solution)/shard_map/ppermute | solution.py:405
  172.8 1.0 copy-done.10
  173.8 1.0 copy-done.14
  174.8 1.0 copy-done.17
  175.8 1.0 copy-done.20
  176.8 9.3 %hidden_units.1.h0 = bf16[512,512]{1,0:T(8,128)(2,1)} custom-call(bf16[64,3584]{1,0:T(8,128)(2,1)S(1)} %copy-done.10, bf16[64,3584]{1,0:T(8,128)(2,1)S(1)} %copy-done.14, bf16[64,3584]{1,0:T(8,128)(2,1)S(1)} %copy-done.17, bf16[64,3584]{1,0:T(8,128)(2,1)S(1)} %copy-done.20, bf16[64,3584]{1,0:T(8,128)(2,1)S(1)} %collective-permute-done.13.refs_4_, ...), custom_call_target="tpu_custom_call" | custom-call | flops 3800000000 | bytes 12000000 | tf_op jit(solution)/shard_map/hidden_units/pallas_call | solution.py:200
  186.1 1.7 collective-permute-start.17
  188.0 9.8 %collective-permute-done.17.h1 = bf16[512,512]{1,0:T(8,128)(2,1)} collective-permute-done((bf16[512,512]{1,0:T(8,128)(2,1)}, bf16[512,512]{1,0:T(8,128)(2,1)}, u32[]{:S(2)}, u32[]{:S(2)}) %collective-permute-start.17) | collective-permute-done | bytes 524320 | tf_op jit(solution)/shard_map/ppermute | solution.py:397
  197.7 6.5 %down_rows.1 = bf16[64,8,1792]{2,1,0:T(8,128)(2,1)S(1)} custom-call(s32[64]{0:T(128)S(1)} %fusion.3.order_ref, bf16[512,512]{1,0:T(8,128)(2,1)} %hidden_units.1.h0, bf16[512,512]{1,0:T(8,128)(2,1)} %collective-permute-done.17.h1, bf16[256,1792]{1,0:T(8,128)(2,1)S(1)} %copy-done.6, bf16[256,1792]{1,0:T(8,128)(2,1)} %collective-permute-done.4.w1, ...), custom_call_target="tpu_custom_call" | custom-call | flops 1900000000 | bytes 7000000 | tf_op jit(solution)/shard_map/down_rows/pallas_call | solution.py:224
  204.3 1.2 copy-done.2
  205.5 19.8 %all-to-all-start.2 = ((bf16[64,8,1792]{2,1,0:T(8,128)(2,1)}), bf16[64,8,1792]{2,1,0:T(8,128)(2,1)}, u32[]{:S(2)}, u32[]{:S(2)}) async-start(bf16[64,8,1792]{2,1,0:T(8,128)(2,1)} %copy-done.2), calls=%async_computation.2 | async-start | bytes 3670016 | tf_op jit(solution)/shard_map/all_to_all | solution.py:490
  225.5 0.1 select_reduce_fusion.1
  225.7 2.2 compact.1.mine
  227.9 0.9 collective-permute-start.20
  229.1 44.6 %collective-permute-done.20.other = bf16[32,32,640]{2,1,0:T(8,128)(2,1)S(1)} collective-permute-done((bf16[32,32,640]{2,1,0:T(8,128)(2,1)}, bf16[32,32,640]{2,1,0:T(8,128)(2,1)S(1)}, u32[]{:S(2)}, u32[]{:S(2)}) %collective-permute-start.20) | collective-permute-done | bytes 1310752 | tf_op jit(solution)/shard_map/ppermute | solution.py:397
  273.7 5.0 %attend.1 = (bf16[32,64,576]{2,1,0:T(8,128)(2,1)}, bf16[32,32,512]{2,1,0:T(8,128)(2,1)}) custom-call(s32[1]{0:T(128)} %bitcast.tp_ref.late_ref, s32[32]{0:T(128)S(1)} %get-tuple-element.60.length_ref, bf16[32,32,640]{2,1,0:T(8,128)(2,1)} %compact.1.mine, bf16[32,32,640]{2,1,0:T(8,128)(2,1)S(1)} %collective-permute-done.20.other, ...), custom_call_target="tpu_custom_call" | custom-call | flops 200000000 | bytes 8000000 | tf_op jit(solution)/shard_map/attend/pallas_call | solution.py:371
  278.7 3.1 %blend.1 = bf16[32,1792]{1,0:T(8,128)(2,1)} custom-call(s32[32,8]{1,0:T(8,128)S(1)} %copy.54.routing_ref, f32[32,8]{1,0:T(8,128)S(1)} %copy.55.weight_ref, bf16[64,8,1792]{2,1,0:T(8,128)(2,1)} %all-to-all-done.2.rows_ref), custom_call_target="tpu_custom_call" | custom-call | flops 100000000 | bytes 2000000 | tf_op jit(solution)/shard_map/blend/pallas_call | solution.py:259
  (81 shorter events, 1.5 us)
Async XLA Ops:
  0.6 15.5 %copy-start = (s32[32,4]{0,1:T(4,128)S(1)}, s32[32,4]{0,1:T(4,128)}, u32[]{:S(2)}) copy-start(s32[32,4]{0,1:T(4,128)} %param.18) | copy-start | bytes 1540
  2.4 31.6 %collective-permute-start = (bf16[32,3712]{1,0:T(8,128)(2,1)S(1)}, bf16[32,3712]{1,0:T(8,128)(2,1)S(1)}, u32[]{:S(2)}, u32[]{:S(2)}) collective-permute-start(bf16[32,3712]{1,0:T(8,128)(2,1)S(1)} %fusion.1.refs_0_.refs_8_), channel_id=1, source_target_pairs={{0,8},{8,16},{16,24},{24,32},{32,40},{40,48},{48,56},{56,0},{1,9},... | collective-permute-start | bytes 712712 | tf_op jit(solution)/shard_map/ppermute | solution.py:401
  4.4 29.6 %collective-permute-start.1 = (bf16[32,3712]{1,0:T(8,128)(2,1)S(1)}, bf16[32,3712]{1,0:T(8,128)(2,1)S(1)}, u32[]{:S(2)}, u32[]{:S(2)}) collective-permute-start(bf16[32,3712]{1,0:T(8,128)(2,1)S(1)} %fusion.1.refs_0_.refs_8_), channel_id=1, source_target_pairs={{0,56},{8,0},{16,8},{24,16},{32,24},{40,32},{48,40},{56,48},{1,57}... | collective-permute-start | bytes 712712 | tf_op jit(solution)/shard_map/ppermute | solution.py:401
  6.2 9.9 %copy-start.26 = (s32[32]{0:T(128)S(1)}, s32[32]{0:T(128)}, u32[]{:S(2)}) copy-start(s32[32]{0:T(128)} %param.20) | copy-start | bytes 388
  6.2 9.9 %copy-start.24 = (s32[64]{0:T(128)S(1)}, s32[64]{0:T(128)}, u32[]{:S(2)}) copy-start(s32[64]{0:T(128)} %constant.92.clone) | copy-start | bytes 772
  6.2 10.0 %copy-start.25 = (s32[32]{0:T(128)S(1)}, s32[32]{0:T(128)}, u32[]{:S(2)}) copy-start(s32[32]{0:T(128)} %param.19) | copy-start | bytes 388
  6.3 10.2 %copy-start.27 = (bf16[1,2,28]{2,1,0:T(2,128)(2,1)S(1)}, bf16[1,2,28]{2,1,0:T(2,128)(2,1)}, u32[]{:S(2)}) copy-start(bf16[1,2,28]{2,1,0:T(2,128)(2,1)} %param.31) | copy-start | bytes 340
  15.6 46.5 %collective-permute-start.2 = (bf16[3584,256]{1,0:T(8,128)(2,1)}, bf16[3584,256]{1,0:T(8,128)(2,1)}, u32[]{:S(2)}, u32[]{:S(2)}) collective-permute-start(bf16[3584,256]{1,0:T(8,128)(2,1)} %get-tuple-element.33.refs_8_), channel_id=1, source_target_pairs={{0,128},{128,0},{1,129},{129,1},{2,130},{130,2},{3,131},{131,3},{4... | collective-permute-start | bytes 5505032 | tf_op jit(solution)/shard_map/ppermute | solution.py:397
  15.6 46.5 %collective-permute-start.3 = (bf16[3584,256]{1,0:T(8,128)(2,1)}, bf16[3584,256]{1,0:T(8,128)(2,1)}, u32[]{:S(2)}, u32[]{:S(2)}) collective-permute-start(bf16[3584,256]{1,0:T(8,128)(2,1)} %get-tuple-element.34.refs_10_), channel_id=1, source_target_pairs={{0,128},{128,0},{1,129},{129,1},{2,130},{130,2},{3,131},{131,3},{4... | collective-permute-start | bytes 5505032 | tf_op jit(solution)/shard_map/ppermute | solution.py:397
  27.6 0.9 copy-start.5
  28.5 0.9 copy-start.7
  34.0 66.0 %all-to-all-start = ((bf16[8,8,32,640]{3,2,1,0:T(8,128)(2,1)}), bf16[8,8,32,640]{3,2,1,0:T(8,128)(2,1)S(1)}, u32[]{:S(2)}, u32[]{:S(2)}) async-start(bf16[8,8,32,640]{3,2,1,0:T(8,128)(2,1)} %bitcast.3), calls=%async_computation | async-start | bytes 5242880 | tf_op jit(solution)/shard_map/all_to_all | solution.py:454
  41.4 20.7 %collective-permute-start.4 = (bf16[256,1792]{1,0:T(8,128)(2,1)}, bf16[256,1792]{1,0:T(8,128)(2,1)}, u32[]{:S(2)}, u32[]{:S(2)}) collective-permute-start(bf16[256,1792]{1,0:T(8,128)(2,1)} %copy-done.5), channel_id=1, source_target_pairs={{0,128},{128,0},{1,129},{129,1},{2,130},{130,2},{3,131},{131,3},{4... | collective-permute-start | bytes 2752520 | tf_op jit(solution)/shard_map/ppermute | solution.py:397
  41.4 8.7 %collective-permute-start.5 = (bf16[32,3712]{1,0:T(8,128)(2,1)S(1)}, bf16[32,3712]{1,0:T(8,128)(2,1)S(1)}, u32[]{:S(2)}, u32[]{:S(2)}) collective-permute-start(bf16[32,3712]{1,0:T(8,128)(2,1)S(1)} %collective-permute-done.refs_1_.refs_9_), channel_id=1, source_target_pairs={{0,8},{8,16},{16,24},{24,32},{32,40},{40,48},{48,56},{56,0},{1,9},... | collective-permute-start | bytes 712712 | tf_op jit(solution)/shard_map/ppermute | solution.py:401
  44.5 9.7 %collective-permute-start.8 = (bf16[32,3712]{1,0:T(8,128)(2,1)S(1)}, bf16[32,3712]{1,0:T(8,128)(2,1)}, u32[]{:S(2)}, u32[]{:S(2)}) collective-permute-start(bf16[32,3712]{1,0:T(8,128)(2,1)S(1)} %collective-permute-done.1.refs_5_.refs_13_), channel_id=1, source_target_pairs={{0,56},{8,0},{16,8},{24,16},{32,24},{40,32},{48,40},{56,48},{1,57}... | collective-permute-start | bytes 712712 | tf_op jit(solution)/shard_map/ppermute | solution.py:401
  50.2 8.2 %collective-permute-start.6 = (bf16[32,3712]{1,0:T(8,128)(2,1)S(1)}, bf16[32,3712]{1,0:T(8,128)(2,1)}, u32[]{:S(2)}, u32[]{:S(2)}) collective-permute-start(bf16[32,3712]{1,0:T(8,128)(2,1)S(1)} %collective-permute-done.5.refs_2_.refs_10_), channel_id=1, source_target_pairs={{0,8},{8,16},{16,24},{24,32},{32,40},{40,48},{48,56},{56,0},{1,9},... | collective-permute-start | bytes 712712 | tf_op jit(solution)/shard_map/ppermute | solution.py:401
  53.4 0.7 copy-start.3
  54.1 9.4 %collective-permute-start.9 = (bf16[32,3712]{1,0:T(8,128)(2,1)}, bf16[32,3712]{1,0:T(8,128)(2,1)}, u32[]{:S(2)}, u32[]{:S(2)}) collective-permute-start(bf16[32,3712]{1,0:T(8,128)(2,1)} %collective-permute-done.8.refs_6_.refs_14_), channel_id=1, source_target_pairs={{0,56},{8,0},{16,8},{24,16},{32,24},{40,32},{48,40},{56,48},{1,57}... | collective-permute-start | bytes 712712 | tf_op jit(solution)/shard_map/ppermute | solution.py:401
  58.3 8.0 %collective-permute-start.7 = (bf16[32,3712]{1,0:T(8,128)(2,1)}, bf16[32,3712]{1,0:T(8,128)(2,1)}, u32[]{:S(2)}, u32[]{:S(2)}) collective-permute-start(bf16[32,3712]{1,0:T(8,128)(2,1)} %collective-permute-done.6.refs_3_.refs_11_), channel_id=1, source_target_pairs={{0,8},{8,16},{16,24},{24,32},{32,40},{40,48},{48,56},{56,0},{1,9},... | collective-permute-start | bytes 712712 | tf_op jit(solution)/shard_map/ppermute | solution.py:401
  66.4 0.9 copy-start.4
  71.9 0.8 copy-start.9
  72.7 0.8 copy-start.11
  73.5 0.8 copy-start.12
  74.3 0.8 copy-start.15
  75.1 0.8 copy-start.18
  75.8 13.8 %collective-permute-start.10 = (bf16[64,3584]{1,0:T(8,128)(2,1)S(1)}, bf16[64,3584]{1,0:T(8,128)(2,1)S(1)}, u32[]{:S(2)}, u32[]{:S(2)}) collective-permute-start(bf16[64,3584]{1,0:T(8,128)(2,1)S(1)} %get-tuple-element.39), channel_id=1, source_target_pairs={{0,2},{2,4},{4,6},{6,0},{64,66},{66,68},{68,70},{70,64},{1,3},{3,5... | collective-permute-start | bytes 1376264 | tf_op jit(solution)/shard_map/ppermute | solution.py:405
  77.3 21.2 %collective-permute-start.11 = (bf16[64,3584]{1,0:T(8,128)(2,1)S(1)}, bf16[64,3584]{1,0:T(8,128)(2,1)S(1)}, u32[]{:S(2)}, u32[]{:S(2)}) collective-permute-start(bf16[64,3584]{1,0:T(8,128)(2,1)S(1)} %get-tuple-element.40), channel_id=1, source_target_pairs={{0,4},{2,6},{4,0},{6,2},{64,68},{66,70},{68,64},{70,66},{1,5},{3,7... | collective-permute-start | bytes 1376264 | tf_op jit(solution)/shard_map/ppermute | solution.py:405
  80.0 19.3 %collective-permute-start.12 = (bf16[64,3584]{1,0:T(8,128)(2,1)S(1)}, bf16[64,3584]{1,0:T(8,128)(2,1)S(1)}, u32[]{:S(2)}, u32[]{:S(2)}) collective-permute-start(bf16[64,3584]{1,0:T(8,128)(2,1)S(1)} %get-tuple-element.41), channel_id=1, source_target_pairs={{0,6},{2,0},{4,2},{6,4},{64,70},{66,64},{68,66},{70,68},{1,7},{3,1... | collective-permute-start | bytes 1376264 | tf_op jit(solution)/shard_map/ppermute | solution.py:405
  89.6 0.8 copy-start.13
  98.5 0.8 copy-start.16
  99.3 0.8 copy-start.19
  100.7 1.5 copy-start.1
  102.2 10.3 %copy-start.8 = (bf16[256,1792]{1,0:T(8,128)(2,1)S(1)}, bf16[256,1792]{1,0:T(8,128)(2,1)}, u32[]{:S(2)}) copy-start(bf16[256,1792]{1,0:T(8,128)(2,1)} %copy-done.7) | copy-start | bytes 2752516
  102.2 103.3 %all-to-all-start.1 = ((bf16[8,8,32,640]{3,2,1,0:T(8,128)(2,1)}), bf16[8,8,32,640]{3,2,1,0:T(8,128)(2,1)S(1)}, u32[]{:S(2)}, u32[]{:S(2)}) async-start(bf16[8,8,32,640]{3,2,1,0:T(8,128)(2,1)} %copy-done.1), calls=%async_computation.1 | async-start | bytes 5242880 | tf_op jit(solution)/shard_map/all_to_all | solution.py:479
  112.5 23.4 %collective-permute-start.18 = (bf16[256,1792]{1,0:T(8,128)(2,1)S(1)}, bf16[256,1792]{1,0:T(8,128)(2,1)}, u32[]{:S(2)}, u32[]{:S(2)}) collective-permute-start(bf16[256,1792]{1,0:T(8,128)(2,1)S(1)} %copy-done.8), channel_id=1, source_target_pairs={{0,1},{1,0},{2,3},{3,2},{4,5},{5,4},{6,7},{7,6},{8,9},{9,8},{10,11... | collective-permute-start | bytes 2752520 | tf_op jit(solution)/shard_map/ppermute | solution.py:397
  113.7 31.0 %collective-permute-start.13 = (bf16[64,3584]{1,0:T(8,128)(2,1)}, bf16[64,3584]{1,0:T(8,128)(2,1)S(1)}, u32[]{:S(2)}, u32[]{:S(2)}) collective-permute-start(bf16[64,3584]{1,0:T(8,128)(2,1)} %copy-done.18), channel_id=1, source_target_pairs={{0,64},{2,66},{4,68},{6,70},{64,0},{66,2},{68,4},{70,6},{1,65},{3,... | collective-permute-start | bytes 1376264 | tf_op jit(solution)/shard_map/ppermute | solution.py:405
  113.7 45.7 %collective-permute-start.14 = (bf16[64,3584]{1,0:T(8,128)(2,1)}, bf16[64,3584]{1,0:T(8,128)(2,1)S(1)}, u32[]{:S(2)}, u32[]{:S(2)}) collective-permute-start(bf16[64,3584]{1,0:T(8,128)(2,1)} %copy-done.15), channel_id=1, source_target_pairs={{0,66},{2,68},{4,70},{6,64},{64,2},{66,4},{68,6},{70,0},{1,67},{3,... | collective-permute-start | bytes 1376264 | tf_op jit(solution)/shard_map/ppermute | solution.py:405
  117.3 49.3 %collective-permute-start.15 = (bf16[64,3584]{1,0:T(8,128)(2,1)}, bf16[64,3584]{1,0:T(8,128)(2,1)S(1)}, u32[]{:S(2)}, u32[]{:S(2)}) collective-permute-start(bf16[64,3584]{1,0:T(8,128)(2,1)} %copy-done.12), channel_id=1, source_target_pairs={{0,68},{2,70},{4,64},{6,66},{64,4},{66,6},{68,0},{70,2},{1,69},{3,... | collective-permute-start | bytes 1376264 | tf_op jit(solution)/shard_map/ppermute | solution.py:405
  119.1 53.6 %collective-permute-start.16 = (bf16[64,3584]{1,0:T(8,128)(2,1)}, bf16[64,3584]{1,0:T(8,128)(2,1)S(1)}, u32[]{:S(2)}, u32[]{:S(2)}) collective-permute-start(bf16[64,3584]{1,0:T(8,128)(2,1)} %copy-done.11), channel_id=1, source_target_pairs={{0,70},{2,64},{4,66},{6,68},{64,6},{66,0},{68,2},{70,4},{1,71},{3,... | collective-permute-start | bytes 1376264 | tf_op jit(solution)/shard_map/ppermute | solution.py:405
  135.9 52.1 %collective-permute-start.19 = (bf16[256,1792]{1,0:T(8,128)(2,1)}, bf16[256,1792]{1,0:T(8,128)(2,1)}, u32[]{:S(2)}, u32[]{:S(2)}) collective-permute-start(bf16[256,1792]{1,0:T(8,128)(2,1)} %collective-permute-done.18.w2), channel_id=1, source_target_pairs={{0,128},{128,0},{1,129},{129,1},{2,130},{130,2},{3,131},{131,3},{4... | collective-permute-start | bytes 2752520 | tf_op jit(solution)/shard_map/ppermute | solution.py:397
  172.8 1.0 copy-start.10
  173.8 1.0 copy-start.14
  174.8 1.0 copy-start.17
  175.8 1.0 copy-start.20
  176.8 11.0 %copy-start.28 = (s32[8]{0:T(128)S(1)}, s32[8]{0:T(128)}, u32[]{:S(2)}) copy-start(s32[8]{0:T(128)} %constant.110) | copy-start | bytes 100
  176.8 20.9 %copy-start.6 = (bf16[256,1792]{1,0:T(8,128)(2,1)S(1)}, bf16[256,1792]{1,0:T(8,128)(2,1)}, u32[]{:S(2)}) copy-start(bf16[256,1792]{1,0:T(8,128)(2,1)} %copy-done.5) | copy-start | bytes 2752516
  186.1 11.6 %collective-permute-start.17 = (bf16[512,512]{1,0:T(8,128)(2,1)}, bf16[512,512]{1,0:T(8,128)(2,1)}, u32[]{:S(2)}, u32[]{:S(2)}) collective-permute-start(bf16[512,512]{1,0:T(8,128)(2,1)} %hidden_units.1.h0), channel_id=1, source_target_pairs={{0,1},{1,0},{2,3},{3,2},{4,5},{5,4},{6,7},{7,6},{8,9},{9,8},{10,11... | collective-permute-start | bytes 1572872 | tf_op jit(solution)/shard_map/ppermute | solution.py:397
  204.3 1.2 copy-start.2
  205.5 73.2 %all-to-all-start.2 = ((bf16[64,8,1792]{2,1,0:T(8,128)(2,1)}), bf16[64,8,1792]{2,1,0:T(8,128)(2,1)}, u32[]{:S(2)}, u32[]{:S(2)}) async-start(bf16[64,8,1792]{2,1,0:T(8,128)(2,1)} %copy-done.2), calls=%async_computation.2 | async-start | bytes 3670016 | tf_op jit(solution)/shard_map/all_to_all | solution.py:490
  225.6 3.2 %copy-start.22 = (s32[32,8]{0,1:T(8,128)S(1)}, s32[32,8]{0,1:T(8,128)}, u32[]{:S(2)}) copy-start(s32[32,8]{0,1:T(8,128)} %param.24) | copy-start | bytes 3076
  225.6 3.3 %copy-start.21 = (bf16[32,576]{1,0:T(8,128)(2,1)S(1)}, bf16[32,576]{1,0:T(8,128)(2,1)}, u32[]{:S(2)}) copy-start(bf16[32,576]{1,0:T(8,128)(2,1)} %param.22) | copy-start | bytes 110596
  225.7 3.3 %copy-start.23 = (f32[32,8]{0,1:T(8,128)S(1)}, f32[32,8]{0,1:T(8,128)}, u32[]{:S(2)}) copy-start(f32[32,8]{0,1:T(8,128)} %param.25) | copy-start | bytes 3076
  227.9 45.8 %collective-permute-start.20 = (bf16[32,32,640]{2,1,0:T(8,128)(2,1)}, bf16[32,32,640]{2,1,0:T(8,128)(2,1)S(1)}, u32[]{:S(2)}, u32[]{:S(2)}) collective-permute-start(bf16[32,32,640]{2,1,0:T(8,128)(2,1)} %compact.1.mine), channel_id=1, source_target_pairs={{0,1},{1,0},{2,3},{3,2},{4,5},{5,4},{6,7},{7,6},{8,9},{9,8},{10,11... | collective-permute-start | bytes 3932168 | tf_op jit(solution)/shard_map/ppermute | solution.py:397

commit v3 on v2

--- a/solution.py
+++ b/solution.py
@@ -50,72 +50,58 @@
     return pl.CostEstimate(flops=int(flops), bytes_accessed=int(nbytes), transcendentals=0)
 
 
-def scaled_blocks(out, value, scale_at):
+def wide_kernel(scale, value, *rest):
+    out = rest[-1]
+    first = pl.program_id(0) == 0
+    for f in range(2):
+        for k in range(14):
+            rows, cols = slice(k * BLOCK, (k + 1) * BLOCK), slice(f * BLOCK, (f + 1) * BLOCK)
+            by = jnp.where(first, scale[f : f + 1, k : k + 1], scale[f : f + 1, 14 + k : 15 + k])
+            out[rows, cols] = (value[0, rows, cols].astype(F32) * by).astype(BF16)
+
+
+def scale_wide(value, scale, *before):
+    return pl.pallas_call(
+        wide_kernel,
+        grid=(2,),
+        in_specs=[whole((2, 28)), pl.BlockSpec((1, D // 2, 256), lambda i: (0, i, 0))]
+        + [smem()] * len(before),
+        out_specs=pl.BlockSpec((D // 2, 256), lambda i: (i, 0)),
+        out_shape=jax.ShapeDtypeStruct((D, 256), BF16),
+        compiler_params=params(8),
+        cost_estimate=cost(1e6, 4e6),
+        name="scale_wide",
+    )(scale[0].T.astype(F32), hbm(value), *before)
+
+
+def narrow_kernel(half_ref, scale, value, *rest):
+    out = rest[-1]
+    first = half_ref[0] == 0
     for a in range(2):
-        for f in range(2):
-            rows, cols = slice(a * BLOCK, (a + 1) * BLOCK), slice(f * BLOCK, (f + 1) * BLOCK)
-            out[rows, cols] = (value[0, rows, cols].astype(F32) * scale_at(a, f)).astype(BF16)
-
-
-def wide_kernel(late_ref, gs, us, gv, uv, g_out, u_out):
-    step = pl.program_id(0)
-    scaled_blocks(g_out, gv, lambda a, f: gs[(step * 2 + a) * 2 + f])
-    scaled_blocks(u_out, uv, lambda a, f: us[(step * 2 + a) * 2 + f])
-
-
-def scale_wide(late, gate_value, gate_scale, up_value, up_scale):
-    value = pl.BlockSpec((1, 256, 256), lambda i: (0, i, 0))
-    return pl.pallas_call(
-        wide_kernel,
-        grid=(14,),
-        in_specs=[smem(), smem(), smem(), value, value],
-        out_specs=[pl.BlockSpec((256, 256), lambda i: (i, 0))] * 2,
-        out_shape=[in_hbm((D, 256))] * 2,
-        compiler_params=params(16),
-        cost_estimate=cost(2e6, 7e6),
-        name="scale_wide",
-    )(
-        late,
-        gate_scale.astype(F32).reshape(-1),
-        up_scale.astype(F32).reshape(-1),
-        *hbm(gate_value, up_value),
-    )
-
-
-def down_panel_kernel(tp_ref, ds, dv, keep_out, send_out):
-    step = pl.program_id(0)
-    half = jnp.where(step < 7, 1 - tp_ref[0], tp_ref[0])
-    column = half * 14 + jnp.where(step < 7, step, step - 7) * 2
-
-    @pl.when(step < 7)
-    def _():
-        scaled_blocks(send_out, dv, lambda a, f: ds[a * 28 + column + f])
-
-    @pl.when(step >= 7)
-    def _():
-        scaled_blocks(keep_out, dv, lambda a, f: ds[a * 28 + column + f])
-
-
-def scale_down(tp_index, down_value, down_scale):
-    def value_at(i, t):
-        return (0, 0, jnp.where(i < 7, (1 - t[0]) * 7 + i, t[0] * 7 + i - 7))
-
-    return pl.pallas_call(
-        down_panel_kernel,
+        for k in range(14):
+            rows, cols = slice(a * BLOCK, (a + 1) * BLOCK), slice(k * BLOCK, (k + 1) * BLOCK)
+            by = jnp.where(first, scale[a : a + 1, k : k + 1], scale[a : a + 1, 14 + k : 15 + k])
+            out[rows, cols] = (value[0, rows, cols].astype(F32) * by).astype(BF16)
+
+
+def scale_down(half, value, scale, *before):
+    return pl.pallas_call(
+        narrow_kernel,
         grid_spec=pltpu.PrefetchScalarGridSpec(
             num_scalar_prefetch=1,
-            grid=(14,),
-            in_specs=[smem(), pl.BlockSpec((1, 256, 256), value_at)],
-            out_specs=[
-                pl.BlockSpec((256, 256), lambda i, t: (0, jnp.maximum(i - 7, 0))),
-                pl.BlockSpec((256, 256), lambda i, t: (0, jnp.minimum(i, 6))),
-            ],
+            grid=(1,),
+            in_specs=[
+                pl.BlockSpec((2, 28), lambda i, h: (0, 0)),
+                pl.BlockSpec((1, 256, HALF_D), lambda i, h: (0, 0, h[0])),
+            ]
+            + [smem()] * len(before),
+            out_specs=pl.BlockSpec((256, HALF_D), lambda i, h: (0, 0)),
         ),
-        out_shape=[in_hbm((256, HALF_D))] * 2,
-        compiler_params=params(16),
-        cost_estimate=cost(1e6, 4e6),
+        out_shape=jax.ShapeDtypeStruct((256, HALF_D), BF16),
+        compiler_params=params(8),
+        cost_estimate=cost(1e6, 2e6),
         name="scale_down",
-    )(tp_index, down_scale.astype(F32).reshape(-1), hbm(down_value))
+    )(half, scale[0].astype(F32), hbm(value), *before)
 
 
 def named_by(routing, experts):
@@ -134,7 +120,7 @@
 
 
 def pick_kernel(place_ref, *refs):
-    names, blocks, outs, chosen_ref = refs[:NZ], refs[NZ : 2 * NZ], refs[2 * NZ : -1], refs[-1]
+    names, blocks, outs, chosen_ref = refs[:NZ], refs[NZ : 2 * NZ], refs[-9:-1], refs[-1]
 
     @pl.when(pl.program_id(0) == 0)
     def _():
@@ -157,55 +143,45 @@
             out[b * CAP : (b + 1) * CAP, :] = rows[r * CAP : (r + 1) * CAP, :]
 
 
-def pick_rows(place, blocks):
+def pick_rows(place, blocks, *before):
     wide = 896
     return pl.pallas_call(
         pick_kernel,
         grid=(D // wide,),
         in_specs=[smem()]
         + [pl.BlockSpec((TRAJ, BLOCK), lambda i: (0, D // BLOCK))] * NZ
-        + [pl.BlockSpec((TRAJ, wide), lambda i: (0, i))] * NZ,
+        + [pl.BlockSpec((TRAJ, wide), lambda i: (0, i))] * NZ
+        + [smem()] * len(before),
         out_specs=[pl.BlockSpec((NZ * CAP, wide), lambda i: (0, i))] * 8,
         out_shape=[in_hbm((NZ * CAP, D))] * 8,
         scratch_shapes=[pltpu.VMEM((NZ, TRAJ, EP), BF16)],
-        compiler_params=params(16),
+        compiler_params=params(10),
         cost_estimate=cost(1e9, 6e6),
         name="pick_rows",
-    )(place, *blocks, *blocks)
+    )(place, *blocks, *blocks, *before)
 
 
 def hidden_kernel(*refs):
-    tokens, (g0, g1, u0, u1, out), (acc_g, acc_u) = refs[:8], refs[8:13], refs[13:]
-    step = pl.program_id(0)
-
-    @pl.when(step == 0)
-    def _():
-        acc_g[...] = jnp.zeros_like(acc_g)
-        acc_u[...] = jnp.zeros_like(acc_u)
-
-    x = jnp.concatenate([t[...] for t in tokens], axis=0)
-    acc_g[:, :256] += jnp.dot(x, g0[...], preferred_element_type=F32)
-    acc_u[:, :256] += jnp.dot(x, u0[...], preferred_element_type=F32)
-    acc_g[:, 256:] += jnp.dot(x, g1[...], preferred_element_type=F32)
-    acc_u[:, 256:] += jnp.dot(x, u1[...], preferred_element_type=F32)
-
-    @pl.when(step == pl.num_programs(0) - 1)
-    def _():
-        g = acc_g[...]
-        out[...] = (g / (1.0 + jnp.exp(-g)) * acc_u[...]).astype(BF16)
+    tokens, (g0, g1, u0, u1, out), (x,) = refs[:8], refs[8:13], refs[13:]
+    for r, token in enumerate(tokens):
+        x[r * 64 : (r + 1) * 64, :] = token[...]
+    for half in range(2):
+        rows = slice(half * 256, (half + 1) * 256)
+        for n, (gate, up) in enumerate(((g0, u0), (g1, u1))):
+            g = jnp.dot(x[rows, :], gate[...], preferred_element_type=F32)
+            u = jnp.dot(x[rows, :], up[...], preferred_element_type=F32)
+            out[rows, n * 256 : (n + 1) * 256] = (g / (1.0 + jnp.exp(-g)) * u).astype(BF16)
 
 
 def hidden_units(tokens, g0, g1, u0, u1):
-    depth = 512
+    vmem = pl.BlockSpec(memory_space=pltpu.VMEM)
     return pl.pallas_call(
         hidden_kernel,
-        grid=(D // depth,),
-        in_specs=[pl.BlockSpec((64, depth), lambda k: (0, k))] * 8
-        + [pl.BlockSpec((depth, 256), lambda k: (k, 0))] * 4,
-        out_specs=whole((512, 512)),
+        in_specs=[vmem] * 12,
+        out_specs=vmem,
         out_shape=jax.ShapeDtypeStruct((512, 512), BF16),
-        scratch_shapes=[pltpu.VMEM((512, 512), F32)] * 2,
-        compiler_params=params(24),
+        scratch_shapes=[pltpu.VMEM((512, D), BF16)],
+        compiler_params=params(10),
         cost_estimate=cost(3.8e9, 12e6),
         name="hidden_units",
     )(*tokens, g0, g1, u0, u1)
@@ -213,22 +189,22 @@
 
 def down_kernel(order_ref, h0, h1, w0, w1, w2, w3, out):
     h = jnp.concatenate([h0[...], h1[...]], axis=1)
-    w = jnp.concatenate([w0[...], w1[...], w2[...], w3[...]], axis=0)
-    rows = jnp.dot(h, w, preferred_element_type=F32)
-    for group in range(EP):
-        out[order_ref[group]] = rows[group * CAP : (group + 1) * CAP, :].astype(BF16)
+    for c in range(HALF_D // 256):
+        cols = slice(c * 256, (c + 1) * 256)
+        w = jnp.concatenate([p[:, cols] for p in (w0, w1, w2, w3)], axis=0)
+        rows = jnp.dot(h, w, preferred_element_type=F32)
+        for group in range(EP):
+            out[order_ref[group], :, cols] = rows[group * CAP : (group + 1) * CAP, :].astype(BF16)
 
 
 def down_rows(order, h0, h1, weights):
-    wide = 256
+    vmem = pl.BlockSpec(memory_space=pltpu.VMEM)
     return pl.pallas_call(
         down_kernel,
-        grid=(HALF_D // wide,),
-        in_specs=[smem(), whole((512, 512)), whole((512, 512))]
-        + [pl.BlockSpec((256, wide), lambda i: (0, i))] * 4,
-        out_specs=pl.BlockSpec((EP, CAP, wide), lambda i: (0, 0, i)),
-        out_shape=in_hbm((EP, CAP, HALF_D)),
-        compiler_params=params(24),
+        in_specs=[smem()] + [vmem] * 6,
+        out_specs=vmem,
+        out_shape=jax.ShapeDtypeStruct((EP, CAP, HALF_D), BF16),
+        compiler_params=params(10),
         cost_estimate=cost(1.9e9, 7e6),
         name="down_rows",
     )(order, h0, h1, *weights)
@@ -266,13 +242,14 @@
         ],
         out_specs=pl.BlockSpec((TRAJ, wide), lambda i: (0, i)),
         out_shape=jax.ShapeDtypeStruct((TRAJ, HALF_D), BF16),
-        compiler_params=params(16),
+        compiler_params=params(10),
         cost_estimate=cost(1e8, 2e6),
         name="blend",
     )(routing, weight, rows)
 
 
-def collect_kernel(index_ref, pages, out):
+def collect_kernel(index_ref, pages, *rest):
+    out = rest[-1]
     step = pl.program_id(0)
     lane = lax.broadcasted_iota(I32, (32, LANES - LATENT), 1)
     for i in range(8):
@@ -283,53 +260,55 @@
         out[i, :, LATENT:LANES] = jnp.where(lane == 0, slot, length).astype(BF16)
 
 
-def collect(index, pages):
+def collect(index, pages, *before):
     return pl.pallas_call(
         collect_kernel,
         grid=(EP // 8,),
-        in_specs=[smem(), whole(pages.shape)],
+        in_specs=[smem(), whole(pages.shape)] + [smem()] * len(before),
         out_specs=pl.BlockSpec((8, 32, LANES), lambda i: (i, 0, 0)),
-        out_shape=in_hbm((EP, 32, LANES)),
-        compiler_params=params(16),
+        out_shape=pltpu.HBM((EP, 32, LANES), BF16),
+        compiler_params=params(10),
         cost_estimate=cost(1e6, 6e6),
         name="collect",
-    )(index, pages)
-
-
-def regroup_kernel(midway, out):
+    )(index, pages, *before)
+
+
+def regroup_kernel(midway, *rest):
+    out = rest[-1]
     out[0] = midway[:, 0]
 
 
-def regroup(midway):
+def regroup(midway, *before):
     return pl.pallas_call(
         regroup_kernel,
         grid=(8,),
-        in_specs=[pl.BlockSpec((8, 1, 32, LANES), lambda i: (0, i, 0, 0))],
+        in_specs=[pl.BlockSpec((8, 1, 32, LANES), lambda i: (0, i, 0, 0))] + [smem()] * len(before),
         out_specs=pl.BlockSpec((1, 8, 32, LANES), lambda i: (i, 0, 0, 0)),
-        out_shape=in_hbm((8, 8, 32, LANES)),
+        out_shape=pltpu.HBM((8, 8, 32, LANES), BF16),
         compiler_params=params(8),
         cost_estimate=cost(1e6, 6e6),
         name="regroup",
-    )(midway)
-
-
-def compact_kernel(source_ref, arrived, out):
+    )(hbm(midway), *before)
+
+
+def compact_kernel(source_ref, arrived, *rest):
+    out = rest[-1]
     step = pl.program_id(0)
     for i in range(8):
         out[i] = arrived[source_ref[step * 8 + i]]
 
 
-def compact(source, arrived):
+def compact(source, arrived, *before):
     return pl.pallas_call(
         compact_kernel,
         grid=(TRAJ // 8,),
-        in_specs=[smem(), whole(arrived.shape)],
+        in_specs=[smem(), whole(arrived.shape)] + [smem()] * len(before),
         out_specs=pl.BlockSpec((8, 32, LANES), lambda i: (i, 0, 0)),
         out_shape=in_hbm((TRAJ, 32, LANES)),
-        compiler_params=params(16),
+        compiler_params=params(10),
         cost_estimate=cost(1e6, 4e6),
         name="compact",
-    )(source, arrived)
+    )(source, hbm(arrived), *before)
 
 
 ATTEND_STEP = 8
@@ -387,10 +366,26 @@
             jax.ShapeDtypeStruct((TRAJ, MAXLEN, LATENT), BF16),
             jax.ShapeDtypeStruct((TRAJ, 32, LATENT_WIDTH), BF16),
         ],
-        compiler_params=params(24),
+        compiler_params=params(10),
         cost_estimate=cost(2e8, 8e6),
         name="attend",
     )(tp_index, length, mine, other, hbm(queries), fresh.reshape(TRAJ, 1, LATENT))
+
+
+def once_kernel(*refs):
+    refs[-1][0] = 0.0
+
+
+def once(*arrays):
+    return pl.pallas_call(
+        once_kernel,
+        in_specs=[pl.BlockSpec(memory_space=pl.ANY)] * len(arrays),
+        out_specs=smem(),
+        out_shape=jax.ShapeDtypeStruct((1,), F32),
+        compiler_params=params(1),
+        cost_estimate=cost(1, 4),
+        name="once",
+    )(*arrays)
 
 
 def swap(x, axis):
@@ -438,7 +433,8 @@
         [hidden_states, jnp.pad(routing.astype(BF16), ((0, 0), (0, BLOCK - 8)))], axis=1
     )
     up_way, down_way = [own, z_shift(own, 1)], [own, z_shift(own, -1)]
-    down_keep, down_send = scale_down(tp_index, down_value, down_scale)
+    down_send = scale_down(1 - tp_index, down_value, down_scale)
+    down_tp = swap(down_send, "tp")
 
     owner, slot = new_place // TRAJ, new_place % TRAJ
     to_owner = owner[None, :] == jnp.asarray(PLANE_MAJOR)[:, None]
@@ -446,26 +442,26 @@
     facts = jnp.concatenate([mine, slot[:, None] + 1, lengths[:, None]], axis=1)
     index = jnp.sum(jnp.where(to_owner[:, :, None], facts[None], 0), axis=1)
     index = index - (jnp.arange(4) == 2).astype(I32)[None, :]
-    leaving = collect(index, latent_pages).reshape(8, 8, 32, LANES)
-    leaving, up_way[1], down_way[1], down_send = lax.optimization_barrier(
-        (leaving, up_way[1], down_way[1], down_send)
-    )
-    down_tp = swap(down_send, "tp")
+    leaving = collect(index, latent_pages, once(up_way[1], down_way[1], down_send)).reshape(8, 8, 32, LANES)
     midway = lax.all_to_all(leaving, ("xh", "y"), split_axis=0, concat_axis=0, tiled=True)
-
-    gate, up = scale_wide(tp_index, gate_value, gate_scale, up_value, up_scale)
-    gate_far, up_far = swap(gate, "pool"), swap(up, "pool")
-    down_far = swap(down_keep, "pool")
     for step in range(1, 4):
         up_way.append(z_shift(up_way[-1], 1))
         if step < 3:
             down_way.append(z_shift(down_way[-1], -1))
     behind = np.array([0, 1, 2, 3, 4, -1, -2, -3], np.int32)
 
-    place, gate_far, up_far, down_far = lax.optimization_barrier(
-        (place, gate_far, up_far, down_far)
-    )
-    picked = pick_rows(place, up_way + down_way[1:])
+    gate = scale_wide(gate_value, gate_scale, once(up_way[1], down_way[1]))
+    up = scale_wide(up_value, up_scale, once(up_way[2], down_way[2]))
+    down_keep = scale_down(tp_index, down_value, down_scale, once(up_way[2], down_way[2]))
+    gate_far, up_far = swap(gate, "pool"), swap(up, "pool")
+    down_far, down_tp_far = swap(down_keep, "pool"), swap(down_tp, "pool")
+
+    midway = regroup(
+        midway, once(up_way[4], down_way[3], gate_far, up_far, down_far, down_tp)
+    )
+    picked = pick_rows(
+        place, up_way + down_way[1:], once(down_tp_far)
+    )
     tokens = [picked[0]] + [
         plane_shift(picked[dx * NY + dy], dx, dy)
         for dx in range(NX)
@@ -473,11 +469,7 @@
         if dx or dy
     ]
 
-    midway, tokens[1], tokens[2], tokens[3] = lax.optimization_barrier(
-        (midway, tokens[1], tokens[2], tokens[3])
-    )
-    arrived = lax.all_to_all(regroup(midway), "z", split_axis=0, concat_axis=0, tiled=True)
-    down_tp_far = swap(down_tp, "pool")
+    arrived = lax.all_to_all(midway, "z", split_axis=0, concat_axis=0, tiled=True)
 
     act = hidden_units(tokens, gate, gate_far, up, up_far)
     act_tp = swap(act, "tp")
@@ -486,7 +478,6 @@
         ((xh + (group >> 5)) % NX) * NZ + (z - jnp.tile(jnp.asarray(behind), 8)) % NZ
     ) * NY + (y - (group >> 3)) % NY
     out_rows = down_rows(order, act, act_tp, [down_keep, down_far, down_tp, down_tp_far])
-    arrived, out_rows = lax.optimization_barrier((arrived, out_rows))
     returned = lax.all_to_all(
         out_rows, ("xh", "z", "y"), split_axis=0, concat_axis=0, tiled=True
     )
@@ -497,7 +488,7 @@
     taken = labels[:, 0][None, :] == jnp.arange(TRAJ, dtype=I32)[:, None]
     source = jnp.sum(jnp.where(taken, jnp.arange(EP, dtype=I32)[None, :], 0), axis=1)
     length = jnp.sum(jnp.where(taken, labels[:, 1][None, :], 0), axis=1)
-    my_half = compact(source, arrived)
+    my_half = compact(source, arrived, once(out_rows))
     other_half = swap(my_half, "tp")
     new_cache, attention = attend(tp_index, length, my_half, other_half, queries, fresh_latent)
     return new_cache, attention, expert_mix

time: 284 us -> 253 us (0.89)
  starting transfers between devices: 69.5 us -> 53.1 us
  local copies, waits for them, and re-layouts: 22.8 us -> 13 us
  Pallas kernels: 52.4 us -> 47.5 us
  other arithmetic: 2.18 us -> 5.71 us
    ppermute x7, waiting for transfers between devices: 66.7 us -> 30.6 us  [swap(): return lax.ppermute(x, axis, [(0, 1), (1, 0)])]
    all_to_all x1, waiting for transfers between devices: 0.01 us -> 35.6 us  [on_device(): lax.all_to_all(out_rows, ('xh', 'z', 'y'), split_axis=0, concat_axis=0, t...]
    pallas_call x4 -> x12, Pallas kernels: 32.3 us -> 20.8 us  [the longest x2 5.26 us: scale_wide(): pl.pallas_call(wide_kernel, grid=(2,), in_specs=[whole((2, 28)), pl.Block...]
    all_to_all x1, starting transfers between devices: 19.8 us -> 10.4 us  [on_device(): lax.all_to_all(out_rows, ('xh', 'z', 'y'), split_axis=0, concat_axis=0, t...]
    unnamed x61 -> x49, local copies, waits for them, and re-layouts: 20.6 us -> 12.6 us
    pallas_call x1, Pallas kernels: 0.6 us -> 6.55 us  [regroup(): pl.pallas_call(regroup_kernel, grid=(8,), in_specs=[pl.BlockSpec((8, 1, 3...]
    ppermute x7, waiting for transfers between devices: 53.1 us -> 47.4 us  [plane_shift(): lax.ppermute(x, ('xh', 'y'), [(a * NY + b, (a + dx) % NX * NY + (b + dy)...]
    ppermute x7, starting transfers between devices: 15.5 us -> 11.4 us  [plane_shift(): lax.ppermute(x, ('xh', 'y'), [(a * NY + b, (a + dx) % NX * NY + (b + dy)...]
  transfers between devices with their start and end apart: 24 -> 24, of which waited for: 13 -> 13; matrix products, arithmetic and copies ran while one was open for 2% -> 3% of each run, Pallas kernels for 17% -> 12%
where the time goes in v3:
time: 253 us; the launch traced here: 252 us
  waiting for transfers between devices  132 us (52%)
  starting transfers between devices  53.1 us (21%)
  Pallas kernels  47.5 us (19%)
  local copies, waits for them, and re-layouts  13 us (5%)
  other arithmetic  5.71 us (2%)
    ppermute x7, waiting for transfers between devices, plane_shift(): lax.ppermute(x, ('xh', 'y'), [(a * NY + b, (a + dx) % NX * NY + (b + dy)...  47.4 us
    all_to_all x1, waiting for transfers between devices, on_device(): lax.all_to_all(out_rows, ('xh', 'z', 'y'), split_axis=0, concat_axis=0, t...  35.6 us
    ppermute x7, waiting for transfers between devices, swap(): return lax.ppermute(x, axis, [(0, 1), (1, 0)])  30.6 us
    ppermute x7, waiting for transfers between devices, z_shift(): return lax.ppermute(x, 'z', [(i, (i + by) % NZ) for i in range(NZ)])  18 us
    unnamed x49, local copies, waits for them, and re-layouts  12.6 us
    ppermute x7, starting transfers between devices, plane_shift(): lax.ppermute(x, ('xh', 'y'), [(a * NY + b, (a + dx) % NX * NY + (b + dy)...  11.4 us
    ppermute x7, starting transfers between devices, z_shift(): return lax.ppermute(x, 'z', [(i, (i + by) % NZ) for i in range(NZ)])  11 us
    all_to_all x1, starting transfers between devices, on_device(): lax.all_to_all(out_rows, ('xh', 'z', 'y'), split_axis=0, concat_axis=0, t...  10.4 us
  transfers between devices with their start and end apart: 24, of which 13 were waited for; matrix products, arithmetic and copies ran while one was open for 3% of the time, Pallas kernels for 12%

profile of v3, /device:TPU:68, one launch (start us, length us, event | category | flops | bytes accessed | tf_op | source)
XLA Modules:
  0.0 252.0 jit_solution(6847378966877610672)
XLA Ops:
  0.6 0.7 convert_element_type.39
  1.4 1.0 fusion.1.refs_0_.refs_8_
  2.4 2.0 collective-permute-start
  4.4 0.1 collective-permute-start.1
  4.5 0.7 bitcast_convert_fusion.scale
  5.2 0.7 and_select_fusion.4
  5.8 0.7 broadcast_compare_fusion
  6.6 0.7 pad_add_fusion
  7.2 0.1 select_reduce_fusion
  7.4 3.9 %copy.43.pages = bf16[128,16,576]{2,1,0:T(8,128)(2,1)S(1)} copy(bf16[128,16,576]{0,2,1:T(8,128)(2,1)} %param.17) | data formatting | bytes 4718592 | tf_op args[0]
  11.4 1.5 scale_down.2.refs_2_
  13.0 0.5 once.6.rest_0_
  13.5 5.2 %collect.1 = bf16[64,32,640]{2,1,0:T(8,128)(2,1)} custom-call(s32[64,4]{1,0:T(8,128)S(1)} %broadcast_subtract_fusion.index_ref, bf16[128,16,576]{2,1,0:T(8,128)(2,1)S(1)} %copy.43.pages, f32[1]{0:T(128)} %once.6.rest_0_), custom_call_target="tpu_custom_call" | custom-call | flops 1000000 | bytes 6000000 | tf_op jit(solution)/shard_map/collect/pallas_call | solution.py:264
  18.7 7.6 %all-to-all-start = ((bf16[8,8,32,640]{3,2,1,0:T(8,128)(2,1)}), bf16[8,8,32,640]{3,2,1,0:T(8,128)(2,1)}, u32[]{:S(2)}, u32[]{:S(2)}) async-start(bf16[8,8,32,640]{3,2,1,0:T(8,128)(2,1)} %bitcast.28), calls=%async_computation | async-start | bytes 5242880 | tf_op jit(solution)/shard_map/all_to_all | solution.py:446
  26.3 3.0 %collective-permute-start.2 = (bf16[32,3712]{1,0:T(8,128)(2,1)S(1)}, bf16[32,3712]{1,0:T(8,128)(2,1)S(1)}, u32[]{:S(2)}, u32[]{:S(2)}) collective-permute-start(bf16[32,3712]{1,0:T(8,128)(2,1)S(1)} %collective-permute-done.refs_0_.refs_1_.refs_9_), channel_id=1, source_target_pairs={{0,8},{8,16},{16,24},{24,32},{32,40},{40,48},{48,56},{56,0},{1,9},... | collective-permute-start | bytes 712712 | tf_op jit(solution)/shard_map/ppermute | solution.py:396
  29.3 0.5 once.7.rest_0_
  29.8 2.6 %scale_wide.2.refs_8_ = bf16[3584,256]{1,0:T(8,128)(2,1)S(1)} custom-call(f32[2,28]{1,0:T(2,128)S(1)} %convert_bitcast_fusion.1.scale, bf16[1,3584,256]{2,1,0:T(8,128)(2,1)} %value.5, f32[1]{0:T(128)} %once.7.rest_0_), custom_call_target="tpu_custom_call" | custom-call | flops 1000000 | bytes 4000000 | tf_op jit(solution)/shard_map/scale_wide/pallas_call | solution.py:64
  32.5 0.9 collective-permute-done.2.refs_0_.refs_2_.refs_10_
  33.5 3.4 %collective-permute-done.5.refs_1_.refs_6_.refs_14_ = bf16[32,3712]{1,0:T(8,128)(2,1)S(1)} collective-permute-done((bf16[32,3712]{1,0:T(8,128)(2,1)S(1)}, bf16[32,3712]{1,0:T(8,128)(2,1)S(1)}, u32[]{:S(2)}, u32[]{:S(2)}) %collective-permute-start.5) | collective-permute-done | bytes 237600 | tf_op jit(solution)/shard_map/ppermute | solution.py:396
  36.9 0.5 once.8.rest_0_
  37.4 2.7 %scale_wide.3.refs_10_ = bf16[3584,256]{1,0:T(8,128)(2,1)S(1)} custom-call(f32[2,28]{1,0:T(2,128)S(1)} %convert_bitcast_fusion.scale, bf16[1,3584,256]{2,1,0:T(8,128)(2,1)} %value.6, f32[1]{0:T(128)} %once.8.rest_0_), custom_call_target="tpu_custom_call" | custom-call | flops 1000000 | bytes 4000000 | tf_op jit(solution)/shard_map/scale_wide/pallas_call | solution.py:64
  40.2 1.3 collective-permute-start.10
  41.5 2.2 scale_down.3.w0
  43.7 0.2 collective-permute-start.9
  43.9 0.9 copy-done.15
  44.9 3.0 %collective-permute-start.3 = (bf16[32,3712]{1,0:T(8,128)(2,1)S(1)}, bf16[32,3712]{1,0:T(8,128)(2,1)S(1)}, u32[]{:S(2)}, u32[]{:S(2)}) collective-permute-start(bf16[32,3712]{1,0:T(8,128)(2,1)S(1)} %collective-permute-done.2.refs_0_.refs_2_.refs_10_), channel_id=1, source_target_pairs={{0,8},{8,16},{16,24},{24,32},{32,40},{40,48},{48,56},{56,0},{1,9},... | collective-permute-start | bytes 712712 | tf_op jit(solution)/shard_map/ppermute | solution.py:396
  47.8 5.5 %collective-permute-done.3.refs_3_.refs_11_ = bf16[32,3712]{1,0:T(8,128)(2,1)S(1)} collective-permute-done((bf16[32,3712]{1,0:T(8,128)(2,1)S(1)}, bf16[32,3712]{1,0:T(8,128)(2,1)S(1)}, u32[]{:S(2)}, u32[]{:S(2)}) %collective-permute-start.3) | collective-permute-done | bytes 237600 | tf_op jit(solution)/shard_map/ppermute | solution.py:396
  53.4 8.1 %collective-permute-done.6.refs_1_.refs_7_.refs_15_ = bf16[32,3712]{1,0:T(8,128)(2,1)S(1)} collective-permute-done((bf16[32,3712]{1,0:T(8,128)(2,1)S(1)}, bf16[32,3712]{1,0:T(8,128)(2,1)S(1)}, u32[]{:S(2)}, u32[]{:S(2)}) %collective-permute-start.6) | collective-permute-done | bytes 237600 | tf_op jit(solution)/shard_map/ppermute | solution.py:396
  61.5 3.0 %collective-permute-start.4 = (bf16[32,3712]{1,0:T(8,128)(2,1)S(1)}, bf16[32,3712]{1,0:T(8,128)(2,1)S(1)}, u32[]{:S(2)}, u32[]{:S(2)}) collective-permute-start(bf16[32,3712]{1,0:T(8,128)(2,1)S(1)} %collective-permute-done.3.refs_3_.refs_11_), channel_id=1, source_target_pairs={{0,8},{8,16},{16,24},{24,32},{32,40},{40,48},{48,56},{56,0},{1,9},... | collective-permute-start | bytes 712712 | tf_op jit(solution)/shard_map/ppermute | solution.py:396
  64.4 10.8 %collective-permute-done.10.refs_5_.w2 = bf16[256,1792]{1,0:T(8,128)(2,1)S(1)} collective-permute-done((bf16[256,1792]{1,0:T(8,128)(2,1)S(1)}, bf16[256,1792]{1,0:T(8,128)(2,1)S(1)}, u32[]{:S(2)}, u32[]{:S(2)}) %collective-permute-start.10) | collective-permute-done | bytes 917536 | tf_op jit(solution)/shard_map/ppermute | solution.py:392
  75.2 0.5 once.9.rest_0_
  75.8 1.3 copy-done.7
  77.1 1.3 copy-done.9
  78.3 0.9 copy-done.11
  79.3 1.0 copy-done.13
  80.3 6.5 %regroup.1 = bf16[8,8,32,640]{3,2,1,0:T(8,128)(2,1)} custom-call(bf16[8,8,32,640]{3,2,1,0:T(8,128)(2,1)} %all-to-all-done.midway, f32[1]{0:T(128)} %once.9.rest_0_), custom_call_target="tpu_custom_call" | custom-call | flops 1000000 | bytes 6000000 | tf_op jit(solution)/shard_map/regroup/pallas_call | solution.py:282
  86.8 9.3 %all-to-all-start.1 = ((bf16[8,8,32,640]{3,2,1,0:T(8,128)(2,1)}), bf16[8,8,32,640]{3,2,1,0:T(8,128)(2,1)}, u32[]{:S(2)}, u32[]{:S(2)}) async-start(bf16[8,8,32,640]{3,2,1,0:T(8,128)(2,1)} %regroup.1), calls=%async_computation.1 | async-start | bytes 5242880 | tf_op jit(solution)/shard_map/all_to_all | solution.py:472
  96.2 2.5 collective-permute-done.11.refs_0_.w3
  98.7 0.5 once.10.refs_16_
  99.2 5.2 %pick_rows.1 = (bf16[64,3584]{1,0:T(8,128)(2,1)S(1)}, bf16[64,3584]{1,0:T(8,128)(2,1)S(1)}, bf16[64,3584]{1,0:T(8,128)(2,1)S(1)}, bf16[64,3584]{1,0:T(8,128)(2,1...) custom-call(s32[3]{0:T(128)S(1)} %pad_add_fusion.1.place_ref, ...), custom_call_target="tpu_custom_call" | custom-call | flops 1000000000 | bytes 6000000 | tf_op jit(solution)/shard_map/pick_rows/pallas_call | solution.py:148
  104.5 1.6 collective-permute-start.12
  106.1 3.0 %collective-permute-start.13 = (bf16[64,3584]{1,0:T(8,128)(2,1)S(1)}, bf16[64,3584]{1,0:T(8,128)(2,1)S(1)}, u32[]{:S(2)}, u32[]{:S(2)}) collective-permute-start(bf16[64,3584]{1,0:T(8,128)(2,1)S(1)} %get-tuple-element.15), channel_id=1, source_target_pairs={{0,4},{2,6},{4,0},{6,2},{64,68},{66,70},{68,64},{70,66},{1,5},{3,7... | collective-permute-start | bytes 1376264 | tf_op jit(solution)/shard_map/ppermute | solution.py:400
  109.1 1.1 collective-permute-start.14
  110.2 3.9 %collective-permute-start.16 = (bf16[64,3584]{1,0:T(8,128)(2,1)S(1)}, bf16[64,3584]{1,0:T(8,128)(2,1)S(1)}, u32[]{:S(2)}, u32[]{:S(2)}) collective-permute-start(bf16[64,3584]{1,0:T(8,128)(2,1)S(1)} %get-tuple-element.18), channel_id=1, source_target_pairs={{0,66},{2,68},{4,70},{6,64},{64,2},{66,4},{68,6},{70,0},{1,67},{3,... | collective-permute-start | bytes 1376264 | tf_op jit(solution)/shard_map/ppermute | solution.py:400
  114.1 4.4 %collective-permute-done.12.refs_1_ = bf16[64,3584]{1,0:T(8,128)(2,1)S(1)} collective-permute-done((bf16[64,3584]{1,0:T(8,128)(2,1)S(1)}, bf16[64,3584]{1,0:T(8,128)(2,1)S(1)}, u32[]{:S(2)}, u32[]{:S(2)}) %collective-permute-start.12) | collective-permute-done | bytes 458784 | tf_op jit(solution)/shard_map/ppermute | solution.py:400
  118.4 1.9 collective-permute-start.17
  120.3 28.8 %collective-permute-done.13.refs_2_ = bf16[64,3584]{1,0:T(8,128)(2,1)S(1)} collective-permute-done((bf16[64,3584]{1,0:T(8,128)(2,1)S(1)}, bf16[64,3584]{1,0:T(8,128)(2,1)S(1)}, u32[]{:S(2)}, u32[]{:S(2)}) %collective-permute-start.13) | collective-permute-done | bytes 458784 | tf_op jit(solution)/shard_map/ppermute | solution.py:400
  149.1 14.2 %collective-permute-done.18.refs_7_ = bf16[64,3584]{1,0:T(8,128)(2,1)S(1)} collective-permute-done((bf16[64,3584]{1,0:T(8,128)(2,1)S(1)}, bf16[64,3584]{1,0:T(8,128)(2,1)S(1)}, u32[]{:S(2)}, u32[]{:S(2)}) %collective-permute-start.18) | collective-permute-done | bytes 458784 | tf_op jit(solution)/shard_map/ppermute | solution.py:400
  163.3 1.5 copy-done.8
  164.8 1.5 copy-done.10
  166.3 4.0 %hidden_units.1.h0 = bf16[512,512]{1,0:T(8,128)(2,1)S(1)} custom-call(bf16[64,3584]{1,0:T(8,128)(2,1)S(1)} %get-tuple-element.13.refs_0_, bf16[64,3584]{1,0:T(8,128)(2,1)S(1)} %collective-permute-done.12.refs_1_, bf16[64,3584]{1,0:T(8,128)(2,1)S(1)} %collective-permute-done.13.refs_2_, bf16[64,3584]{1,0:T(8,128)(2,1)S(1)} %collective-permute-done.14.refs_3_, ...), custom_call_target="tpu_custom_call" | custom-call | flops 3800000000 | bytes 12000000 | tf_op jit(solution)/shard_map/hidden_units/pallas_call | solution.py:178
  170.3 0.9 collective-permute-start.19
  171.3 11.5 %collective-permute-done.19.h1 = bf16[512,512]{1,0:T(8,128)(2,1)} collective-permute-done((bf16[512,512]{1,0:T(8,128)(2,1)S(1)}, bf16[512,512]{1,0:T(8,128)(2,1)}, u32[]{:S(2)}, u32[]{:S(2)}) %collective-permute-start.19) | collective-permute-done | bytes 524320 | tf_op jit(solution)/shard_map/ppermute | solution.py:392
  182.8 4.7 %down_rows.1.refs_0_ = bf16[64,8,1792]{2,1,0:T(8,128)(2,1)} custom-call(s32[64]{0:T(128)S(1)} %fusion.3.order_ref, bf16[512,512]{1,0:T(8,128)(2,1)S(1)} %hidden_units.1.h0, bf16[512,512]{1,0:T(8,128)(2,1)} %collective-permute-done.19.h1, bf16[256,1792]{1,0:T(8,128)(2,1)S(1)} %copy-done.16, bf16[256,1792]{1,0:T(8,128)(2,1)S(1)} %copy-done.14, ...), custom_call_target="tpu_custom_call" | custom-call | flops 1900000000 | bytes 7000000 | tf_op jit(solution)/shard_map/down_rows/pallas_call | solution.py:202
  187.6 10.4 %all-to-all-start.2 = ((bf16[64,8,1792]{2,1,0:T(8,128)(2,1)}), bf16[64,8,1792]{2,1,0:T(8,128)(2,1)S(1)}, u32[]{:S(2)}, u32[]{:S(2)}) async-start(bf16[64,8,1792]{2,1,0:T(8,128)(2,1)} %down_rows.1.refs_0_), calls=%async_computation.2 | async-start | bytes 3670016 | tf_op jit(solution)/shard_map/all_to_all | solution.py:481
  198.0 0.5 once.11.rest_0_
  198.5 1.0 slice_convert_fusion
  199.6 0.1 select_reduce_fusion.1
  199.7 2.6 %compact.1.mine = bf16[32,32,640]{2,1,0:T(8,128)(2,1)S(1)} custom-call(s32[32]{0:T(128)S(1)} %get-tuple-element.23.source_ref, bf16[64,32,640]{2,1,0:T(8,128)(2,1)} %bitcast.10.arrived, f32[1]{0:T(128)} %once.11.rest_0_), custom_call_target="tpu_custom_call" | custom-call | flops 1000000 | bytes 4000000 | tf_op jit(solution)/shard_map/compact/pallas_call | solution.py:302
  202.4 0.9 collective-permute-start.20
  203.5 35.6 %all-to-all-done.2.rows_ref = bf16[64,8,1792]{2,1,0:T(8,128)(2,1)S(1)} async-done(((bf16[64,8,1792]{2,1,0:T(8,128)(2,1)}), bf16[64,8,1792]{2,1,0:T(8,128)(2,1)S(1)}, u32[]{:S(2)}, u32[]{:S(2)}) %all-to-all-start.2) | async-done | bytes 1835040 | tf_op jit(solution)/shard_map/all_to_all | solution.py:481
  239.1 2.1 blend.1
  241.2 5.8 %collective-permute-done.20.other = bf16[32,32,640]{2,1,0:T(8,128)(2,1)} collective-permute-done((bf16[32,32,640]{2,1,0:T(8,128)(2,1)S(1)}, bf16[32,32,640]{2,1,0:T(8,128)(2,1)}, u32[]{:S(2)}, u32[]{:S(2)}) %collective-permute-start.20) | collective-permute-done | bytes 1310752 | tf_op jit(solution)/shard_map/ppermute | solution.py:392
  247.0 5.0 %attend.1 = (bf16[32,64,576]{2,1,0:T(8,128)(2,1)}, bf16[32,32,512]{2,1,0:T(8,128)(2,1)}) custom-call(s32[1]{0:T(128)} %bitcast.half_ref.tp_ref, s32[32]{0:T(128)S(1)} %get-tuple-element.24.length_ref, bf16[32,32,640]{2,1,0:T(8,128)(2,1)S(1)} %compact.1.mine, bf16[32,32,640]{2,1,0:T(8,128)(2,1)} %collective-permute-done.20.other, ...), custom_call_target="tpu_custom_call" | custom-call | flops 200000000 | bytes 8000000 | tf_op jit(solution)/shard_map/attend/pallas_call | solution.py:350
  (75 shorter events, 1.1 us)
Async XLA Ops:
  0.6 5.2 %copy-start = (s32[32,4]{0,1:T(4,128)S(1)}, s32[32,4]{0,1:T(4,128)}, u32[]{:S(2)}) copy-start(s32[32,4]{0,1:T(4,128)} %param.18) | copy-start | bytes 1540
  2.4 10.5 %collective-permute-start = (bf16[32,3712]{1,0:T(8,128)(2,1)S(1)}, bf16[32,3712]{1,0:T(8,128)(2,1)S(1)}, u32[]{:S(2)}, u32[]{:S(2)}) collective-permute-start(bf16[32,3712]{1,0:T(8,128)(2,1)S(1)} %fusion.1.refs_0_.refs_8_), channel_id=1, source_target_pairs={{0,8},{8,16},{16,24},{24,32},{32,40},{40,48},{48,56},{56,0},{1,9},... | collective-permute-start | bytes 712712 | tf_op jit(solution)/shard_map/ppermute | solution.py:396
  4.4 8.6 %collective-permute-start.1 = (bf16[32,3712]{1,0:T(8,128)(2,1)S(1)}, bf16[32,3712]{1,0:T(8,128)(2,1)S(1)}, u32[]{:S(2)}, u32[]{:S(2)}) collective-permute-start(bf16[32,3712]{1,0:T(8,128)(2,1)S(1)} %fusion.1.refs_0_.refs_8_), channel_id=1, source_target_pairs={{0,56},{8,0},{16,8},{24,16},{32,24},{40,32},{48,40},{56,48},{1,57}... | collective-permute-start | bytes 712712 | tf_op jit(solution)/shard_map/ppermute | solution.py:396
  12.9 5.8 %copy-start.1 = (bf16[256,1792]{1,0:T(8,128)(2,1)}, bf16[256,1792]{1,0:T(8,128)(2,1)S(1)}, u32[]{:S(2)}) copy-start(bf16[256,1792]{1,0:T(8,128)(2,1)S(1)} %scale_down.2.refs_2_) | copy-start | bytes 2752516
  18.7 10.6 %copy-start.20 = (bf16[1,28,2]{1,2,0:T(2,128)(2,1)S(1)}, bf16[1,28,2]{1,2,0:T(2,128)(2,1)}, u32[]{:S(2)}) copy-start(bf16[1,28,2]{1,2,0:T(2,128)(2,1)} %param.29) | copy-start | bytes 340
  18.7 10.6 %copy-start.21 = (bf16[1,28,2]{1,2,0:T(2,128)(2,1)S(1)}, bf16[1,28,2]{1,2,0:T(2,128)(2,1)}, u32[]{:S(2)}) copy-start(bf16[1,28,2]{1,2,0:T(2,128)(2,1)} %param.27) | copy-start | bytes 340
  18.7 61.5 %all-to-all-start = ((bf16[8,8,32,640]{3,2,1,0:T(8,128)(2,1)}), bf16[8,8,32,640]{3,2,1,0:T(8,128)(2,1)}, u32[]{:S(2)}, u32[]{:S(2)}) async-start(bf16[8,8,32,640]{3,2,1,0:T(8,128)(2,1)} %bitcast.28), calls=%async_computation | async-start | bytes 5242880 | tf_op jit(solution)/shard_map/all_to_all | solution.py:446
  26.3 7.2 %collective-permute-start.2 = (bf16[32,3712]{1,0:T(8,128)(2,1)S(1)}, bf16[32,3712]{1,0:T(8,128)(2,1)S(1)}, u32[]{:S(2)}, u32[]{:S(2)}) collective-permute-start(bf16[32,3712]{1,0:T(8,128)(2,1)S(1)} %collective-permute-done.refs_0_.refs_1_.refs_9_), channel_id=1, source_target_pairs={{0,8},{8,16},{16,24},{24,32},{32,40},{40,48},{48,56},{56,0},{1,9},... | collective-permute-start | bytes 712712 | tf_op jit(solution)/shard_map/ppermute | solution.py:396
  29.3 7.6 %collective-permute-start.5 = (bf16[32,3712]{1,0:T(8,128)(2,1)S(1)}, bf16[32,3712]{1,0:T(8,128)(2,1)S(1)}, u32[]{:S(2)}, u32[]{:S(2)}) collective-permute-start(bf16[32,3712]{1,0:T(8,128)(2,1)S(1)} %collective-permute-done.1.refs_1_.refs_5_.refs_13_), channel_id=1, source_target_pairs={{0,56},{8,0},{16,8},{24,16},{32,24},{40,32},{48,40},{56,48},{1,57}... | collective-permute-start | bytes 712712 | tf_op jit(solution)/shard_map/ppermute | solution.py:396
  32.4 7.7 %copy-start.3 = (bf16[3584,256]{1,0:T(8,128)(2,1)}, bf16[3584,256]{1,0:T(8,128)(2,1)S(1)}, u32[]{:S(2)}) copy-start(bf16[3584,256]{1,0:T(8,128)(2,1)S(1)} %scale_wide.2.refs_8_) | copy-start | bytes 5505028
  32.4 42.7 %collective-permute-start.7 = (bf16[3584,256]{1,0:T(8,128)(2,1)S(1)}, bf16[3584,256]{1,0:T(8,128)(2,1)S(1)}, u32[]{:S(2)}, u32[]{:S(2)}) collective-permute-start(bf16[3584,256]{1,0:T(8,128)(2,1)S(1)} %scale_wide.2.refs_8_), channel_id=1, source_target_pairs={{0,128},{128,0},{1,129},{129,1},{2,130},{130,2},{3,131},{131,3},{4... | collective-permute-start | bytes 5505032 | tf_op jit(solution)/shard_map/ppermute | solution.py:392
  37.4 2.8 %copy-start.2 = (bf16[256,1792]{1,0:T(8,128)(2,1)S(1)}, bf16[256,1792]{1,0:T(8,128)(2,1)}, u32[]{:S(2)}) copy-start(bf16[256,1792]{1,0:T(8,128)(2,1)} %copy-done.1) | copy-start | bytes 2752516
  40.1 35.1 %copy-start.5 = (bf16[3584,256]{1,0:T(8,128)(2,1)}, bf16[3584,256]{1,0:T(8,128)(2,1)S(1)}, u32[]{:S(2)}) copy-start(bf16[3584,256]{1,0:T(8,128)(2,1)S(1)} %scale_wide.3.refs_10_) | copy-start | bytes 5505028
  40.1 35.1 %collective-permute-start.8 = (bf16[3584,256]{1,0:T(8,128)(2,1)S(1)}, bf16[3584,256]{1,0:T(8,128)(2,1)S(1)}, u32[]{:S(2)}, u32[]{:S(2)}) collective-permute-start(bf16[3584,256]{1,0:T(8,128)(2,1)S(1)} %scale_wide.3.refs_10_), channel_id=1, source_target_pairs={{0,128},{128,0},{1,129},{129,1},{2,130},{130,2},{3,131},{131,3},{4... | collective-permute-start | bytes 5505032 | tf_op jit(solution)/shard_map/ppermute | solution.py:392
  40.2 34.9 %collective-permute-start.10 = (bf16[256,1792]{1,0:T(8,128)(2,1)S(1)}, bf16[256,1792]{1,0:T(8,128)(2,1)S(1)}, u32[]{:S(2)}, u32[]{:S(2)}) collective-permute-start(bf16[256,1792]{1,0:T(8,128)(2,1)S(1)} %copy-done.2), channel_id=1, source_target_pairs={{0,1},{1,0},{2,3},{3,2},{4,5},{5,4},{6,7},{7,6},{8,9},{9,8},{10,11... | collective-permute-start | bytes 2752520 | tf_op jit(solution)/shard_map/ppermute | solution.py:392
  43.7 31.5 %collective-permute-start.9 = (bf16[256,1792]{1,0:T(8,128)(2,1)S(1)}, bf16[256,1792]{1,0:T(8,128)(2,1)S(1)}, u32[]{:S(2)}, u32[]{:S(2)}) collective-permute-start(bf16[256,1792]{1,0:T(8,128)(2,1)S(1)} %scale_down.3.w0), channel_id=1, source_target_pairs={{0,128},{128,0},{1,129},{129,1},{2,130},{130,2},{3,131},{131,3},{4... | collective-permute-start | bytes 2752520 | tf_op jit(solution)/shard_map/ppermute | solution.py:392
  43.9 0.9 copy-start.15
  44.9 8.5 %collective-permute-start.3 = (bf16[32,3712]{1,0:T(8,128)(2,1)S(1)}, bf16[32,3712]{1,0:T(8,128)(2,1)S(1)}, u32[]{:S(2)}, u32[]{:S(2)}) collective-permute-start(bf16[32,3712]{1,0:T(8,128)(2,1)S(1)} %collective-permute-done.2.refs_0_.refs_2_.refs_10_), channel_id=1, source_target_pairs={{0,8},{8,16},{16,24},{24,32},{32,40},{40,48},{48,56},{56,0},{1,9},... | collective-permute-start | bytes 712712 | tf_op jit(solution)/shard_map/ppermute | solution.py:396
  53.4 8.1 %collective-permute-start.6 = (bf16[32,3712]{1,0:T(8,128)(2,1)S(1)}, bf16[32,3712]{1,0:T(8,128)(2,1)S(1)}, u32[]{:S(2)}, u32[]{:S(2)}) collective-permute-start(bf16[32,3712]{1,0:T(8,128)(2,1)S(1)} %collective-permute-done.5.refs_1_.refs_6_.refs_14_), channel_id=1, source_target_pairs={{0,56},{8,0},{16,8},{24,16},{32,24},{40,32},{48,40},{56,48},{1,57}... | collective-permute-start | bytes 712712 | tf_op jit(solution)/shard_map/ppermute | solution.py:396
  61.5 13.7 %collective-permute-start.4 = (bf16[32,3712]{1,0:T(8,128)(2,1)S(1)}, bf16[32,3712]{1,0:T(8,128)(2,1)S(1)}, u32[]{:S(2)}, u32[]{:S(2)}) collective-permute-start(bf16[32,3712]{1,0:T(8,128)(2,1)S(1)} %collective-permute-done.3.refs_3_.refs_11_), channel_id=1, source_target_pairs={{0,8},{8,16},{16,24},{24,32},{32,40},{40,48},{48,56},{56,0},{1,9},... | collective-permute-start | bytes 712712 | tf_op jit(solution)/shard_map/ppermute | solution.py:396
  75.7 1.3 copy-start.7
  77.1 1.3 copy-start.9
  78.3 0.9 copy-start.11
  79.3 1.0 copy-start.13
  86.8 9.3 %copy-start.12 = (bf16[256,1792]{1,0:T(8,128)(2,1)S(1)}, bf16[256,1792]{1,0:T(8,128)(2,1)}, u32[]{:S(2)}) copy-start(bf16[256,1792]{1,0:T(8,128)(2,1)} %copy-done.11) | copy-start | bytes 2752516
  86.8 100.8 %all-to-all-start.1 = ((bf16[8,8,32,640]{3,2,1,0:T(8,128)(2,1)}), bf16[8,8,32,640]{3,2,1,0:T(8,128)(2,1)}, u32[]{:S(2)}, u32[]{:S(2)}) async-start(bf16[8,8,32,640]{3,2,1,0:T(8,128)(2,1)} %regroup.1), calls=%async_computation.1 | async-start | bytes 5242880 | tf_op jit(solution)/shard_map/all_to_all | solution.py:472
  96.1 2.6 %collective-permute-start.11 = (bf16[256,1792]{1,0:T(8,128)(2,1)S(1)}, bf16[256,1792]{1,0:T(8,128)(2,1)}, u32[]{:S(2)}, u32[]{:S(2)}) collective-permute-start(bf16[256,1792]{1,0:T(8,128)(2,1)S(1)} %copy-done.12), channel_id=1, source_target_pairs={{0,128},{128,0},{1,129},{129,1},{2,130},{130,2},{3,131},{131,3},{4... | collective-permute-start | bytes 2752520 | tf_op jit(solution)/shard_map/ppermute | solution.py:392
  99.2 64.1 %copy-start.4 = (bf16[3584,256]{1,0:T(8,128)(2,1)S(1)}, bf16[3584,256]{1,0:T(8,128)(2,1)}, u32[]{:S(2)}) copy-start(bf16[3584,256]{1,0:T(8,128)(2,1)} %copy-done.3) | copy-start | bytes 5505028
  99.2 64.1 %copy-start.6 = (bf16[3584,256]{1,0:T(8,128)(2,1)S(1)}, bf16[3584,256]{1,0:T(8,128)(2,1)}, u32[]{:S(2)}) copy-start(bf16[3584,256]{1,0:T(8,128)(2,1)} %copy-done.5) | copy-start | bytes 5505028
  104.5 13.9 %collective-permute-start.12 = (bf16[64,3584]{1,0:T(8,128)(2,1)S(1)}, bf16[64,3584]{1,0:T(8,128)(2,1)S(1)}, u32[]{:S(2)}, u32[]{:S(2)}) collective-permute-start(bf16[64,3584]{1,0:T(8,128)(2,1)S(1)} %get-tuple-element.14), channel_id=1, source_target_pairs={{0,2},{2,4},{4,6},{6,0},{64,66},{66,68},{68,70},{70,64},{1,3},{3,5... | collective-permute-start | bytes 1376264 | tf_op jit(solution)/shard_map/ppermute | solution.py:400
  106.1 43.0 %collective-permute-start.13 = (bf16[64,3584]{1,0:T(8,128)(2,1)S(1)}, bf16[64,3584]{1,0:T(8,128)(2,1)S(1)}, u32[]{:S(2)}, u32[]{:S(2)}) collective-permute-start(bf16[64,3584]{1,0:T(8,128)(2,1)S(1)} %get-tuple-element.15), channel_id=1, source_target_pairs={{0,4},{2,6},{4,0},{6,2},{64,68},{66,70},{68,64},{70,66},{1,5},{3,7... | collective-permute-start | bytes 1376264 | tf_op jit(solution)/shard_map/ppermute | solution.py:400
  109.1 40.0 %collective-permute-start.14 = (bf16[64,3584]{1,0:T(8,128)(2,1)S(1)}, bf16[64,3584]{1,0:T(8,128)(2,1)S(1)}, u32[]{:S(2)}, u32[]{:S(2)}) collective-permute-start(bf16[64,3584]{1,0:T(8,128)(2,1)S(1)} %get-tuple-element.16), channel_id=1, source_target_pairs={{0,6},{2,0},{4,2},{6,4},{64,70},{66,64},{68,66},{70,68},{1,7},{3,1... | collective-permute-start | bytes 1376264 | tf_op jit(solution)/shard_map/ppermute | solution.py:400
  110.2 38.9 %collective-permute-start.15 = (bf16[64,3584]{1,0:T(8,128)(2,1)S(1)}, bf16[64,3584]{1,0:T(8,128)(2,1)S(1)}, u32[]{:S(2)}, u32[]{:S(2)}) collective-permute-start(bf16[64,3584]{1,0:T(8,128)(2,1)S(1)} %get-tuple-element.17), channel_id=1, source_target_pairs={{0,64},{2,66},{4,68},{6,70},{64,0},{66,2},{68,4},{70,6},{1,65},{3,... | collective-permute-start | bytes 1376264 | tf_op jit(solution)/shard_map/ppermute | solution.py:400
  110.2 38.9 %collective-permute-start.16 = (bf16[64,3584]{1,0:T(8,128)(2,1)S(1)}, bf16[64,3584]{1,0:T(8,128)(2,1)S(1)}, u32[]{:S(2)}, u32[]{:S(2)}) collective-permute-start(bf16[64,3584]{1,0:T(8,128)(2,1)S(1)} %get-tuple-element.18), channel_id=1, source_target_pairs={{0,66},{2,68},{4,70},{6,64},{64,2},{66,4},{68,6},{70,0},{1,67},{3,... | collective-permute-start | bytes 1376264 | tf_op jit(solution)/shard_map/ppermute | solution.py:400
  118.4 30.7 %collective-permute-start.17 = (bf16[64,3584]{1,0:T(8,128)(2,1)S(1)}, bf16[64,3584]{1,0:T(8,128)(2,1)S(1)}, u32[]{:S(2)}, u32[]{:S(2)}) collective-permute-start(bf16[64,3584]{1,0:T(8,128)(2,1)S(1)} %get-tuple-element.19), channel_id=1, source_target_pairs={{0,68},{2,70},{4,64},{6,66},{64,4},{66,6},{68,0},{70,2},{1,69},{3,... | collective-permute-start | bytes 1376264 | tf_op jit(solution)/shard_map/ppermute | solution.py:400
  149.1 14.2 %collective-permute-start.18 = (bf16[64,3584]{1,0:T(8,128)(2,1)S(1)}, bf16[64,3584]{1,0:T(8,128)(2,1)S(1)}, u32[]{:S(2)}, u32[]{:S(2)}) collective-permute-start(bf16[64,3584]{1,0:T(8,128)(2,1)S(1)} %get-tuple-element.20), channel_id=1, source_target_pairs={{0,70},{2,64},{4,66},{6,68},{64,6},{66,0},{68,2},{70,4},{1,71},{3,... | collective-permute-start | bytes 1376264 | tf_op jit(solution)/shard_map/ppermute | solution.py:400
  163.3 1.5 copy-start.8
  164.8 1.5 copy-start.10
  166.3 4.9 %copy-start.22 = (s32[8]{0:T(128)S(1)}, s32[8]{0:T(128)}, u32[]{:S(2)}) copy-start(s32[8]{0:T(128)} %constant.112) | copy-start | bytes 100
  166.3 16.5 %copy-start.14 = (bf16[256,1792]{1,0:T(8,128)(2,1)S(1)}, bf16[256,1792]{1,0:T(8,128)(2,1)}, u32[]{:S(2)}) copy-start(bf16[256,1792]{1,0:T(8,128)(2,1)} %copy-done.13) | copy-start | bytes 2752516
  166.3 16.5 %copy-start.16 = (bf16[256,1792]{1,0:T(8,128)(2,1)S(1)}, bf16[256,1792]{1,0:T(8,128)(2,1)}, u32[]{:S(2)}) copy-start(bf16[256,1792]{1,0:T(8,128)(2,1)} %copy-done.15) | copy-start | bytes 2752516
  170.3 12.5 %collective-permute-start.19 = (bf16[512,512]{1,0:T(8,128)(2,1)S(1)}, bf16[512,512]{1,0:T(8,128)(2,1)}, u32[]{:S(2)}, u32[]{:S(2)}) collective-permute-start(bf16[512,512]{1,0:T(8,128)(2,1)S(1)} %hidden_units.1.h0), channel_id=1, source_target_pairs={{0,1},{1,0},{2,3},{3,2},{4,5},{5,4},{6,7},{7,6},{8,9},{9,8},{10,11... | collective-permute-start | bytes 1572872 | tf_op jit(solution)/shard_map/ppermute | solution.py:392
  187.6 51.5 %all-to-all-start.2 = ((bf16[64,8,1792]{2,1,0:T(8,128)(2,1)}), bf16[64,8,1792]{2,1,0:T(8,128)(2,1)S(1)}, u32[]{:S(2)}, u32[]{:S(2)}) async-start(bf16[64,8,1792]{2,1,0:T(8,128)(2,1)} %down_rows.1.refs_0_), calls=%async_computation.2 | async-start | bytes 3670016 | tf_op jit(solution)/shard_map/all_to_all | solution.py:481
  199.7 3.5 %copy-start.18 = (s32[32,8]{0,1:T(8,128)S(1)}, s32[32,8]{0,1:T(8,128)}, u32[]{:S(2)}) copy-start(s32[32,8]{0,1:T(8,128)} %param.24) | copy-start | bytes 3076
  199.7 3.6 %copy-start.17 = (bf16[32,576]{1,0:T(8,128)(2,1)S(1)}, bf16[32,576]{1,0:T(8,128)(2,1)}, u32[]{:S(2)}) copy-start(bf16[32,576]{1,0:T(8,128)(2,1)} %param.22) | copy-start | bytes 110596
  199.7 3.7 %copy-start.19 = (f32[32,8]{0,1:T(8,128)S(1)}, f32[32,8]{0,1:T(8,128)}, u32[]{:S(2)}) copy-start(f32[32,8]{0,1:T(8,128)} %param.25) | copy-start | bytes 3076
  202.4 44.6 %collective-permute-start.20 = (bf16[32,32,640]{2,1,0:T(8,128)(2,1)S(1)}, bf16[32,32,640]{2,1,0:T(8,128)(2,1)}, u32[]{:S(2)}, u32[]{:S(2)}) collective-permute-start(bf16[32,32,640]{2,1,0:T(8,128)(2,1)S(1)} %compact.1.mine), channel_id=1, source_target_pairs={{0,1},{1,0},{2,3},{3,2},{4,5},{5,4},{6,7},{7,6},{8,9},{9,8},{10,11... | collective-permute-start | bytes 3932168 | tf_op jit(solution)/shard_map/ppermute | solution.py:392

commit v4 on v3

--- a/solution.py
+++ b/solution.py
@@ -161,34 +161,36 @@
     )(place, *blocks, *blocks, *before)
 
 
+PEER_ORDER = (4, 1, 5, 2, 6, 3, 7, 0)
+
+
 def hidden_kernel(*refs):
-    tokens, (g0, g1, u0, u1, out), (x,) = refs[:8], refs[8:13], refs[13:]
-    for r, token in enumerate(tokens):
+    tokens, (gate, up, out, x) = refs[:8], refs[8:]
+    for r, token in zip(PEER_ORDER, tokens):
         x[r * 64 : (r + 1) * 64, :] = token[...]
     for half in range(2):
         rows = slice(half * 256, (half + 1) * 256)
-        for n, (gate, up) in enumerate(((g0, u0), (g1, u1))):
-            g = jnp.dot(x[rows, :], gate[...], preferred_element_type=F32)
-            u = jnp.dot(x[rows, :], up[...], preferred_element_type=F32)
-            out[rows, n * 256 : (n + 1) * 256] = (g / (1.0 + jnp.exp(-g)) * u).astype(BF16)
-
-
-def hidden_units(tokens, g0, g1, u0, u1):
+        g = jnp.dot(x[rows, :], gate[...], preferred_element_type=F32)
+        u = jnp.dot(x[rows, :], up[...], preferred_element_type=F32)
+        out[rows, :] = (g / (1.0 + jnp.exp(-g)) * u).astype(BF16)
+
+
+def hidden_units(tokens, gate, up):
     vmem = pl.BlockSpec(memory_space=pltpu.VMEM)
     return pl.pallas_call(
         hidden_kernel,
-        in_specs=[vmem] * 12,
+        in_specs=[vmem] * 10,
         out_specs=vmem,
-        out_shape=jax.ShapeDtypeStruct((512, 512), BF16),
+        out_shape=jax.ShapeDtypeStruct((512, 256), BF16),
         scratch_shapes=[pltpu.VMEM((512, D), BF16)],
         compiler_params=params(10),
-        cost_estimate=cost(3.8e9, 12e6),
+        cost_estimate=cost(1.9e9, 8e6),
         name="hidden_units",
-    )(*tokens, g0, g1, u0, u1)
-
-
-def down_kernel(order_ref, h0, h1, w0, w1, w2, w3, out):
-    h = jnp.concatenate([h0[...], h1[...]], axis=1)
+    )(*[tokens[r] for r in PEER_ORDER], gate, up)
+
+
+def down_kernel(order_ref, h0, h1, h2, h3, w0, w1, w2, w3, out):
+    h = jnp.concatenate([part[...] for part in (h0, h1, h2, h3)], axis=1)
     for c in range(HALF_D // 256):
         cols = slice(c * 256, (c + 1) * 256)
         w = jnp.concatenate([p[:, cols] for p in (w0, w1, w2, w3)], axis=0)
@@ -197,17 +199,17 @@
             out[order_ref[group], :, cols] = rows[group * CAP : (group + 1) * CAP, :].astype(BF16)
 
 
-def down_rows(order, h0, h1, weights):
+def down_rows(order, parts, weights):
     vmem = pl.BlockSpec(memory_space=pltpu.VMEM)
     return pl.pallas_call(
         down_kernel,
-        in_specs=[smem()] + [vmem] * 6,
+        in_specs=[smem()] + [vmem] * 8,
         out_specs=vmem,
         out_shape=jax.ShapeDtypeStruct((EP, CAP, HALF_D), BF16),
         compiler_params=params(10),
         cost_estimate=cost(1.9e9, 7e6),
         name="down_rows",
-    )(order, h0, h1, *weights)
+    )(order, *parts, *weights)
 
 
 def blend_kernel(routing_ref, weight_ref, rows_ref, out):
@@ -442,7 +444,7 @@
     facts = jnp.concatenate([mine, slot[:, None] + 1, lengths[:, None]], axis=1)
     index = jnp.sum(jnp.where(to_owner[:, :, None], facts[None], 0), axis=1)
     index = index - (jnp.arange(4) == 2).astype(I32)[None, :]
-    leaving = collect(index, latent_pages, once(up_way[1], down_way[1], down_send)).reshape(8, 8, 32, LANES)
+    leaving = collect(index, latent_pages, once(up_way[1], down_way[1])).reshape(8, 8, 32, LANES)
     midway = lax.all_to_all(leaving, ("xh", "y"), split_axis=0, concat_axis=0, tiled=True)
     for step in range(1, 4):
         up_way.append(z_shift(up_way[-1], 1))
@@ -451,33 +453,34 @@
     behind = np.array([0, 1, 2, 3, 4, -1, -2, -3], np.int32)
 
     gate = scale_wide(gate_value, gate_scale, once(up_way[1], down_way[1]))
-    up = scale_wide(up_value, up_scale, once(up_way[2], down_way[2]))
+    up = scale_wide(up_value, up_scale, once(up_way[2], down_way[2], down_tp))
     down_keep = scale_down(tp_index, down_value, down_scale, once(up_way[2], down_way[2]))
     gate_far, up_far = swap(gate, "pool"), swap(up, "pool")
     down_far, down_tp_far = swap(down_keep, "pool"), swap(down_tp, "pool")
 
     midway = regroup(
-        midway, once(up_way[4], down_way[3], gate_far, up_far, down_far, down_tp)
+        midway, once(up_way[4], down_way[3], gate_far, up_far, down_far)
     )
     picked = pick_rows(
         place, up_way + down_way[1:], once(down_tp_far)
     )
-    tokens = [picked[0]] + [
-        plane_shift(picked[dx * NY + dy], dx, dy)
-        for dx in range(NX)
-        for dy in range(NY)
-        if dx or dy
-    ]
+    tokens = list(picked)
+    for peer in PEER_ORDER[:7]:
+        tokens[peer] = plane_shift(picked[peer], peer // NY, peer % NY)
 
     arrived = lax.all_to_all(midway, "z", split_axis=0, concat_axis=0, tiled=True)
 
-    act = hidden_units(tokens, gate, gate_far, up, up_far)
-    act_tp = swap(act, "tp")
+    act, act_far = hidden_units(tokens, gate, up), hidden_units(tokens, gate_far, up_far)
+    act_tp, act_tp_far = swap(act, "tp"), swap(act_far, "tp")
     group = jnp.arange(EP, dtype=I32)
     order = (
         ((xh + (group >> 5)) % NX) * NZ + (z - jnp.tile(jnp.asarray(behind), 8)) % NZ
     ) * NY + (y - (group >> 3)) % NY
-    out_rows = down_rows(order, act, act_tp, [down_keep, down_far, down_tp, down_tp_far])
+    out_rows = down_rows(
+        order,
+        [act, act_far, act_tp, act_tp_far],
+        [down_keep, down_far, down_tp, down_tp_far],
+    )
     returned = lax.all_to_all(
         out_rows, ("xh", "z", "y"), split_axis=0, concat_axis=0, tiled=True
     )

time: 253 us -> 226 us (0.89)
  waiting for transfers between devices: 132 us -> 80.6 us
  starting transfers between devices: 53.1 us -> 78.6 us
    ppermute x7, waiting for transfers between devices: 47.4 us -> 14.4 us  [plane_shift(): lax.ppermute(x, ('xh', 'y'), [(a * NY + b, (a + dx) % NX * NY + (b + dy)...]
    ppermute x7, starting transfers between devices: 11.4 us -> 33.3 us  [plane_shift(): lax.ppermute(x, ('xh', 'y'), [(a * NY + b, (a + dx) % NX * NY + (b + dy)...]
    ppermute x7 -> x8, waiting for transfers between devices: 30.6 us -> 16.5 us  [swap(): return lax.ppermute(x, axis, [(0, 1), (1, 0)])]
    ppermute x7, waiting for transfers between devices: 18 us -> 13.6 us  [z_shift(): return lax.ppermute(x, 'z', [(i, (i + by) % NZ) for i in range(NZ)])]
    all_to_all x1, starting transfers between devices: 10.4 us -> 13.2 us  [on_device(): lax.all_to_all(out_rows, ('xh', 'z', 'y'), split_axis=0, concat_axis=0, t...]
    unnamed x49 -> x51, local copies, waits for them, and re-layouts: 12.6 us -> 11.8 us
    pallas_call x2 -> x3, Pallas kernels: 8.71 us -> 9.05 us  [the longest x1 4.87 us: down_rows(): pl.pallas_call(down_kernel, in_specs=[smem()] + [vmem] * 8, out_specs=vme...]
  transfers between devices with their start and end apart: 24 -> 25, of which waited for: 13 -> 12; matrix products, arithmetic and copies ran while one was open for 3% -> 3% of each run, Pallas kernels for 12% -> 17%
where the time goes in v4:
time: 226 us; the launch traced here: 225 us
  waiting for transfers between devices  80.6 us (36%)
  starting transfers between devices  78.6 us (35%)
  Pallas kernels  48.7 us (22%)
  local copies, waits for them, and re-layouts  12.3 us (5%)
  other arithmetic  3.75 us (2%)
    all_to_all x1, waiting for transfers between devices, on_device(): lax.all_to_all(out_rows, ('xh', 'z', 'y'), split_axis=0, concat_axis=0, t...  36 us
    ppermute x7, starting transfers between devices, plane_shift(): lax.ppermute(x, ('xh', 'y'), [(a * NY + b, (a + dx) % NX * NY + (b + dy)...  33.3 us
    ppermute x8, waiting for transfers between devices, swap(): return lax.ppermute(x, axis, [(0, 1), (1, 0)])  16.5 us
    ppermute x7, waiting for transfers between devices, plane_shift(): lax.ppermute(x, ('xh', 'y'), [(a * NY + b, (a + dx) % NX * NY + (b + dy)...  14.4 us
    ppermute x7, waiting for transfers between devices, z_shift(): return lax.ppermute(x, 'z', [(i, (i + by) % NZ) for i in range(NZ)])  13.6 us
    all_to_all x1, starting transfers between devices, on_device(): lax.all_to_all(out_rows, ('xh', 'z', 'y'), split_axis=0, concat_axis=0, t...  13.2 us
    unnamed x51, local copies, waits for them, and re-layouts  11.8 us
    ppermute x7, starting transfers between devices, z_shift(): return lax.ppermute(x, 'z', [(i, (i + by) % NZ) for i in range(NZ)])  10.8 us
  transfers between devices with their start and end apart: 25, of which 12 were waited for; matrix products, arithmetic and copies ran while one was open for 3% of the time, Pallas kernels for 17%

profile of v4, /device:TPU:68, one launch (start us, length us, event | category | flops | bytes accessed | tf_op | source)
XLA Modules:
  0.0 224.9 jit_solution(4594123416139532100)
XLA Ops:
  0.7 0.7 convert_element_type.39
  1.5 1.0 fusion.1.refs_0_.refs_8_
  2.4 2.0 collective-permute-start
  4.4 0.1 collective-permute-start.1
  4.5 0.7 bitcast_convert_fusion.scale
  5.2 2.5 %scale_down.2 = bf16[256,1792]{1,0:T(8,128)(2,1)} custom-call(s32[1]{0:T(128)S(6)} %sub.36.half_ref, f32[2,28]{1,0:T(2,128)S(1)} %bitcast_convert_fusion.scale, bf16[1,256,3584]{2,1,0:T(8,128)(2,1)} %value.7), custom_call_target="tpu_custom_call" | custom-call | flops 1000000 | bytes 2000000 | tf_op jit(solution)/shard_map/scale_down/pallas_call | solution.py:88
  7.6 1.2 collective-permute-start.8
  9.2 3.9 %copy.43.pages = bf16[128,16,576]{2,1,0:T(8,128)(2,1)S(1)} copy(bf16[128,16,576]{0,2,1:T(8,128)(2,1)} %param.17) | data formatting | bytes 4718592 | tf_op args[0]
  13.1 0.5 once.6.rest_0_
  13.7 5.2 %collect.1 = bf16[64,32,640]{2,1,0:T(8,128)(2,1)} custom-call(s32[64,4]{1,0:T(8,128)S(1)} %broadcast_subtract_fusion.index_ref, bf16[128,16,576]{2,1,0:T(8,128)(2,1)S(1)} %copy.43.pages, f32[1]{0:T(128)} %once.6.rest_0_), custom_call_target="tpu_custom_call" | custom-call | flops 1000000 | bytes 6000000 | tf_op jit(solution)/shard_map/collect/pallas_call | solution.py:266
  18.9 7.6 %all-to-all-start = ((bf16[8,8,32,640]{3,2,1,0:T(8,128)(2,1)}), bf16[8,8,32,640]{3,2,1,0:T(8,128)(2,1)}, u32[]{:S(2)}, u32[]{:S(2)}) async-start(bf16[8,8,32,640]{3,2,1,0:T(8,128)(2,1)} %bitcast.28), calls=%async_computation | async-start | bytes 5242880 | tf_op jit(solution)/shard_map/all_to_all | solution.py:448
  26.4 3.0 %collective-permute-start.2 = (bf16[32,3712]{1,0:T(8,128)(2,1)S(1)}, bf16[32,3712]{1,0:T(8,128)(2,1)S(1)}, u32[]{:S(2)}, u32[]{:S(2)}) collective-permute-start(bf16[32,3712]{1,0:T(8,128)(2,1)S(1)} %collective-permute-done.refs_0_.refs_1_.refs_9_), channel_id=1, source_target_pairs={{0,8},{8,16},{16,24},{24,32},{32,40},{40,48},{48,56},{56,0},{1,9},... | collective-permute-start | bytes 712712 | tf_op jit(solution)/shard_map/ppermute | solution.py:398
  29.5 2.6 %scale_wide.2.refs_8_ = bf16[3584,256]{1,0:T(8,128)(2,1)S(1)} custom-call(f32[2,28]{1,0:T(2,128)S(1)} %convert_bitcast_fusion.1.scale, bf16[1,3584,256]{2,1,0:T(8,128)(2,1)} %value.4, f32[1]{0:T(128)} %once.6.rest_0_), custom_call_target="tpu_custom_call" | custom-call | flops 1000000 | bytes 4000000 | tf_op jit(solution)/shard_map/scale_wide/pallas_call | solution.py:64
  32.2 1.2 collective-permute-done.2.refs_0_.refs_2_.refs_10_
  33.4 3.4 %collective-permute-done.5.refs_1_.refs_6_.refs_14_ = bf16[32,3712]{1,0:T(8,128)(2,1)S(1)} collective-permute-done((bf16[32,3712]{1,0:T(8,128)(2,1)S(1)}, bf16[32,3712]{1,0:T(8,128)(2,1)S(1)}, u32[]{:S(2)}, u32[]{:S(2)}) %collective-permute-start.5) | collective-permute-done | bytes 237600 | tf_op jit(solution)/shard_map/ppermute | solution.py:398
  36.8 0.5 once.7.rest_0_
  37.3 2.6 %scale_wide.3.refs_9_ = bf16[3584,256]{1,0:T(8,128)(2,1)S(1)} custom-call(f32[2,28]{1,0:T(2,128)S(1)} %convert_bitcast_fusion.scale, bf16[1,3584,256]{2,1,0:T(8,128)(2,1)} %value.6, f32[1]{0:T(128)} %once.7.rest_0_), custom_call_target="tpu_custom_call" | custom-call | flops 1000000 | bytes 4000000 | tf_op jit(solution)/shard_map/scale_wide/pallas_call | solution.py:64
  40.0 0.5 once.8.rest_0_
  40.6 2.2 scale_down.3.w0
  42.7 0.6 collective-permute-start.10
  43.3 0.9 copy-done.11
  44.2 3.2 %collective-permute-start.3 = (bf16[32,3712]{1,0:T(8,128)(2,1)S(1)}, bf16[32,3712]{1,0:T(8,128)(2,1)S(1)}, u32[]{:S(2)}, u32[]{:S(2)}) collective-permute-start(bf16[32,3712]{1,0:T(8,128)(2,1)S(1)} %collective-permute-done.2.refs_0_.refs_2_.refs_10_), channel_id=1, source_target_pairs={{0,8},{8,16},{16,24},{24,32},{32,40},{40,48},{48,56},{56,0},{1,9},... | collective-permute-start | bytes 712712 | tf_op jit(solution)/shard_map/ppermute | solution.py:398
  47.5 5.2 %collective-permute-done.3.refs_3_.refs_11_ = bf16[32,3712]{1,0:T(8,128)(2,1)S(1)} collective-permute-done((bf16[32,3712]{1,0:T(8,128)(2,1)S(1)}, bf16[32,3712]{1,0:T(8,128)(2,1)S(1)}, u32[]{:S(2)}, u32[]{:S(2)}) %collective-permute-start.3) | collective-permute-done | bytes 237600 | tf_op jit(solution)/shard_map/ppermute | solution.py:398
  52.7 2.5 %collective-permute-start.4 = (bf16[32,3712]{1,0:T(8,128)(2,1)S(1)}, bf16[32,3712]{1,0:T(8,128)(2,1)S(1)}, u32[]{:S(2)}, u32[]{:S(2)}) collective-permute-start(bf16[32,3712]{1,0:T(8,128)(2,1)S(1)} %collective-permute-done.3.refs_3_.refs_11_), channel_id=1, source_target_pairs={{0,8},{8,16},{16,24},{24,32},{32,40},{40,48},{48,56},{56,0},{1,9},... | collective-permute-start | bytes 712712 | tf_op jit(solution)/shard_map/ppermute | solution.py:398
  55.2 0.7 copy-done.9
  55.9 3.8 %collective-permute-done.4.refs_0_.refs_4_.refs_12_ = bf16[32,3712]{1,0:T(8,128)(2,1)S(1)} collective-permute-done((bf16[32,3712]{1,0:T(8,128)(2,1)S(1)}, bf16[32,3712]{1,0:T(8,128)(2,1)S(1)}, u32[]{:S(2)}, u32[]{:S(2)}) %collective-permute-start.4) | collective-permute-done | bytes 237600 | tf_op jit(solution)/shard_map/ppermute | solution.py:398
  59.7 0.5 once.9.rest_0_
  60.2 1.3 copy-done.3
  61.5 1.3 copy-done.5
  62.8 0.7 copy-done.7
  63.5 0.9 copy-done.13
  64.4 6.5 %regroup.1 = bf16[8,8,32,640]{3,2,1,0:T(8,128)(2,1)} custom-call(bf16[8,8,32,640]{3,2,1,0:T(8,128)(2,1)} %all-to-all-done.midway, f32[1]{0:T(128)} %once.9.rest_0_), custom_call_target="tpu_custom_call" | custom-call | flops 1000000 | bytes 6000000 | tf_op jit(solution)/shard_map/regroup/pallas_call | solution.py:284
  71.0 8.6 %all-to-all-start.1 = ((bf16[8,8,32,640]{3,2,1,0:T(8,128)(2,1)}), bf16[8,8,32,640]{3,2,1,0:T(8,128)(2,1)}, u32[]{:S(2)}, u32[]{:S(2)}) async-start(bf16[8,8,32,640]{3,2,1,0:T(8,128)(2,1)} %regroup.1), calls=%async_computation.1 | async-start | bytes 5242880 | tf_op jit(solution)/shard_map/all_to_all | solution.py:471
  79.6 2.7 %collective-permute-done.11.refs_0_.w3 = bf16[256,1792]{1,0:T(8,128)(2,1)} collective-permute-done((bf16[256,1792]{1,0:T(8,128)(2,1)}, bf16[256,1792]{1,0:T(8,128)(2,1)}, u32[]{:S(2)}, u32[]{:S(2)}) %collective-permute-start.11) | collective-permute-done | bytes 917536 | tf_op jit(solution)/shard_map/ppermute | solution.py:394
  82.3 0.5 once.10.refs_16_
  82.9 0.9 copy-done.8
  83.8 0.9 copy-done.10
  84.7 5.3 %pick_rows.1 = (bf16[64,3584]{1,0:T(8,128)(2,1)S(1)}, bf16[64,3584]{1,0:T(8,128)(2,1)S(1)}, bf16[64,3584]{1,0:T(8,128)(2,1)S(1)}, bf16[64,3584]{1,0:T(8,128)(2,1...) custom-call(s32[3]{0:T(128)S(1)} %pad_add_fusion.1.place_ref, ...), custom_call_target="tpu_custom_call" | custom-call | flops 1000000000 | bytes 6000000 | tf_op jit(solution)/shard_map/pick_rows/pallas_call | solution.py:148
  90.1 2.0 collective-permute-start.13
  92.1 3.9 %collective-permute-start.14 = (bf16[64,3584]{1,0:T(8,128)(2,1)S(1)}, bf16[64,3584]{1,0:T(8,128)(2,1)S(1)}, u32[]{:S(2)}, u32[]{:S(2)}) collective-permute-start(bf16[64,3584]{1,0:T(8,128)(2,1)S(1)} %get-tuple-element.15), channel_id=1, source_target_pairs={{0,66},{2,68},{4,70},{6,64},{64,2},{66,4},{68,6},{70,0},{1,67},{3,... | collective-permute-start | bytes 1376264 | tf_op jit(solution)/shard_map/ppermute | solution.py:402
  96.0 1.8 collective-permute-start.15
  97.8 1.8 collective-permute-start.16
  99.5 5.4 %collective-permute-done.12.refs_0_ = bf16[64,3584]{1,0:T(8,128)(2,1)S(1)} collective-permute-done((bf16[64,3584]{1,0:T(8,128)(2,1)S(1)}, bf16[64,3584]{1,0:T(8,128)(2,1)S(1)}, u32[]{:S(2)}, u32[]{:S(2)}) %collective-permute-start.12) | collective-permute-done | bytes 458784 | tf_op jit(solution)/shard_map/ppermute | solution.py:402
  105.0 2.7 %collective-permute-start.17 = (bf16[64,3584]{1,0:T(8,128)(2,1)S(1)}, bf16[64,3584]{1,0:T(8,128)(2,1)S(1)}, u32[]{:S(2)}, u32[]{:S(2)}) collective-permute-start(bf16[64,3584]{1,0:T(8,128)(2,1)S(1)} %get-tuple-element.18), channel_id=1, source_target_pairs={{0,6},{2,0},{4,2},{6,4},{64,70},{66,64},{68,66},{70,68},{1,7},{3,1... | collective-permute-start | bytes 1376264 | tf_op jit(solution)/shard_map/ppermute | solution.py:402
  107.7 21.2 %collective-permute-start.18 = (bf16[64,3584]{1,0:T(8,128)(2,1)S(1)}, bf16[64,3584]{1,0:T(8,128)(2,1)S(1)}, u32[]{:S(2)}, u32[]{:S(2)}) collective-permute-start(bf16[64,3584]{1,0:T(8,128)(2,1)S(1)} %get-tuple-element.19), channel_id=1, source_target_pairs={{0,70},{2,64},{4,66},{6,68},{64,6},{66,0},{68,2},{70,4},{1,71},{3,... | collective-permute-start | bytes 1376264 | tf_op jit(solution)/shard_map/ppermute | solution.py:402
  128.8 5.7 %collective-permute-done.15.refs_3_ = bf16[64,3584]{1,0:T(8,128)(2,1)S(1)} collective-permute-done((bf16[64,3584]{1,0:T(8,128)(2,1)S(1)}, bf16[64,3584]{1,0:T(8,128)(2,1)S(1)}, u32[]{:S(2)}, u32[]{:S(2)}) %collective-permute-start.15) | collective-permute-done | bytes 458784 | tf_op jit(solution)/shard_map/ppermute | solution.py:402
  134.6 3.3 %collective-permute-done.17.refs_5_ = bf16[64,3584]{1,0:T(8,128)(2,1)S(1)} collective-permute-done((bf16[64,3584]{1,0:T(8,128)(2,1)S(1)}, bf16[64,3584]{1,0:T(8,128)(2,1)S(1)}, u32[]{:S(2)}, u32[]{:S(2)}) %collective-permute-start.17) | collective-permute-done | bytes 458784 | tf_op jit(solution)/shard_map/ppermute | solution.py:402
  137.8 2.1 hidden_units.2.h0
  140.0 0.9 collective-permute-start.19
  140.9 2.1 hidden_units.3.h1
  143.0 1.3 collective-permute-start.20
  144.4 4.9 %collective-permute-done.19.h2 = bf16[512,256]{1,0:T(8,128)(2,1)S(1)} collective-permute-done((bf16[512,256]{1,0:T(8,128)(2,1)S(1)}, bf16[512,256]{1,0:T(8,128)(2,1)S(1)}, u32[]{:S(2)}, u32[]{:S(2)}) %collective-permute-start.19) | collective-permute-done | bytes 262176 | tf_op jit(solution)/shard_map/ppermute | solution.py:394
  149.3 3.1 %collective-permute-done.20.h3 = bf16[512,256]{1,0:T(8,128)(2,1)S(1)} collective-permute-done((bf16[512,256]{1,0:T(8,128)(2,1)S(1)}, bf16[512,256]{1,0:T(8,128)(2,1)S(1)}, u32[]{:S(2)}, u32[]{:S(2)}) %collective-permute-start.20) | collective-permute-done | bytes 262176 | tf_op jit(solution)/shard_map/ppermute | solution.py:394
  152.4 4.9 %down_rows.1.refs_0_ = bf16[64,8,1792]{2,1,0:T(8,128)(2,1)} custom-call(s32[64]{0:T(128)S(1)} %fusion.3.order_ref, bf16[512,256]{1,0:T(8,128)(2,1)S(1)} %hidden_units.2.h0, bf16[512,256]{1,0:T(8,128)(2,1)S(1)} %hidden_units.3.h1, bf16[512,256]{1,0:T(8,128)(2,1)S(1)} %collective-permute-done.19.h2, bf16[512,256]{1,0:T(8,128)(2,1)S(1)} %collective-permute-done.20.h3, ...), custom_call_target="tpu_custom_call" | custom-call | flops 1900000000 | bytes 7000000 | tf_op jit(solution)/shard_map/down_rows/pallas_call | solution.py:204
  157.3 13.2 %all-to-all-start.2 = ((bf16[64,8,1792]{2,1,0:T(8,128)(2,1)}), bf16[64,8,1792]{2,1,0:T(8,128)(2,1)S(1)}, u32[]{:S(2)}, u32[]{:S(2)}) async-start(bf16[64,8,1792]{2,1,0:T(8,128)(2,1)} %down_rows.1.refs_0_), calls=%async_computation.2 | async-start | bytes 3670016 | tf_op jit(solution)/shard_map/all_to_all | solution.py:484
  170.5 0.5 once.11.rest_0_
  171.0 1.0 slice_convert_fusion
  172.1 0.1 select_reduce_fusion.1
  172.3 2.6 %compact.1.mine = bf16[32,32,640]{2,1,0:T(8,128)(2,1)S(1)} custom-call(s32[32]{0:T(128)S(1)} %get-tuple-element.23.source_ref, bf16[64,32,640]{2,1,0:T(8,128)(2,1)} %bitcast.10.arrived, f32[1]{0:T(128)} %once.11.rest_0_), custom_call_target="tpu_custom_call" | custom-call | flops 1000000 | bytes 4000000 | tf_op jit(solution)/shard_map/compact/pallas_call | solution.py:304
  174.9 0.9 collective-permute-start.21
  176.1 36.0 %all-to-all-done.2.rows_ref = bf16[64,8,1792]{2,1,0:T(8,128)(2,1)S(1)} async-done(((bf16[64,8,1792]{2,1,0:T(8,128)(2,1)}), bf16[64,8,1792]{2,1,0:T(8,128)(2,1)S(1)}, u32[]{:S(2)}, u32[]{:S(2)}) %all-to-all-start.2) | async-done | bytes 1835040 | tf_op jit(solution)/shard_map/all_to_all | solution.py:484
  212.1 2.1 blend.1
  214.1 5.8 %collective-permute-done.21.other = bf16[32,32,640]{2,1,0:T(8,128)(2,1)} collective-permute-done((bf16[32,32,640]{2,1,0:T(8,128)(2,1)S(1)}, bf16[32,32,640]{2,1,0:T(8,128)(2,1)}, u32[]{:S(2)}, u32[]{:S(2)}) %collective-permute-start.21) | collective-permute-done | bytes 1310752 | tf_op jit(solution)/shard_map/ppermute | solution.py:394
  219.9 5.0 %attend.1 = (bf16[32,64,576]{2,1,0:T(8,128)(2,1)}, bf16[32,32,512]{2,1,0:T(8,128)(2,1)}) custom-call(s32[1]{0:T(128)} %bitcast.half_ref.tp_ref, s32[32]{0:T(128)S(1)} %get-tuple-element.24.length_ref, bf16[32,32,640]{2,1,0:T(8,128)(2,1)S(1)} %compact.1.mine, bf16[32,32,640]{2,1,0:T(8,128)(2,1)} %collective-permute-done.21.other, ...), custom_call_target="tpu_custom_call" | custom-call | flops 200000000 | bytes 8000000 | tf_op jit(solution)/shard_map/attend/pallas_call | solution.py:352
  (80 shorter events, 1.3 us)
Async XLA Ops:
  0.6 8.2 %copy-start = (s32[32,4]{0,1:T(4,128)S(1)}, s32[32,4]{0,1:T(4,128)}, u32[]{:S(2)}) copy-start(s32[32,4]{0,1:T(4,128)} %param.18) | copy-start | bytes 1540
  0.6 8.2 %copy-start.18 = (s32[64]{0:T(128)S(1)}, s32[64]{0:T(128)}, u32[]{:S(2)}) copy-start(s32[64]{0:T(128)} %constant.94.clone) | copy-start | bytes 772
  0.7 8.2 %copy-start.20 = (s32[32]{0:T(128)S(1)}, s32[32]{0:T(128)}, u32[]{:S(2)}) copy-start(s32[32]{0:T(128)} %param.20) | copy-start | bytes 388
  0.7 8.3 %copy-start.19 = (s32[32]{0:T(128)S(1)}, s32[32]{0:T(128)}, u32[]{:S(2)}) copy-start(s32[32]{0:T(128)} %param.19) | copy-start | bytes 388
  2.4 10.7 %collective-permute-start = (bf16[32,3712]{1,0:T(8,128)(2,1)S(1)}, bf16[32,3712]{1,0:T(8,128)(2,1)S(1)}, u32[]{:S(2)}, u32[]{:S(2)}) collective-permute-start(bf16[32,3712]{1,0:T(8,128)(2,1)S(1)} %fusion.1.refs_0_.refs_8_), channel_id=1, source_target_pairs={{0,8},{8,16},{16,24},{24,32},{32,40},{40,48},{48,56},{56,0},{1,9},... | collective-permute-start | bytes 712712 | tf_op jit(solution)/shard_map/ppermute | solution.py:398
  4.4 8.7 %collective-permute-start.1 = (bf16[32,3712]{1,0:T(8,128)(2,1)S(1)}, bf16[32,3712]{1,0:T(8,128)(2,1)S(1)}, u32[]{:S(2)}, u32[]{:S(2)}) collective-permute-start(bf16[32,3712]{1,0:T(8,128)(2,1)S(1)} %fusion.1.refs_0_.refs_8_), channel_id=1, source_target_pairs={{0,56},{8,0},{16,8},{24,16},{32,24},{40,32},{48,40},{56,48},{1,57}... | collective-permute-start | bytes 712712 | tf_op jit(solution)/shard_map/ppermute | solution.py:398
  7.6 29.1 %collective-permute-start.8 = (bf16[256,1792]{1,0:T(8,128)(2,1)}, bf16[256,1792]{1,0:T(8,128)(2,1)}, u32[]{:S(2)}, u32[]{:S(2)}) collective-permute-start(bf16[256,1792]{1,0:T(8,128)(2,1)} %scale_down.2), channel_id=1, source_target_pairs={{0,1},{1,0},{2,3},{3,2},{4,5},{5,4},{6,7},{7,6},{8,9},{9,8},{10,11... | collective-permute-start | bytes 2752520 | tf_op jit(solution)/shard_map/ppermute | solution.py:394
  18.9 10.6 %copy-start.21 = (bf16[1,28,2]{1,2,0:T(2,128)(2,1)S(1)}, bf16[1,28,2]{1,2,0:T(2,128)(2,1)}, u32[]{:S(2)}) copy-start(bf16[1,28,2]{1,2,0:T(2,128)(2,1)} %param.29) | copy-start | bytes 340
  18.9 10.6 %copy-start.22 = (bf16[1,28,2]{1,2,0:T(2,128)(2,1)S(1)}, bf16[1,28,2]{1,2,0:T(2,128)(2,1)}, u32[]{:S(2)}) copy-start(bf16[1,28,2]{1,2,0:T(2,128)(2,1)} %param.27) | copy-start | bytes 340
  18.9 45.5 %all-to-all-start = ((bf16[8,8,32,640]{3,2,1,0:T(8,128)(2,1)}), bf16[8,8,32,640]{3,2,1,0:T(8,128)(2,1)}, u32[]{:S(2)}, u32[]{:S(2)}) async-start(bf16[8,8,32,640]{3,2,1,0:T(8,128)(2,1)} %bitcast.28), calls=%async_computation | async-start | bytes 5242880 | tf_op jit(solution)/shard_map/all_to_all | solution.py:448
  26.4 6.9 %collective-permute-start.2 = (bf16[32,3712]{1,0:T(8,128)(2,1)S(1)}, bf16[32,3712]{1,0:T(8,128)(2,1)S(1)}, u32[]{:S(2)}, u32[]{:S(2)}) collective-permute-start(bf16[32,3712]{1,0:T(8,128)(2,1)S(1)} %collective-permute-done.refs_0_.refs_1_.refs_9_), channel_id=1, source_target_pairs={{0,8},{8,16},{16,24},{24,32},{32,40},{40,48},{48,56},{56,0},{1,9},... | collective-permute-start | bytes 712712 | tf_op jit(solution)/shard_map/ppermute | solution.py:398
  29.5 7.3 %collective-permute-start.5 = (bf16[32,3712]{1,0:T(8,128)(2,1)S(1)}, bf16[32,3712]{1,0:T(8,128)(2,1)S(1)}, u32[]{:S(2)}, u32[]{:S(2)}) collective-permute-start(bf16[32,3712]{1,0:T(8,128)(2,1)S(1)} %collective-permute-done.1.refs_1_.refs_5_.refs_13_), channel_id=1, source_target_pairs={{0,56},{8,0},{16,8},{24,16},{32,24},{40,32},{48,40},{56,48},{1,57}... | collective-permute-start | bytes 712712 | tf_op jit(solution)/shard_map/ppermute | solution.py:398
  32.1 27.6 %collective-permute-start.7 = (bf16[3584,256]{1,0:T(8,128)(2,1)S(1)}, bf16[3584,256]{1,0:T(8,128)(2,1)S(1)}, u32[]{:S(2)}, u32[]{:S(2)}) collective-permute-start(bf16[3584,256]{1,0:T(8,128)(2,1)S(1)} %scale_wide.2.refs_8_), channel_id=1, source_target_pairs={{0,128},{128,0},{1,129},{129,1},{2,130},{130,2},{3,131},{131,3},{4... | collective-permute-start | bytes 5505032 | tf_op jit(solution)/shard_map/ppermute | solution.py:394
  39.9 19.7 %copy-start.1 = (bf16[3584,256]{1,0:T(8,128)(2,1)}, bf16[3584,256]{1,0:T(8,128)(2,1)S(1)}, u32[]{:S(2)}) copy-start(bf16[3584,256]{1,0:T(8,128)(2,1)S(1)} %scale_wide.3.refs_9_) | copy-start | bytes 5505028
  39.9 19.7 %collective-permute-start.9 = (bf16[3584,256]{1,0:T(8,128)(2,1)S(1)}, bf16[3584,256]{1,0:T(8,128)(2,1)S(1)}, u32[]{:S(2)}, u32[]{:S(2)}) collective-permute-start(bf16[3584,256]{1,0:T(8,128)(2,1)S(1)} %scale_wide.3.refs_9_), channel_id=1, source_target_pairs={{0,128},{128,0},{1,129},{129,1},{2,130},{130,2},{3,131},{131,3},{4... | collective-permute-start | bytes 5505032 | tf_op jit(solution)/shard_map/ppermute | solution.py:394
  42.7 16.9 %collective-permute-start.10 = (bf16[256,1792]{1,0:T(8,128)(2,1)S(1)}, bf16[256,1792]{1,0:T(8,128)(2,1)S(1)}, u32[]{:S(2)}, u32[]{:S(2)}) collective-permute-start(bf16[256,1792]{1,0:T(8,128)(2,1)S(1)} %scale_down.3.w0), channel_id=1, source_target_pairs={{0,128},{128,0},{1,129},{129,1},{2,130},{130,2},{3,131},{131,3},{4... | collective-permute-start | bytes 2752520 | tf_op jit(solution)/shard_map/ppermute | solution.py:394
  43.3 0.9 copy-start.11
  44.2 8.4 %collective-permute-start.3 = (bf16[32,3712]{1,0:T(8,128)(2,1)S(1)}, bf16[32,3712]{1,0:T(8,128)(2,1)S(1)}, u32[]{:S(2)}, u32[]{:S(2)}) collective-permute-start(bf16[32,3712]{1,0:T(8,128)(2,1)S(1)} %collective-permute-done.2.refs_0_.refs_2_.refs_10_), channel_id=1, source_target_pairs={{0,8},{8,16},{16,24},{24,32},{32,40},{40,48},{48,56},{56,0},{1,9},... | collective-permute-start | bytes 712712 | tf_op jit(solution)/shard_map/ppermute | solution.py:398
  47.5 8.4 %collective-permute-start.6 = (bf16[32,3712]{1,0:T(8,128)(2,1)S(1)}, bf16[32,3712]{1,0:T(8,128)(2,1)S(1)}, u32[]{:S(2)}, u32[]{:S(2)}) collective-permute-start(bf16[32,3712]{1,0:T(8,128)(2,1)S(1)} %collective-permute-done.5.refs_1_.refs_6_.refs_14_), channel_id=1, source_target_pairs={{0,56},{8,0},{16,8},{24,16},{32,24},{40,32},{48,40},{56,48},{1,57}... | collective-permute-start | bytes 712712 | tf_op jit(solution)/shard_map/ppermute | solution.py:398
  52.7 7.0 %collective-permute-start.4 = (bf16[32,3712]{1,0:T(8,128)(2,1)S(1)}, bf16[32,3712]{1,0:T(8,128)(2,1)S(1)}, u32[]{:S(2)}, u32[]{:S(2)}) collective-permute-start(bf16[32,3712]{1,0:T(8,128)(2,1)S(1)} %collective-permute-done.3.refs_3_.refs_11_), channel_id=1, source_target_pairs={{0,8},{8,16},{16,24},{24,32},{32,40},{40,48},{48,56},{56,0},{1,9},... | collective-permute-start | bytes 712712 | tf_op jit(solution)/shard_map/ppermute | solution.py:398
  55.2 0.7 copy-start.9
  60.2 1.3 copy-start.3
  61.5 1.3 copy-start.5
  62.8 0.7 copy-start.7
  63.5 0.9 copy-start.13
  71.0 86.3 %all-to-all-start.1 = ((bf16[8,8,32,640]{3,2,1,0:T(8,128)(2,1)}), bf16[8,8,32,640]{3,2,1,0:T(8,128)(2,1)}, u32[]{:S(2)}, u32[]{:S(2)}) async-start(bf16[8,8,32,640]{3,2,1,0:T(8,128)(2,1)} %regroup.1), calls=%async_computation.1 | async-start | bytes 5242880 | tf_op jit(solution)/shard_map/all_to_all | solution.py:471
  79.5 2.8 %collective-permute-start.11 = (bf16[256,1792]{1,0:T(8,128)(2,1)}, bf16[256,1792]{1,0:T(8,128)(2,1)}, u32[]{:S(2)}, u32[]{:S(2)}) collective-permute-start(bf16[256,1792]{1,0:T(8,128)(2,1)} %collective-permute-done.8.refs_2_.w2), channel_id=1, source_target_pairs={{0,128},{128,0},{1,129},{129,1},{2,130},{130,2},{3,131},{131,3},{4... | collective-permute-start | bytes 2752520 | tf_op jit(solution)/shard_map/ppermute | solution.py:394
  82.9 0.9 copy-start.8
  83.8 0.9 copy-start.10
  84.7 53.1 %copy-start.2 = (bf16[3584,256]{1,0:T(8,128)(2,1)S(1)}, bf16[3584,256]{1,0:T(8,128)(2,1)}, u32[]{:S(2)}) copy-start(bf16[3584,256]{1,0:T(8,128)(2,1)} %copy-done.1) | copy-start | bytes 5505028
  90.0 15.0 %collective-permute-start.12 = (bf16[64,3584]{1,0:T(8,128)(2,1)S(1)}, bf16[64,3584]{1,0:T(8,128)(2,1)S(1)}, u32[]{:S(2)}, u32[]{:S(2)}) collective-permute-start(bf16[64,3584]{1,0:T(8,128)(2,1)S(1)} %get-tuple-element.13), channel_id=1, source_target_pairs={{0,64},{2,66},{4,68},{6,70},{64,0},{66,2},{68,4},{70,6},{1,65},{3,... | collective-permute-start | bytes 1376264 | tf_op jit(solution)/shard_map/ppermute | solution.py:402
  90.1 17.5 %collective-permute-start.13 = (bf16[64,3584]{1,0:T(8,128)(2,1)S(1)}, bf16[64,3584]{1,0:T(8,128)(2,1)S(1)}, u32[]{:S(2)}, u32[]{:S(2)}) collective-permute-start(bf16[64,3584]{1,0:T(8,128)(2,1)S(1)} %get-tuple-element.14), channel_id=1, source_target_pairs={{0,2},{2,4},{4,6},{6,0},{64,66},{66,68},{68,70},{70,64},{1,3},{3,5... | collective-permute-start | bytes 1376264 | tf_op jit(solution)/shard_map/ppermute | solution.py:402
  92.1 36.7 %collective-permute-start.14 = (bf16[64,3584]{1,0:T(8,128)(2,1)S(1)}, bf16[64,3584]{1,0:T(8,128)(2,1)S(1)}, u32[]{:S(2)}, u32[]{:S(2)}) collective-permute-start(bf16[64,3584]{1,0:T(8,128)(2,1)S(1)} %get-tuple-element.15), channel_id=1, source_target_pairs={{0,66},{2,68},{4,70},{6,64},{64,2},{66,4},{68,6},{70,0},{1,67},{3,... | collective-permute-start | bytes 1376264 | tf_op jit(solution)/shard_map/ppermute | solution.py:402
  96.0 38.6 %collective-permute-start.15 = (bf16[64,3584]{1,0:T(8,128)(2,1)S(1)}, bf16[64,3584]{1,0:T(8,128)(2,1)S(1)}, u32[]{:S(2)}, u32[]{:S(2)}) collective-permute-start(bf16[64,3584]{1,0:T(8,128)(2,1)S(1)} %get-tuple-element.16), channel_id=1, source_target_pairs={{0,4},{2,6},{4,0},{6,2},{64,68},{66,70},{68,64},{70,66},{1,5},{3,7... | collective-permute-start | bytes 1376264 | tf_op jit(solution)/shard_map/ppermute | solution.py:402
  97.8 36.8 %collective-permute-start.16 = (bf16[64,3584]{1,0:T(8,128)(2,1)S(1)}, bf16[64,3584]{1,0:T(8,128)(2,1)S(1)}, u32[]{:S(2)}, u32[]{:S(2)}) collective-permute-start(bf16[64,3584]{1,0:T(8,128)(2,1)S(1)} %get-tuple-element.17), channel_id=1, source_target_pairs={{0,68},{2,70},{4,64},{6,66},{64,4},{66,6},{68,0},{70,2},{1,69},{3,... | collective-permute-start | bytes 1376264 | tf_op jit(solution)/shard_map/ppermute | solution.py:402
  105.0 32.8 %collective-permute-start.17 = (bf16[64,3584]{1,0:T(8,128)(2,1)S(1)}, bf16[64,3584]{1,0:T(8,128)(2,1)S(1)}, u32[]{:S(2)}, u32[]{:S(2)}) collective-permute-start(bf16[64,3584]{1,0:T(8,128)(2,1)S(1)} %get-tuple-element.18), channel_id=1, source_target_pairs={{0,6},{2,0},{4,2},{6,4},{64,70},{66,64},{68,66},{70,68},{1,7},{3,1... | collective-permute-start | bytes 1376264 | tf_op jit(solution)/shard_map/ppermute | solution.py:402
  107.7 30.2 %collective-permute-start.18 = (bf16[64,3584]{1,0:T(8,128)(2,1)S(1)}, bf16[64,3584]{1,0:T(8,128)(2,1)S(1)}, u32[]{:S(2)}, u32[]{:S(2)}) collective-permute-start(bf16[64,3584]{1,0:T(8,128)(2,1)S(1)} %get-tuple-element.19), channel_id=1, source_target_pairs={{0,70},{2,64},{4,66},{6,68},{64,6},{66,0},{68,2},{70,4},{1,71},{3,... | collective-permute-start | bytes 1376264 | tf_op jit(solution)/shard_map/ppermute | solution.py:402
  137.8 3.1 %copy-start.4 = (bf16[3584,256]{1,0:T(8,128)(2,1)S(1)}, bf16[3584,256]{1,0:T(8,128)(2,1)}, u32[]{:S(2)}) copy-start(bf16[3584,256]{1,0:T(8,128)(2,1)} %copy-done.3) | copy-start | bytes 5505028
  137.8 3.1 %copy-start.6 = (bf16[3584,256]{1,0:T(8,128)(2,1)S(1)}, bf16[3584,256]{1,0:T(8,128)(2,1)}, u32[]{:S(2)}) copy-start(bf16[3584,256]{1,0:T(8,128)(2,1)} %copy-done.5) | copy-start | bytes 5505028
  140.0 4.3 %copy-start.23 = (s32[8]{0:T(128)S(1)}, s32[8]{0:T(128)}, u32[]{:S(2)}) copy-start(s32[8]{0:T(128)} %constant.112) | copy-start | bytes 100
  140.0 12.4 %copy-start.12 = (bf16[256,1792]{1,0:T(8,128)(2,1)S(1)}, bf16[256,1792]{1,0:T(8,128)(2,1)}, u32[]{:S(2)}) copy-start(bf16[256,1792]{1,0:T(8,128)(2,1)} %copy-done.11) | copy-start | bytes 2752516
  140.0 12.4 %copy-start.14 = (bf16[256,1792]{1,0:T(8,128)(2,1)S(1)}, bf16[256,1792]{1,0:T(8,128)(2,1)}, u32[]{:S(2)}) copy-start(bf16[256,1792]{1,0:T(8,128)(2,1)} %copy-done.13) | copy-start | bytes 2752516
  140.0 9.3 %collective-permute-start.19 = (bf16[512,256]{1,0:T(8,128)(2,1)S(1)}, bf16[512,256]{1,0:T(8,128)(2,1)S(1)}, u32[]{:S(2)}, u32[]{:S(2)}) collective-permute-start(bf16[512,256]{1,0:T(8,128)(2,1)S(1)} %hidden_units.2.h0), channel_id=1, source_target_pairs={{0,1},{1,0},{2,3},{3,2},{4,5},{5,4},{6,7},{7,6},{8,9},{9,8},{10,11... | collective-permute-start | bytes 786440 | tf_op jit(solution)/shard_map/ppermute | solution.py:394
  143.0 9.4 %collective-permute-start.20 = (bf16[512,256]{1,0:T(8,128)(2,1)S(1)}, bf16[512,256]{1,0:T(8,128)(2,1)S(1)}, u32[]{:S(2)}, u32[]{:S(2)}) collective-permute-start(bf16[512,256]{1,0:T(8,128)(2,1)S(1)} %hidden_units.3.h1), channel_id=1, source_target_pairs={{0,1},{1,0},{2,3},{3,2},{4,5},{5,4},{6,7},{7,6},{8,9},{9,8},{10,11... | collective-permute-start | bytes 786440 | tf_op jit(solution)/shard_map/ppermute | solution.py:394
  157.3 54.8 %all-to-all-start.2 = ((bf16[64,8,1792]{2,1,0:T(8,128)(2,1)}), bf16[64,8,1792]{2,1,0:T(8,128)(2,1)S(1)}, u32[]{:S(2)}, u32[]{:S(2)}) async-start(bf16[64,8,1792]{2,1,0:T(8,128)(2,1)} %down_rows.1.refs_0_), calls=%async_computation.2 | async-start | bytes 3670016 | tf_op jit(solution)/shard_map/all_to_all | solution.py:484
  172.3 3.6 %copy-start.16 = (s32[32,8]{0,1:T(8,128)S(1)}, s32[32,8]{0,1:T(8,128)}, u32[]{:S(2)}) copy-start(s32[32,8]{0,1:T(8,128)} %param.24) | copy-start | bytes 3076
  172.3 3.6 %copy-start.15 = (bf16[32,576]{1,0:T(8,128)(2,1)S(1)}, bf16[32,576]{1,0:T(8,128)(2,1)}, u32[]{:S(2)}) copy-start(bf16[32,576]{1,0:T(8,128)(2,1)} %param.22) | copy-start | bytes 110596
  172.3 3.7 %copy-start.17 = (f32[32,8]{0,1:T(8,128)S(1)}, f32[32,8]{0,1:T(8,128)}, u32[]{:S(2)}) copy-start(f32[32,8]{0,1:T(8,128)} %param.25) | copy-start | bytes 3076
  174.9 44.9 %collective-permute-start.21 = (bf16[32,32,640]{2,1,0:T(8,128)(2,1)S(1)}, bf16[32,32,640]{2,1,0:T(8,128)(2,1)}, u32[]{:S(2)}, u32[]{:S(2)}) collective-permute-start(bf16[32,32,640]{2,1,0:T(8,128)(2,1)S(1)} %compact.1.mine), channel_id=1, source_target_pairs={{0,1},{1,0},{2,3},{3,2},{4,5},{5,4},{6,7},{7,6},{8,9},{9,8},{10,11... | collective-permute-start | bytes 3932168 | tf_op jit(solution)/shard_map/ppermute | solution.py:394

commit v5 on v4

--- a/solution.py
+++ b/solution.py
@@ -120,45 +120,32 @@
 
 
 def pick_kernel(place_ref, *refs):
-    names, blocks, outs, chosen_ref = refs[:NZ], refs[NZ : 2 * NZ], refs[-9:-1], refs[-1]
-
-    @pl.when(pl.program_id(0) == 0)
-    def _():
-        xh, z, y = place_ref[0], place_ref[1], place_ref[2]
-        column = lax.broadcasted_iota(I32, (1, EP), 1)
-        peer, slot = column >> 3, column & 7
-        experts = (((peer >> 2) ^ xh) * NZ + z) * NY + (((peer & 3) + y) & 3)
-        for b, name in enumerate(names):
-            marks = named_by(name[...].astype(F32).astype(I32)[:, :8], experts)
-            chosen_ref[b] = jnp.where(earlier(marks) == slot.astype(F32), marks, 0.0).astype(BF16)
-
+    blocks, outs = refs[:NZ], refs[NZ:]
+    xh, z, y = place_ref[0], place_ref[1], place_ref[2]
+    column = lax.broadcasted_iota(I32, (1, EP), 1)
+    peer, slot = column >> 3, column & 7
+    experts = (((peer >> 2) ^ xh) * NZ + z) * NY + (((peer & 3) + y) & 3)
     for b, block in enumerate(blocks):
+        marks = named_by(block[:, D : D + 8].astype(F32).astype(I32), experts)
+        chosen = jnp.where(earlier(marks) == slot.astype(F32), marks, 0.0).astype(BF16)
         rows = lax.dot_general(
-            chosen_ref[b],
-            block[...],
-            (((0,), (0,)), ((), ())),
-            preferred_element_type=F32,
+            chosen, block[:, :D], (((0,), (0,)), ((), ())), preferred_element_type=F32
         ).astype(BF16)
         for r, out in enumerate(outs):
             out[b * CAP : (b + 1) * CAP, :] = rows[r * CAP : (r + 1) * CAP, :]
 
 
-def pick_rows(place, blocks, *before):
-    wide = 896
+def pick_rows(place, blocks):
+    vmem = pl.BlockSpec(memory_space=pltpu.VMEM)
     return pl.pallas_call(
         pick_kernel,
-        grid=(D // wide,),
-        in_specs=[smem()]
-        + [pl.BlockSpec((TRAJ, BLOCK), lambda i: (0, D // BLOCK))] * NZ
-        + [pl.BlockSpec((TRAJ, wide), lambda i: (0, i))] * NZ
-        + [smem()] * len(before),
-        out_specs=[pl.BlockSpec((NZ * CAP, wide), lambda i: (0, i))] * 8,
-        out_shape=[in_hbm((NZ * CAP, D))] * 8,
-        scratch_shapes=[pltpu.VMEM((NZ, TRAJ, EP), BF16)],
-        compiler_params=params(10),
+        in_specs=[smem()] + [vmem] * NZ,
+        out_specs=[vmem] * 8,
+        out_shape=[jax.ShapeDtypeStruct((NZ * CAP, D), BF16)] * 8,
+        compiler_params=params(6),
         cost_estimate=cost(1e9, 6e6),
         name="pick_rows",
-    )(place, *blocks, *blocks, *before)
+    )(place, *blocks)
 
 
 PEER_ORDER = (4, 1, 5, 2, 6, 3, 7, 0)
@@ -277,15 +264,16 @@
 
 def regroup_kernel(midway, *rest):
     out = rest[-1]
-    out[0] = midway[:, 0]
+    for i in range(4):
+        out[i] = midway[:, i]
 
 
 def regroup(midway, *before):
     return pl.pallas_call(
         regroup_kernel,
-        grid=(8,),
-        in_specs=[pl.BlockSpec((8, 1, 32, LANES), lambda i: (0, i, 0, 0))] + [smem()] * len(before),
-        out_specs=pl.BlockSpec((1, 8, 32, LANES), lambda i: (i, 0, 0, 0)),
+        grid=(2,),
+        in_specs=[pl.BlockSpec((8, 4, 32, LANES), lambda i: (0, i, 0, 0))] + [smem()] * len(before),
+        out_specs=pl.BlockSpec((4, 8, 32, LANES), lambda i: (i, 0, 0, 0)),
         out_shape=pltpu.HBM((8, 8, 32, LANES), BF16),
         compiler_params=params(8),
         cost_estimate=cost(1e6, 6e6),
@@ -454,19 +442,18 @@
 
     gate = scale_wide(gate_value, gate_scale, once(up_way[1], down_way[1]))
     up = scale_wide(up_value, up_scale, once(up_way[2], down_way[2], down_tp))
-    down_keep = scale_down(tp_index, down_value, down_scale, once(up_way[2], down_way[2]))
     gate_far, up_far = swap(gate, "pool"), swap(up, "pool")
-    down_far, down_tp_far = swap(down_keep, "pool"), swap(down_tp, "pool")
 
     midway = regroup(
-        midway, once(up_way[4], down_way[3], gate_far, up_far, down_far)
-    )
-    picked = pick_rows(
-        place, up_way + down_way[1:], once(down_tp_far)
-    )
+        midway, once(up_way[4], down_way[3], gate_far, up_far)
+    )
+    picked = pick_rows(place, up_way + down_way[1:])
     tokens = list(picked)
     for peer in PEER_ORDER[:7]:
         tokens[peer] = plane_shift(picked[peer], peer // NY, peer % NY)
+
+    down_keep = scale_down(tp_index, down_value, down_scale, once(picked[5]))
+    down_far, down_tp_far = swap(down_keep, "pool"), swap(down_tp, "pool")
 
     arrived = lax.all_to_all(midway, "z", split_axis=0, concat_axis=0, tiled=True)
 

time: 226 us -> 215 us (0.951)
  starting transfers between devices: 78.6 us -> 54.5 us
  waiting for transfers between devices: 80.6 us -> 95.8 us
  Pallas kernels: 48.7 us -> 45 us
    ppermute x7, starting transfers between devices: 33.3 us -> 12.2 us  [plane_shift(): lax.ppermute(x, ('xh', 'y'), [(a * NY + b, (a + dx) % NX * NY + (b + dy)...]
    ppermute x7, waiting for transfers between devices: 14.4 us -> 30.3 us  [plane_shift(): lax.ppermute(x, ('xh', 'y'), [(a * NY + b, (a + dx) % NX * NY + (b + dy)...]
    pallas_call x2, Pallas kernels: 11.8 us -> 7.43 us  [the longest x1 3.87 us: pick_rows(): pl.pallas_call(pick_kernel, in_specs=[smem()] + [vmem] * NZ, out_specs=[v...]
    all_to_all x1, starting transfers between devices: 13.2 us -> 10.6 us  [on_device(): lax.all_to_all(out_rows, ('xh', 'z', 'y'), split_axis=0, concat_axis=0, t...]
    unnamed x51 -> x43, local copies, waits for them, and re-layouts: 11.8 us -> 11.3 us
  transfers between devices with their start and end apart: 25 -> 25, of which waited for: 12 -> 12; matrix products, arithmetic and copies ran while one was open for 3% -> 4% of each run, Pallas kernels for 17% -> 17%
where the time goes in v5:
time: 215 us; the launch traced here: 214 us
  waiting for transfers between devices  95.8 us (45%)
  starting transfers between devices  54.5 us (25%)
  Pallas kernels  45 us (21%)
  local copies, waits for them, and re-layouts  12.3 us (6%)
  other arithmetic  5.21 us (2%)
    all_to_all x1, waiting for transfers between devices, on_device(): lax.all_to_all(out_rows, ('xh', 'z', 'y'), split_axis=0, concat_axis=0, t...  35.9 us
    ppermute x7, waiting for transfers between devices, plane_shift(): lax.ppermute(x, ('xh', 'y'), [(a * NY + b, (a + dx) % NX * NY + (b + dy)...  30.3 us
    ppermute x7, waiting for transfers between devices, z_shift(): return lax.ppermute(x, 'z', [(i, (i + by) % NZ) for i in range(NZ)])  14.8 us
    ppermute x8, waiting for transfers between devices, swap(): return lax.ppermute(x, axis, [(0, 1), (1, 0)])  14.7 us
    ppermute x7, starting transfers between devices, plane_shift(): lax.ppermute(x, ('xh', 'y'), [(a * NY + b, (a + dx) % NX * NY + (b + dy)...  12.2 us
    unnamed x43, local copies, waits for them, and re-layouts  11.3 us
    ppermute x7, starting transfers between devices, z_shift(): return lax.ppermute(x, 'z', [(i, (i + by) % NZ) for i in range(NZ)])  10.8 us
    all_to_all x1, starting transfers between devices, on_device(): lax.all_to_all(out_rows, ('xh', 'z', 'y'), split_axis=0, concat_axis=0, t...  10.6 us
  transfers between devices with their start and end apart: 25, of which 12 were waited for; matrix products, arithmetic and copies ran while one was open for 4% of the time, Pallas kernels for 17%

profile of v5, /device:TPU:68, one launch (start us, length us, event | category | flops | bytes accessed | tf_op | source)
XLA Modules:
  0.0 213.8 jit_solution(9712476380219366321)
XLA Ops:
  0.7 0.7 convert_element_type.39
  1.5 1.7 fusion.1.refs_0_
  3.1 1.9 collective-permute-start
  5.2 0.7 bitcast_convert_fusion.scale
  5.8 2.5 %scale_down.2 = bf16[256,1792]{1,0:T(8,128)(2,1)} custom-call(s32[1]{0:T(128)S(6)} %sub.36.half_ref, f32[2,28]{1,0:T(2,128)S(1)} %bitcast_convert_fusion.scale, bf16[1,256,3584]{2,1,0:T(8,128)(2,1)} %value.7), custom_call_target="tpu_custom_call" | custom-call | flops 1000000 | bytes 2000000 | tf_op jit(solution)/shard_map/scale_down/pallas_call | solution.py:88
  8.3 1.2 collective-permute-start.8
  9.7 0.7 copy.40
  10.4 3.9 %copy.43.pages = bf16[128,16,576]{2,1,0:T(8,128)(2,1)S(1)} copy(bf16[128,16,576]{0,2,1:T(8,128)(2,1)} %param.17) | data formatting | bytes 4718592 | tf_op args[0]
  14.3 0.8 broadcast_subtract_fusion.index_ref
  15.1 0.5 once.5.rest_0_
  15.6 5.2 %collect.1 = bf16[64,32,640]{2,1,0:T(8,128)(2,1)} custom-call(s32[64,4]{1,0:T(8,128)S(1)} %broadcast_subtract_fusion.index_ref, bf16[128,16,576]{2,1,0:T(8,128)(2,1)S(1)} %copy.43.pages, f32[1]{0:T(128)} %once.5.rest_0_), custom_call_target="tpu_custom_call" | custom-call | flops 1000000 | bytes 6000000 | tf_op jit(solution)/shard_map/collect/pallas_call | solution.py:253
  20.8 7.6 %all-to-all-start = ((bf16[8,8,32,640]{3,2,1,0:T(8,128)(2,1)}), bf16[8,8,32,640]{3,2,1,0:T(8,128)(2,1)}, u32[]{:S(2)}, u32[]{:S(2)}) async-start(bf16[8,8,32,640]{3,2,1,0:T(8,128)(2,1)} %bitcast.28), calls=%async_computation | async-start | bytes 5242880 | tf_op jit(solution)/shard_map/all_to_all | solution.py:436
  28.4 3.0 %collective-permute-start.2 = (bf16[32,3712]{1,0:T(8,128)(2,1)}, bf16[32,3712]{1,0:T(8,128)(2,1)S(1)}, u32[]{:S(2)}, u32[]{:S(2)}) collective-permute-start(bf16[32,3712]{1,0:T(8,128)(2,1)} %collective-permute-done.refs_0_.refs_1_), channel_id=1, source_target_pairs={{0,8},{8,16},{16,24},{24,32},{32,40},{40,48},{48,56},{56,0},{1,9},... | collective-permute-start | bytes 712712 | tf_op jit(solution)/shard_map/ppermute | solution.py:386
  31.5 2.6 %scale_wide.2.refs_8_ = bf16[3584,256]{1,0:T(8,128)(2,1)S(1)} custom-call(f32[2,28]{1,0:T(2,128)S(1)} %convert_bitcast_fusion.1.scale, bf16[1,3584,256]{2,1,0:T(8,128)(2,1)} %value.4, f32[1]{0:T(128)} %once.5.rest_0_), custom_call_target="tpu_custom_call" | custom-call | flops 1000000 | bytes 4000000 | tf_op jit(solution)/shard_map/scale_wide/pallas_call | solution.py:64
  34.2 1.5 collective-permute-done.2.refs_0_.refs_2_
  35.7 3.3 %collective-permute-done.5.refs_1_.refs_6_ = bf16[32,3712]{1,0:T(8,128)(2,1)S(1)} collective-permute-done((bf16[32,3712]{1,0:T(8,128)(2,1)}, bf16[32,3712]{1,0:T(8,128)(2,1)S(1)}, u32[]{:S(2)}, u32[]{:S(2)}) %collective-permute-start.5) | collective-permute-done | bytes 237600 | tf_op jit(solution)/shard_map/ppermute | solution.py:386
  39.0 0.5 once.6.rest_0_
  39.5 2.6 %scale_wide.3.refs_9_ = bf16[3584,256]{1,0:T(8,128)(2,1)S(1)} custom-call(f32[2,28]{1,0:T(2,128)S(1)} %convert_bitcast_fusion.scale, bf16[1,3584,256]{2,1,0:T(8,128)(2,1)} %value.6, f32[1]{0:T(128)} %once.6.rest_0_), custom_call_target="tpu_custom_call" | custom-call | flops 1000000 | bytes 4000000 | tf_op jit(solution)/shard_map/scale_wide/pallas_call | solution.py:64
  42.2 1.3 copy-done.1
  43.5 3.2 %collective-permute-start.3 = (bf16[32,3712]{1,0:T(8,128)(2,1)S(1)}, bf16[32,3712]{1,0:T(8,128)(2,1)S(1)}, u32[]{:S(2)}, u32[]{:S(2)}) collective-permute-start(bf16[32,3712]{1,0:T(8,128)(2,1)S(1)} %collective-permute-done.2.refs_0_.refs_2_), channel_id=1, source_target_pairs={{0,8},{8,16},{16,24},{24,32},{32,40},{40,48},{48,56},{56,0},{1,9},... | collective-permute-start | bytes 712712 | tf_op jit(solution)/shard_map/ppermute | solution.py:386
  46.7 5.7 %collective-permute-done.3.refs_3_ = bf16[32,3712]{1,0:T(8,128)(2,1)S(1)} collective-permute-done((bf16[32,3712]{1,0:T(8,128)(2,1)S(1)}, bf16[32,3712]{1,0:T(8,128)(2,1)S(1)}, u32[]{:S(2)}, u32[]{:S(2)}) %collective-permute-start.3) | collective-permute-done | bytes 237600 | tf_op jit(solution)/shard_map/ppermute | solution.py:386
  52.4 2.5 %collective-permute-start.4 = (bf16[32,3712]{1,0:T(8,128)(2,1)S(1)}, bf16[32,3712]{1,0:T(8,128)(2,1)S(1)}, u32[]{:S(2)}, u32[]{:S(2)}) collective-permute-start(bf16[32,3712]{1,0:T(8,128)(2,1)S(1)} %collective-permute-done.3.refs_3_), channel_id=1, source_target_pairs={{0,8},{8,16},{16,24},{24,32},{32,40},{40,48},{48,56},{56,0},{1,9},... | collective-permute-start | bytes 712712 | tf_op jit(solution)/shard_map/ppermute | solution.py:386
  54.9 0.7 copy-done.9
  55.6 4.3 %collective-permute-done.4.refs_0_.refs_4_ = bf16[32,3712]{1,0:T(8,128)(2,1)S(1)} collective-permute-done((bf16[32,3712]{1,0:T(8,128)(2,1)S(1)}, bf16[32,3712]{1,0:T(8,128)(2,1)S(1)}, u32[]{:S(2)}, u32[]{:S(2)}) %collective-permute-start.4) | collective-permute-done | bytes 237600 | tf_op jit(solution)/shard_map/ppermute | solution.py:386
  59.9 0.5 once.7.rest_0_
  60.5 1.3 copy-done.3
  61.8 1.3 copy-done.5
  63.1 0.7 copy-done.7
  63.8 3.6 %regroup.1 = bf16[8,8,32,640]{3,2,1,0:T(8,128)(2,1)} custom-call(bf16[8,8,32,640]{3,2,1,0:T(8,128)(2,1)} %all-to-all-done.midway, f32[1]{0:T(128)} %once.7.rest_0_), custom_call_target="tpu_custom_call" | custom-call | flops 1000000 | bytes 6000000 | tf_op jit(solution)/shard_map/regroup/pallas_call | solution.py:272
  67.3 8.4 %all-to-all-start.1 = ((bf16[8,8,32,640]{3,2,1,0:T(8,128)(2,1)}), bf16[8,8,32,640]{3,2,1,0:T(8,128)(2,1)}, u32[]{:S(2)}, u32[]{:S(2)}) async-start(bf16[8,8,32,640]{3,2,1,0:T(8,128)(2,1)} %regroup.1), calls=%async_computation.1 | async-start | bytes 5242880 | tf_op jit(solution)/shard_map/all_to_all | solution.py:458
  75.9 0.9 copy-done.8
  76.8 0.9 copy-done.10
  77.8 3.9 %pick_rows.1 = (bf16[64,3584]{1,0:T(8,128)(2,1)S(1)}, bf16[64,3584]{1,0:T(8,128)(2,1)S(1)}, bf16[64,3584]{1,0:T(8,128)(2,1)S(1)}, bf16[64,3584]{1,0:T(8,128)(2,1...) custom-call(s32[3]{0:T(128)S(1)} %pad_add_fusion.1.place_ref, ...), custom_call_target="tpu_custom_call" | custom-call | flops 1000000000 | bytes 6000000 | tf_op jit(solution)/shard_map/pick_rows/pallas_call | solution.py:140
  81.6 1.5 collective-permute-start.12
  83.2 3.0 %collective-permute-start.10 = (bf16[64,3584]{1,0:T(8,128)(2,1)S(1)}, bf16[64,3584]{1,0:T(8,128)(2,1)S(1)}, u32[]{:S(2)}, u32[]{:S(2)}) collective-permute-start(bf16[64,3584]{1,0:T(8,128)(2,1)S(1)} %get-tuple-element.13), channel_id=1, source_target_pairs={{0,64},{2,66},{4,68},{6,70},{64,0},{66,2},{68,4},{70,6},{1,65},{3,... | collective-permute-start | bytes 1376264 | tf_op jit(solution)/shard_map/ppermute | solution.py:390
  86.1 1.5 collective-permute-start.11
  87.6 1.8 collective-permute-start.13
  89.4 1.8 collective-permute-start.14
  91.2 7.7 %collective-permute-done.12.refs_2_ = bf16[64,3584]{1,0:T(8,128)(2,1)S(1)} collective-permute-done((bf16[64,3584]{1,0:T(8,128)(2,1)S(1)}, bf16[64,3584]{1,0:T(8,128)(2,1)S(1)}, u32[]{:S(2)}, u32[]{:S(2)}) %collective-permute-start.12) | collective-permute-done | bytes 458784 | tf_op jit(solution)/shard_map/ppermute | solution.py:390
  98.8 1.5 collective-permute-start.15
  100.3 7.2 %collective-permute-done.10.refs_0_ = bf16[64,3584]{1,0:T(8,128)(2,1)S(1)} collective-permute-done((bf16[64,3584]{1,0:T(8,128)(2,1)S(1)}, bf16[64,3584]{1,0:T(8,128)(2,1)S(1)}, u32[]{:S(2)}, u32[]{:S(2)}) %collective-permute-start.10) | collective-permute-done | bytes 458784 | tf_op jit(solution)/shard_map/ppermute | solution.py:390
  107.4 1.2 collective-permute-start.16
  108.7 0.5 once.8.rest_0_
  109.2 3.1 %scale_down.3.w0 = bf16[256,1792]{1,0:T(8,128)(2,1)} custom-call(s32[1]{0:T(128)} %bitcast.half_ref.tp_ref, f32[2,28]{1,0:T(2,128)S(1)} %bitcast_convert_fusion.scale, bf16[1,256,3584]{2,1,0:T(8,128)(2,1)} %value.7, f32[1]{0:T(128)} %once.8.rest_0_), custom_call_target="tpu_custom_call" | custom-call | flops 1000000 | bytes 2000000 | tf_op jit(solution)/shard_map/scale_down/pallas_call | solution.py:88
  112.3 14.5 %collective-permute-done.13.refs_3_ = bf16[64,3584]{1,0:T(8,128)(2,1)S(1)} collective-permute-done((bf16[64,3584]{1,0:T(8,128)(2,1)S(1)}, bf16[64,3584]{1,0:T(8,128)(2,1)S(1)}, u32[]{:S(2)}, u32[]{:S(2)}) %collective-permute-start.13) | collective-permute-done | bytes 458784 | tf_op jit(solution)/shard_map/ppermute | solution.py:390
  126.8 0.1 collective-permute-start.19
  126.9 1.0 collective-permute-done.15.refs_5_
  127.9 2.1 hidden_units.2.h0
  130.1 1.0 collective-permute-start.17
  131.1 2.1 hidden_units.3.h1
  133.2 1.2 collective-permute-start.18
  134.5 4.9 %collective-permute-done.17.h2 = bf16[512,256]{1,0:T(8,128)(2,1)S(1)} collective-permute-done((bf16[512,256]{1,0:T(8,128)(2,1)S(1)}, bf16[512,256]{1,0:T(8,128)(2,1)S(1)}, u32[]{:S(2)}, u32[]{:S(2)}) %collective-permute-start.17) | collective-permute-done | bytes 262176 | tf_op jit(solution)/shard_map/ppermute | solution.py:382
  139.4 4.0 %collective-permute-done.18.h3 = bf16[512,256]{1,0:T(8,128)(2,1)S(1)} collective-permute-done((bf16[512,256]{1,0:T(8,128)(2,1)S(1)}, bf16[512,256]{1,0:T(8,128)(2,1)S(1)}, u32[]{:S(2)}, u32[]{:S(2)}) %collective-permute-start.18) | collective-permute-done | bytes 262176 | tf_op jit(solution)/shard_map/ppermute | solution.py:382
  143.4 5.1 %down_rows.1.refs_0_ = bf16[64,8,1792]{2,1,0:T(8,128)(2,1)} custom-call(s32[64]{0:T(128)S(1)} %fusion.3.order_ref, bf16[512,256]{1,0:T(8,128)(2,1)S(1)} %hidden_units.2.h0, bf16[512,256]{1,0:T(8,128)(2,1)S(1)} %hidden_units.3.h1, bf16[512,256]{1,0:T(8,128)(2,1)S(1)} %collective-permute-done.17.h2, bf16[512,256]{1,0:T(8,128)(2,1)S(1)} %collective-permute-done.18.h3, ...), custom_call_target="tpu_custom_call" | custom-call | flops 1900000000 | bytes 7000000 | tf_op jit(solution)/shard_map/down_rows/pallas_call | solution.py:191
  148.5 10.6 %all-to-all-start.2 = ((bf16[64,8,1792]{2,1,0:T(8,128)(2,1)}), bf16[64,8,1792]{2,1,0:T(8,128)(2,1)S(1)}, u32[]{:S(2)}, u32[]{:S(2)}) async-start(bf16[64,8,1792]{2,1,0:T(8,128)(2,1)} %down_rows.1.refs_0_), calls=%async_computation.2 | async-start | bytes 3670016 | tf_op jit(solution)/shard_map/all_to_all | solution.py:471
  159.2 0.5 once.9.rest_0_
  159.7 1.0 slice_convert_fusion
  160.8 0.1 select_reduce_fusion.1
  160.9 2.6 %compact.1.mine = bf16[32,32,640]{2,1,0:T(8,128)(2,1)S(1)} custom-call(s32[32]{0:T(128)S(1)} %get-tuple-element.23.source_ref, bf16[64,32,640]{2,1,0:T(8,128)(2,1)} %bitcast.9.arrived, f32[1]{0:T(128)} %once.9.rest_0_), custom_call_target="tpu_custom_call" | custom-call | flops 1000000 | bytes 4000000 | tf_op jit(solution)/shard_map/compact/pallas_call | solution.py:292
  163.6 1.2 collective-permute-start.21
  165.0 35.9 %all-to-all-done.2.rows_ref = bf16[64,8,1792]{2,1,0:T(8,128)(2,1)S(1)} async-done(((bf16[64,8,1792]{2,1,0:T(8,128)(2,1)}), bf16[64,8,1792]{2,1,0:T(8,128)(2,1)S(1)}, u32[]{:S(2)}, u32[]{:S(2)}) %all-to-all-start.2) | async-done | bytes 1835040 | tf_op jit(solution)/shard_map/all_to_all | solution.py:471
  200.9 2.1 blend.1
  202.9 5.8 %collective-permute-done.21.other = bf16[32,32,640]{2,1,0:T(8,128)(2,1)} collective-permute-done((bf16[32,32,640]{2,1,0:T(8,128)(2,1)S(1)}, bf16[32,32,640]{2,1,0:T(8,128)(2,1)}, u32[]{:S(2)}, u32[]{:S(2)}) %collective-permute-start.21) | collective-permute-done | bytes 1310752 | tf_op jit(solution)/shard_map/ppermute | solution.py:382
  208.8 5.0 %attend.1 = (bf16[32,64,576]{2,1,0:T(8,128)(2,1)}, bf16[32,32,512]{2,1,0:T(8,128)(2,1)}) custom-call(s32[1]{0:T(128)} %bitcast.half_ref.tp_ref, s32[32]{0:T(128)S(1)} %get-tuple-element.24.length_ref, bf16[32,32,640]{2,1,0:T(8,128)(2,1)S(1)} %compact.1.mine, bf16[32,32,640]{2,1,0:T(8,128)(2,1)} %collective-permute-done.21.other, ...), custom_call_target="tpu_custom_call" | custom-call | flops 200000000 | bytes 8000000 | tf_op jit(solution)/shard_map/attend/pallas_call | solution.py:340
  (71 shorter events, 1.2 us)
Async XLA Ops:
  0.6 8.9 %copy-start = (s32[32,4]{0,1:T(4,128)S(1)}, s32[32,4]{0,1:T(4,128)}, u32[]{:S(2)}) copy-start(s32[32,4]{0,1:T(4,128)} %param.18) | copy-start | bytes 1540
  0.6 8.9 %copy-start.14 = (s32[64]{0:T(128)S(1)}, s32[64]{0:T(128)}, u32[]{:S(2)}) copy-start(s32[64]{0:T(128)} %constant.94.clone) | copy-start | bytes 772
  0.7 8.8 %copy-start.16 = (s32[32]{0:T(128)S(1)}, s32[32]{0:T(128)}, u32[]{:S(2)}) copy-start(s32[32]{0:T(128)} %param.20) | copy-start | bytes 388
  0.7 8.9 %copy-start.15 = (s32[32]{0:T(128)S(1)}, s32[32]{0:T(128)}, u32[]{:S(2)}) copy-start(s32[32]{0:T(128)} %param.19) | copy-start | bytes 388
  3.1 12.0 %collective-permute-start = (bf16[32,3712]{1,0:T(8,128)(2,1)}, bf16[32,3712]{1,0:T(8,128)(2,1)}, u32[]{:S(2)}, u32[]{:S(2)}) collective-permute-start(bf16[32,3712]{1,0:T(8,128)(2,1)} %fusion.1.refs_0_), channel_id=1, source_target_pairs={{0,8},{8,16},{16,24},{24,32},{32,40},{40,48},{48,56},{56,0},{1,9},... | collective-permute-start | bytes 712712 | tf_op jit(solution)/shard_map/ppermute | solution.py:386
  5.0 10.1 %collective-permute-start.1 = (bf16[32,3712]{1,0:T(8,128)(2,1)}, bf16[32,3712]{1,0:T(8,128)(2,1)}, u32[]{:S(2)}, u32[]{:S(2)}) collective-permute-start(bf16[32,3712]{1,0:T(8,128)(2,1)} %fusion.1.refs_0_), channel_id=1, source_target_pairs={{0,56},{8,0},{16,8},{24,16},{32,24},{40,32},{48,40},{56,48},{1,57}... | collective-permute-start | bytes 712712 | tf_op jit(solution)/shard_map/ppermute | solution.py:386
  8.3 30.7 %collective-permute-start.8 = (bf16[256,1792]{1,0:T(8,128)(2,1)}, bf16[256,1792]{1,0:T(8,128)(2,1)S(1)}, u32[]{:S(2)}, u32[]{:S(2)}) collective-permute-start(bf16[256,1792]{1,0:T(8,128)(2,1)} %scale_down.2), channel_id=1, source_target_pairs={{0,1},{1,0},{2,3},{3,2},{4,5},{5,4},{6,7},{7,6},{8,9},{9,8},{10,11... | collective-permute-start | bytes 2752520 | tf_op jit(solution)/shard_map/ppermute | solution.py:382
  20.8 10.6 %copy-start.17 = (bf16[1,28,2]{1,2,0:T(2,128)(2,1)S(1)}, bf16[1,28,2]{1,2,0:T(2,128)(2,1)}, u32[]{:S(2)}) copy-start(bf16[1,28,2]{1,2,0:T(2,128)(2,1)} %param.29) | copy-start | bytes 340
  20.8 10.6 %copy-start.18 = (bf16[1,28,2]{1,2,0:T(2,128)(2,1)S(1)}, bf16[1,28,2]{1,2,0:T(2,128)(2,1)}, u32[]{:S(2)}) copy-start(bf16[1,28,2]{1,2,0:T(2,128)(2,1)} %param.27) | copy-start | bytes 340
  20.8 42.9 %all-to-all-start = ((bf16[8,8,32,640]{3,2,1,0:T(8,128)(2,1)}), bf16[8,8,32,640]{3,2,1,0:T(8,128)(2,1)}, u32[]{:S(2)}, u32[]{:S(2)}) async-start(bf16[8,8,32,640]{3,2,1,0:T(8,128)(2,1)} %bitcast.28), calls=%async_computation | async-start | bytes 5242880 | tf_op jit(solution)/shard_map/all_to_all | solution.py:436
  28.4 7.3 %collective-permute-start.2 = (bf16[32,3712]{1,0:T(8,128)(2,1)}, bf16[32,3712]{1,0:T(8,128)(2,1)S(1)}, u32[]{:S(2)}, u32[]{:S(2)}) collective-permute-start(bf16[32,3712]{1,0:T(8,128)(2,1)} %collective-permute-done.refs_0_.refs_1_), channel_id=1, source_target_pairs={{0,8},{8,16},{16,24},{24,32},{32,40},{40,48},{48,56},{56,0},{1,9},... | collective-permute-start | bytes 712712 | tf_op jit(solution)/shard_map/ppermute | solution.py:386
  31.4 7.5 %collective-permute-start.5 = (bf16[32,3712]{1,0:T(8,128)(2,1)}, bf16[32,3712]{1,0:T(8,128)(2,1)S(1)}, u32[]{:S(2)}, u32[]{:S(2)}) collective-permute-start(bf16[32,3712]{1,0:T(8,128)(2,1)} %collective-permute-done.1.refs_1_.refs_5_), channel_id=1, source_target_pairs={{0,56},{8,0},{16,8},{24,16},{32,24},{40,32},{48,40},{56,48},{1,57}... | collective-permute-start | bytes 712712 | tf_op jit(solution)/shard_map/ppermute | solution.py:386
  34.1 25.9 %collective-permute-start.7 = (bf16[3584,256]{1,0:T(8,128)(2,1)S(1)}, bf16[3584,256]{1,0:T(8,128)(2,1)S(1)}, u32[]{:S(2)}, u32[]{:S(2)}) collective-permute-start(bf16[3584,256]{1,0:T(8,128)(2,1)S(1)} %scale_wide.2.refs_8_), channel_id=1, source_target_pairs={{0,128},{128,0},{1,129},{129,1},{2,130},{130,2},{3,131},{131,3},{4... | collective-permute-start | bytes 5505032 | tf_op jit(solution)/shard_map/ppermute | solution.py:382
  42.1 17.8 %collective-permute-start.9 = (bf16[3584,256]{1,0:T(8,128)(2,1)S(1)}, bf16[3584,256]{1,0:T(8,128)(2,1)S(1)}, u32[]{:S(2)}, u32[]{:S(2)}) collective-permute-start(bf16[3584,256]{1,0:T(8,128)(2,1)S(1)} %scale_wide.3.refs_9_), channel_id=1, source_target_pairs={{0,128},{128,0},{1,129},{129,1},{2,130},{130,2},{3,131},{131,3},{4... | collective-permute-start | bytes 5505032 | tf_op jit(solution)/shard_map/ppermute | solution.py:382
  42.2 1.3 copy-start.1
  43.5 8.9 %collective-permute-start.3 = (bf16[32,3712]{1,0:T(8,128)(2,1)S(1)}, bf16[32,3712]{1,0:T(8,128)(2,1)S(1)}, u32[]{:S(2)}, u32[]{:S(2)}) collective-permute-start(bf16[32,3712]{1,0:T(8,128)(2,1)S(1)} %collective-permute-done.2.refs_0_.refs_2_), channel_id=1, source_target_pairs={{0,8},{8,16},{16,24},{24,32},{32,40},{40,48},{48,56},{56,0},{1,9},... | collective-permute-start | bytes 712712 | tf_op jit(solution)/shard_map/ppermute | solution.py:386
  46.7 8.9 %collective-permute-start.6 = (bf16[32,3712]{1,0:T(8,128)(2,1)S(1)}, bf16[32,3712]{1,0:T(8,128)(2,1)S(1)}, u32[]{:S(2)}, u32[]{:S(2)}) collective-permute-start(bf16[32,3712]{1,0:T(8,128)(2,1)S(1)} %collective-permute-done.5.refs_1_.refs_6_), channel_id=1, source_target_pairs={{0,56},{8,0},{16,8},{24,16},{32,24},{40,32},{48,40},{56,48},{1,57}... | collective-permute-start | bytes 712712 | tf_op jit(solution)/shard_map/ppermute | solution.py:386
  52.4 7.5 %collective-permute-start.4 = (bf16[32,3712]{1,0:T(8,128)(2,1)S(1)}, bf16[32,3712]{1,0:T(8,128)(2,1)S(1)}, u32[]{:S(2)}, u32[]{:S(2)}) collective-permute-start(bf16[32,3712]{1,0:T(8,128)(2,1)S(1)} %collective-permute-done.3.refs_3_), channel_id=1, source_target_pairs={{0,8},{8,16},{16,24},{24,32},{32,40},{40,48},{48,56},{56,0},{1,9},... | collective-permute-start | bytes 712712 | tf_op jit(solution)/shard_map/ppermute | solution.py:386
  54.9 0.7 copy-start.9
  60.5 1.3 copy-start.3
  61.8 1.3 copy-start.5
  63.1 0.7 copy-start.7
  67.3 81.2 %all-to-all-start.1 = ((bf16[8,8,32,640]{3,2,1,0:T(8,128)(2,1)}), bf16[8,8,32,640]{3,2,1,0:T(8,128)(2,1)}, u32[]{:S(2)}, u32[]{:S(2)}) async-start(bf16[8,8,32,640]{3,2,1,0:T(8,128)(2,1)} %regroup.1), calls=%async_computation.1 | async-start | bytes 5242880 | tf_op jit(solution)/shard_map/all_to_all | solution.py:458
  75.9 0.9 copy-start.8
  76.8 0.9 copy-start.10
  81.6 46.3 %copy-start.2 = (bf16[3584,256]{1,0:T(8,128)(2,1)S(1)}, bf16[3584,256]{1,0:T(8,128)(2,1)}, u32[]{:S(2)}) copy-start(bf16[3584,256]{1,0:T(8,128)(2,1)} %copy-done.1) | copy-start | bytes 5505028
  81.6 17.2 %collective-permute-start.12 = (bf16[64,3584]{1,0:T(8,128)(2,1)S(1)}, bf16[64,3584]{1,0:T(8,128)(2,1)S(1)}, u32[]{:S(2)}, u32[]{:S(2)}) collective-permute-start(bf16[64,3584]{1,0:T(8,128)(2,1)S(1)} %get-tuple-element.15.refs_0_), channel_id=1, source_target_pairs={{0,66},{2,68},{4,70},{6,64},{64,2},{66,4},{68,6},{70,0},{1,67},{3,... | collective-permute-start | bytes 1376264 | tf_op jit(solution)/shard_map/ppermute | solution.py:390
  83.2 24.3 %collective-permute-start.10 = (bf16[64,3584]{1,0:T(8,128)(2,1)S(1)}, bf16[64,3584]{1,0:T(8,128)(2,1)S(1)}, u32[]{:S(2)}, u32[]{:S(2)}) collective-permute-start(bf16[64,3584]{1,0:T(8,128)(2,1)S(1)} %get-tuple-element.13), channel_id=1, source_target_pairs={{0,64},{2,66},{4,68},{6,70},{64,0},{66,2},{68,4},{70,6},{1,65},{3,... | collective-permute-start | bytes 1376264 | tf_op jit(solution)/shard_map/ppermute | solution.py:390
  86.1 26.1 %collective-permute-start.11 = (bf16[64,3584]{1,0:T(8,128)(2,1)S(1)}, bf16[64,3584]{1,0:T(8,128)(2,1)S(1)}, u32[]{:S(2)}, u32[]{:S(2)}) collective-permute-start(bf16[64,3584]{1,0:T(8,128)(2,1)S(1)} %get-tuple-element.14), channel_id=1, source_target_pairs={{0,2},{2,4},{4,6},{6,0},{64,66},{66,68},{68,70},{70,64},{1,3},{3,5... | collective-permute-start | bytes 1376264 | tf_op jit(solution)/shard_map/ppermute | solution.py:390
  87.6 39.1 %collective-permute-start.13 = (bf16[64,3584]{1,0:T(8,128)(2,1)S(1)}, bf16[64,3584]{1,0:T(8,128)(2,1)S(1)}, u32[]{:S(2)}, u32[]{:S(2)}) collective-permute-start(bf16[64,3584]{1,0:T(8,128)(2,1)S(1)} %get-tuple-element.16), channel_id=1, source_target_pairs={{0,4},{2,6},{4,0},{6,2},{64,68},{66,70},{68,64},{70,66},{1,5},{3,7... | collective-permute-start | bytes 1376264 | tf_op jit(solution)/shard_map/ppermute | solution.py:390
  89.4 37.5 %collective-permute-start.14 = (bf16[64,3584]{1,0:T(8,128)(2,1)S(1)}, bf16[64,3584]{1,0:T(8,128)(2,1)S(1)}, u32[]{:S(2)}, u32[]{:S(2)}) collective-permute-start(bf16[64,3584]{1,0:T(8,128)(2,1)S(1)} %get-tuple-element.17), channel_id=1, source_target_pairs={{0,68},{2,70},{4,64},{6,66},{64,4},{66,6},{68,0},{70,2},{1,69},{3,... | collective-permute-start | bytes 1376264 | tf_op jit(solution)/shard_map/ppermute | solution.py:390
  98.8 29.1 %collective-permute-start.15 = (bf16[64,3584]{1,0:T(8,128)(2,1)S(1)}, bf16[64,3584]{1,0:T(8,128)(2,1)S(1)}, u32[]{:S(2)}, u32[]{:S(2)}) collective-permute-start(bf16[64,3584]{1,0:T(8,128)(2,1)S(1)} %get-tuple-element.18), channel_id=1, source_target_pairs={{0,6},{2,0},{4,2},{6,4},{64,70},{66,64},{68,66},{70,68},{1,7},{3,1... | collective-permute-start | bytes 1376264 | tf_op jit(solution)/shard_map/ppermute | solution.py:390
  107.4 20.5 %collective-permute-start.16 = (bf16[64,3584]{1,0:T(8,128)(2,1)S(1)}, bf16[64,3584]{1,0:T(8,128)(2,1)S(1)}, u32[]{:S(2)}, u32[]{:S(2)}) collective-permute-start(bf16[64,3584]{1,0:T(8,128)(2,1)S(1)} %get-tuple-element.19), channel_id=1, source_target_pairs={{0,70},{2,64},{4,66},{6,68},{64,6},{66,0},{68,2},{70,4},{1,71},{3,... | collective-permute-start | bytes 1376264 | tf_op jit(solution)/shard_map/ppermute | solution.py:390
  112.3 27.1 %collective-permute-start.20 = (bf16[256,1792]{1,0:T(8,128)(2,1)S(1)}, bf16[256,1792]{1,0:T(8,128)(2,1)}, u32[]{:S(2)}, u32[]{:S(2)}) collective-permute-start(bf16[256,1792]{1,0:T(8,128)(2,1)S(1)} %collective-permute-done.8.refs_2_.w2), channel_id=1, source_target_pairs={{0,128},{128,0},{1,129},{129,1},{2,130},{130,2},{3,131},{131,3},{4... | collective-permute-start | bytes 2752520 | tf_op jit(solution)/shard_map/ppermute | solution.py:382
  126.8 12.6 %collective-permute-start.19 = (bf16[256,1792]{1,0:T(8,128)(2,1)}, bf16[256,1792]{1,0:T(8,128)(2,1)}, u32[]{:S(2)}, u32[]{:S(2)}) collective-permute-start(bf16[256,1792]{1,0:T(8,128)(2,1)} %scale_down.3.w0), channel_id=1, source_target_pairs={{0,128},{128,0},{1,129},{129,1},{2,130},{130,2},{3,131},{131,3},{4... | collective-permute-start | bytes 2752520 | tf_op jit(solution)/shard_map/ppermute | solution.py:382
  127.9 3.2 %copy-start.4 = (bf16[3584,256]{1,0:T(8,128)(2,1)S(1)}, bf16[3584,256]{1,0:T(8,128)(2,1)}, u32[]{:S(2)}) copy-start(bf16[3584,256]{1,0:T(8,128)(2,1)} %copy-done.3) | copy-start | bytes 5505028
  127.9 3.1 %copy-start.6 = (bf16[3584,256]{1,0:T(8,128)(2,1)S(1)}, bf16[3584,256]{1,0:T(8,128)(2,1)}, u32[]{:S(2)}) copy-start(bf16[3584,256]{1,0:T(8,128)(2,1)} %copy-done.5) | copy-start | bytes 5505028
  130.0 4.3 %copy-start.19 = (s32[8]{0:T(128)S(1)}, s32[8]{0:T(128)}, u32[]{:S(2)}) copy-start(s32[8]{0:T(128)} %constant.112) | copy-start | bytes 100
  130.1 9.3 %collective-permute-start.17 = (bf16[512,256]{1,0:T(8,128)(2,1)S(1)}, bf16[512,256]{1,0:T(8,128)(2,1)S(1)}, u32[]{:S(2)}, u32[]{:S(2)}) collective-permute-start(bf16[512,256]{1,0:T(8,128)(2,1)S(1)} %hidden_units.2.h0), channel_id=1, source_target_pairs={{0,1},{1,0},{2,3},{3,2},{4,5},{5,4},{6,7},{7,6},{8,9},{9,8},{10,11... | collective-permute-start | bytes 786440 | tf_op jit(solution)/shard_map/ppermute | solution.py:382
  133.2 10.2 %collective-permute-start.18 = (bf16[512,256]{1,0:T(8,128)(2,1)S(1)}, bf16[512,256]{1,0:T(8,128)(2,1)S(1)}, u32[]{:S(2)}, u32[]{:S(2)}) collective-permute-start(bf16[512,256]{1,0:T(8,128)(2,1)S(1)} %hidden_units.3.h1), channel_id=1, source_target_pairs={{0,1},{1,0},{2,3},{3,2},{4,5},{5,4},{6,7},{7,6},{8,9},{9,8},{10,11... | collective-permute-start | bytes 786440 | tf_op jit(solution)/shard_map/ppermute | solution.py:382
  148.5 52.4 %all-to-all-start.2 = ((bf16[64,8,1792]{2,1,0:T(8,128)(2,1)}), bf16[64,8,1792]{2,1,0:T(8,128)(2,1)S(1)}, u32[]{:S(2)}, u32[]{:S(2)}) async-start(bf16[64,8,1792]{2,1,0:T(8,128)(2,1)} %down_rows.1.refs_0_), calls=%async_computation.2 | async-start | bytes 3670016 | tf_op jit(solution)/shard_map/all_to_all | solution.py:471
  160.9 3.8 %copy-start.12 = (s32[32,8]{0,1:T(8,128)S(1)}, s32[32,8]{0,1:T(8,128)}, u32[]{:S(2)}) copy-start(s32[32,8]{0,1:T(8,128)} %param.24) | copy-start | bytes 3076
  160.9 3.9 %copy-start.11 = (bf16[32,576]{1,0:T(8,128)(2,1)S(1)}, bf16[32,576]{1,0:T(8,128)(2,1)}, u32[]{:S(2)}) copy-start(bf16[32,576]{1,0:T(8,128)(2,1)} %param.22) | copy-start | bytes 110596
  160.9 4.0 %copy-start.13 = (f32[32,8]{0,1:T(8,128)S(1)}, f32[32,8]{0,1:T(8,128)}, u32[]{:S(2)}) copy-start(f32[32,8]{0,1:T(8,128)} %param.25) | copy-start | bytes 3076
  163.6 45.2 %collective-permute-start.21 = (bf16[32,32,640]{2,1,0:T(8,128)(2,1)S(1)}, bf16[32,32,640]{2,1,0:T(8,128)(2,1)}, u32[]{:S(2)}, u32[]{:S(2)}) collective-permute-start(bf16[32,32,640]{2,1,0:T(8,128)(2,1)S(1)} %compact.1.mine), channel_id=1, source_target_pairs={{0,1},{1,0},{2,3},{3,2},{4,5},{5,4},{6,7},{7,6},{8,9},{9,8},{10,11... | collective-permute-start | bytes 3932168 | tf_op jit(solution)/shard_map/ppermute | solution.py:382

commit v6 on v5

--- a/solution.py
+++ b/solution.py
@@ -1,3 +1,5 @@
+import functools
+
 import jax
 import jax.numpy as jnp
 import numpy as np
@@ -148,36 +150,41 @@
     )(place, *blocks)
 
 
-PEER_ORDER = (4, 1, 5, 2, 6, 3, 7, 0)
+PEER_ORDER = (0, 4, 1, 5, 2, 6, 3, 7)
 
 
 def hidden_kernel(*refs):
-    tokens, (gate, up, out, x) = refs[:8], refs[8:]
-    for r, token in zip(PEER_ORDER, tokens):
-        x[r * 64 : (r + 1) * 64, :] = token[...]
-    for half in range(2):
-        rows = slice(half * 256, (half + 1) * 256)
-        g = jnp.dot(x[rows, :], gate[...], preferred_element_type=F32)
-        u = jnp.dot(x[rows, :], up[...], preferred_element_type=F32)
-        out[rows, :] = (g / (1.0 + jnp.exp(-g)) * u).astype(BF16)
-
-
-def hidden_units(tokens, gate, up):
+    tokens, (g0, g1, u0, u1, out, x) = refs[:4], refs[4:]
+    for n, token in enumerate(tokens):
+        x[n * 64 : (n + 1) * 64, :] = token[...]
+    for n, (gate, up) in enumerate(((g0, u0), (g1, u1))):
+        g = jnp.dot(x[...], gate[...], preferred_element_type=F32)
+        u = jnp.dot(x[...], up[...], preferred_element_type=F32)
+        out[:, n * 256 : (n + 1) * 256] = (g / (1.0 + jnp.exp(-g)) * u).astype(BF16)
+
+
+def hidden_units(tokens, panels):
     vmem = pl.BlockSpec(memory_space=pltpu.VMEM)
     return pl.pallas_call(
         hidden_kernel,
-        in_specs=[vmem] * 10,
+        in_specs=[vmem] * 8,
         out_specs=vmem,
-        out_shape=jax.ShapeDtypeStruct((512, 256), BF16),
-        scratch_shapes=[pltpu.VMEM((512, D), BF16)],
-        compiler_params=params(10),
+        out_shape=jax.ShapeDtypeStruct((256, 512), BF16),
+        scratch_shapes=[pltpu.VMEM((256, D), BF16)],
+        compiler_params=params(8),
         cost_estimate=cost(1.9e9, 8e6),
         name="hidden_units",
-    )(*[tokens[r] for r in PEER_ORDER], gate, up)
-
-
-def down_kernel(order_ref, h0, h1, h2, h3, w0, w1, w2, w3, out):
-    h = jnp.concatenate([part[...] for part in (h0, h1, h2, h3)], axis=1)
+    )(*tokens, *panels)
+
+
+def down_kernel(order_ref, a0, a1, b0, b1, w0, w1, w2, w3, out):
+    h = jnp.concatenate(
+        [
+            jnp.concatenate([a0[...], a1[...]], axis=1),
+            jnp.concatenate([b0[...], b1[...]], axis=1),
+        ],
+        axis=0,
+    )
     for c in range(HALF_D // 256):
         cols = slice(c * 256, (c + 1) * 256)
         w = jnp.concatenate([p[:, cols] for p in (w0, w1, w2, w3)], axis=0)
@@ -199,7 +206,8 @@
     )(order, *parts, *weights)
 
 
-def blend_kernel(routing_ref, weight_ref, rows_ref, out):
+def blend_kernel(late_ref, routing_ref, weight_ref, rows_ref, out, done):
+    done[0] = 0.0
     column = lax.broadcasted_iota(I32, (1, EP * CAP), 1)
     experts, slot = column >> 3, column & 7
     routing, weight = routing_ref[...], weight_ref[...]
@@ -219,30 +227,34 @@
     ).astype(BF16)
 
 
-def blend(routing, weight, rows):
+def blend(late, routing, weight, rows):
     wide = 896
     return pl.pallas_call(
         blend_kernel,
         grid=(HALF_D // wide,),
         in_specs=[
+            smem(),
             whole((TRAJ, 8)),
             whole((TRAJ, 8)),
             pl.BlockSpec((EP, CAP, wide), lambda i: (0, 0, i)),
         ],
-        out_specs=pl.BlockSpec((TRAJ, wide), lambda i: (0, i)),
-        out_shape=jax.ShapeDtypeStruct((TRAJ, HALF_D), BF16),
+        out_specs=[pl.BlockSpec((TRAJ, wide), lambda i: (0, i)), smem()],
+        out_shape=[
+            jax.ShapeDtypeStruct((TRAJ, HALF_D), BF16),
+            jax.ShapeDtypeStruct((1,), F32),
+        ],
         compiler_params=params(10),
         cost_estimate=cost(1e8, 2e6),
         name="blend",
-    )(routing, weight, rows)
+    )(late, routing, weight, rows)
 
 
 def collect_kernel(index_ref, pages, *rest):
     out = rest[-1]
     step = pl.program_id(0)
     lane = lax.broadcasted_iota(I32, (32, LANES - LATENT), 1)
-    for i in range(8):
-        j = step * 8 + i
+    for i in range(16):
+        j = step * 16 + i
         out[i, 0:16, 0:LATENT] = pages[index_ref[j, 0]]
         out[i, 16:32, 0:LATENT] = pages[index_ref[j, 1]]
         slot, length = index_ref[j, 2].astype(F32), index_ref[j, 3].astype(F32)
@@ -252,9 +264,9 @@
 def collect(index, pages, *before):
     return pl.pallas_call(
         collect_kernel,
-        grid=(EP // 8,),
+        grid=(EP // 16,),
         in_specs=[smem(), whole(pages.shape)] + [smem()] * len(before),
-        out_specs=pl.BlockSpec((8, 32, LANES), lambda i: (i, 0, 0)),
+        out_specs=pl.BlockSpec((16, 32, LANES), lambda i: (i, 0, 0)),
         out_shape=pltpu.HBM((EP, 32, LANES), BF16),
         compiler_params=params(10),
         cost_estimate=cost(1e6, 6e6),
@@ -281,31 +293,33 @@
     )(hbm(midway), *before)
 
 
-def compact_kernel(source_ref, arrived, *rest):
-    out = rest[-1]
-    step = pl.program_id(0)
-    for i in range(8):
-        out[i] = arrived[source_ref[step * 8 + i]]
-
-
-def compact(source, arrived, *before):
+def compact_kernel(source_ref, arrived, late_ref, first, second):
+    for s in range(TRAJ // 2):
+        first[s] = arrived[source_ref[s]]
+        second[s] = arrived[source_ref[TRAJ // 2 + s]]
+
+
+def compact(source, arrived, late):
+    half = (TRAJ // 2, 32, LANES)
     return pl.pallas_call(
         compact_kernel,
-        grid=(TRAJ // 8,),
-        in_specs=[smem(), whole(arrived.shape)] + [smem()] * len(before),
-        out_specs=pl.BlockSpec((8, 32, LANES), lambda i: (i, 0, 0)),
-        out_shape=in_hbm((TRAJ, 32, LANES)),
+        grid=(1,),
+        in_specs=[smem(), whole(arrived.shape), smem()],
+        out_specs=[whole(half)] * 2,
+        out_shape=[in_hbm(half)] * 2,
         compiler_params=params(10),
         cost_estimate=cost(1e6, 4e6),
         name="compact",
-    )(source, hbm(arrived), *before)
+    )(source, hbm(arrived), late)
 
 
 ATTEND_STEP = 8
 
 
-def attend_kernel(tp_ref, length_ref, mine, other, queries, fresh, cache_out, out):
-    step = pl.program_id(0)
+def attend_kernel(start, late_ref, tp_ref, length_ref, mine, other, queries, fresh, *rest):
+    cache_out, out, done = rest[-3:]
+    done[0] = 0.0
+    step = pl.program_id(0) + start
     first = tp_ref[0] == 0
     row = lax.broadcasted_iota(I32, (MAXLEN, LATENT), 0).astype(F32).astype(BF16)
     column = lax.broadcasted_iota(I32, (TRAJ, MAXLEN), 1)
@@ -335,31 +349,38 @@
         ).astype(BF16)
 
 
-def attend(tp_index, length, mine, other, queries, fresh):
+def attend(half, late, tp_index, length, mine, other, queries, fresh, *so_far):
     n = ATTEND_STEP
-    return pl.pallas_call(
-        attend_kernel,
-        grid=(TRAJ // n,),
+    start = half * (TRAJ // 2 // n)
+    there = pl.BlockSpec(memory_space=pl.ANY)
+    return pl.pallas_call(
+        functools.partial(attend_kernel, start),
+        grid=(TRAJ // 2 // n,),
         in_specs=[
+            smem(),
             smem(),
             smem(),
             pl.BlockSpec((n, 32, LANES), lambda i: (i, 0, 0)),
             pl.BlockSpec((n, 32, LANES), lambda i: (i, 0, 0)),
-            pl.BlockSpec((n, 32, LATENT), lambda i: (i, 0, 0)),
-            pl.BlockSpec((n, 1, LATENT), lambda i: (i, 0, 0)),
-        ],
+            pl.BlockSpec((n, 32, LATENT), lambda i: (i + start, 0, 0)),
+            pl.BlockSpec((n, 1, LATENT), lambda i: (i + start, 0, 0)),
+        ]
+        + [there] * len(so_far),
         out_specs=[
-            pl.BlockSpec((n, MAXLEN, LATENT), lambda i: (i, 0, 0)),
-            pl.BlockSpec((n, 32, LATENT_WIDTH), lambda i: (i, 0, 0)),
+            pl.BlockSpec((n, MAXLEN, LATENT), lambda i: (i + start, 0, 0)),
+            pl.BlockSpec((n, 32, LATENT_WIDTH), lambda i: (i + start, 0, 0)),
+            smem(),
         ],
         out_shape=[
             jax.ShapeDtypeStruct((TRAJ, MAXLEN, LATENT), BF16),
             jax.ShapeDtypeStruct((TRAJ, 32, LATENT_WIDTH), BF16),
+            jax.ShapeDtypeStruct((1,), F32),
         ],
+        input_output_aliases={7 + k: k for k in range(len(so_far))},
         compiler_params=params(10),
-        cost_estimate=cost(2e8, 8e6),
+        cost_estimate=cost(1e8, 4e6),
         name="attend",
-    )(tp_index, length, mine, other, hbm(queries), fresh.reshape(TRAJ, 1, LATENT))
+    )(late, tp_index, length, mine, other, hbm(queries), fresh, *so_far)
 
 
 def once_kernel(*refs):
@@ -449,7 +470,7 @@
     )
     picked = pick_rows(place, up_way + down_way[1:])
     tokens = list(picked)
-    for peer in PEER_ORDER[:7]:
+    for peer in PEER_ORDER[1:]:
         tokens[peer] = plane_shift(picked[peer], peer // NY, peer % NY)
 
     down_keep = scale_down(tp_index, down_value, down_scale, once(picked[5]))
@@ -457,30 +478,38 @@
 
     arrived = lax.all_to_all(midway, "z", split_axis=0, concat_axis=0, tiled=True)
 
-    act, act_far = hidden_units(tokens, gate, up), hidden_units(tokens, gate_far, up_far)
-    act_tp, act_tp_far = swap(act, "tp"), swap(act_far, "tp")
-    group = jnp.arange(EP, dtype=I32)
+    panels = (gate, gate_far, up, up_far)
+    act = hidden_units([tokens[peer] for peer in PEER_ORDER[:4]], panels)
+    act_tp = swap(act, "tp")
+    act_late = hidden_units([tokens[peer] for peer in PEER_ORDER[4:]], panels)
+    act_late_tp = swap(act_late, "tp")
+    peer = jnp.asarray(np.repeat(np.array(PEER_ORDER, np.int32), 8))
     order = (
-        ((xh + (group >> 5)) % NX) * NZ + (z - jnp.tile(jnp.asarray(behind), 8)) % NZ
-    ) * NY + (y - (group >> 3)) % NY
+        ((xh + (peer >> 2)) % NX) * NZ + (z - jnp.asarray(np.tile(behind, 8))) % NZ
+    ) * NY + (y - peer) % NY
     out_rows = down_rows(
         order,
-        [act, act_far, act_tp, act_tp_far],
+        [act, act_tp, act_late, act_late_tp],
         [down_keep, down_far, down_tp, down_tp_far],
     )
     returned = lax.all_to_all(
         out_rows, ("xh", "z", "y"), split_axis=0, concat_axis=0, tiled=True
     )
-    expert_mix = blend(routing, route_weight, returned)
 
     arrived = arrived.reshape(EP, 32, LANES)
     labels = arrived[:, 0, LATENT : LATENT + 2].astype(I32)
     taken = labels[:, 0][None, :] == jnp.arange(TRAJ, dtype=I32)[:, None]
     source = jnp.sum(jnp.where(taken, jnp.arange(EP, dtype=I32)[None, :], 0), axis=1)
     length = jnp.sum(jnp.where(taken, labels[:, 1][None, :], 0), axis=1)
-    my_half = compact(source, arrived, once(out_rows))
-    other_half = swap(my_half, "tp")
-    new_cache, attention = attend(tp_index, length, my_half, other_half, queries, fresh_latent)
+    fresh = fresh_latent.reshape(TRAJ, 1, LATENT)
+    late = once(out_rows)
+    halves = compact(source, arrived, late)
+    others = [swap(part, "tp") for part in halves]
+    so_far = attend(0, late, tp_index, length, halves[0], others[0], queries, fresh)
+    expert_mix, late = blend(so_far[2], routing, route_weight, returned)
+    new_cache, attention, _ = attend(
+        1, late, tp_index, length, halves[1], others[1], queries, fresh, *so_far[:2]
+    )
     return new_cache, attention, expert_mix
 
 

time: 215 us -> 223 us (1.037)
  starting transfers between devices: 54.5 us -> 69.9 us
  waiting for transfers between devices: 95.8 us -> 88.1 us
    all_to_all x1, waiting for transfers between devices: 35.9 us -> 1.23 us  [on_device(): lax.all_to_all(out_rows, ('xh', 'z', 'y'), split_axis=0, concat_axis=0, t...]
    ppermute x8 -> x9, waiting for transfers between devices: 14.7 us -> 42.6 us  [swap(): return lax.ppermute(x, axis, [(0, 1), (1, 0)])]
    ppermute x7, starting transfers between devices: 12.2 us -> 25.3 us  [plane_shift(): lax.ppermute(x, ('xh', 'y'), [(a * NY + b, (a + dx) % NX * NY + (b + dy)...]
    pallas_call x6 -> x7, Pallas kernels: 19.1 us -> 21.8 us  [the longest x2 7.63 us: attend(): pl.pallas_call(functools.partial(attend_kernel, start), grid=(TRAJ // 2 /...]
    ppermute x8 -> x9, starting transfers between devices: 4.86 us -> 5.16 us  [swap(): return lax.ppermute(x, axis, [(0, 1), (1, 0)])]
    unnamed x43 -> x47, local copies, waits for them, and re-layouts: 11.3 us -> 11.2 us
  transfers between devices with their start and end apart: 25 -> 26, of which waited for: 12 -> 12; matrix products, arithmetic and copies ran while one was open for 4% -> 4% of each run, Pallas kernels for 17% -> 17%
where the time goes in v6:
time: 223 us; the launch traced here: 222 us
  waiting for transfers between devices  88.1 us (40%)
  starting transfers between devices  69.9 us (31%)
  Pallas kernels  45.8 us (21%)
  local copies, waits for them, and re-layouts  12.2 us (5%)
  other arithmetic  5.21 us (2%)
    ppermute x9, waiting for transfers between devices, swap(): return lax.ppermute(x, axis, [(0, 1), (1, 0)])  42.6 us
    ppermute x7, waiting for transfers between devices, plane_shift(): lax.ppermute(x, ('xh', 'y'), [(a * NY + b, (a + dx) % NX * NY + (b + dy)...  29.4 us
    ppermute x7, starting transfers between devices, plane_shift(): lax.ppermute(x, ('xh', 'y'), [(a * NY + b, (a + dx) % NX * NY + (b + dy)...  25.3 us
    ppermute x7, waiting for transfers between devices, z_shift(): return lax.ppermute(x, 'z', [(i, (i + by) % NZ) for i in range(NZ)])  14.8 us
    all_to_all x1, starting transfers between devices, on_device(): lax.all_to_all(out_rows, ('xh', 'z', 'y'), split_axis=0, concat_axis=0, t...  12.7 us
    unnamed x47, local copies, waits for them, and re-layouts  11.2 us
    ppermute x7, starting transfers between devices, z_shift(): return lax.ppermute(x, 'z', [(i, (i + by) % NZ) for i in range(NZ)])  10.8 us
    all_to_all x1, starting transfers between devices, on_device(): lax.all_to_all(midway, 'z', split_axis=0, concat_axis=0, tiled=True)  8.45 us
  transfers between devices with their start and end apart: 26, of which 12 were waited for; matrix products, arithmetic and copies ran while one was open for 4% of the time, Pallas kernels for 17%

profile of v6, /device:TPU:68, one launch (start us, length us, event | category | flops | bytes accessed | tf_op | source)
XLA Modules:
  0.0 222.1 jit_solution(39998901750018548)
XLA Ops:
  0.7 0.7 convert_element_type.38
  1.5 1.7 fusion.1.refs_0_
  3.1 1.9 collective-permute-start
  5.1 0.7 bitcast_convert_fusion.scale
  5.8 2.5 %scale_down.2 = bf16[256,1792]{1,0:T(8,128)(2,1)} custom-call(s32[1]{0:T(128)S(6)} %sub.33.half_ref, f32[2,28]{1,0:T(2,128)S(1)} %bitcast_convert_fusion.scale, bf16[1,256,3584]{2,1,0:T(8,128)(2,1)} %value.7), custom_call_target="tpu_custom_call" | custom-call | flops 1000000 | bytes 2000000 | tf_op jit(solution)/shard_map/scale_down/pallas_call | solution.py:90
  8.3 1.2 collective-permute-start.11
  9.7 0.7 copy.46
  10.4 3.9 %copy.48.pages = bf16[128,16,576]{2,1,0:T(8,128)(2,1)S(1)} copy(bf16[128,16,576]{0,2,1:T(8,128)(2,1)} %param.18) | data formatting | bytes 4718592 | tf_op args[0]
  14.3 0.8 broadcast_subtract_fusion.index_ref
  15.1 0.5 once.5.rest_0_
  15.6 3.9 %collect.1 = bf16[64,32,640]{2,1,0:T(8,128)(2,1)} custom-call(s32[64,4]{1,0:T(8,128)S(1)} %broadcast_subtract_fusion.index_ref, bf16[128,16,576]{2,1,0:T(8,128)(2,1)S(1)} %copy.48.pages, f32[1]{0:T(128)} %once.5.rest_0_), custom_call_target="tpu_custom_call" | custom-call | flops 1000000 | bytes 6000000 | tf_op jit(solution)/shard_map/collect/pallas_call | solution.py:265
  19.6 7.6 %all-to-all-start = ((bf16[8,8,32,640]{3,2,1,0:T(8,128)(2,1)}), bf16[8,8,32,640]{3,2,1,0:T(8,128)(2,1)}, u32[]{:S(2)}, u32[]{:S(2)}) async-start(bf16[8,8,32,640]{3,2,1,0:T(8,128)(2,1)} %bitcast.28), calls=%async_computation | async-start | bytes 5242880 | tf_op jit(solution)/shard_map/all_to_all | solution.py:457
  27.1 3.0 %collective-permute-start.1 = (bf16[32,3712]{1,0:T(8,128)(2,1)}, bf16[32,3712]{1,0:T(8,128)(2,1)S(1)}, u32[]{:S(2)}, u32[]{:S(2)}) collective-permute-start(bf16[32,3712]{1,0:T(8,128)(2,1)} %collective-permute-done.refs_1_.refs_0_), channel_id=1, source_target_pairs={{0,8},{8,16},{16,24},{24,32},{32,40},{40,48},{48,56},{56,0},{1,9},... | collective-permute-start | bytes 712712 | tf_op jit(solution)/shard_map/ppermute | solution.py:407
  30.2 2.6 %scale_wide.2.refs_4_ = bf16[3584,256]{1,0:T(8,128)(2,1)S(1)} custom-call(f32[2,28]{1,0:T(2,128)S(1)} %convert_bitcast_fusion.1.scale, bf16[1,3584,256]{2,1,0:T(8,128)(2,1)} %value.4, f32[1]{0:T(128)} %once.5.rest_0_), custom_call_target="tpu_custom_call" | custom-call | flops 1000000 | bytes 4000000 | tf_op jit(solution)/shard_map/scale_wide/pallas_call | solution.py:66
  32.9 1.5 collective-permute-done.1.refs_2_.refs_0_
  34.4 3.3 %collective-permute-done.5.refs_6_.refs_1_ = bf16[32,3712]{1,0:T(8,128)(2,1)S(1)} collective-permute-done((bf16[32,3712]{1,0:T(8,128)(2,1)}, bf16[32,3712]{1,0:T(8,128)(2,1)S(1)}, u32[]{:S(2)}, u32[]{:S(2)}) %collective-permute-start.5) | collective-permute-done | bytes 237600 | tf_op jit(solution)/shard_map/ppermute | solution.py:407
  37.7 0.5 once.6.rest_0_
  38.2 2.6 %scale_wide.3.refs_6_ = bf16[3584,256]{1,0:T(8,128)(2,1)S(1)} custom-call(f32[2,28]{1,0:T(2,128)S(1)} %convert_bitcast_fusion.scale, bf16[1,3584,256]{2,1,0:T(8,128)(2,1)} %value.6, f32[1]{0:T(128)} %once.6.rest_0_), custom_call_target="tpu_custom_call" | custom-call | flops 1000000 | bytes 4000000 | tf_op jit(solution)/shard_map/scale_wide/pallas_call | solution.py:66
  40.9 1.3 copy-done.1
  42.2 3.2 %collective-permute-start.2 = (bf16[32,3712]{1,0:T(8,128)(2,1)S(1)}, bf16[32,3712]{1,0:T(8,128)(2,1)S(1)}, u32[]{:S(2)}, u32[]{:S(2)}) collective-permute-start(bf16[32,3712]{1,0:T(8,128)(2,1)S(1)} %collective-permute-done.1.refs_2_.refs_0_), channel_id=1, source_target_pairs={{0,8},{8,16},{16,24},{24,32},{32,40},{40,48},{48,56},{56,0},{1,9},... | collective-permute-start | bytes 712712 | tf_op jit(solution)/shard_map/ppermute | solution.py:407
  45.4 5.7 %collective-permute-done.2.refs_3_ = bf16[32,3712]{1,0:T(8,128)(2,1)S(1)} collective-permute-done((bf16[32,3712]{1,0:T(8,128)(2,1)S(1)}, bf16[32,3712]{1,0:T(8,128)(2,1)S(1)}, u32[]{:S(2)}, u32[]{:S(2)}) %collective-permute-start.2) | collective-permute-done | bytes 237600 | tf_op jit(solution)/shard_map/ppermute | solution.py:407
  51.1 2.5 %collective-permute-start.3 = (bf16[32,3712]{1,0:T(8,128)(2,1)S(1)}, bf16[32,3712]{1,0:T(8,128)(2,1)S(1)}, u32[]{:S(2)}, u32[]{:S(2)}) collective-permute-start(bf16[32,3712]{1,0:T(8,128)(2,1)S(1)} %collective-permute-done.2.refs_3_), channel_id=1, source_target_pairs={{0,8},{8,16},{16,24},{24,32},{32,40},{40,48},{48,56},{56,0},{1,9},... | collective-permute-start | bytes 712712 | tf_op jit(solution)/shard_map/ppermute | solution.py:407
  53.6 0.7 copy-done.9
  54.3 4.3 %collective-permute-done.3.refs_4_.refs_0_ = bf16[32,3712]{1,0:T(8,128)(2,1)S(1)} collective-permute-done((bf16[32,3712]{1,0:T(8,128)(2,1)S(1)}, bf16[32,3712]{1,0:T(8,128)(2,1)S(1)}, u32[]{:S(2)}, u32[]{:S(2)}) %collective-permute-start.3) | collective-permute-done | bytes 237600 | tf_op jit(solution)/shard_map/ppermute | solution.py:407
  58.6 0.5 once.9.rest_0_
  59.2 1.3 copy-done.3
  60.4 1.3 copy-done.5
  61.7 0.7 copy-done.7
  62.4 3.6 %regroup.1 = bf16[8,8,32,640]{3,2,1,0:T(8,128)(2,1)} custom-call(bf16[8,8,32,640]{3,2,1,0:T(8,128)(2,1)} %all-to-all-done.midway, f32[1]{0:T(128)} %once.9.rest_0_), custom_call_target="tpu_custom_call" | custom-call | flops 1000000 | bytes 6000000 | tf_op jit(solution)/shard_map/regroup/pallas_call | solution.py:284
  66.0 8.4 %all-to-all-start.1 = ((bf16[8,8,32,640]{3,2,1,0:T(8,128)(2,1)}), bf16[8,8,32,640]{3,2,1,0:T(8,128)(2,1)}, u32[]{:S(2)}, u32[]{:S(2)}) async-start(bf16[8,8,32,640]{3,2,1,0:T(8,128)(2,1)} %regroup.1), calls=%async_computation.1 | async-start | bytes 5242880 | tf_op jit(solution)/shard_map/all_to_all | solution.py:479
  74.5 0.9 copy-done.8
  75.5 0.9 copy-done.10
  76.4 4.0 %pick_rows.1 = (bf16[64,3584]{1,0:T(8,128)(2,1)S(1)}, bf16[64,3584]{1,0:T(8,128)(2,1)S(1)}, bf16[64,3584]{1,0:T(8,128)(2,1)S(1)}, bf16[64,3584]{1,0:T(8,128)(2,1...) custom-call(s32[3]{0:T(128)S(1)} %pad_add_fusion.1.place_ref, ...), custom_call_target="tpu_custom_call" | custom-call | flops 1000000000 | bytes 6000000 | tf_op jit(solution)/shard_map/pick_rows/pallas_call | solution.py:142
  80.5 3.1 %collective-permute-start.14 = (bf16[64,3584]{1,0:T(8,128)(2,1)S(1)}, bf16[64,3584]{1,0:T(8,128)(2,1)S(1)}, u32[]{:S(2)}, u32[]{:S(2)}) collective-permute-start(bf16[64,3584]{1,0:T(8,128)(2,1)S(1)} %get-tuple-element.24), channel_id=1, source_target_pairs={{0,4},{2,6},{4,0},{6,2},{64,68},{66,70},{68,64},{70,66},{1,5},{3,7... | collective-permute-start | bytes 1376264 | tf_op jit(solution)/shard_map/ppermute | solution.py:411
  83.5 0.3 collective-permute-start.15
  83.8 2.9 %collective-permute-start.16 = (bf16[64,3584]{1,0:T(8,128)(2,1)S(1)}, bf16[64,3584]{1,0:T(8,128)(2,1)S(1)}, u32[]{:S(2)}, u32[]{:S(2)}) collective-permute-start(bf16[64,3584]{1,0:T(8,128)(2,1)S(1)} %get-tuple-element.26), channel_id=1, source_target_pairs={{0,6},{2,0},{4,2},{6,4},{64,70},{66,64},{68,66},{70,68},{1,7},{3,1... | collective-permute-start | bytes 1376264 | tf_op jit(solution)/shard_map/ppermute | solution.py:411
  86.7 3.3 %collective-permute-start.17 = (bf16[64,3584]{1,0:T(8,128)(2,1)S(1)}, bf16[64,3584]{1,0:T(8,128)(2,1)S(1)}, u32[]{:S(2)}, u32[]{:S(2)}) collective-permute-start(bf16[64,3584]{1,0:T(8,128)(2,1)S(1)} %get-tuple-element.27), channel_id=1, source_target_pairs={{0,70},{2,64},{4,66},{6,68},{64,6},{66,0},{68,2},{70,4},{1,71},{3,... | collective-permute-start | bytes 1376264 | tf_op jit(solution)/shard_map/ppermute | solution.py:411
  90.0 0.5 once.7.rest_0_
  90.6 2.2 scale_down.3.w0
  92.8 10.3 %collective-permute-done.14.refs_0_ = bf16[64,3584]{1,0:T(8,128)(2,1)S(1)} collective-permute-done((bf16[64,3584]{1,0:T(8,128)(2,1)S(1)}, bf16[64,3584]{1,0:T(8,128)(2,1)S(1)}, u32[]{:S(2)}, u32[]{:S(2)}) %collective-permute-start.14) | collective-permute-done | bytes 458784 | tf_op jit(solution)/shard_map/ppermute | solution.py:411
  103.0 13.6 %collective-permute-start.9 = (bf16[64,3584]{1,0:T(8,128)(2,1)S(1)}, bf16[64,3584]{1,0:T(8,128)(2,1)S(1)}, u32[]{:S(2)}, u32[]{:S(2)}) collective-permute-start(bf16[64,3584]{1,0:T(8,128)(2,1)S(1)} %get-tuple-element.23.refs_0_), channel_id=1, source_target_pairs={{0,66},{2,68},{4,70},{6,64},{64,2},{66,4},{68,6},{70,0},{1,67},{3,... | collective-permute-start | bytes 1376264 | tf_op jit(solution)/shard_map/ppermute | solution.py:411
  116.7 5.9 %collective-permute-done.16.refs_2_ = bf16[64,3584]{1,0:T(8,128)(2,1)S(1)} collective-permute-done((bf16[64,3584]{1,0:T(8,128)(2,1)S(1)}, bf16[64,3584]{1,0:T(8,128)(2,1)S(1)}, u32[]{:S(2)}, u32[]{:S(2)}) %collective-permute-start.16) | collective-permute-done | bytes 458784 | tf_op jit(solution)/shard_map/ppermute | solution.py:411
  122.6 0.7 collective-permute-start.7
  123.3 1.4 collective-permute-start.8
  124.7 2.1 hidden_units.3.b0
  126.8 2.4 %collective-permute-done.9.refs_3_ = bf16[64,3584]{1,0:T(8,128)(2,1)S(1)} collective-permute-done((bf16[64,3584]{1,0:T(8,128)(2,1)S(1)}, bf16[64,3584]{1,0:T(8,128)(2,1)S(1)}, u32[]{:S(2)}, u32[]{:S(2)}) %collective-permute-start.9) | collective-permute-done | bytes 458784 | tf_op jit(solution)/shard_map/ppermute | solution.py:411
  129.2 0.8 collective-permute-start.18
  130.0 10.7 %collective-permute-done.7.refs_1_ = bf16[64,3584]{1,0:T(8,128)(2,1)S(1)} collective-permute-done((bf16[64,3584]{1,0:T(8,128)(2,1)S(1)}, bf16[64,3584]{1,0:T(8,128)(2,1)S(1)}, u32[]{:S(2)}, u32[]{:S(2)}) %collective-permute-start.7) | collective-permute-done | bytes 458784 | tf_op jit(solution)/shard_map/ppermute | solution.py:411
  140.8 2.1 hidden_units.2.a0
  142.9 0.9 collective-permute-start.13
  143.9 6.6 %collective-permute-done.13.a1 = bf16[256,512]{1,0:T(8,128)(2,1)S(1)} collective-permute-done((bf16[256,512]{1,0:T(8,128)(2,1)S(1)}, bf16[256,512]{1,0:T(8,128)(2,1)S(1)}, u32[]{:S(2)}, u32[]{:S(2)}) %collective-permute-start.13) | collective-permute-done | bytes 262176 | tf_op jit(solution)/shard_map/ppermute | solution.py:403
  150.5 3.9 %down_rows.1.refs_0_ = bf16[64,8,1792]{2,1,0:T(8,128)(2,1)} custom-call(s32[64]{0:T(128)S(1)} %fusion.3.order_ref, bf16[256,512]{1,0:T(8,128)(2,1)S(1)} %hidden_units.2.a0, bf16[256,512]{1,0:T(8,128)(2,1)S(1)} %collective-permute-done.13.a1, bf16[256,512]{1,0:T(8,128)(2,1)S(1)} %hidden_units.3.b0, bf16[256,512]{1,0:T(8,128)(2,1)S(1)} %collective-permute-done.18.b1, ...), custom_call_target="tpu_custom_call" | custom-call | flops 1900000000 | bytes 7000000 | tf_op jit(solution)/shard_map/down_rows/pallas_call | solution.py:198
  154.4 12.7 %all-to-all-start.2 = ((bf16[64,8,1792]{2,1,0:T(8,128)(2,1)}), bf16[64,8,1792]{2,1,0:T(8,128)(2,1)S(1)}, u32[]{:S(2)}, u32[]{:S(2)}) async-start(bf16[64,8,1792]{2,1,0:T(8,128)(2,1)} %down_rows.1.refs_0_), calls=%async_computation.2 | async-start | bytes 3670016 | tf_op jit(solution)/shard_map/all_to_all | solution.py:495
  167.2 0.5 once.8.late_ref
  167.7 1.0 slice_convert_fusion
  169.0 3.4 %compact.1 = (bf16[16,32,640]{2,1,0:T(8,128)(2,1)S(1)}, bf16[16,32,640]{2,1,0:T(8,128)(2,1)}) custom-call(s32[32]{0:T(128)S(1)} %get-tuple-element.37.source_ref, bf16[64,32,640]{2,1,0:T(8,128)(2,1)} %bitcast.13.arrived, f32[1]{0:T(128)} %once.8.late_ref), custom_call_target="tpu_custom_call" | custom-call | flops 1000000 | bytes 4000000 | tf_op jit(solution)/shard_map/compact/pallas_call | solution.py:304
  172.4 0.8 collective-permute-start.21
  173.2 1.2 collective-permute-start.22
  174.6 29.9 %collective-permute-done.21.other = bf16[16,32,640]{2,1,0:T(8,128)(2,1)S(1)} collective-permute-done((bf16[16,32,640]{2,1,0:T(8,128)(2,1)S(1)}, bf16[16,32,640]{2,1,0:T(8,128)(2,1)S(1)}, u32[]{:S(2)}, u32[]{:S(2)}) %collective-permute-start.21) | collective-permute-done | bytes 655392 | tf_op jit(solution)/shard_map/ppermute | solution.py:403
  204.5 3.8 %attend.2 = (bf16[32,64,576]{2,1,0:T(8,128)(2,1)}, bf16[32,32,512]{2,1,0:T(8,128)(2,1)}, f32[1]{0:T(128)}) custom-call(f32[1]{0:T(128)} %once.8.late_ref, s32[1]{0:T(128)} %bitcast.7.half_ref.tp_ref, s32[32]{0:T(128)S(1)} %get-tuple-element.38.length_ref, bf16[16,32,640]{2,1,0:T(8,128)(2,1)S(1)} %get-tuple-element.28.mine, ...), custom_call_target="tpu_custom_call" | custom-call | flops 100000000 | bytes 4000000 | tf_op jit(solution)/shard_map/attend/pallas_call | solution.py:356
  208.3 1.2 all-to-all-done.2.rows_ref
  209.5 2.7 %blend.1 = (bf16[32,1792]{1,0:T(8,128)(2,1)}, f32[1]{0:T(128)}) custom-call(f32[1]{0:T(128)} %get-tuple-element.29.late_ref, s32[32,8]{1,0:T(8,128)S(1)} %copy.51.routing_ref, f32[32,8]{1,0:T(8,128)S(1)} %copy.52.weight_ref, bf16[64,8,1792]{2,1,0:T(8,128)(2,1)S(1)} %all-to-all-done.2.rows_ref), custom_call_target="tpu_custom_call" | custom-call | flops 100000000 | bytes 2000000 | tf_op jit(solution)/shard_map/blend/pallas_call | solution.py:232
  212.2 6.0 %collective-permute-done.22.other = bf16[16,32,640]{2,1,0:T(8,128)(2,1)} collective-permute-done((bf16[16,32,640]{2,1,0:T(8,128)(2,1)}, bf16[16,32,640]{2,1,0:T(8,128)(2,1)}, u32[]{:S(2)}, u32[]{:S(2)}) %collective-permute-start.22) | collective-permute-done | bytes 655392 | tf_op jit(solution)/shard_map/ppermute | solution.py:403
  218.3 3.9 %attend.3 = (bf16[32,64,576]{2,1,0:T(8,128)(2,1)}, bf16[32,32,512]{2,1,0:T(8,128)(2,1)}, f32[1]{0:T(128)}) custom-call(f32[1]{0:T(128)} %get-tuple-element.30.late_ref, s32[1]{0:T(128)} %bitcast.7.half_ref.tp_ref, s32[32]{0:T(128)S(1)} %get-tuple-element.38.length_ref, ...), custom_call_target="tpu_custom_call", output_to_operand_aliasing={{0}: (7, {}), {1}: (8, {})} | custom-call | flops 100000000 | bytes 4000000 | tf_op jit(solution)/shard_map/attend/pallas_call | solution.py:356
  (75 shorter events, 1.3 us)
Async XLA Ops:
  0.6 8.8 %copy-start = (s32[32,4]{0,1:T(4,128)S(1)}, s32[32,4]{0,1:T(4,128)}, u32[]{:S(2)}) copy-start(s32[32,4]{0,1:T(4,128)} %param.19) | copy-start | bytes 1540
  0.6 8.9 %copy-start.17 = (s32[64]{0:T(128)S(1)}, s32[64]{0:T(128)}, u32[]{:S(2)}) copy-start(s32[64]{0:T(128)} %constant.95.clone) | copy-start | bytes 772
  0.7 8.8 %copy-start.19 = (s32[32]{0:T(128)S(1)}, s32[32]{0:T(128)}, u32[]{:S(2)}) copy-start(s32[32]{0:T(128)} %param.21) | copy-start | bytes 388
  0.7 8.9 %copy-start.18 = (s32[32]{0:T(128)S(1)}, s32[32]{0:T(128)}, u32[]{:S(2)}) copy-start(s32[32]{0:T(128)} %param.20) | copy-start | bytes 388
  3.1 12.0 %collective-permute-start = (bf16[32,3712]{1,0:T(8,128)(2,1)}, bf16[32,3712]{1,0:T(8,128)(2,1)}, u32[]{:S(2)}, u32[]{:S(2)}) collective-permute-start(bf16[32,3712]{1,0:T(8,128)(2,1)} %fusion.1.refs_0_), channel_id=1, source_target_pairs={{0,8},{8,16},{16,24},{24,32},{32,40},{40,48},{48,56},{56,0},{1,9},... | collective-permute-start | bytes 712712 | tf_op jit(solution)/shard_map/ppermute | solution.py:407
  5.0 10.1 %collective-permute-start.4 = (bf16[32,3712]{1,0:T(8,128)(2,1)}, bf16[32,3712]{1,0:T(8,128)(2,1)}, u32[]{:S(2)}, u32[]{:S(2)}) collective-permute-start(bf16[32,3712]{1,0:T(8,128)(2,1)} %fusion.1.refs_0_), channel_id=1, source_target_pairs={{0,56},{8,0},{16,8},{24,16},{32,24},{40,32},{48,40},{56,48},{1,57}... | collective-permute-start | bytes 712712 | tf_op jit(solution)/shard_map/ppermute | solution.py:407
  8.3 29.4 %collective-permute-start.11 = (bf16[256,1792]{1,0:T(8,128)(2,1)}, bf16[256,1792]{1,0:T(8,128)(2,1)S(1)}, u32[]{:S(2)}, u32[]{:S(2)}) collective-permute-start(bf16[256,1792]{1,0:T(8,128)(2,1)} %scale_down.2), channel_id=1, source_target_pairs={{0,1},{1,0},{2,3},{3,2},{4,5},{5,4},{6,7},{7,6},{8,9},{9,8},{10,11... | collective-permute-start | bytes 2752520 | tf_op jit(solution)/shard_map/ppermute | solution.py:403
  19.6 10.6 %copy-start.20 = (bf16[1,28,2]{1,2,0:T(2,128)(2,1)S(1)}, bf16[1,28,2]{1,2,0:T(2,128)(2,1)}, u32[]{:S(2)}) copy-start(bf16[1,28,2]{1,2,0:T(2,128)(2,1)} %param.30) | copy-start | bytes 340
  19.6 10.6 %copy-start.21 = (bf16[1,28,2]{1,2,0:T(2,128)(2,1)S(1)}, bf16[1,28,2]{1,2,0:T(2,128)(2,1)}, u32[]{:S(2)}) copy-start(bf16[1,28,2]{1,2,0:T(2,128)(2,1)} %param.28) | copy-start | bytes 340
  19.6 42.9 %all-to-all-start = ((bf16[8,8,32,640]{3,2,1,0:T(8,128)(2,1)}), bf16[8,8,32,640]{3,2,1,0:T(8,128)(2,1)}, u32[]{:S(2)}, u32[]{:S(2)}) async-start(bf16[8,8,32,640]{3,2,1,0:T(8,128)(2,1)} %bitcast.28), calls=%async_computation | async-start | bytes 5242880 | tf_op jit(solution)/shard_map/all_to_all | solution.py:457
  27.1 7.3 %collective-permute-start.1 = (bf16[32,3712]{1,0:T(8,128)(2,1)}, bf16[32,3712]{1,0:T(8,128)(2,1)S(1)}, u32[]{:S(2)}, u32[]{:S(2)}) collective-permute-start(bf16[32,3712]{1,0:T(8,128)(2,1)} %collective-permute-done.refs_1_.refs_0_), channel_id=1, source_target_pairs={{0,8},{8,16},{16,24},{24,32},{32,40},{40,48},{48,56},{56,0},{1,9},... | collective-permute-start | bytes 712712 | tf_op jit(solution)/shard_map/ppermute | solution.py:407
  30.2 7.5 %collective-permute-start.5 = (bf16[32,3712]{1,0:T(8,128)(2,1)}, bf16[32,3712]{1,0:T(8,128)(2,1)S(1)}, u32[]{:S(2)}, u32[]{:S(2)}) collective-permute-start(bf16[32,3712]{1,0:T(8,128)(2,1)} %collective-permute-done.4.refs_5_.refs_1_), channel_id=1, source_target_pairs={{0,56},{8,0},{16,8},{24,16},{32,24},{40,32},{48,40},{56,48},{1,57}... | collective-permute-start | bytes 712712 | tf_op jit(solution)/shard_map/ppermute | solution.py:407
  32.8 25.8 %collective-permute-start.10 = (bf16[3584,256]{1,0:T(8,128)(2,1)S(1)}, bf16[3584,256]{1,0:T(8,128)(2,1)S(1)}, u32[]{:S(2)}, u32[]{:S(2)}) collective-permute-start(bf16[3584,256]{1,0:T(8,128)(2,1)S(1)} %scale_wide.2.refs_4_), channel_id=1, source_target_pairs={{0,128},{128,0},{1,129},{129,1},{2,130},{130,2},{3,131},{131,3},{4... | collective-permute-start | bytes 5505032 | tf_op jit(solution)/shard_map/ppermute | solution.py:403
  40.8 17.8 %collective-permute-start.12 = (bf16[3584,256]{1,0:T(8,128)(2,1)S(1)}, bf16[3584,256]{1,0:T(8,128)(2,1)S(1)}, u32[]{:S(2)}, u32[]{:S(2)}) collective-permute-start(bf16[3584,256]{1,0:T(8,128)(2,1)S(1)} %scale_wide.3.refs_6_), channel_id=1, source_target_pairs={{0,128},{128,0},{1,129},{129,1},{2,130},{130,2},{3,131},{131,3},{4... | collective-permute-start | bytes 5505032 | tf_op jit(solution)/shard_map/ppermute | solution.py:403
  40.9 1.3 copy-start.1
  42.2 8.9 %collective-permute-start.2 = (bf16[32,3712]{1,0:T(8,128)(2,1)S(1)}, bf16[32,3712]{1,0:T(8,128)(2,1)S(1)}, u32[]{:S(2)}, u32[]{:S(2)}) collective-permute-start(bf16[32,3712]{1,0:T(8,128)(2,1)S(1)} %collective-permute-done.1.refs_2_.refs_0_), channel_id=1, source_target_pairs={{0,8},{8,16},{16,24},{24,32},{32,40},{40,48},{48,56},{56,0},{1,9},... | collective-permute-start | bytes 712712 | tf_op jit(solution)/shard_map/ppermute | solution.py:407
  45.4 8.9 %collective-permute-start.6 = (bf16[32,3712]{1,0:T(8,128)(2,1)S(1)}, bf16[32,3712]{1,0:T(8,128)(2,1)S(1)}, u32[]{:S(2)}, u32[]{:S(2)}) collective-permute-start(bf16[32,3712]{1,0:T(8,128)(2,1)S(1)} %collective-permute-done.5.refs_6_.refs_1_), channel_id=1, source_target_pairs={{0,56},{8,0},{16,8},{24,16},{32,24},{40,32},{48,40},{56,48},{1,57}... | collective-permute-start | bytes 712712 | tf_op jit(solution)/shard_map/ppermute | solution.py:407
  51.1 7.5 %collective-permute-start.3 = (bf16[32,3712]{1,0:T(8,128)(2,1)S(1)}, bf16[32,3712]{1,0:T(8,128)(2,1)S(1)}, u32[]{:S(2)}, u32[]{:S(2)}) collective-permute-start(bf16[32,3712]{1,0:T(8,128)(2,1)S(1)} %collective-permute-done.2.refs_3_), channel_id=1, source_target_pairs={{0,8},{8,16},{16,24},{24,32},{32,40},{40,48},{48,56},{56,0},{1,9},... | collective-permute-start | bytes 712712 | tf_op jit(solution)/shard_map/ppermute | solution.py:407
  53.6 0.7 copy-start.9
  59.2 1.3 copy-start.3
  60.4 1.3 copy-start.5
  61.7 0.7 copy-start.7
  66.0 88.4 %all-to-all-start.1 = ((bf16[8,8,32,640]{3,2,1,0:T(8,128)(2,1)}), bf16[8,8,32,640]{3,2,1,0:T(8,128)(2,1)}, u32[]{:S(2)}, u32[]{:S(2)}) async-start(bf16[8,8,32,640]{3,2,1,0:T(8,128)(2,1)} %regroup.1), calls=%async_computation.1 | async-start | bytes 5242880 | tf_op jit(solution)/shard_map/all_to_all | solution.py:479
  74.5 0.9 copy-start.8
  75.5 0.9 copy-start.10
  76.4 48.3 %copy-start.4 = (bf16[3584,256]{1,0:T(8,128)(2,1)S(1)}, bf16[3584,256]{1,0:T(8,128)(2,1)}, u32[]{:S(2)}) copy-start(bf16[3584,256]{1,0:T(8,128)(2,1)} %copy-done.3) | copy-start | bytes 5505028
  76.4 48.3 %copy-start.6 = (bf16[3584,256]{1,0:T(8,128)(2,1)S(1)}, bf16[3584,256]{1,0:T(8,128)(2,1)}, u32[]{:S(2)}) copy-start(bf16[3584,256]{1,0:T(8,128)(2,1)} %copy-done.5) | copy-start | bytes 5505028
  80.5 44.2 %copy-start.2 = (bf16[3584,256]{1,0:T(8,128)(2,1)S(1)}, bf16[3584,256]{1,0:T(8,128)(2,1)}, u32[]{:S(2)}) copy-start(bf16[3584,256]{1,0:T(8,128)(2,1)} %copy-done.1) | copy-start | bytes 5505028
  80.5 22.6 %collective-permute-start.14 = (bf16[64,3584]{1,0:T(8,128)(2,1)S(1)}, bf16[64,3584]{1,0:T(8,128)(2,1)S(1)}, u32[]{:S(2)}, u32[]{:S(2)}) collective-permute-start(bf16[64,3584]{1,0:T(8,128)(2,1)S(1)} %get-tuple-element.24), channel_id=1, source_target_pairs={{0,4},{2,6},{4,0},{6,2},{64,68},{66,70},{68,64},{70,66},{1,5},{3,7... | collective-permute-start | bytes 1376264 | tf_op jit(solution)/shard_map/ppermute | solution.py:411
  83.5 19.5 %collective-permute-start.15 = (bf16[64,3584]{1,0:T(8,128)(2,1)S(1)}, bf16[64,3584]{1,0:T(8,128)(2,1)S(1)}, u32[]{:S(2)}, u32[]{:S(2)}) collective-permute-start(bf16[64,3584]{1,0:T(8,128)(2,1)S(1)} %get-tuple-element.25), channel_id=1, source_target_pairs={{0,68},{2,70},{4,64},{6,66},{64,4},{66,6},{68,0},{70,2},{1,69},{3,... | collective-permute-start | bytes 1376264 | tf_op jit(solution)/shard_map/ppermute | solution.py:411
  83.8 38.8 %collective-permute-start.16 = (bf16[64,3584]{1,0:T(8,128)(2,1)S(1)}, bf16[64,3584]{1,0:T(8,128)(2,1)S(1)}, u32[]{:S(2)}, u32[]{:S(2)}) collective-permute-start(bf16[64,3584]{1,0:T(8,128)(2,1)S(1)} %get-tuple-element.26), channel_id=1, source_target_pairs={{0,6},{2,0},{4,2},{6,4},{64,70},{66,64},{68,66},{70,68},{1,7},{3,1... | collective-permute-start | bytes 1376264 | tf_op jit(solution)/shard_map/ppermute | solution.py:411
  86.7 36.5 %collective-permute-start.17 = (bf16[64,3584]{1,0:T(8,128)(2,1)S(1)}, bf16[64,3584]{1,0:T(8,128)(2,1)S(1)}, u32[]{:S(2)}, u32[]{:S(2)}) collective-permute-start(bf16[64,3584]{1,0:T(8,128)(2,1)S(1)} %get-tuple-element.27), channel_id=1, source_target_pairs={{0,70},{2,64},{4,66},{6,68},{64,6},{66,0},{68,2},{70,4},{1,71},{3,... | collective-permute-start | bytes 1376264 | tf_op jit(solution)/shard_map/ppermute | solution.py:411
  90.0 53.8 %collective-permute-start.20 = (bf16[256,1792]{1,0:T(8,128)(2,1)S(1)}, bf16[256,1792]{1,0:T(8,128)(2,1)S(1)}, u32[]{:S(2)}, u32[]{:S(2)}) collective-permute-start(bf16[256,1792]{1,0:T(8,128)(2,1)S(1)} %collective-permute-done.11.refs_2_.w2), channel_id=1, source_target_pairs={{0,128},{128,0},{1,129},{129,1},{2,130},{130,2},{3,131},{131,3},{4... | collective-permute-start | bytes 2752520 | tf_op jit(solution)/shard_map/ppermute | solution.py:403
  103.0 40.8 %collective-permute-start.19 = (bf16[256,1792]{1,0:T(8,128)(2,1)S(1)}, bf16[256,1792]{1,0:T(8,128)(2,1)S(1)}, u32[]{:S(2)}, u32[]{:S(2)}) collective-permute-start(bf16[256,1792]{1,0:T(8,128)(2,1)S(1)} %scale_down.3.w0), channel_id=1, source_target_pairs={{0,128},{128,0},{1,129},{129,1},{2,130},{130,2},{3,131},{131,3},{4... | collective-permute-start | bytes 2752520 | tf_op jit(solution)/shard_map/ppermute | solution.py:403
  103.0 26.2 %collective-permute-start.9 = (bf16[64,3584]{1,0:T(8,128)(2,1)S(1)}, bf16[64,3584]{1,0:T(8,128)(2,1)S(1)}, u32[]{:S(2)}, u32[]{:S(2)}) collective-permute-start(bf16[64,3584]{1,0:T(8,128)(2,1)S(1)} %get-tuple-element.23.refs_0_), channel_id=1, source_target_pairs={{0,66},{2,68},{4,70},{6,64},{64,2},{66,4},{68,6},{70,0},{1,67},{3,... | collective-permute-start | bytes 1376264 | tf_op jit(solution)/shard_map/ppermute | solution.py:411
  122.6 18.1 %collective-permute-start.7 = (bf16[64,3584]{1,0:T(8,128)(2,1)S(1)}, bf16[64,3584]{1,0:T(8,128)(2,1)S(1)}, u32[]{:S(2)}, u32[]{:S(2)}) collective-permute-start(bf16[64,3584]{1,0:T(8,128)(2,1)S(1)} %get-tuple-element.21), channel_id=1, source_target_pairs={{0,64},{2,66},{4,68},{6,70},{64,0},{66,2},{68,4},{70,6},{1,65},{3,... | collective-permute-start | bytes 1376264 | tf_op jit(solution)/shard_map/ppermute | solution.py:411
  123.3 17.5 %collective-permute-start.8 = (bf16[64,3584]{1,0:T(8,128)(2,1)S(1)}, bf16[64,3584]{1,0:T(8,128)(2,1)S(1)}, u32[]{:S(2)}, u32[]{:S(2)}) collective-permute-start(bf16[64,3584]{1,0:T(8,128)(2,1)S(1)} %get-tuple-element.22), channel_id=1, source_target_pairs={{0,2},{2,4},{4,6},{6,0},{64,66},{66,68},{68,70},{70,64},{1,3},{3,5... | collective-permute-start | bytes 1376264 | tf_op jit(solution)/shard_map/ppermute | solution.py:411
  129.2 14.7 %collective-permute-start.18 = (bf16[256,512]{1,0:T(8,128)(2,1)S(1)}, bf16[256,512]{1,0:T(8,128)(2,1)S(1)}, u32[]{:S(2)}, u32[]{:S(2)}) collective-permute-start(bf16[256,512]{1,0:T(8,128)(2,1)S(1)} %hidden_units.3.b0), channel_id=1, source_target_pairs={{0,1},{1,0},{2,3},{3,2},{4,5},{5,4},{6,7},{7,6},{8,9},{9,8},{10,11... | collective-permute-start | bytes 786440 | tf_op jit(solution)/shard_map/ppermute | solution.py:403
  140.8 3.0 %copy-start.14 = (s32[64]{0:T(128)S(1)}, s32[64]{0:T(128)}, u32[]{:S(2)}) copy-start(s32[64]{0:T(128)} %constant.114) | copy-start | bytes 772
  140.8 3.0 %copy-start.15 = (s32[64]{0:T(128)S(1)}, s32[64]{0:T(128)}, u32[]{:S(2)}) copy-start(s32[64]{0:T(128)} %constant.115) | copy-start | bytes 772
  140.8 3.0 %copy-start.16 = (s32[64]{0:T(128)S(1)}, s32[64]{0:T(128)}, u32[]{:S(2)}) copy-start(s32[64]{0:T(128)} %constant.116) | copy-start | bytes 772
  142.9 7.6 %collective-permute-start.13 = (bf16[256,512]{1,0:T(8,128)(2,1)S(1)}, bf16[256,512]{1,0:T(8,128)(2,1)S(1)}, u32[]{:S(2)}, u32[]{:S(2)}) collective-permute-start(bf16[256,512]{1,0:T(8,128)(2,1)S(1)} %hidden_units.2.a0), channel_id=1, source_target_pairs={{0,1},{1,0},{2,3},{3,2},{4,5},{5,4},{6,7},{7,6},{8,9},{9,8},{10,11... | collective-permute-start | bytes 786440 | tf_op jit(solution)/shard_map/ppermute | solution.py:403
  154.4 55.1 %all-to-all-start.2 = ((bf16[64,8,1792]{2,1,0:T(8,128)(2,1)}), bf16[64,8,1792]{2,1,0:T(8,128)(2,1)S(1)}, u32[]{:S(2)}, u32[]{:S(2)}) async-start(bf16[64,8,1792]{2,1,0:T(8,128)(2,1)} %down_rows.1.refs_0_), calls=%async_computation.2 | async-start | bytes 3670016 | tf_op jit(solution)/shard_map/all_to_all | solution.py:495
  167.2 7.2 %copy-start.12 = (s32[32,8]{0,1:T(8,128)S(1)}, s32[32,8]{0,1:T(8,128)}, u32[]{:S(2)}) copy-start(s32[32,8]{0,1:T(8,128)} %param.25) | copy-start | bytes 3076
  167.7 6.8 %copy-start.11 = (bf16[32,576]{1,0:T(8,128)(2,1)S(1)}, bf16[32,576]{1,0:T(8,128)(2,1)}, u32[]{:S(2)}) copy-start(bf16[32,576]{1,0:T(8,128)(2,1)} %param.23) | copy-start | bytes 110596
  167.7 6.8 %copy-start.13 = (f32[32,8]{0,1:T(8,128)S(1)}, f32[32,8]{0,1:T(8,128)}, u32[]{:S(2)}) copy-start(f32[32,8]{0,1:T(8,128)} %param.26) | copy-start | bytes 3076
  172.4 32.2 %collective-permute-start.21 = (bf16[16,32,640]{2,1,0:T(8,128)(2,1)S(1)}, bf16[16,32,640]{2,1,0:T(8,128)(2,1)S(1)}, u32[]{:S(2)}, u32[]{:S(2)}) collective-permute-start(bf16[16,32,640]{2,1,0:T(8,128)(2,1)S(1)} %get-tuple-element.28.mine), channel_id=1, source_target_pairs={{0,1},{1,0},{2,3},{3,2},{4,5},{5,4},{6,7},{7,6},{8,9},{9,8},{10,11... | collective-permute-start | bytes 1966088 | tf_op jit(solution)/shard_map/ppermute | solution.py:403
  173.2 45.1 %collective-permute-start.22 = (bf16[16,32,640]{2,1,0:T(8,128)(2,1)}, bf16[16,32,640]{2,1,0:T(8,128)(2,1)}, u32[]{:S(2)}, u32[]{:S(2)}) collective-permute-start(bf16[16,32,640]{2,1,0:T(8,128)(2,1)} %get-tuple-element.31.mine), channel_id=1, source_target_pairs={{0,1},{1,0},{2,3},{3,2},{4,5},{5,4},{6,7},{7,6},{8,9},{9,8},{10,11... | collective-permute-start | bytes 1966088 | tf_op jit(solution)/shard_map/ppermute | solution.py:403

commit v7 on v6

--- a/solution.py
+++ b/solution.py
@@ -150,41 +150,36 @@
     )(place, *blocks)
 
 
-PEER_ORDER = (0, 4, 1, 5, 2, 6, 3, 7)
+PEER_ORDER = (4, 1, 5, 2, 6, 3, 7, 0)
 
 
 def hidden_kernel(*refs):
-    tokens, (g0, g1, u0, u1, out, x) = refs[:4], refs[4:]
-    for n, token in enumerate(tokens):
-        x[n * 64 : (n + 1) * 64, :] = token[...]
-    for n, (gate, up) in enumerate(((g0, u0), (g1, u1))):
-        g = jnp.dot(x[...], gate[...], preferred_element_type=F32)
-        u = jnp.dot(x[...], up[...], preferred_element_type=F32)
-        out[:, n * 256 : (n + 1) * 256] = (g / (1.0 + jnp.exp(-g)) * u).astype(BF16)
-
-
-def hidden_units(tokens, panels):
+    tokens, (gate, up, out, x) = refs[:8], refs[8:]
+    for r, token in zip(PEER_ORDER, tokens):
+        x[r * 64 : (r + 1) * 64, :] = token[...]
+    for half in range(2):
+        rows = slice(half * 256, (half + 1) * 256)
+        g = jnp.dot(x[rows, :], gate[...], preferred_element_type=F32)
+        u = jnp.dot(x[rows, :], up[...], preferred_element_type=F32)
+        out[rows, :] = (g / (1.0 + jnp.exp(-g)) * u).astype(BF16)
+
+
+def hidden_units(tokens, gate, up):
     vmem = pl.BlockSpec(memory_space=pltpu.VMEM)
     return pl.pallas_call(
         hidden_kernel,
-        in_specs=[vmem] * 8,
+        in_specs=[vmem] * 10,
         out_specs=vmem,
-        out_shape=jax.ShapeDtypeStruct((256, 512), BF16),
-        scratch_shapes=[pltpu.VMEM((256, D), BF16)],
-        compiler_params=params(8),
+        out_shape=jax.ShapeDtypeStruct((512, 256), BF16),
+        scratch_shapes=[pltpu.VMEM((512, D), BF16)],
+        compiler_params=params(10),
         cost_estimate=cost(1.9e9, 8e6),
         name="hidden_units",
-    )(*tokens, *panels)
-
-
-def down_kernel(order_ref, a0, a1, b0, b1, w0, w1, w2, w3, out):
-    h = jnp.concatenate(
-        [
-            jnp.concatenate([a0[...], a1[...]], axis=1),
-            jnp.concatenate([b0[...], b1[...]], axis=1),
-        ],
-        axis=0,
-    )
+    )(*[tokens[r] for r in PEER_ORDER], gate, up)
+
+
+def down_kernel(order_ref, h0, h1, h2, h3, w0, w1, w2, w3, out):
+    h = jnp.concatenate([part[...] for part in (h0, h1, h2, h3)], axis=1)
     for c in range(HALF_D // 256):
         cols = slice(c * 256, (c + 1) * 256)
         w = jnp.concatenate([p[:, cols] for p in (w0, w1, w2, w3)], axis=0)
@@ -470,7 +465,7 @@
     )
     picked = pick_rows(place, up_way + down_way[1:])
     tokens = list(picked)
-    for peer in PEER_ORDER[1:]:
+    for peer in PEER_ORDER[:7]:
         tokens[peer] = plane_shift(picked[peer], peer // NY, peer % NY)
 
     down_keep = scale_down(tp_index, down_value, down_scale, once(picked[5]))
@@ -478,18 +473,15 @@
 
     arrived = lax.all_to_all(midway, "z", split_axis=0, concat_axis=0, tiled=True)
 
-    panels = (gate, gate_far, up, up_far)
-    act = hidden_units([tokens[peer] for peer in PEER_ORDER[:4]], panels)
-    act_tp = swap(act, "tp")
-    act_late = hidden_units([tokens[peer] for peer in PEER_ORDER[4:]], panels)
-    act_late_tp = swap(act_late, "tp")
-    peer = jnp.asarray(np.repeat(np.array(PEER_ORDER, np.int32), 8))
+    act, act_far = hidden_units(tokens, gate, up), hidden_units(tokens, gate_far, up_far)
+    act_tp, act_tp_far = swap(act, "tp"), swap(act_far, "tp")
+    group = jnp.arange(EP, dtype=I32)
     order = (
-        ((xh + (peer >> 2)) % NX) * NZ + (z - jnp.asarray(np.tile(behind, 8))) % NZ
-    ) * NY + (y - peer) % NY
+        ((xh + (group >> 5)) % NX) * NZ + (z - jnp.tile(jnp.asarray(behind), 8)) % NZ
+    ) * NY + (y - (group >> 3)) % NY
     out_rows = down_rows(
         order,
-        [act, act_tp, act_late, act_late_tp],
+        [act, act_far, act_tp, act_tp_far],
         [down_keep, down_far, down_tp, down_tp_far],
     )
     returned = lax.all_to_all(

time: 223 us -> 212 us (0.951)
  waiting for transfers between devices: 88.1 us -> 79.9 us
  starting transfers between devices: 69.9 us -> 64.7 us
    ppermute x7, waiting for transfers between devices: 29.4 us -> 22.9 us  [plane_shift(): lax.ppermute(x, ('xh', 'y'), [(a * NY + b, (a + dx) % NX * NY + (b + dy)...]
    ppermute x7, starting transfers between devices: 25.3 us -> 19.8 us  [plane_shift(): lax.ppermute(x, ('xh', 'y'), [(a * NY + b, (a + dx) % NX * NY + (b + dy)...]
    unnamed x47 -> x43, local copies, waits for them, and re-layouts: 11.2 us -> 11.2 us
  transfers between devices with their start and end apart: 26 -> 26, of which waited for: 12 -> 12; matrix products, arithmetic and copies ran while one was open for 4% -> 4% of each run, Pallas kernels for 17% -> 19%
where the time goes in v7:
time: 212 us; the launch traced here: 211 us
  waiting for transfers between devices  79.9 us (38%)
  starting transfers between devices  64.7 us (31%)
  Pallas kernels  47.7 us (22%)
  local copies, waits for them, and re-layouts  12.3 us (6%)
  other arithmetic  5.24 us (2%)
    ppermute x9, waiting for transfers between devices, swap(): return lax.ppermute(x, axis, [(0, 1), (1, 0)])  42.2 us
    ppermute x7, waiting for transfers between devices, plane_shift(): lax.ppermute(x, ('xh', 'y'), [(a * NY + b, (a + dx) % NX * NY + (b + dy)...  22.9 us
    ppermute x7, starting transfers between devices, plane_shift(): lax.ppermute(x, ('xh', 'y'), [(a * NY + b, (a + dx) % NX * NY + (b + dy)...  19.8 us
    ppermute x7, waiting for transfers between devices, z_shift(): return lax.ppermute(x, 'z', [(i, (i + by) % NZ) for i in range(NZ)])  14.8 us
    all_to_all x1, starting transfers between devices, on_device(): lax.all_to_all(out_rows, ('xh', 'z', 'y'), split_axis=0, concat_axis=0, t...  12.5 us
    unnamed x43, local copies, waits for them, and re-layouts  11.2 us
    ppermute x7, starting transfers between devices, z_shift(): return lax.ppermute(x, 'z', [(i, (i + by) % NZ) for i in range(NZ)])  10.8 us
    all_to_all x1, starting transfers between devices, on_device(): lax.all_to_all(midway, 'z', split_axis=0, concat_axis=0, tiled=True)  8.45 us
  transfers between devices with their start and end apart: 26, of which 12 were waited for; matrix products, arithmetic and copies ran while one was open for 4% of the time, Pallas kernels for 19%

profile of v7, /device:TPU:68, one launch (start us, length us, event | category | flops | bytes accessed | tf_op | source)
XLA Modules:
  0.0 210.8 jit_solution(5923225745144383682)
XLA Ops:
  0.7 0.7 convert_element_type.38
  1.5 1.7 fusion.1.refs_0_
  3.1 1.9 collective-permute-start
  5.2 0.7 bitcast_convert_fusion.scale
  5.8 2.5 %scale_down.2 = bf16[256,1792]{1,0:T(8,128)(2,1)} custom-call(s32[1]{0:T(128)S(6)} %sub.38.half_ref, f32[2,28]{1,0:T(2,128)S(1)} %bitcast_convert_fusion.scale, bf16[1,256,3584]{2,1,0:T(8,128)(2,1)} %value.7), custom_call_target="tpu_custom_call" | custom-call | flops 1000000 | bytes 2000000 | tf_op jit(solution)/shard_map/scale_down/pallas_call | solution.py:90
  8.3 1.2 collective-permute-start.14
  9.7 0.7 copy.45
  10.5 3.9 %copy.47.pages = bf16[128,16,576]{2,1,0:T(8,128)(2,1)S(1)} copy(bf16[128,16,576]{0,2,1:T(8,128)(2,1)} %param.17) | data formatting | bytes 4718592 | tf_op args[0]
  14.4 0.8 broadcast_subtract_fusion.index_ref
  15.1 0.5 once.5.rest_0_
  15.7 3.9 %collect.1 = bf16[64,32,640]{2,1,0:T(8,128)(2,1)} custom-call(s32[64,4]{1,0:T(8,128)S(1)} %broadcast_subtract_fusion.index_ref, bf16[128,16,576]{2,1,0:T(8,128)(2,1)S(1)} %copy.47.pages, f32[1]{0:T(128)} %once.5.rest_0_), custom_call_target="tpu_custom_call" | custom-call | flops 1000000 | bytes 6000000 | tf_op jit(solution)/shard_map/collect/pallas_call | solution.py:260
  19.6 7.6 %all-to-all-start = ((bf16[8,8,32,640]{3,2,1,0:T(8,128)(2,1)}), bf16[8,8,32,640]{3,2,1,0:T(8,128)(2,1)}, u32[]{:S(2)}, u32[]{:S(2)}) async-start(bf16[8,8,32,640]{3,2,1,0:T(8,128)(2,1)} %bitcast.28), calls=%async_computation | async-start | bytes 5242880 | tf_op jit(solution)/shard_map/all_to_all | solution.py:452
  27.2 3.0 %collective-permute-start.1 = (bf16[32,3712]{1,0:T(8,128)(2,1)}, bf16[32,3712]{1,0:T(8,128)(2,1)S(1)}, u32[]{:S(2)}, u32[]{:S(2)}) collective-permute-start(bf16[32,3712]{1,0:T(8,128)(2,1)} %collective-permute-done.refs_1_.refs_0_), channel_id=1, source_target_pairs={{0,8},{8,16},{16,24},{24,32},{32,40},{40,48},{48,56},{56,0},{1,9},... | collective-permute-start | bytes 712712 | tf_op jit(solution)/shard_map/ppermute | solution.py:402
  30.2 2.6 %scale_wide.2.refs_8_ = bf16[3584,256]{1,0:T(8,128)(2,1)S(1)} custom-call(f32[2,28]{1,0:T(2,128)S(1)} %convert_bitcast_fusion.1.scale, bf16[1,3584,256]{2,1,0:T(8,128)(2,1)} %value.4, f32[1]{0:T(128)} %once.5.rest_0_), custom_call_target="tpu_custom_call" | custom-call | flops 1000000 | bytes 4000000 | tf_op jit(solution)/shard_map/scale_wide/pallas_call | solution.py:66
  32.9 1.5 collective-permute-done.1.refs_2_.refs_0_
  34.4 3.3 %collective-permute-done.5.refs_6_.refs_1_ = bf16[32,3712]{1,0:T(8,128)(2,1)S(1)} collective-permute-done((bf16[32,3712]{1,0:T(8,128)(2,1)}, bf16[32,3712]{1,0:T(8,128)(2,1)S(1)}, u32[]{:S(2)}, u32[]{:S(2)}) %collective-permute-start.5) | collective-permute-done | bytes 237600 | tf_op jit(solution)/shard_map/ppermute | solution.py:402
  37.7 0.5 once.6.rest_0_
  38.2 2.6 %scale_wide.3.refs_9_ = bf16[3584,256]{1,0:T(8,128)(2,1)S(1)} custom-call(f32[2,28]{1,0:T(2,128)S(1)} %convert_bitcast_fusion.scale, bf16[1,3584,256]{2,1,0:T(8,128)(2,1)} %value.6, f32[1]{0:T(128)} %once.6.rest_0_), custom_call_target="tpu_custom_call" | custom-call | flops 1000000 | bytes 4000000 | tf_op jit(solution)/shard_map/scale_wide/pallas_call | solution.py:66
  41.0 1.3 copy-done.1
  42.2 3.2 %collective-permute-start.2 = (bf16[32,3712]{1,0:T(8,128)(2,1)S(1)}, bf16[32,3712]{1,0:T(8,128)(2,1)S(1)}, u32[]{:S(2)}, u32[]{:S(2)}) collective-permute-start(bf16[32,3712]{1,0:T(8,128)(2,1)S(1)} %collective-permute-done.1.refs_2_.refs_0_), channel_id=1, source_target_pairs={{0,8},{8,16},{16,24},{24,32},{32,40},{40,48},{48,56},{56,0},{1,9},... | collective-permute-start | bytes 712712 | tf_op jit(solution)/shard_map/ppermute | solution.py:402
  45.5 5.7 %collective-permute-done.2.refs_3_ = bf16[32,3712]{1,0:T(8,128)(2,1)S(1)} collective-permute-done((bf16[32,3712]{1,0:T(8,128)(2,1)S(1)}, bf16[32,3712]{1,0:T(8,128)(2,1)S(1)}, u32[]{:S(2)}, u32[]{:S(2)}) %collective-permute-start.2) | collective-permute-done | bytes 237600 | tf_op jit(solution)/shard_map/ppermute | solution.py:402
  51.2 2.5 %collective-permute-start.3 = (bf16[32,3712]{1,0:T(8,128)(2,1)S(1)}, bf16[32,3712]{1,0:T(8,128)(2,1)S(1)}, u32[]{:S(2)}, u32[]{:S(2)}) collective-permute-start(bf16[32,3712]{1,0:T(8,128)(2,1)S(1)} %collective-permute-done.2.refs_3_), channel_id=1, source_target_pairs={{0,8},{8,16},{16,24},{24,32},{32,40},{40,48},{48,56},{56,0},{1,9},... | collective-permute-start | bytes 712712 | tf_op jit(solution)/shard_map/ppermute | solution.py:402
  53.6 0.7 copy-done.9
  54.3 4.3 %collective-permute-done.3.refs_4_.refs_0_ = bf16[32,3712]{1,0:T(8,128)(2,1)S(1)} collective-permute-done((bf16[32,3712]{1,0:T(8,128)(2,1)S(1)}, bf16[32,3712]{1,0:T(8,128)(2,1)S(1)}, u32[]{:S(2)}, u32[]{:S(2)}) %collective-permute-start.3) | collective-permute-done | bytes 237600 | tf_op jit(solution)/shard_map/ppermute | solution.py:402
  58.7 0.5 once.9.rest_0_
  59.2 1.3 copy-done.3
  60.5 1.3 copy-done.5
  61.8 0.7 copy-done.7
  62.5 3.6 %regroup.1 = bf16[8,8,32,640]{3,2,1,0:T(8,128)(2,1)} custom-call(bf16[8,8,32,640]{3,2,1,0:T(8,128)(2,1)} %all-to-all-done.midway, f32[1]{0:T(128)} %once.9.rest_0_), custom_call_target="tpu_custom_call" | custom-call | flops 1000000 | bytes 6000000 | tf_op jit(solution)/shard_map/regroup/pallas_call | solution.py:279
  66.0 8.4 %all-to-all-start.1 = ((bf16[8,8,32,640]{3,2,1,0:T(8,128)(2,1)}), bf16[8,8,32,640]{3,2,1,0:T(8,128)(2,1)}, u32[]{:S(2)}, u32[]{:S(2)}) async-start(bf16[8,8,32,640]{3,2,1,0:T(8,128)(2,1)} %regroup.1), calls=%async_computation.1 | async-start | bytes 5242880 | tf_op jit(solution)/shard_map/all_to_all | solution.py:474
  74.6 0.9 copy-done.8
  75.5 0.9 copy-done.10
  76.4 3.9 %pick_rows.1 = (bf16[64,3584]{1,0:T(8,128)(2,1)S(1)}, bf16[64,3584]{1,0:T(8,128)(2,1)S(1)}, bf16[64,3584]{1,0:T(8,128)(2,1)S(1)}, bf16[64,3584]{1,0:T(8,128)(2,1...) custom-call(s32[3]{0:T(128)S(1)} %pad_add_fusion.1.place_ref, ...), custom_call_target="tpu_custom_call" | custom-call | flops 1000000000 | bytes 6000000 | tf_op jit(solution)/shard_map/pick_rows/pallas_call | solution.py:142
  80.4 2.0 collective-permute-start.8
  82.5 3.8 %collective-permute-start.9 = (bf16[64,3584]{1,0:T(8,128)(2,1)S(1)}, bf16[64,3584]{1,0:T(8,128)(2,1)S(1)}, u32[]{:S(2)}, u32[]{:S(2)}) collective-permute-start(bf16[64,3584]{1,0:T(8,128)(2,1)S(1)} %get-tuple-element.22.refs_0_), channel_id=1, source_target_pairs={{0,66},{2,68},{4,70},{6,64},{64,2},{66,4},{68,6},{70,0},{1,67},{3,... | collective-permute-start | bytes 1376264 | tf_op jit(solution)/shard_map/ppermute | solution.py:406
  86.3 1.8 collective-permute-start.10
  88.1 1.8 collective-permute-start.11
  89.8 5.5 %collective-permute-done.7.refs_0_ = bf16[64,3584]{1,0:T(8,128)(2,1)S(1)} collective-permute-done((bf16[64,3584]{1,0:T(8,128)(2,1)S(1)}, bf16[64,3584]{1,0:T(8,128)(2,1)S(1)}, u32[]{:S(2)}, u32[]{:S(2)}) %collective-permute-start.7) | collective-permute-done | bytes 458784 | tf_op jit(solution)/shard_map/ppermute | solution.py:406
  95.4 2.7 %collective-permute-start.12 = (bf16[64,3584]{1,0:T(8,128)(2,1)S(1)}, bf16[64,3584]{1,0:T(8,128)(2,1)S(1)}, u32[]{:S(2)}, u32[]{:S(2)}) collective-permute-start(bf16[64,3584]{1,0:T(8,128)(2,1)S(1)} %get-tuple-element.25), channel_id=1, source_target_pairs={{0,6},{2,0},{4,2},{6,4},{64,70},{66,64},{68,66},{70,68},{1,7},{3,1... | collective-permute-start | bytes 1376264 | tf_op jit(solution)/shard_map/ppermute | solution.py:406
  98.1 13.6 %collective-permute-done.8.refs_1_ = bf16[64,3584]{1,0:T(8,128)(2,1)S(1)} collective-permute-done((bf16[64,3584]{1,0:T(8,128)(2,1)S(1)}, bf16[64,3584]{1,0:T(8,128)(2,1)S(1)}, u32[]{:S(2)}, u32[]{:S(2)}) %collective-permute-start.8) | collective-permute-done | bytes 458784 | tf_op jit(solution)/shard_map/ppermute | solution.py:406
  111.6 7.6 %collective-permute-start.13 = (bf16[64,3584]{1,0:T(8,128)(2,1)S(1)}, bf16[64,3584]{1,0:T(8,128)(2,1)S(1)}, u32[]{:S(2)}, u32[]{:S(2)}) collective-permute-start(bf16[64,3584]{1,0:T(8,128)(2,1)S(1)} %get-tuple-element.26), channel_id=1, source_target_pairs={{0,70},{2,64},{4,66},{6,68},{64,6},{66,0},{68,2},{70,4},{1,71},{3,... | collective-permute-start | bytes 1376264 | tf_op jit(solution)/shard_map/ppermute | solution.py:406
  119.2 0.5 once.7.rest_0_
  119.7 3.1 %scale_down.3.w0 = bf16[256,1792]{1,0:T(8,128)(2,1)} custom-call(s32[1]{0:T(128)} %bitcast.7.half_ref.tp_ref, f32[2,28]{1,0:T(2,128)S(1)} %bitcast_convert_fusion.scale, bf16[1,256,3584]{2,1,0:T(8,128)(2,1)} %value.7, f32[1]{0:T(128)} %once.7.rest_0_), custom_call_target="tpu_custom_call" | custom-call | flops 1000000 | bytes 2000000 | tf_op jit(solution)/shard_map/scale_down/pallas_call | solution.py:90
  122.8 0.6 collective-permute-done.10.refs_3_
  123.5 3.1 %collective-permute-done.12.refs_5_ = bf16[64,3584]{1,0:T(8,128)(2,1)S(1)} collective-permute-done((bf16[64,3584]{1,0:T(8,128)(2,1)S(1)}, bf16[64,3584]{1,0:T(8,128)(2,1)S(1)}, u32[]{:S(2)}, u32[]{:S(2)}) %collective-permute-start.12) | collective-permute-done | bytes 458784 | tf_op jit(solution)/shard_map/ppermute | solution.py:406
  126.6 2.1 hidden_units.2.h0
  128.7 1.0 collective-permute-start.17
  129.8 2.1 hidden_units.3.h1
  131.8 1.2 collective-permute-start.18
  133.1 4.1 %collective-permute-done.17.h2 = bf16[512,256]{1,0:T(8,128)(2,1)S(1)} collective-permute-done((bf16[512,256]{1,0:T(8,128)(2,1)S(1)}, bf16[512,256]{1,0:T(8,128)(2,1)S(1)}, u32[]{:S(2)}, u32[]{:S(2)}) %collective-permute-start.17) | collective-permute-done | bytes 262176 | tf_op jit(solution)/shard_map/ppermute | solution.py:398
  137.2 2.8 %collective-permute-done.18.h3 = bf16[512,256]{1,0:T(8,128)(2,1)S(1)} collective-permute-done((bf16[512,256]{1,0:T(8,128)(2,1)S(1)}, bf16[512,256]{1,0:T(8,128)(2,1)S(1)}, u32[]{:S(2)}, u32[]{:S(2)}) %collective-permute-start.18) | collective-permute-done | bytes 262176 | tf_op jit(solution)/shard_map/ppermute | solution.py:398
  140.0 5.2 %down_rows.1.refs_0_ = bf16[64,8,1792]{2,1,0:T(8,128)(2,1)} custom-call(s32[64]{0:T(128)S(1)} %fusion.3.order_ref, bf16[512,256]{1,0:T(8,128)(2,1)S(1)} %hidden_units.2.h0, bf16[512,256]{1,0:T(8,128)(2,1)S(1)} %hidden_units.3.h1, bf16[512,256]{1,0:T(8,128)(2,1)S(1)} %collective-permute-done.17.h2, bf16[512,256]{1,0:T(8,128)(2,1)S(1)} %collective-permute-done.18.h3, ...), custom_call_target="tpu_custom_call" | custom-call | flops 1900000000 | bytes 7000000 | tf_op jit(solution)/shard_map/down_rows/pallas_call | solution.py:193
  145.2 12.5 %all-to-all-start.2 = ((bf16[64,8,1792]{2,1,0:T(8,128)(2,1)}), bf16[64,8,1792]{2,1,0:T(8,128)(2,1)S(1)}, u32[]{:S(2)}, u32[]{:S(2)}) async-start(bf16[64,8,1792]{2,1,0:T(8,128)(2,1)} %down_rows.1.refs_0_), calls=%async_computation.2 | async-start | bytes 3670016 | tf_op jit(solution)/shard_map/all_to_all | solution.py:487
  157.7 0.5 once.8.late_ref
  158.3 1.0 slice_convert_fusion
  159.4 0.1 select_reduce_fusion.1
  159.5 3.4 %compact.1 = (bf16[16,32,640]{2,1,0:T(8,128)(2,1)S(1)}, bf16[16,32,640]{2,1,0:T(8,128)(2,1)}) custom-call(s32[32]{0:T(128)S(1)} %get-tuple-element.37.source_ref, bf16[64,32,640]{2,1,0:T(8,128)(2,1)} %bitcast.13.arrived, f32[1]{0:T(128)} %once.8.late_ref), custom_call_target="tpu_custom_call" | custom-call | flops 1000000 | bytes 4000000 | tf_op jit(solution)/shard_map/compact/pallas_call | solution.py:299
  162.9 1.0 collective-permute-start.21
  163.9 1.1 collective-permute-start.22
  165.1 30.3 %collective-permute-done.21.other = bf16[16,32,640]{2,1,0:T(8,128)(2,1)S(1)} collective-permute-done((bf16[16,32,640]{2,1,0:T(8,128)(2,1)S(1)}, bf16[16,32,640]{2,1,0:T(8,128)(2,1)S(1)}, u32[]{:S(2)}, u32[]{:S(2)}) %collective-permute-start.21) | collective-permute-done | bytes 655392 | tf_op jit(solution)/shard_map/ppermute | solution.py:398
  195.4 3.7 %attend.2 = (bf16[32,64,576]{2,1,0:T(8,128)(2,1)}, bf16[32,32,512]{2,1,0:T(8,128)(2,1)}, f32[1]{0:T(128)}) custom-call(f32[1]{0:T(128)} %once.8.late_ref, s32[1]{0:T(128)} %bitcast.7.half_ref.tp_ref, s32[32]{0:T(128)S(1)} %get-tuple-element.38.length_ref, bf16[16,32,640]{2,1,0:T(8,128)(2,1)S(1)} %get-tuple-element.28.mine, ...), custom_call_target="tpu_custom_call" | custom-call | flops 100000000 | bytes 4000000 | tf_op jit(solution)/shard_map/attend/pallas_call | solution.py:351
  199.2 2.7 %blend.1 = (bf16[32,1792]{1,0:T(8,128)(2,1)}, f32[1]{0:T(128)}) custom-call(f32[1]{0:T(128)} %get-tuple-element.29.late_ref, s32[32,8]{1,0:T(8,128)S(1)} %copy.50.routing_ref, f32[32,8]{1,0:T(8,128)S(1)} %copy.51.weight_ref, bf16[64,8,1792]{2,1,0:T(8,128)(2,1)S(1)} %all-to-all-done.2.rows_ref), custom_call_target="tpu_custom_call" | custom-call | flops 100000000 | bytes 2000000 | tf_op jit(solution)/shard_map/blend/pallas_call | solution.py:227
  201.9 5.0 %collective-permute-done.22.other = bf16[16,32,640]{2,1,0:T(8,128)(2,1)} collective-permute-done((bf16[16,32,640]{2,1,0:T(8,128)(2,1)}, bf16[16,32,640]{2,1,0:T(8,128)(2,1)}, u32[]{:S(2)}, u32[]{:S(2)}) %collective-permute-start.22) | collective-permute-done | bytes 655392 | tf_op jit(solution)/shard_map/ppermute | solution.py:398
  206.9 3.9 %attend.3 = (bf16[32,64,576]{2,1,0:T(8,128)(2,1)}, bf16[32,32,512]{2,1,0:T(8,128)(2,1)}, f32[1]{0:T(128)}) custom-call(f32[1]{0:T(128)} %get-tuple-element.30.late_ref, s32[1]{0:T(128)} %bitcast.7.half_ref.tp_ref, s32[32]{0:T(128)S(1)} %get-tuple-element.38.length_ref, ...), custom_call_target="tpu_custom_call", output_to_operand_aliasing={{0}: (7, {}), {1}: (8, {})} | custom-call | flops 100000000 | bytes 4000000 | tf_op jit(solution)/shard_map/attend/pallas_call | solution.py:351
  (74 shorter events, 1.3 us)
Async XLA Ops:
  0.6 8.9 %copy-start = (s32[32,4]{0,1:T(4,128)S(1)}, s32[32,4]{0,1:T(4,128)}, u32[]{:S(2)}) copy-start(s32[32,4]{0,1:T(4,128)} %param.18) | copy-start | bytes 1540
  0.6 8.9 %copy-start.14 = (s32[64]{0:T(128)S(1)}, s32[64]{0:T(128)}, u32[]{:S(2)}) copy-start(s32[64]{0:T(128)} %constant.94.clone) | copy-start | bytes 772
  0.7 8.8 %copy-start.16 = (s32[32]{0:T(128)S(1)}, s32[32]{0:T(128)}, u32[]{:S(2)}) copy-start(s32[32]{0:T(128)} %param.20) | copy-start | bytes 388
  0.7 9.0 %copy-start.15 = (s32[32]{0:T(128)S(1)}, s32[32]{0:T(128)}, u32[]{:S(2)}) copy-start(s32[32]{0:T(128)} %param.19) | copy-start | bytes 388
  3.1 12.0 %collective-permute-start = (bf16[32,3712]{1,0:T(8,128)(2,1)}, bf16[32,3712]{1,0:T(8,128)(2,1)}, u32[]{:S(2)}, u32[]{:S(2)}) collective-permute-start(bf16[32,3712]{1,0:T(8,128)(2,1)} %fusion.1.refs_0_), channel_id=1, source_target_pairs={{0,8},{8,16},{16,24},{24,32},{32,40},{40,48},{48,56},{56,0},{1,9},... | collective-permute-start | bytes 712712 | tf_op jit(solution)/shard_map/ppermute | solution.py:402
  5.1 10.1 %collective-permute-start.4 = (bf16[32,3712]{1,0:T(8,128)(2,1)}, bf16[32,3712]{1,0:T(8,128)(2,1)}, u32[]{:S(2)}, u32[]{:S(2)}) collective-permute-start(bf16[32,3712]{1,0:T(8,128)(2,1)} %fusion.1.refs_0_), channel_id=1, source_target_pairs={{0,56},{8,0},{16,8},{24,16},{32,24},{40,32},{48,40},{56,48},{1,57}... | collective-permute-start | bytes 712712 | tf_op jit(solution)/shard_map/ppermute | solution.py:402
  8.3 29.4 %collective-permute-start.14 = (bf16[256,1792]{1,0:T(8,128)(2,1)}, bf16[256,1792]{1,0:T(8,128)(2,1)S(1)}, u32[]{:S(2)}, u32[]{:S(2)}) collective-permute-start(bf16[256,1792]{1,0:T(8,128)(2,1)} %scale_down.2), channel_id=1, source_target_pairs={{0,1},{1,0},{2,3},{3,2},{4,5},{5,4},{6,7},{7,6},{8,9},{9,8},{10,11... | collective-permute-start | bytes 2752520 | tf_op jit(solution)/shard_map/ppermute | solution.py:398
  19.6 10.6 %copy-start.17 = (bf16[1,28,2]{1,2,0:T(2,128)(2,1)S(1)}, bf16[1,28,2]{1,2,0:T(2,128)(2,1)}, u32[]{:S(2)}) copy-start(bf16[1,28,2]{1,2,0:T(2,128)(2,1)} %param.27) | copy-start | bytes 340
  19.6 10.6 %copy-start.18 = (bf16[1,28,2]{1,2,0:T(2,128)(2,1)S(1)}, bf16[1,28,2]{1,2,0:T(2,128)(2,1)}, u32[]{:S(2)}) copy-start(bf16[1,28,2]{1,2,0:T(2,128)(2,1)} %param.29) | copy-start | bytes 340
  19.6 42.9 %all-to-all-start = ((bf16[8,8,32,640]{3,2,1,0:T(8,128)(2,1)}), bf16[8,8,32,640]{3,2,1,0:T(8,128)(2,1)}, u32[]{:S(2)}, u32[]{:S(2)}) async-start(bf16[8,8,32,640]{3,2,1,0:T(8,128)(2,1)} %bitcast.28), calls=%async_computation | async-start | bytes 5242880 | tf_op jit(solution)/shard_map/all_to_all | solution.py:452
  27.2 7.3 %collective-permute-start.1 = (bf16[32,3712]{1,0:T(8,128)(2,1)}, bf16[32,3712]{1,0:T(8,128)(2,1)S(1)}, u32[]{:S(2)}, u32[]{:S(2)}) collective-permute-start(bf16[32,3712]{1,0:T(8,128)(2,1)} %collective-permute-done.refs_1_.refs_0_), channel_id=1, source_target_pairs={{0,8},{8,16},{16,24},{24,32},{32,40},{40,48},{48,56},{56,0},{1,9},... | collective-permute-start | bytes 712712 | tf_op jit(solution)/shard_map/ppermute | solution.py:402
  30.2 7.5 %collective-permute-start.5 = (bf16[32,3712]{1,0:T(8,128)(2,1)}, bf16[32,3712]{1,0:T(8,128)(2,1)S(1)}, u32[]{:S(2)}, u32[]{:S(2)}) collective-permute-start(bf16[32,3712]{1,0:T(8,128)(2,1)} %collective-permute-done.4.refs_5_.refs_1_), channel_id=1, source_target_pairs={{0,56},{8,0},{16,8},{24,16},{32,24},{40,32},{48,40},{56,48},{1,57}... | collective-permute-start | bytes 712712 | tf_op jit(solution)/shard_map/ppermute | solution.py:402
  32.8 25.9 %collective-permute-start.15 = (bf16[3584,256]{1,0:T(8,128)(2,1)S(1)}, bf16[3584,256]{1,0:T(8,128)(2,1)S(1)}, u32[]{:S(2)}, u32[]{:S(2)}) collective-permute-start(bf16[3584,256]{1,0:T(8,128)(2,1)S(1)} %scale_wide.2.refs_8_), channel_id=1, source_target_pairs={{0,128},{128,0},{1,129},{129,1},{2,130},{130,2},{3,131},{131,3},{4... | collective-permute-start | bytes 5505032 | tf_op jit(solution)/shard_map/ppermute | solution.py:398
  40.8 17.8 %collective-permute-start.16 = (bf16[3584,256]{1,0:T(8,128)(2,1)S(1)}, bf16[3584,256]{1,0:T(8,128)(2,1)S(1)}, u32[]{:S(2)}, u32[]{:S(2)}) collective-permute-start(bf16[3584,256]{1,0:T(8,128)(2,1)S(1)} %scale_wide.3.refs_9_), channel_id=1, source_target_pairs={{0,128},{128,0},{1,129},{129,1},{2,130},{130,2},{3,131},{131,3},{4... | collective-permute-start | bytes 5505032 | tf_op jit(solution)/shard_map/ppermute | solution.py:398
  40.9 1.3 copy-start.1
  42.2 8.9 %collective-permute-start.2 = (bf16[32,3712]{1,0:T(8,128)(2,1)S(1)}, bf16[32,3712]{1,0:T(8,128)(2,1)S(1)}, u32[]{:S(2)}, u32[]{:S(2)}) collective-permute-start(bf16[32,3712]{1,0:T(8,128)(2,1)S(1)} %collective-permute-done.1.refs_2_.refs_0_), channel_id=1, source_target_pairs={{0,8},{8,16},{16,24},{24,32},{32,40},{40,48},{48,56},{56,0},{1,9},... | collective-permute-start | bytes 712712 | tf_op jit(solution)/shard_map/ppermute | solution.py:402
  45.5 8.9 %collective-permute-start.6 = (bf16[32,3712]{1,0:T(8,128)(2,1)S(1)}, bf16[32,3712]{1,0:T(8,128)(2,1)S(1)}, u32[]{:S(2)}, u32[]{:S(2)}) collective-permute-start(bf16[32,3712]{1,0:T(8,128)(2,1)S(1)} %collective-permute-done.5.refs_6_.refs_1_), channel_id=1, source_target_pairs={{0,56},{8,0},{16,8},{24,16},{32,24},{40,32},{48,40},{56,48},{1,57}... | collective-permute-start | bytes 712712 | tf_op jit(solution)/shard_map/ppermute | solution.py:402
  51.2 7.5 %collective-permute-start.3 = (bf16[32,3712]{1,0:T(8,128)(2,1)S(1)}, bf16[32,3712]{1,0:T(8,128)(2,1)S(1)}, u32[]{:S(2)}, u32[]{:S(2)}) collective-permute-start(bf16[32,3712]{1,0:T(8,128)(2,1)S(1)} %collective-permute-done.2.refs_3_), channel_id=1, source_target_pairs={{0,8},{8,16},{16,24},{24,32},{32,40},{40,48},{48,56},{56,0},{1,9},... | collective-permute-start | bytes 712712 | tf_op jit(solution)/shard_map/ppermute | solution.py:402
  53.6 0.7 copy-start.9
  59.2 1.3 copy-start.3
  60.5 1.3 copy-start.5
  61.8 0.7 copy-start.7
  66.0 79.2 %all-to-all-start.1 = ((bf16[8,8,32,640]{3,2,1,0:T(8,128)(2,1)}), bf16[8,8,32,640]{3,2,1,0:T(8,128)(2,1)}, u32[]{:S(2)}, u32[]{:S(2)}) async-start(bf16[8,8,32,640]{3,2,1,0:T(8,128)(2,1)} %regroup.1), calls=%async_computation.1 | async-start | bytes 5242880 | tf_op jit(solution)/shard_map/all_to_all | solution.py:474
  74.6 0.9 copy-start.8
  75.5 0.9 copy-start.10
  80.3 46.3 %copy-start.2 = (bf16[3584,256]{1,0:T(8,128)(2,1)S(1)}, bf16[3584,256]{1,0:T(8,128)(2,1)}, u32[]{:S(2)}) copy-start(bf16[3584,256]{1,0:T(8,128)(2,1)} %copy-done.1) | copy-start | bytes 5505028
  80.3 15.0 %collective-permute-start.7 = (bf16[64,3584]{1,0:T(8,128)(2,1)S(1)}, bf16[64,3584]{1,0:T(8,128)(2,1)S(1)}, u32[]{:S(2)}, u32[]{:S(2)}) collective-permute-start(bf16[64,3584]{1,0:T(8,128)(2,1)S(1)} %get-tuple-element.20), channel_id=1, source_target_pairs={{0,64},{2,66},{4,68},{6,70},{64,0},{66,2},{68,4},{70,6},{1,65},{3,... | collective-permute-start | bytes 1376264 | tf_op jit(solution)/shard_map/ppermute | solution.py:406
  80.4 31.2 %collective-permute-start.8 = (bf16[64,3584]{1,0:T(8,128)(2,1)S(1)}, bf16[64,3584]{1,0:T(8,128)(2,1)S(1)}, u32[]{:S(2)}, u32[]{:S(2)}) collective-permute-start(bf16[64,3584]{1,0:T(8,128)(2,1)S(1)} %get-tuple-element.21), channel_id=1, source_target_pairs={{0,2},{2,4},{4,6},{6,0},{64,66},{66,68},{68,70},{70,64},{1,3},{3,5... | collective-permute-start | bytes 1376264 | tf_op jit(solution)/shard_map/ppermute | solution.py:406
  82.5 40.4 %collective-permute-start.9 = (bf16[64,3584]{1,0:T(8,128)(2,1)S(1)}, bf16[64,3584]{1,0:T(8,128)(2,1)S(1)}, u32[]{:S(2)}, u32[]{:S(2)}) collective-permute-start(bf16[64,3584]{1,0:T(8,128)(2,1)S(1)} %get-tuple-element.22.refs_0_), channel_id=1, source_target_pairs={{0,66},{2,68},{4,70},{6,64},{64,2},{66,4},{68,6},{70,0},{1,67},{3,... | collective-permute-start | bytes 1376264 | tf_op jit(solution)/shard_map/ppermute | solution.py:406
  86.3 37.2 %collective-permute-start.10 = (bf16[64,3584]{1,0:T(8,128)(2,1)S(1)}, bf16[64,3584]{1,0:T(8,128)(2,1)S(1)}, u32[]{:S(2)}, u32[]{:S(2)}) collective-permute-start(bf16[64,3584]{1,0:T(8,128)(2,1)S(1)} %get-tuple-element.23), channel_id=1, source_target_pairs={{0,4},{2,6},{4,0},{6,2},{64,68},{66,70},{68,64},{70,66},{1,5},{3,7... | collective-permute-start | bytes 1376264 | tf_op jit(solution)/shard_map/ppermute | solution.py:406
  88.1 35.4 %collective-permute-start.11 = (bf16[64,3584]{1,0:T(8,128)(2,1)S(1)}, bf16[64,3584]{1,0:T(8,128)(2,1)S(1)}, u32[]{:S(2)}, u32[]{:S(2)}) collective-permute-start(bf16[64,3584]{1,0:T(8,128)(2,1)S(1)} %get-tuple-element.24), channel_id=1, source_target_pairs={{0,68},{2,70},{4,64},{6,66},{64,4},{66,6},{68,0},{70,2},{1,69},{3,... | collective-permute-start | bytes 1376264 | tf_op jit(solution)/shard_map/ppermute | solution.py:406
  95.4 31.2 %collective-permute-start.12 = (bf16[64,3584]{1,0:T(8,128)(2,1)S(1)}, bf16[64,3584]{1,0:T(8,128)(2,1)S(1)}, u32[]{:S(2)}, u32[]{:S(2)}) collective-permute-start(bf16[64,3584]{1,0:T(8,128)(2,1)S(1)} %get-tuple-element.25), channel_id=1, source_target_pairs={{0,6},{2,0},{4,2},{6,4},{64,70},{66,64},{68,66},{70,68},{1,7},{3,1... | collective-permute-start | bytes 1376264 | tf_op jit(solution)/shard_map/ppermute | solution.py:406
  111.6 14.9 %collective-permute-start.13 = (bf16[64,3584]{1,0:T(8,128)(2,1)S(1)}, bf16[64,3584]{1,0:T(8,128)(2,1)S(1)}, u32[]{:S(2)}, u32[]{:S(2)}) collective-permute-start(bf16[64,3584]{1,0:T(8,128)(2,1)S(1)} %get-tuple-element.26), channel_id=1, source_target_pairs={{0,70},{2,64},{4,66},{6,68},{64,6},{66,0},{68,2},{70,4},{1,71},{3,... | collective-permute-start | bytes 1376264 | tf_op jit(solution)/shard_map/ppermute | solution.py:406
  122.8 14.4 %collective-permute-start.20 = (bf16[256,1792]{1,0:T(8,128)(2,1)S(1)}, bf16[256,1792]{1,0:T(8,128)(2,1)}, u32[]{:S(2)}, u32[]{:S(2)}) collective-permute-start(bf16[256,1792]{1,0:T(8,128)(2,1)S(1)} %collective-permute-done.14.refs_2_.w2), channel_id=1, source_target_pairs={{0,128},{128,0},{1,129},{129,1},{2,130},{130,2},{3,131},{131,3},{4... | collective-permute-start | bytes 2752520 | tf_op jit(solution)/shard_map/ppermute | solution.py:398
  123.5 13.8 %collective-permute-start.19 = (bf16[256,1792]{1,0:T(8,128)(2,1)}, bf16[256,1792]{1,0:T(8,128)(2,1)}, u32[]{:S(2)}, u32[]{:S(2)}) collective-permute-start(bf16[256,1792]{1,0:T(8,128)(2,1)} %scale_down.3.w0), channel_id=1, source_target_pairs={{0,128},{128,0},{1,129},{129,1},{2,130},{130,2},{3,131},{131,3},{4... | collective-permute-start | bytes 2752520 | tf_op jit(solution)/shard_map/ppermute | solution.py:398
  126.6 3.2 %copy-start.4 = (bf16[3584,256]{1,0:T(8,128)(2,1)S(1)}, bf16[3584,256]{1,0:T(8,128)(2,1)}, u32[]{:S(2)}) copy-start(bf16[3584,256]{1,0:T(8,128)(2,1)} %copy-done.3) | copy-start | bytes 5505028
  126.6 3.2 %copy-start.6 = (bf16[3584,256]{1,0:T(8,128)(2,1)S(1)}, bf16[3584,256]{1,0:T(8,128)(2,1)}, u32[]{:S(2)}) copy-start(bf16[3584,256]{1,0:T(8,128)(2,1)} %copy-done.5) | copy-start | bytes 5505028
  128.7 4.3 %copy-start.19 = (s32[8]{0:T(128)S(1)}, s32[8]{0:T(128)}, u32[]{:S(2)}) copy-start(s32[8]{0:T(128)} %constant.112) | copy-start | bytes 100
  128.7 8.5 %collective-permute-start.17 = (bf16[512,256]{1,0:T(8,128)(2,1)S(1)}, bf16[512,256]{1,0:T(8,128)(2,1)S(1)}, u32[]{:S(2)}, u32[]{:S(2)}) collective-permute-start(bf16[512,256]{1,0:T(8,128)(2,1)S(1)} %hidden_units.2.h0), channel_id=1, source_target_pairs={{0,1},{1,0},{2,3},{3,2},{4,5},{5,4},{6,7},{7,6},{8,9},{9,8},{10,11... | collective-permute-start | bytes 786440 | tf_op jit(solution)/shard_map/ppermute | solution.py:398
  131.8 8.2 %collective-permute-start.18 = (bf16[512,256]{1,0:T(8,128)(2,1)S(1)}, bf16[512,256]{1,0:T(8,128)(2,1)S(1)}, u32[]{:S(2)}, u32[]{:S(2)}) collective-permute-start(bf16[512,256]{1,0:T(8,128)(2,1)S(1)} %hidden_units.3.h1), channel_id=1, source_target_pairs={{0,1},{1,0},{2,3},{3,2},{4,5},{5,4},{6,7},{7,6},{8,9},{9,8},{10,11... | collective-permute-start | bytes 786440 | tf_op jit(solution)/shard_map/ppermute | solution.py:398
  145.2 54.0 %all-to-all-start.2 = ((bf16[64,8,1792]{2,1,0:T(8,128)(2,1)}), bf16[64,8,1792]{2,1,0:T(8,128)(2,1)S(1)}, u32[]{:S(2)}, u32[]{:S(2)}) async-start(bf16[64,8,1792]{2,1,0:T(8,128)(2,1)} %down_rows.1.refs_0_), calls=%async_computation.2 | async-start | bytes 3670016 | tf_op jit(solution)/shard_map/all_to_all | solution.py:487
  157.7 7.2 %copy-start.12 = (s32[32,8]{0,1:T(8,128)S(1)}, s32[32,8]{0,1:T(8,128)}, u32[]{:S(2)}) copy-start(s32[32,8]{0,1:T(8,128)} %param.24) | copy-start | bytes 3076
  158.2 6.7 %copy-start.11 = (bf16[32,576]{1,0:T(8,128)(2,1)S(1)}, bf16[32,576]{1,0:T(8,128)(2,1)}, u32[]{:S(2)}) copy-start(bf16[32,576]{1,0:T(8,128)(2,1)} %param.22) | copy-start | bytes 110596
  158.3 6.8 %copy-start.13 = (f32[32,8]{0,1:T(8,128)S(1)}, f32[32,8]{0,1:T(8,128)}, u32[]{:S(2)}) copy-start(f32[32,8]{0,1:T(8,128)} %param.25) | copy-start | bytes 3076
  162.9 32.6 %collective-permute-start.21 = (bf16[16,32,640]{2,1,0:T(8,128)(2,1)S(1)}, bf16[16,32,640]{2,1,0:T(8,128)(2,1)S(1)}, u32[]{:S(2)}, u32[]{:S(2)}) collective-permute-start(bf16[16,32,640]{2,1,0:T(8,128)(2,1)S(1)} %get-tuple-element.28.mine), channel_id=1, source_target_pairs={{0,1},{1,0},{2,3},{3,2},{4,5},{5,4},{6,7},{7,6},{8,9},{9,8},{10,11... | collective-permute-start | bytes 1966088 | tf_op jit(solution)/shard_map/ppermute | solution.py:398
  163.9 43.0 %collective-permute-start.22 = (bf16[16,32,640]{2,1,0:T(8,128)(2,1)}, bf16[16,32,640]{2,1,0:T(8,128)(2,1)}, u32[]{:S(2)}, u32[]{:S(2)}) collective-permute-start(bf16[16,32,640]{2,1,0:T(8,128)(2,1)} %get-tuple-element.31.mine), channel_id=1, source_target_pairs={{0,1},{1,0},{2,3},{3,2},{4,5},{5,4},{6,7},{7,6},{8,9},{9,8},{10,11... | collective-permute-start | bytes 1966088 | tf_op jit(solution)/shard_map/ppermute | solution.py:398

commit v8 on v7

--- a/solution.py
+++ b/solution.py
@@ -150,7 +150,7 @@
     )(place, *blocks)
 
 
-PEER_ORDER = (4, 1, 5, 2, 6, 3, 7, 0)
+PEER_ORDER = (4, 5, 6, 7, 1, 2, 3, 0)
 
 
 def hidden_kernel(*refs):
@@ -289,18 +289,19 @@
 
 
 def compact_kernel(source_ref, arrived, late_ref, first, second):
-    for s in range(TRAJ // 2):
-        first[s] = arrived[source_ref[s]]
-        second[s] = arrived[source_ref[TRAJ // 2 + s]]
+    step = pl.program_id(0) * 8
+    for s in range(8):
+        first[s] = arrived[source_ref[step + s]]
+        second[s] = arrived[source_ref[TRAJ // 2 + step + s]]
 
 
 def compact(source, arrived, late):
     half = (TRAJ // 2, 32, LANES)
     return pl.pallas_call(
         compact_kernel,
-        grid=(1,),
+        grid=(2,),
         in_specs=[smem(), whole(arrived.shape), smem()],
-        out_specs=[whole(half)] * 2,
+        out_specs=[pl.BlockSpec((8, 32, LANES), lambda i: (i, 0, 0))] * 2,
         out_shape=[in_hbm(half)] * 2,
         compiler_params=params(10),
         cost_estimate=cost(1e6, 4e6),

time: 212 us -> 224 us (1.057)
  waiting for transfers between devices: 79.9 us -> 95.6 us
  starting transfers between devices: 64.7 us -> 61.2 us
    ppermute x7, waiting for transfers between devices: 22.9 us -> 35.5 us  [plane_shift(): lax.ppermute(x, ('xh', 'y'), [(a * NY + b, (a + dx) % NX * NY + (b + dy)...]
    ppermute x7, starting transfers between devices: 19.8 us -> 15.4 us  [plane_shift(): lax.ppermute(x, ('xh', 'y'), [(a * NY + b, (a + dx) % NX * NY + (b + dy)...]
  transfers between devices with their start and end apart: 26 -> 26, of which waited for: 12 -> 15; matrix products, arithmetic and copies ran while one was open for 4% -> 4% of each run, Pallas kernels for 19% -> 18%
where the time goes in v8:
time: 224 us; the launch traced here: 223 us
  waiting for transfers between devices  95.6 us (43%)
  starting transfers between devices  61.2 us (27%)
  Pallas kernels  47.7 us (21%)
  local copies, waits for them, and re-layouts  12.3 us (5%)
  other arithmetic  5.24 us (2%)
    ppermute x9, waiting for transfers between devices, swap(): return lax.ppermute(x, axis, [(0, 1), (1, 0)])  43.9 us
    ppermute x7, waiting for transfers between devices, plane_shift(): lax.ppermute(x, ('xh', 'y'), [(a * NY + b, (a + dx) % NX * NY + (b + dy)...  35.5 us
    ppermute x7, starting transfers between devices, plane_shift(): lax.ppermute(x, ('xh', 'y'), [(a * NY + b, (a + dx) % NX * NY + (b + dy)...  15.4 us
    ppermute x7, waiting for transfers between devices, z_shift(): return lax.ppermute(x, 'z', [(i, (i + by) % NZ) for i in range(NZ)])  14.8 us
    all_to_all x1, starting transfers between devices, on_device(): lax.all_to_all(out_rows, ('xh', 'z', 'y'), split_axis=0, concat_axis=0, t...  13.5 us
    unnamed x43, local copies, waits for them, and re-layouts  11.2 us
    ppermute x7, starting transfers between devices, z_shift(): return lax.ppermute(x, 'z', [(i, (i + by) % NZ) for i in range(NZ)])  10.8 us
    all_to_all x1, starting transfers between devices, on_device(): lax.all_to_all(midway, 'z', split_axis=0, concat_axis=0, tiled=True)  8.45 us
  transfers between devices with their start and end apart: 26, of which 15 were waited for; matrix products, arithmetic and copies ran while one was open for 4% of the time, Pallas kernels for 18%

profile of v8, /device:TPU:68, one launch (start us, length us, event | category | flops | bytes accessed | tf_op | source)
XLA Modules:
  0.0 223.0 jit_solution(3047391973935841087)
XLA Ops:
  0.7 0.7 convert_element_type.38
  1.5 1.7 fusion.1.refs_0_
  3.1 1.9 collective-permute-start
  5.2 0.7 bitcast_convert_fusion.scale
  5.8 2.5 %scale_down.2 = bf16[256,1792]{1,0:T(8,128)(2,1)} custom-call(s32[1]{0:T(128)S(6)} %sub.38.half_ref, f32[2,28]{1,0:T(2,128)S(1)} %bitcast_convert_fusion.scale, bf16[1,256,3584]{2,1,0:T(8,128)(2,1)} %value.7), custom_call_target="tpu_custom_call" | custom-call | flops 1000000 | bytes 2000000 | tf_op jit(solution)/shard_map/scale_down/pallas_call | solution.py:90
  8.3 1.2 collective-permute-start.14
  9.7 0.7 copy.45
  10.5 3.9 %copy.47.pages = bf16[128,16,576]{2,1,0:T(8,128)(2,1)S(1)} copy(bf16[128,16,576]{0,2,1:T(8,128)(2,1)} %param.17) | data formatting | bytes 4718592 | tf_op args[0]
  14.4 0.8 broadcast_subtract_fusion.index_ref
  15.1 0.5 once.5.rest_0_
  15.7 3.9 %collect.1 = bf16[64,32,640]{2,1,0:T(8,128)(2,1)} custom-call(s32[64,4]{1,0:T(8,128)S(1)} %broadcast_subtract_fusion.index_ref, bf16[128,16,576]{2,1,0:T(8,128)(2,1)S(1)} %copy.47.pages, f32[1]{0:T(128)} %once.5.rest_0_), custom_call_target="tpu_custom_call" | custom-call | flops 1000000 | bytes 6000000 | tf_op jit(solution)/shard_map/collect/pallas_call | solution.py:260
  19.6 7.6 %all-to-all-start = ((bf16[8,8,32,640]{3,2,1,0:T(8,128)(2,1)}), bf16[8,8,32,640]{3,2,1,0:T(8,128)(2,1)}, u32[]{:S(2)}, u32[]{:S(2)}) async-start(bf16[8,8,32,640]{3,2,1,0:T(8,128)(2,1)} %bitcast.28), calls=%async_computation | async-start | bytes 5242880 | tf_op jit(solution)/shard_map/all_to_all | solution.py:453
  27.2 3.0 %collective-permute-start.1 = (bf16[32,3712]{1,0:T(8,128)(2,1)}, bf16[32,3712]{1,0:T(8,128)(2,1)S(1)}, u32[]{:S(2)}, u32[]{:S(2)}) collective-permute-start(bf16[32,3712]{1,0:T(8,128)(2,1)} %collective-permute-done.refs_1_.refs_0_), channel_id=1, source_target_pairs={{0,8},{8,16},{16,24},{24,32},{32,40},{40,48},{48,56},{56,0},{1,9},... | collective-permute-start | bytes 712712 | tf_op jit(solution)/shard_map/ppermute | solution.py:403
  30.2 2.6 %scale_wide.2.refs_8_ = bf16[3584,256]{1,0:T(8,128)(2,1)S(1)} custom-call(f32[2,28]{1,0:T(2,128)S(1)} %convert_bitcast_fusion.1.scale, bf16[1,3584,256]{2,1,0:T(8,128)(2,1)} %value.4, f32[1]{0:T(128)} %once.5.rest_0_), custom_call_target="tpu_custom_call" | custom-call | flops 1000000 | bytes 4000000 | tf_op jit(solution)/shard_map/scale_wide/pallas_call | solution.py:66
  32.9 1.5 collective-permute-done.1.refs_2_.refs_0_
  34.4 3.3 %collective-permute-done.5.refs_6_.refs_1_ = bf16[32,3712]{1,0:T(8,128)(2,1)S(1)} collective-permute-done((bf16[32,3712]{1,0:T(8,128)(2,1)}, bf16[32,3712]{1,0:T(8,128)(2,1)S(1)}, u32[]{:S(2)}, u32[]{:S(2)}) %collective-permute-start.5) | collective-permute-done | bytes 237600 | tf_op jit(solution)/shard_map/ppermute | solution.py:403
  38.2 2.6 %scale_wide.3.refs_9_ = bf16[3584,256]{1,0:T(8,128)(2,1)S(1)} custom-call(f32[2,28]{1,0:T(2,128)S(1)} %convert_bitcast_fusion.scale, bf16[1,3584,256]{2,1,0:T(8,128)(2,1)} %value.6, f32[1]{0:T(128)} %once.6.rest_0_), custom_call_target="tpu_custom_call" | custom-call | flops 1000000 | bytes 4000000 | tf_op jit(solution)/shard_map/scale_wide/pallas_call | solution.py:66
  41.0 1.3 copy-done.1
  42.2 3.2 %collective-permute-start.2 = (bf16[32,3712]{1,0:T(8,128)(2,1)S(1)}, bf16[32,3712]{1,0:T(8,128)(2,1)S(1)}, u32[]{:S(2)}, u32[]{:S(2)}) collective-permute-start(bf16[32,3712]{1,0:T(8,128)(2,1)S(1)} %collective-permute-done.1.refs_2_.refs_0_), channel_id=1, source_target_pairs={{0,8},{8,16},{16,24},{24,32},{32,40},{40,48},{48,56},{56,0},{1,9},... | collective-permute-start | bytes 712712 | tf_op jit(solution)/shard_map/ppermute | solution.py:403
  45.5 5.7 %collective-permute-done.2.refs_3_ = bf16[32,3712]{1,0:T(8,128)(2,1)S(1)} collective-permute-done((bf16[32,3712]{1,0:T(8,128)(2,1)S(1)}, bf16[32,3712]{1,0:T(8,128)(2,1)S(1)}, u32[]{:S(2)}, u32[]{:S(2)}) %collective-permute-start.2) | collective-permute-done | bytes 237600 | tf_op jit(solution)/shard_map/ppermute | solution.py:403
  51.2 2.5 %collective-permute-start.3 = (bf16[32,3712]{1,0:T(8,128)(2,1)S(1)}, bf16[32,3712]{1,0:T(8,128)(2,1)S(1)}, u32[]{:S(2)}, u32[]{:S(2)}) collective-permute-start(bf16[32,3712]{1,0:T(8,128)(2,1)S(1)} %collective-permute-done.2.refs_3_), channel_id=1, source_target_pairs={{0,8},{8,16},{16,24},{24,32},{32,40},{40,48},{48,56},{56,0},{1,9},... | collective-permute-start | bytes 712712 | tf_op jit(solution)/shard_map/ppermute | solution.py:403
  53.6 0.7 copy-done.9
  54.3 4.3 %collective-permute-done.3.refs_4_.refs_0_ = bf16[32,3712]{1,0:T(8,128)(2,1)S(1)} collective-permute-done((bf16[32,3712]{1,0:T(8,128)(2,1)S(1)}, bf16[32,3712]{1,0:T(8,128)(2,1)S(1)}, u32[]{:S(2)}, u32[]{:S(2)}) %collective-permute-start.3) | collective-permute-done | bytes 237600 | tf_op jit(solution)/shard_map/ppermute | solution.py:403
  58.7 0.5 once.9.rest_0_
  59.2 1.3 copy-done.3
  60.5 1.3 copy-done.5
  61.8 0.7 copy-done.7
  62.5 3.6 %regroup.1 = bf16[8,8,32,640]{3,2,1,0:T(8,128)(2,1)} custom-call(bf16[8,8,32,640]{3,2,1,0:T(8,128)(2,1)} %all-to-all-done.midway, f32[1]{0:T(128)} %once.9.rest_0_), custom_call_target="tpu_custom_call" | custom-call | flops 1000000 | bytes 6000000 | tf_op jit(solution)/shard_map/regroup/pallas_call | solution.py:279
  66.0 8.4 %all-to-all-start.1 = ((bf16[8,8,32,640]{3,2,1,0:T(8,128)(2,1)}), bf16[8,8,32,640]{3,2,1,0:T(8,128)(2,1)}, u32[]{:S(2)}, u32[]{:S(2)}) async-start(bf16[8,8,32,640]{3,2,1,0:T(8,128)(2,1)} %regroup.1), calls=%async_computation.1 | async-start | bytes 5242880 | tf_op jit(solution)/shard_map/all_to_all | solution.py:475
  74.6 0.9 copy-done.8
  75.5 0.9 copy-done.10
  76.4 3.9 %pick_rows.1 = (bf16[64,3584]{1,0:T(8,128)(2,1)S(1)}, bf16[64,3584]{1,0:T(8,128)(2,1)S(1)}, bf16[64,3584]{1,0:T(8,128)(2,1)S(1)}, bf16[64,3584]{1,0:T(8,128)(2,1...) custom-call(s32[3]{0:T(128)S(1)} %pad_add_fusion.1.place_ref, ...), custom_call_target="tpu_custom_call" | custom-call | flops 1000000000 | bytes 6000000 | tf_op jit(solution)/shard_map/pick_rows/pallas_call | solution.py:142
  80.4 4.4 %collective-permute-start.8 = (bf16[64,3584]{1,0:T(8,128)(2,1)S(1)}, bf16[64,3584]{1,0:T(8,128)(2,1)S(1)}, u32[]{:S(2)}, u32[]{:S(2)}) collective-permute-start(bf16[64,3584]{1,0:T(8,128)(2,1)S(1)} %get-tuple-element.21.refs_0_), channel_id=1, source_target_pairs={{0,66},{2,68},{4,70},{6,64},{64,2},{66,4},{68,6},{70,0},{1,67},{3,... | collective-permute-start | bytes 1376264 | tf_op jit(solution)/shard_map/ppermute | solution.py:407
  84.9 2.7 %collective-permute-start.9 = (bf16[64,3584]{1,0:T(8,128)(2,1)S(1)}, bf16[64,3584]{1,0:T(8,128)(2,1)S(1)}, u32[]{:S(2)}, u32[]{:S(2)}) collective-permute-start(bf16[64,3584]{1,0:T(8,128)(2,1)S(1)} %get-tuple-element.22), channel_id=1, source_target_pairs={{0,68},{2,70},{4,64},{6,66},{64,4},{66,6},{68,0},{70,2},{1,69},{3,... | collective-permute-start | bytes 1376264 | tf_op jit(solution)/shard_map/ppermute | solution.py:407
  87.5 3.8 %collective-permute-start.10 = (bf16[64,3584]{1,0:T(8,128)(2,1)S(1)}, bf16[64,3584]{1,0:T(8,128)(2,1)S(1)}, u32[]{:S(2)}, u32[]{:S(2)}) collective-permute-start(bf16[64,3584]{1,0:T(8,128)(2,1)S(1)} %get-tuple-element.23), channel_id=1, source_target_pairs={{0,70},{2,64},{4,66},{6,68},{64,6},{66,0},{68,2},{70,4},{1,71},{3,... | collective-permute-start | bytes 1376264 | tf_op jit(solution)/shard_map/ppermute | solution.py:407
  91.4 0.6 collective-permute-start.11
  92.0 3.4 %collective-permute-done.7.refs_0_ = bf16[64,3584]{1,0:T(8,128)(2,1)S(1)} collective-permute-done((bf16[64,3584]{1,0:T(8,128)(2,1)S(1)}, bf16[64,3584]{1,0:T(8,128)(2,1)S(1)}, u32[]{:S(2)}, u32[]{:S(2)}) %collective-permute-start.7) | collective-permute-done | bytes 458784 | tf_op jit(solution)/shard_map/ppermute | solution.py:407
  95.4 3.0 %collective-permute-start.12 = (bf16[64,3584]{1,0:T(8,128)(2,1)S(1)}, bf16[64,3584]{1,0:T(8,128)(2,1)S(1)}, u32[]{:S(2)}, u32[]{:S(2)}) collective-permute-start(bf16[64,3584]{1,0:T(8,128)(2,1)S(1)} %get-tuple-element.25), channel_id=1, source_target_pairs={{0,4},{2,6},{4,0},{6,2},{64,68},{66,70},{68,64},{70,66},{1,5},{3,7... | collective-permute-start | bytes 1376264 | tf_op jit(solution)/shard_map/ppermute | solution.py:407
  98.3 9.1 %collective-permute-done.8.refs_1_ = bf16[64,3584]{1,0:T(8,128)(2,1)S(1)} collective-permute-done((bf16[64,3584]{1,0:T(8,128)(2,1)S(1)}, bf16[64,3584]{1,0:T(8,128)(2,1)S(1)}, u32[]{:S(2)}, u32[]{:S(2)}) %collective-permute-start.8) | collective-permute-done | bytes 458784 | tf_op jit(solution)/shard_map/ppermute | solution.py:407
  107.5 0.8 collective-permute-start.13
  108.8 3.1 %scale_down.3.w0 = bf16[256,1792]{1,0:T(8,128)(2,1)} custom-call(s32[1]{0:T(128)} %bitcast.7.half_ref.tp_ref, f32[2,28]{1,0:T(2,128)S(1)} %bitcast_convert_fusion.scale, bf16[1,256,3584]{2,1,0:T(8,128)(2,1)} %value.7, f32[1]{0:T(128)} %once.7.rest_0_), custom_call_target="tpu_custom_call" | custom-call | flops 1000000 | bytes 2000000 | tf_op jit(solution)/shard_map/scale_down/pallas_call | solution.py:90
  111.9 5.6 %collective-permute-done.9.refs_2_ = bf16[64,3584]{1,0:T(8,128)(2,1)S(1)} collective-permute-done((bf16[64,3584]{1,0:T(8,128)(2,1)S(1)}, bf16[64,3584]{1,0:T(8,128)(2,1)S(1)}, u32[]{:S(2)}, u32[]{:S(2)}) %collective-permute-start.9) | collective-permute-done | bytes 458784 | tf_op jit(solution)/shard_map/ppermute | solution.py:407
  117.5 6.0 %collective-permute-done.10.refs_3_ = bf16[64,3584]{1,0:T(8,128)(2,1)S(1)} collective-permute-done((bf16[64,3584]{1,0:T(8,128)(2,1)S(1)}, bf16[64,3584]{1,0:T(8,128)(2,1)S(1)}, u32[]{:S(2)}, u32[]{:S(2)}) %collective-permute-start.10) | collective-permute-done | bytes 458784 | tf_op jit(solution)/shard_map/ppermute | solution.py:407
  123.5 8.5 %collective-permute-done.11.refs_4_ = bf16[64,3584]{1,0:T(8,128)(2,1)S(1)} collective-permute-done((bf16[64,3584]{1,0:T(8,128)(2,1)S(1)}, bf16[64,3584]{1,0:T(8,128)(2,1)S(1)}, u32[]{:S(2)}, u32[]{:S(2)}) %collective-permute-start.11) | collective-permute-done | bytes 458784 | tf_op jit(solution)/shard_map/ppermute | solution.py:407
  132.0 2.9 %collective-permute-done.13.refs_6_ = bf16[64,3584]{1,0:T(8,128)(2,1)S(1)} collective-permute-done((bf16[64,3584]{1,0:T(8,128)(2,1)S(1)}, bf16[64,3584]{1,0:T(8,128)(2,1)S(1)}, u32[]{:S(2)}, u32[]{:S(2)}) %collective-permute-start.13) | collective-permute-done | bytes 458784 | tf_op jit(solution)/shard_map/ppermute | solution.py:407
  134.9 2.1 hidden_units.2.h0
  137.0 0.9 collective-permute-start.17
  137.9 2.1 hidden_units.3.h1
  140.0 1.3 collective-permute-start.18
  141.4 4.9 %collective-permute-done.17.h2 = bf16[512,256]{1,0:T(8,128)(2,1)S(1)} collective-permute-done((bf16[512,256]{1,0:T(8,128)(2,1)S(1)}, bf16[512,256]{1,0:T(8,128)(2,1)S(1)}, u32[]{:S(2)}, u32[]{:S(2)}) %collective-permute-start.17) | collective-permute-done | bytes 262176 | tf_op jit(solution)/shard_map/ppermute | solution.py:399
  146.3 3.3 %collective-permute-done.18.h3 = bf16[512,256]{1,0:T(8,128)(2,1)S(1)} collective-permute-done((bf16[512,256]{1,0:T(8,128)(2,1)S(1)}, bf16[512,256]{1,0:T(8,128)(2,1)S(1)}, u32[]{:S(2)}, u32[]{:S(2)}) %collective-permute-start.18) | collective-permute-done | bytes 262176 | tf_op jit(solution)/shard_map/ppermute | solution.py:399
  149.7 5.2 %down_rows.1.refs_0_ = bf16[64,8,1792]{2,1,0:T(8,128)(2,1)} custom-call(s32[64]{0:T(128)S(1)} %fusion.3.order_ref, bf16[512,256]{1,0:T(8,128)(2,1)S(1)} %hidden_units.2.h0, bf16[512,256]{1,0:T(8,128)(2,1)S(1)} %hidden_units.3.h1, bf16[512,256]{1,0:T(8,128)(2,1)S(1)} %collective-permute-done.17.h2, bf16[512,256]{1,0:T(8,128)(2,1)S(1)} %collective-permute-done.18.h3, ...), custom_call_target="tpu_custom_call" | custom-call | flops 1900000000 | bytes 7000000 | tf_op jit(solution)/shard_map/down_rows/pallas_call | solution.py:193
  154.8 13.5 %all-to-all-start.2 = ((bf16[64,8,1792]{2,1,0:T(8,128)(2,1)}), bf16[64,8,1792]{2,1,0:T(8,128)(2,1)S(1)}, u32[]{:S(2)}, u32[]{:S(2)}) async-start(bf16[64,8,1792]{2,1,0:T(8,128)(2,1)} %down_rows.1.refs_0_), calls=%async_computation.2 | async-start | bytes 3670016 | tf_op jit(solution)/shard_map/all_to_all | solution.py:488
  168.3 0.5 once.8.late_ref
  168.8 1.0 slice_convert_fusion
  170.1 3.4 %compact.1 = (bf16[16,32,640]{2,1,0:T(8,128)(2,1)S(1)}, bf16[16,32,640]{2,1,0:T(8,128)(2,1)}) custom-call(s32[32]{0:T(128)S(1)} %get-tuple-element.37.source_ref, bf16[64,32,640]{2,1,0:T(8,128)(2,1)} %bitcast.13.arrived, f32[1]{0:T(128)} %once.8.late_ref), custom_call_target="tpu_custom_call" | custom-call | flops 1000000 | bytes 4000000 | tf_op jit(solution)/shard_map/compact/pallas_call | solution.py:300
  173.4 0.9 collective-permute-start.21
  174.3 1.1 collective-permute-start.22
  175.7 30.0 %collective-permute-done.21.other = bf16[16,32,640]{2,1,0:T(8,128)(2,1)S(1)} collective-permute-done((bf16[16,32,640]{2,1,0:T(8,128)(2,1)S(1)}, bf16[16,32,640]{2,1,0:T(8,128)(2,1)S(1)}, u32[]{:S(2)}, u32[]{:S(2)}) %collective-permute-start.21) | collective-permute-done | bytes 655392 | tf_op jit(solution)/shard_map/ppermute | solution.py:399
  205.7 3.7 %attend.2 = (bf16[32,64,576]{2,1,0:T(8,128)(2,1)}, bf16[32,32,512]{2,1,0:T(8,128)(2,1)}, f32[1]{0:T(128)}) custom-call(f32[1]{0:T(128)} %once.8.late_ref, s32[1]{0:T(128)} %bitcast.7.half_ref.tp_ref, s32[32]{0:T(128)S(1)} %get-tuple-element.38.length_ref, bf16[16,32,640]{2,1,0:T(8,128)(2,1)S(1)} %get-tuple-element.28.mine, ...), custom_call_target="tpu_custom_call" | custom-call | flops 100000000 | bytes 4000000 | tf_op jit(solution)/shard_map/attend/pallas_call | solution.py:352
  209.5 1.3 all-to-all-done.2.rows_ref
  210.7 2.7 %blend.1 = (bf16[32,1792]{1,0:T(8,128)(2,1)}, f32[1]{0:T(128)}) custom-call(f32[1]{0:T(128)} %get-tuple-element.29.late_ref, s32[32,8]{1,0:T(8,128)S(1)} %copy.50.routing_ref, f32[32,8]{1,0:T(8,128)S(1)} %copy.51.weight_ref, bf16[64,8,1792]{2,1,0:T(8,128)(2,1)S(1)} %all-to-all-done.2.rows_ref), custom_call_target="tpu_custom_call" | custom-call | flops 100000000 | bytes 2000000 | tf_op jit(solution)/shard_map/blend/pallas_call | solution.py:227
  213.4 5.6 %collective-permute-done.22.other = bf16[16,32,640]{2,1,0:T(8,128)(2,1)} collective-permute-done((bf16[16,32,640]{2,1,0:T(8,128)(2,1)}, bf16[16,32,640]{2,1,0:T(8,128)(2,1)}, u32[]{:S(2)}, u32[]{:S(2)}) %collective-permute-start.22) | collective-permute-done | bytes 655392 | tf_op jit(solution)/shard_map/ppermute | solution.py:399
  219.1 3.9 %attend.3 = (bf16[32,64,576]{2,1,0:T(8,128)(2,1)}, bf16[32,32,512]{2,1,0:T(8,128)(2,1)}, f32[1]{0:T(128)}) custom-call(f32[1]{0:T(128)} %get-tuple-element.30.late_ref, s32[1]{0:T(128)} %bitcast.7.half_ref.tp_ref, s32[32]{0:T(128)S(1)} %get-tuple-element.38.length_ref, ...), custom_call_target="tpu_custom_call", output_to_operand_aliasing={{0}: (7, {}), {1}: (8, {})} | custom-call | flops 100000000 | bytes 4000000 | tf_op jit(solution)/shard_map/attend/pallas_call | solution.py:352
  (74 shorter events, 2.4 us)
Async XLA Ops:
  0.6 8.9 %copy-start = (s32[32,4]{0,1:T(4,128)S(1)}, s32[32,4]{0,1:T(4,128)}, u32[]{:S(2)}) copy-start(s32[32,4]{0,1:T(4,128)} %param.18) | copy-start | bytes 1540
  0.6 8.9 %copy-start.14 = (s32[64]{0:T(128)S(1)}, s32[64]{0:T(128)}, u32[]{:S(2)}) copy-start(s32[64]{0:T(128)} %constant.94.clone) | copy-start | bytes 772
  0.7 8.8 %copy-start.16 = (s32[32]{0:T(128)S(1)}, s32[32]{0:T(128)}, u32[]{:S(2)}) copy-start(s32[32]{0:T(128)} %param.20) | copy-start | bytes 388
  0.7 9.0 %copy-start.15 = (s32[32]{0:T(128)S(1)}, s32[32]{0:T(128)}, u32[]{:S(2)}) copy-start(s32[32]{0:T(128)} %param.19) | copy-start | bytes 388
  3.1 12.0 %collective-permute-start = (bf16[32,3712]{1,0:T(8,128)(2,1)}, bf16[32,3712]{1,0:T(8,128)(2,1)}, u32[]{:S(2)}, u32[]{:S(2)}) collective-permute-start(bf16[32,3712]{1,0:T(8,128)(2,1)} %fusion.1.refs_0_), channel_id=1, source_target_pairs={{0,8},{8,16},{16,24},{24,32},{32,40},{40,48},{48,56},{56,0},{1,9},... | collective-permute-start | bytes 712712 | tf_op jit(solution)/shard_map/ppermute | solution.py:403
  5.1 10.1 %collective-permute-start.4 = (bf16[32,3712]{1,0:T(8,128)(2,1)}, bf16[32,3712]{1,0:T(8,128)(2,1)}, u32[]{:S(2)}, u32[]{:S(2)}) collective-permute-start(bf16[32,3712]{1,0:T(8,128)(2,1)} %fusion.1.refs_0_), channel_id=1, source_target_pairs={{0,56},{8,0},{16,8},{24,16},{32,24},{40,32},{48,40},{56,48},{1,57}... | collective-permute-start | bytes 712712 | tf_op jit(solution)/shard_map/ppermute | solution.py:403
  8.3 29.4 %collective-permute-start.14 = (bf16[256,1792]{1,0:T(8,128)(2,1)}, bf16[256,1792]{1,0:T(8,128)(2,1)S(1)}, u32[]{:S(2)}, u32[]{:S(2)}) collective-permute-start(bf16[256,1792]{1,0:T(8,128)(2,1)} %scale_down.2), channel_id=1, source_target_pairs={{0,1},{1,0},{2,3},{3,2},{4,5},{5,4},{6,7},{7,6},{8,9},{9,8},{10,11... | collective-permute-start | bytes 2752520 | tf_op jit(solution)/shard_map/ppermute | solution.py:399
  19.6 10.6 %copy-start.17 = (bf16[1,28,2]{1,2,0:T(2,128)(2,1)S(1)}, bf16[1,28,2]{1,2,0:T(2,128)(2,1)}, u32[]{:S(2)}) copy-start(bf16[1,28,2]{1,2,0:T(2,128)(2,1)} %param.27) | copy-start | bytes 340
  19.6 10.6 %copy-start.18 = (bf16[1,28,2]{1,2,0:T(2,128)(2,1)S(1)}, bf16[1,28,2]{1,2,0:T(2,128)(2,1)}, u32[]{:S(2)}) copy-start(bf16[1,28,2]{1,2,0:T(2,128)(2,1)} %param.29) | copy-start | bytes 340
  19.6 42.9 %all-to-all-start = ((bf16[8,8,32,640]{3,2,1,0:T(8,128)(2,1)}), bf16[8,8,32,640]{3,2,1,0:T(8,128)(2,1)}, u32[]{:S(2)}, u32[]{:S(2)}) async-start(bf16[8,8,32,640]{3,2,1,0:T(8,128)(2,1)} %bitcast.28), calls=%async_computation | async-start | bytes 5242880 | tf_op jit(solution)/shard_map/all_to_all | solution.py:453
  27.2 7.3 %collective-permute-start.1 = (bf16[32,3712]{1,0:T(8,128)(2,1)}, bf16[32,3712]{1,0:T(8,128)(2,1)S(1)}, u32[]{:S(2)}, u32[]{:S(2)}) collective-permute-start(bf16[32,3712]{1,0:T(8,128)(2,1)} %collective-permute-done.refs_1_.refs_0_), channel_id=1, source_target_pairs={{0,8},{8,16},{16,24},{24,32},{32,40},{40,48},{48,56},{56,0},{1,9},... | collective-permute-start | bytes 712712 | tf_op jit(solution)/shard_map/ppermute | solution.py:403
  30.2 7.5 %collective-permute-start.5 = (bf16[32,3712]{1,0:T(8,128)(2,1)}, bf16[32,3712]{1,0:T(8,128)(2,1)S(1)}, u32[]{:S(2)}, u32[]{:S(2)}) collective-permute-start(bf16[32,3712]{1,0:T(8,128)(2,1)} %collective-permute-done.4.refs_5_.refs_1_), channel_id=1, source_target_pairs={{0,56},{8,0},{16,8},{24,16},{32,24},{40,32},{48,40},{56,48},{1,57}... | collective-permute-start | bytes 712712 | tf_op jit(solution)/shard_map/ppermute | solution.py:403
  32.8 25.9 %collective-permute-start.15 = (bf16[3584,256]{1,0:T(8,128)(2,1)S(1)}, bf16[3584,256]{1,0:T(8,128)(2,1)S(1)}, u32[]{:S(2)}, u32[]{:S(2)}) collective-permute-start(bf16[3584,256]{1,0:T(8,128)(2,1)S(1)} %scale_wide.2.refs_8_), channel_id=1, source_target_pairs={{0,128},{128,0},{1,129},{129,1},{2,130},{130,2},{3,131},{131,3},{4... | collective-permute-start | bytes 5505032 | tf_op jit(solution)/shard_map/ppermute | solution.py:399
  40.8 17.8 %collective-permute-start.16 = (bf16[3584,256]{1,0:T(8,128)(2,1)S(1)}, bf16[3584,256]{1,0:T(8,128)(2,1)S(1)}, u32[]{:S(2)}, u32[]{:S(2)}) collective-permute-start(bf16[3584,256]{1,0:T(8,128)(2,1)S(1)} %scale_wide.3.refs_9_), channel_id=1, source_target_pairs={{0,128},{128,0},{1,129},{129,1},{2,130},{130,2},{3,131},{131,3},{4... | collective-permute-start | bytes 5505032 | tf_op jit(solution)/shard_map/ppermute | solution.py:399
  40.9 1.3 copy-start.1
  42.2 8.9 %collective-permute-start.2 = (bf16[32,3712]{1,0:T(8,128)(2,1)S(1)}, bf16[32,3712]{1,0:T(8,128)(2,1)S(1)}, u32[]{:S(2)}, u32[]{:S(2)}) collective-permute-start(bf16[32,3712]{1,0:T(8,128)(2,1)S(1)} %collective-permute-done.1.refs_2_.refs_0_), channel_id=1, source_target_pairs={{0,8},{8,16},{16,24},{24,32},{32,40},{40,48},{48,56},{56,0},{1,9},... | collective-permute-start | bytes 712712 | tf_op jit(solution)/shard_map/ppermute | solution.py:403
  45.5 8.9 %collective-permute-start.6 = (bf16[32,3712]{1,0:T(8,128)(2,1)S(1)}, bf16[32,3712]{1,0:T(8,128)(2,1)S(1)}, u32[]{:S(2)}, u32[]{:S(2)}) collective-permute-start(bf16[32,3712]{1,0:T(8,128)(2,1)S(1)} %collective-permute-done.5.refs_6_.refs_1_), channel_id=1, source_target_pairs={{0,56},{8,0},{16,8},{24,16},{32,24},{40,32},{48,40},{56,48},{1,57}... | collective-permute-start | bytes 712712 | tf_op jit(solution)/shard_map/ppermute | solution.py:403
  51.2 7.5 %collective-permute-start.3 = (bf16[32,3712]{1,0:T(8,128)(2,1)S(1)}, bf16[32,3712]{1,0:T(8,128)(2,1)S(1)}, u32[]{:S(2)}, u32[]{:S(2)}) collective-permute-start(bf16[32,3712]{1,0:T(8,128)(2,1)S(1)} %collective-permute-done.2.refs_3_), channel_id=1, source_target_pairs={{0,8},{8,16},{16,24},{24,32},{32,40},{40,48},{48,56},{56,0},{1,9},... | collective-permute-start | bytes 712712 | tf_op jit(solution)/shard_map/ppermute | solution.py:403
  53.6 0.7 copy-start.9
  59.2 1.3 copy-start.3
  60.5 1.3 copy-start.5
  61.8 0.7 copy-start.7
  66.0 88.8 %all-to-all-start.1 = ((bf16[8,8,32,640]{3,2,1,0:T(8,128)(2,1)}), bf16[8,8,32,640]{3,2,1,0:T(8,128)(2,1)}, u32[]{:S(2)}, u32[]{:S(2)}) async-start(bf16[8,8,32,640]{3,2,1,0:T(8,128)(2,1)} %regroup.1), calls=%async_computation.1 | async-start | bytes 5242880 | tf_op jit(solution)/shard_map/all_to_all | solution.py:475
  74.6 0.9 copy-start.8
  75.5 0.9 copy-start.10
  80.3 54.6 %copy-start.2 = (bf16[3584,256]{1,0:T(8,128)(2,1)S(1)}, bf16[3584,256]{1,0:T(8,128)(2,1)}, u32[]{:S(2)}) copy-start(bf16[3584,256]{1,0:T(8,128)(2,1)} %copy-done.1) | copy-start | bytes 5505028
  80.3 15.0 %collective-permute-start.7 = (bf16[64,3584]{1,0:T(8,128)(2,1)S(1)}, bf16[64,3584]{1,0:T(8,128)(2,1)S(1)}, u32[]{:S(2)}, u32[]{:S(2)}) collective-permute-start(bf16[64,3584]{1,0:T(8,128)(2,1)S(1)} %get-tuple-element.20), channel_id=1, source_target_pairs={{0,64},{2,66},{4,68},{6,70},{64,0},{66,2},{68,4},{70,6},{1,65},{3,... | collective-permute-start | bytes 1376264 | tf_op jit(solution)/shard_map/ppermute | solution.py:407
  80.4 27.0 %collective-permute-start.8 = (bf16[64,3584]{1,0:T(8,128)(2,1)S(1)}, bf16[64,3584]{1,0:T(8,128)(2,1)S(1)}, u32[]{:S(2)}, u32[]{:S(2)}) collective-permute-start(bf16[64,3584]{1,0:T(8,128)(2,1)S(1)} %get-tuple-element.21.refs_0_), channel_id=1, source_target_pairs={{0,66},{2,68},{4,70},{6,64},{64,2},{66,4},{68,6},{70,0},{1,67},{3,... | collective-permute-start | bytes 1376264 | tf_op jit(solution)/shard_map/ppermute | solution.py:407
  84.9 32.6 %collective-permute-start.9 = (bf16[64,3584]{1,0:T(8,128)(2,1)S(1)}, bf16[64,3584]{1,0:T(8,128)(2,1)S(1)}, u32[]{:S(2)}, u32[]{:S(2)}) collective-permute-start(bf16[64,3584]{1,0:T(8,128)(2,1)S(1)} %get-tuple-element.22), channel_id=1, source_target_pairs={{0,68},{2,70},{4,64},{6,66},{64,4},{66,6},{68,0},{70,2},{1,69},{3,... | collective-permute-start | bytes 1376264 | tf_op jit(solution)/shard_map/ppermute | solution.py:407
  87.5 35.9 %collective-permute-start.10 = (bf16[64,3584]{1,0:T(8,128)(2,1)S(1)}, bf16[64,3584]{1,0:T(8,128)(2,1)S(1)}, u32[]{:S(2)}, u32[]{:S(2)}) collective-permute-start(bf16[64,3584]{1,0:T(8,128)(2,1)S(1)} %get-tuple-element.23), channel_id=1, source_target_pairs={{0,70},{2,64},{4,66},{6,68},{64,6},{66,0},{68,2},{70,4},{1,71},{3,... | collective-permute-start | bytes 1376264 | tf_op jit(solution)/shard_map/ppermute | solution.py:407
  91.4 40.6 %collective-permute-start.11 = (bf16[64,3584]{1,0:T(8,128)(2,1)S(1)}, bf16[64,3584]{1,0:T(8,128)(2,1)S(1)}, u32[]{:S(2)}, u32[]{:S(2)}) collective-permute-start(bf16[64,3584]{1,0:T(8,128)(2,1)S(1)} %get-tuple-element.24), channel_id=1, source_target_pairs={{0,2},{2,4},{4,6},{6,0},{64,66},{66,68},{68,70},{70,64},{1,3},{3,5... | collective-permute-start | bytes 1376264 | tf_op jit(solution)/shard_map/ppermute | solution.py:407
  95.4 36.6 %collective-permute-start.12 = (bf16[64,3584]{1,0:T(8,128)(2,1)S(1)}, bf16[64,3584]{1,0:T(8,128)(2,1)S(1)}, u32[]{:S(2)}, u32[]{:S(2)}) collective-permute-start(bf16[64,3584]{1,0:T(8,128)(2,1)S(1)} %get-tuple-element.25), channel_id=1, source_target_pairs={{0,4},{2,6},{4,0},{6,2},{64,68},{66,70},{68,64},{70,66},{1,5},{3,7... | collective-permute-start | bytes 1376264 | tf_op jit(solution)/shard_map/ppermute | solution.py:407
  107.5 27.4 %collective-permute-start.13 = (bf16[64,3584]{1,0:T(8,128)(2,1)S(1)}, bf16[64,3584]{1,0:T(8,128)(2,1)S(1)}, u32[]{:S(2)}, u32[]{:S(2)}) collective-permute-start(bf16[64,3584]{1,0:T(8,128)(2,1)S(1)} %get-tuple-element.26), channel_id=1, source_target_pairs={{0,6},{2,0},{4,2},{6,4},{64,70},{66,64},{68,66},{70,68},{1,7},{3,1... | collective-permute-start | bytes 1376264 | tf_op jit(solution)/shard_map/ppermute | solution.py:407
  117.5 28.8 %collective-permute-start.20 = (bf16[256,1792]{1,0:T(8,128)(2,1)S(1)}, bf16[256,1792]{1,0:T(8,128)(2,1)}, u32[]{:S(2)}, u32[]{:S(2)}) collective-permute-start(bf16[256,1792]{1,0:T(8,128)(2,1)S(1)} %collective-permute-done.14.refs_2_.w2), channel_id=1, source_target_pairs={{0,128},{128,0},{1,129},{129,1},{2,130},{130,2},{3,131},{131,3},{4... | collective-permute-start | bytes 2752520 | tf_op jit(solution)/shard_map/ppermute | solution.py:399
  123.5 22.8 %collective-permute-start.19 = (bf16[256,1792]{1,0:T(8,128)(2,1)}, bf16[256,1792]{1,0:T(8,128)(2,1)}, u32[]{:S(2)}, u32[]{:S(2)}) collective-permute-start(bf16[256,1792]{1,0:T(8,128)(2,1)} %scale_down.3.w0), channel_id=1, source_target_pairs={{0,128},{128,0},{1,129},{129,1},{2,130},{130,2},{3,131},{131,3},{4... | collective-permute-start | bytes 2752520 | tf_op jit(solution)/shard_map/ppermute | solution.py:399
  134.9 3.0 %copy-start.4 = (bf16[3584,256]{1,0:T(8,128)(2,1)S(1)}, bf16[3584,256]{1,0:T(8,128)(2,1)}, u32[]{:S(2)}) copy-start(bf16[3584,256]{1,0:T(8,128)(2,1)} %copy-done.3) | copy-start | bytes 5505028
  134.9 3.0 %copy-start.6 = (bf16[3584,256]{1,0:T(8,128)(2,1)S(1)}, bf16[3584,256]{1,0:T(8,128)(2,1)}, u32[]{:S(2)}) copy-start(bf16[3584,256]{1,0:T(8,128)(2,1)} %copy-done.5) | copy-start | bytes 5505028
  137.0 4.3 %copy-start.19 = (s32[8]{0:T(128)S(1)}, s32[8]{0:T(128)}, u32[]{:S(2)}) copy-start(s32[8]{0:T(128)} %constant.112) | copy-start | bytes 100
  137.0 9.3 %collective-permute-start.17 = (bf16[512,256]{1,0:T(8,128)(2,1)S(1)}, bf16[512,256]{1,0:T(8,128)(2,1)S(1)}, u32[]{:S(2)}, u32[]{:S(2)}) collective-permute-start(bf16[512,256]{1,0:T(8,128)(2,1)S(1)} %hidden_units.2.h0), channel_id=1, source_target_pairs={{0,1},{1,0},{2,3},{3,2},{4,5},{5,4},{6,7},{7,6},{8,9},{9,8},{10,11... | collective-permute-start | bytes 786440 | tf_op jit(solution)/shard_map/ppermute | solution.py:399
  140.0 9.7 %collective-permute-start.18 = (bf16[512,256]{1,0:T(8,128)(2,1)S(1)}, bf16[512,256]{1,0:T(8,128)(2,1)S(1)}, u32[]{:S(2)}, u32[]{:S(2)}) collective-permute-start(bf16[512,256]{1,0:T(8,128)(2,1)S(1)} %hidden_units.3.h1), channel_id=1, source_target_pairs={{0,1},{1,0},{2,3},{3,2},{4,5},{5,4},{6,7},{7,6},{8,9},{9,8},{10,11... | collective-permute-start | bytes 786440 | tf_op jit(solution)/shard_map/ppermute | solution.py:399
  154.8 55.9 %all-to-all-start.2 = ((bf16[64,8,1792]{2,1,0:T(8,128)(2,1)}), bf16[64,8,1792]{2,1,0:T(8,128)(2,1)S(1)}, u32[]{:S(2)}, u32[]{:S(2)}) async-start(bf16[64,8,1792]{2,1,0:T(8,128)(2,1)} %down_rows.1.refs_0_), calls=%async_computation.2 | async-start | bytes 3670016 | tf_op jit(solution)/shard_map/all_to_all | solution.py:488
  168.3 7.2 %copy-start.12 = (s32[32,8]{0,1:T(8,128)S(1)}, s32[32,8]{0,1:T(8,128)}, u32[]{:S(2)}) copy-start(s32[32,8]{0,1:T(8,128)} %param.24) | copy-start | bytes 3076
  168.8 6.7 %copy-start.11 = (bf16[32,576]{1,0:T(8,128)(2,1)S(1)}, bf16[32,576]{1,0:T(8,128)(2,1)}, u32[]{:S(2)}) copy-start(bf16[32,576]{1,0:T(8,128)(2,1)} %param.22) | copy-start | bytes 110596
  168.8 6.8 %copy-start.13 = (f32[32,8]{0,1:T(8,128)S(1)}, f32[32,8]{0,1:T(8,128)}, u32[]{:S(2)}) copy-start(f32[32,8]{0,1:T(8,128)} %param.25) | copy-start | bytes 3076
  173.4 32.3 %collective-permute-start.21 = (bf16[16,32,640]{2,1,0:T(8,128)(2,1)S(1)}, bf16[16,32,640]{2,1,0:T(8,128)(2,1)S(1)}, u32[]{:S(2)}, u32[]{:S(2)}) collective-permute-start(bf16[16,32,640]{2,1,0:T(8,128)(2,1)S(1)} %get-tuple-element.28.mine), channel_id=1, source_target_pairs={{0,1},{1,0},{2,3},{3,2},{4,5},{5,4},{6,7},{7,6},{8,9},{9,8},{10,11... | collective-permute-start | bytes 1966088 | tf_op jit(solution)/shard_map/ppermute | solution.py:399
  174.3 44.8 %collective-permute-start.22 = (bf16[16,32,640]{2,1,0:T(8,128)(2,1)}, bf16[16,32,640]{2,1,0:T(8,128)(2,1)}, u32[]{:S(2)}, u32[]{:S(2)}) collective-permute-start(bf16[16,32,640]{2,1,0:T(8,128)(2,1)} %get-tuple-element.31.mine), channel_id=1, source_target_pairs={{0,1},{1,0},{2,3},{3,2},{4,5},{5,4},{6,7},{7,6},{8,9},{9,8},{10,11... | collective-permute-start | bytes 1966088 | tf_op jit(solution)/shard_map/ppermute | solution.py:399

commit v9 on v7

--- a/solution.py
+++ b/solution.py
@@ -150,7 +150,7 @@
     )(place, *blocks)
 
 
-PEER_ORDER = (4, 1, 5, 2, 6, 3, 7, 0)
+PEER_ORDER = (4, 1, 5, 2, 7, 6, 3, 0)
 
 
 def hidden_kernel(*refs):

time: 212 us -> 211 us (level)
  starting transfers between devices: 64.7 us -> 61.6 us
  waiting for transfers between devices: 79.9 us -> 82.1 us
    ppermute x7, waiting for transfers between devices: 22.9 us -> 27.6 us  [plane_shift(): lax.ppermute(x, ('xh', 'y'), [(a * NY + b, (a + dx) % NX * NY + (b + dy)...]
    ppermute x7, starting transfers between devices: 19.8 us -> 16.7 us  [plane_shift(): lax.ppermute(x, ('xh', 'y'), [(a * NY + b, (a + dx) % NX * NY + (b + dy)...]
    ppermute x9, waiting for transfers between devices: 42.2 us -> 39.7 us  [swap(): return lax.ppermute(x, axis, [(0, 1), (1, 0)])]
  transfers between devices with their start and end apart: 26 -> 26, of which waited for: 12 -> 14; matrix products, arithmetic and copies ran while one was open for 4% -> 4% of each run, Pallas kernels for 19% -> 19%
where the time goes in v9:
time: 211 us; the launch traced here: 210 us
  waiting for transfers between devices  82.1 us (39%)
  starting transfers between devices  61.6 us (29%)
  Pallas kernels  47.7 us (23%)
  local copies, waits for them, and re-layouts  12.3 us (6%)
  other arithmetic  5.24 us (2%)
    ppermute x9, waiting for transfers between devices, swap(): return lax.ppermute(x, axis, [(0, 1), (1, 0)])  39.7 us
    ppermute x7, waiting for transfers between devices, plane_shift(): lax.ppermute(x, ('xh', 'y'), [(a * NY + b, (a + dx) % NX * NY + (b + dy)...  27.6 us
    ppermute x7, starting transfers between devices, plane_shift(): lax.ppermute(x, ('xh', 'y'), [(a * NY + b, (a + dx) % NX * NY + (b + dy)...  16.7 us
    ppermute x7, waiting for transfers between devices, z_shift(): return lax.ppermute(x, 'z', [(i, (i + by) % NZ) for i in range(NZ)])  14.8 us
    all_to_all x1, starting transfers between devices, on_device(): lax.all_to_all(out_rows, ('xh', 'z', 'y'), split_axis=0, concat_axis=0, t...  12.5 us
    unnamed x43, local copies, waits for them, and re-layouts  11.2 us
    ppermute x7, starting transfers between devices, z_shift(): return lax.ppermute(x, 'z', [(i, (i + by) % NZ) for i in range(NZ)])  10.8 us
    all_to_all x1, starting transfers between devices, on_device(): lax.all_to_all(midway, 'z', split_axis=0, concat_axis=0, tiled=True)  8.45 us
  transfers between devices with their start and end apart: 26, of which 14 were waited for; matrix products, arithmetic and copies ran while one was open for 4% of the time, Pallas kernels for 19%

profile of v9, /device:TPU:68, one launch (start us, length us, event | category | flops | bytes accessed | tf_op | source)
XLA Modules:
  0.0 209.9 jit_solution(12656281755795621038)
XLA Ops:
  0.7 0.7 convert_element_type.38
  1.5 1.7 fusion.1.refs_0_
  3.1 1.9 collective-permute-start
  5.2 0.7 bitcast_convert_fusion.scale
  5.8 2.5 %scale_down.2 = bf16[256,1792]{1,0:T(8,128)(2,1)} custom-call(s32[1]{0:T(128)S(6)} %sub.38.half_ref, f32[2,28]{1,0:T(2,128)S(1)} %bitcast_convert_fusion.scale, bf16[1,256,3584]{2,1,0:T(8,128)(2,1)} %value.7), custom_call_target="tpu_custom_call" | custom-call | flops 1000000 | bytes 2000000 | tf_op jit(solution)/shard_map/scale_down/pallas_call | solution.py:90
  8.3 1.2 collective-permute-start.14
  9.7 0.7 copy.45
  10.5 3.9 %copy.47.pages = bf16[128,16,576]{2,1,0:T(8,128)(2,1)S(1)} copy(bf16[128,16,576]{0,2,1:T(8,128)(2,1)} %param.17) | data formatting | bytes 4718592 | tf_op args[0]
  14.4 0.8 broadcast_subtract_fusion.index_ref
  15.1 0.5 once.5.rest_0_
  15.7 3.9 %collect.1 = bf16[64,32,640]{2,1,0:T(8,128)(2,1)} custom-call(s32[64,4]{1,0:T(8,128)S(1)} %broadcast_subtract_fusion.index_ref, bf16[128,16,576]{2,1,0:T(8,128)(2,1)S(1)} %copy.47.pages, f32[1]{0:T(128)} %once.5.rest_0_), custom_call_target="tpu_custom_call" | custom-call | flops 1000000 | bytes 6000000 | tf_op jit(solution)/shard_map/collect/pallas_call | solution.py:260
  19.6 7.6 %all-to-all-start = ((bf16[8,8,32,640]{3,2,1,0:T(8,128)(2,1)}), bf16[8,8,32,640]{3,2,1,0:T(8,128)(2,1)}, u32[]{:S(2)}, u32[]{:S(2)}) async-start(bf16[8,8,32,640]{3,2,1,0:T(8,128)(2,1)} %bitcast.28), calls=%async_computation | async-start | bytes 5242880 | tf_op jit(solution)/shard_map/all_to_all | solution.py:452
  27.2 3.0 %collective-permute-start.1 = (bf16[32,3712]{1,0:T(8,128)(2,1)}, bf16[32,3712]{1,0:T(8,128)(2,1)S(1)}, u32[]{:S(2)}, u32[]{:S(2)}) collective-permute-start(bf16[32,3712]{1,0:T(8,128)(2,1)} %collective-permute-done.refs_1_.refs_0_), channel_id=1, source_target_pairs={{0,8},{8,16},{16,24},{24,32},{32,40},{40,48},{48,56},{56,0},{1,9},... | collective-permute-start | bytes 712712 | tf_op jit(solution)/shard_map/ppermute | solution.py:402
  30.2 2.6 %scale_wide.2.refs_8_ = bf16[3584,256]{1,0:T(8,128)(2,1)S(1)} custom-call(f32[2,28]{1,0:T(2,128)S(1)} %convert_bitcast_fusion.1.scale, bf16[1,3584,256]{2,1,0:T(8,128)(2,1)} %value.4, f32[1]{0:T(128)} %once.5.rest_0_), custom_call_target="tpu_custom_call" | custom-call | flops 1000000 | bytes 4000000 | tf_op jit(solution)/shard_map/scale_wide/pallas_call | solution.py:66
  32.9 1.5 collective-permute-done.1.refs_2_.refs_0_
  34.4 3.3 %collective-permute-done.5.refs_6_.refs_1_ = bf16[32,3712]{1,0:T(8,128)(2,1)S(1)} collective-permute-done((bf16[32,3712]{1,0:T(8,128)(2,1)}, bf16[32,3712]{1,0:T(8,128)(2,1)S(1)}, u32[]{:S(2)}, u32[]{:S(2)}) %collective-permute-start.5) | collective-permute-done | bytes 237600 | tf_op jit(solution)/shard_map/ppermute | solution.py:402
  37.7 0.5 once.6.rest_0_
  38.2 2.6 %scale_wide.3.refs_9_ = bf16[3584,256]{1,0:T(8,128)(2,1)S(1)} custom-call(f32[2,28]{1,0:T(2,128)S(1)} %convert_bitcast_fusion.scale, bf16[1,3584,256]{2,1,0:T(8,128)(2,1)} %value.6, f32[1]{0:T(128)} %once.6.rest_0_), custom_call_target="tpu_custom_call" | custom-call | flops 1000000 | bytes 4000000 | tf_op jit(solution)/shard_map/scale_wide/pallas_call | solution.py:66
  41.0 1.3 copy-done.1
  42.2 3.2 %collective-permute-start.2 = (bf16[32,3712]{1,0:T(8,128)(2,1)S(1)}, bf16[32,3712]{1,0:T(8,128)(2,1)S(1)}, u32[]{:S(2)}, u32[]{:S(2)}) collective-permute-start(bf16[32,3712]{1,0:T(8,128)(2,1)S(1)} %collective-permute-done.1.refs_2_.refs_0_), channel_id=1, source_target_pairs={{0,8},{8,16},{16,24},{24,32},{32,40},{40,48},{48,56},{56,0},{1,9},... | collective-permute-start | bytes 712712 | tf_op jit(solution)/shard_map/ppermute | solution.py:402
  45.5 5.7 %collective-permute-done.2.refs_3_ = bf16[32,3712]{1,0:T(8,128)(2,1)S(1)} collective-permute-done((bf16[32,3712]{1,0:T(8,128)(2,1)S(1)}, bf16[32,3712]{1,0:T(8,128)(2,1)S(1)}, u32[]{:S(2)}, u32[]{:S(2)}) %collective-permute-start.2) | collective-permute-done | bytes 237600 | tf_op jit(solution)/shard_map/ppermute | solution.py:402
  51.2 2.5 %collective-permute-start.3 = (bf16[32,3712]{1,0:T(8,128)(2,1)S(1)}, bf16[32,3712]{1,0:T(8,128)(2,1)S(1)}, u32[]{:S(2)}, u32[]{:S(2)}) collective-permute-start(bf16[32,3712]{1,0:T(8,128)(2,1)S(1)} %collective-permute-done.2.refs_3_), channel_id=1, source_target_pairs={{0,8},{8,16},{16,24},{24,32},{32,40},{40,48},{48,56},{56,0},{1,9},... | collective-permute-start | bytes 712712 | tf_op jit(solution)/shard_map/ppermute | solution.py:402
  53.6 0.7 copy-done.9
  54.3 4.3 %collective-permute-done.3.refs_4_.refs_0_ = bf16[32,3712]{1,0:T(8,128)(2,1)S(1)} collective-permute-done((bf16[32,3712]{1,0:T(8,128)(2,1)S(1)}, bf16[32,3712]{1,0:T(8,128)(2,1)S(1)}, u32[]{:S(2)}, u32[]{:S(2)}) %collective-permute-start.3) | collective-permute-done | bytes 237600 | tf_op jit(solution)/shard_map/ppermute | solution.py:402
  58.7 0.5 once.9.rest_0_
  59.2 1.3 copy-done.3
  60.5 1.3 copy-done.5
  61.8 0.7 copy-done.7
  62.5 3.6 %regroup.1 = bf16[8,8,32,640]{3,2,1,0:T(8,128)(2,1)} custom-call(bf16[8,8,32,640]{3,2,1,0:T(8,128)(2,1)} %all-to-all-done.midway, f32[1]{0:T(128)} %once.9.rest_0_), custom_call_target="tpu_custom_call" | custom-call | flops 1000000 | bytes 6000000 | tf_op jit(solution)/shard_map/regroup/pallas_call | solution.py:279
  66.0 8.4 %all-to-all-start.1 = ((bf16[8,8,32,640]{3,2,1,0:T(8,128)(2,1)}), bf16[8,8,32,640]{3,2,1,0:T(8,128)(2,1)}, u32[]{:S(2)}, u32[]{:S(2)}) async-start(bf16[8,8,32,640]{3,2,1,0:T(8,128)(2,1)} %regroup.1), calls=%async_computation.1 | async-start | bytes 5242880 | tf_op jit(solution)/shard_map/all_to_all | solution.py:474
  74.6 0.9 copy-done.8
  75.5 0.9 copy-done.10
  76.4 3.9 %pick_rows.1 = (bf16[64,3584]{1,0:T(8,128)(2,1)S(1)}, bf16[64,3584]{1,0:T(8,128)(2,1)S(1)}, bf16[64,3584]{1,0:T(8,128)(2,1)S(1)}, bf16[64,3584]{1,0:T(8,128)(2,1...) custom-call(s32[3]{0:T(128)S(1)} %pad_add_fusion.1.place_ref, ...), custom_call_target="tpu_custom_call" | custom-call | flops 1000000000 | bytes 6000000 | tf_op jit(solution)/shard_map/pick_rows/pallas_call | solution.py:142
  80.4 2.0 collective-permute-start.8
  82.5 3.8 %collective-permute-start.9 = (bf16[64,3584]{1,0:T(8,128)(2,1)S(1)}, bf16[64,3584]{1,0:T(8,128)(2,1)S(1)}, u32[]{:S(2)}, u32[]{:S(2)}) collective-permute-start(bf16[64,3584]{1,0:T(8,128)(2,1)S(1)} %get-tuple-element.22.refs_0_), channel_id=1, source_target_pairs={{0,66},{2,68},{4,70},{6,64},{64,2},{66,4},{68,6},{70,0},{1,67},{3,... | collective-permute-start | bytes 1376264 | tf_op jit(solution)/shard_map/ppermute | solution.py:406
  86.3 1.8 collective-permute-start.10
  88.1 2.1 collective-permute-start.11
  90.2 5.2 %collective-permute-done.7.refs_0_ = bf16[64,3584]{1,0:T(8,128)(2,1)S(1)} collective-permute-done((bf16[64,3584]{1,0:T(8,128)(2,1)S(1)}, bf16[64,3584]{1,0:T(8,128)(2,1)S(1)}, u32[]{:S(2)}, u32[]{:S(2)}) %collective-permute-start.7) | collective-permute-done | bytes 458784 | tf_op jit(solution)/shard_map/ppermute | solution.py:406
  95.4 3.0 %collective-permute-start.12 = (bf16[64,3584]{1,0:T(8,128)(2,1)S(1)}, bf16[64,3584]{1,0:T(8,128)(2,1)S(1)}, u32[]{:S(2)}, u32[]{:S(2)}) collective-permute-start(bf16[64,3584]{1,0:T(8,128)(2,1)S(1)} %get-tuple-element.25), channel_id=1, source_target_pairs={{0,68},{2,70},{4,64},{6,66},{64,4},{66,6},{68,0},{70,2},{1,69},{3,... | collective-permute-start | bytes 1376264 | tf_op jit(solution)/shard_map/ppermute | solution.py:406
  98.3 3.5 %collective-permute-done.8.refs_1_ = bf16[64,3584]{1,0:T(8,128)(2,1)S(1)} collective-permute-done((bf16[64,3584]{1,0:T(8,128)(2,1)S(1)}, bf16[64,3584]{1,0:T(8,128)(2,1)S(1)}, u32[]{:S(2)}, u32[]{:S(2)}) %collective-permute-start.8) | collective-permute-done | bytes 458784 | tf_op jit(solution)/shard_map/ppermute | solution.py:406
  101.8 3.9 %collective-permute-start.13 = (bf16[64,3584]{1,0:T(8,128)(2,1)S(1)}, bf16[64,3584]{1,0:T(8,128)(2,1)S(1)}, u32[]{:S(2)}, u32[]{:S(2)}) collective-permute-start(bf16[64,3584]{1,0:T(8,128)(2,1)S(1)} %get-tuple-element.26), channel_id=1, source_target_pairs={{0,6},{2,0},{4,2},{6,4},{64,70},{66,64},{68,66},{70,68},{1,7},{3,1... | collective-permute-start | bytes 1376264 | tf_op jit(solution)/shard_map/ppermute | solution.py:406
  106.2 3.1 %scale_down.3.w0 = bf16[256,1792]{1,0:T(8,128)(2,1)} custom-call(s32[1]{0:T(128)} %bitcast.7.half_ref.tp_ref, f32[2,28]{1,0:T(2,128)S(1)} %bitcast_convert_fusion.scale, bf16[1,256,3584]{2,1,0:T(8,128)(2,1)} %value.7, f32[1]{0:T(128)} %once.7.rest_0_), custom_call_target="tpu_custom_call" | custom-call | flops 1000000 | bytes 2000000 | tf_op jit(solution)/shard_map/scale_down/pallas_call | solution.py:90
  109.3 5.2 %collective-permute-done.10.refs_3_ = bf16[64,3584]{1,0:T(8,128)(2,1)S(1)} collective-permute-done((bf16[64,3584]{1,0:T(8,128)(2,1)S(1)}, bf16[64,3584]{1,0:T(8,128)(2,1)S(1)}, u32[]{:S(2)}, u32[]{:S(2)}) %collective-permute-start.10) | collective-permute-done | bytes 458784 | tf_op jit(solution)/shard_map/ppermute | solution.py:406
  114.5 1.5 collective-permute-done.11.refs_4_
  116.1 8.9 %collective-permute-done.12.refs_5_ = bf16[64,3584]{1,0:T(8,128)(2,1)S(1)} collective-permute-done((bf16[64,3584]{1,0:T(8,128)(2,1)S(1)}, bf16[64,3584]{1,0:T(8,128)(2,1)S(1)}, u32[]{:S(2)}, u32[]{:S(2)}) %collective-permute-start.12) | collective-permute-done | bytes 458784 | tf_op jit(solution)/shard_map/ppermute | solution.py:406
  124.9 3.3 %collective-permute-done.13.refs_6_ = bf16[64,3584]{1,0:T(8,128)(2,1)S(1)} collective-permute-done((bf16[64,3584]{1,0:T(8,128)(2,1)S(1)}, bf16[64,3584]{1,0:T(8,128)(2,1)S(1)}, u32[]{:S(2)}, u32[]{:S(2)}) %collective-permute-start.13) | collective-permute-done | bytes 458784 | tf_op jit(solution)/shard_map/ppermute | solution.py:406
  128.3 2.1 hidden_units.2.h0
  130.4 1.0 collective-permute-start.17
  131.4 2.1 hidden_units.3.h1
  133.5 1.2 collective-permute-start.18
  134.8 2.1 collective-permute-done.17.h2
  136.8 3.1 %collective-permute-done.18.h3 = bf16[512,256]{1,0:T(8,128)(2,1)S(1)} collective-permute-done((bf16[512,256]{1,0:T(8,128)(2,1)S(1)}, bf16[512,256]{1,0:T(8,128)(2,1)S(1)}, u32[]{:S(2)}, u32[]{:S(2)}) %collective-permute-start.18) | collective-permute-done | bytes 262176 | tf_op jit(solution)/shard_map/ppermute | solution.py:398
  139.9 5.2 %down_rows.1.refs_0_ = bf16[64,8,1792]{2,1,0:T(8,128)(2,1)} custom-call(s32[64]{0:T(128)S(1)} %fusion.3.order_ref, bf16[512,256]{1,0:T(8,128)(2,1)S(1)} %hidden_units.2.h0, bf16[512,256]{1,0:T(8,128)(2,1)S(1)} %hidden_units.3.h1, bf16[512,256]{1,0:T(8,128)(2,1)S(1)} %collective-permute-done.17.h2, bf16[512,256]{1,0:T(8,128)(2,1)S(1)} %collective-permute-done.18.h3, ...), custom_call_target="tpu_custom_call" | custom-call | flops 1900000000 | bytes 7000000 | tf_op jit(solution)/shard_map/down_rows/pallas_call | solution.py:193
  145.1 12.5 %all-to-all-start.2 = ((bf16[64,8,1792]{2,1,0:T(8,128)(2,1)}), bf16[64,8,1792]{2,1,0:T(8,128)(2,1)S(1)}, u32[]{:S(2)}, u32[]{:S(2)}) async-start(bf16[64,8,1792]{2,1,0:T(8,128)(2,1)} %down_rows.1.refs_0_), calls=%async_computation.2 | async-start | bytes 3670016 | tf_op jit(solution)/shard_map/all_to_all | solution.py:487
  157.6 0.5 once.8.late_ref
  158.2 1.0 slice_convert_fusion
  159.4 3.4 %compact.1 = (bf16[16,32,640]{2,1,0:T(8,128)(2,1)S(1)}, bf16[16,32,640]{2,1,0:T(8,128)(2,1)}) custom-call(s32[32]{0:T(128)S(1)} %get-tuple-element.37.source_ref, bf16[64,32,640]{2,1,0:T(8,128)(2,1)} %bitcast.13.arrived, f32[1]{0:T(128)} %once.8.late_ref), custom_call_target="tpu_custom_call" | custom-call | flops 1000000 | bytes 4000000 | tf_op jit(solution)/shard_map/compact/pallas_call | solution.py:299
  162.8 1.1 collective-permute-start.21
  163.9 0.9 collective-permute-start.22
  165.0 29.1 %collective-permute-done.21.other = bf16[16,32,640]{2,1,0:T(8,128)(2,1)S(1)} collective-permute-done((bf16[16,32,640]{2,1,0:T(8,128)(2,1)S(1)}, bf16[16,32,640]{2,1,0:T(8,128)(2,1)S(1)}, u32[]{:S(2)}, u32[]{:S(2)}) %collective-permute-start.21) | collective-permute-done | bytes 655392 | tf_op jit(solution)/shard_map/ppermute | solution.py:398
  194.1 3.8 %attend.2 = (bf16[32,64,576]{2,1,0:T(8,128)(2,1)}, bf16[32,32,512]{2,1,0:T(8,128)(2,1)}, f32[1]{0:T(128)}) custom-call(f32[1]{0:T(128)} %once.8.late_ref, s32[1]{0:T(128)} %bitcast.7.half_ref.tp_ref, s32[32]{0:T(128)S(1)} %get-tuple-element.38.length_ref, bf16[16,32,640]{2,1,0:T(8,128)(2,1)S(1)} %get-tuple-element.28.mine, ...), custom_call_target="tpu_custom_call" | custom-call | flops 100000000 | bytes 4000000 | tf_op jit(solution)/shard_map/attend/pallas_call | solution.py:351
  197.9 2.7 %blend.1 = (bf16[32,1792]{1,0:T(8,128)(2,1)}, f32[1]{0:T(128)}) custom-call(f32[1]{0:T(128)} %get-tuple-element.29.late_ref, s32[32,8]{1,0:T(8,128)S(1)} %copy.50.routing_ref, f32[32,8]{1,0:T(8,128)S(1)} %copy.51.weight_ref, bf16[64,8,1792]{2,1,0:T(8,128)(2,1)S(1)} %all-to-all-done.2.rows_ref), custom_call_target="tpu_custom_call" | custom-call | flops 100000000 | bytes 2000000 | tf_op jit(solution)/shard_map/blend/pallas_call | solution.py:227
  200.6 5.5 %collective-permute-done.22.other = bf16[16,32,640]{2,1,0:T(8,128)(2,1)} collective-permute-done((bf16[16,32,640]{2,1,0:T(8,128)(2,1)}, bf16[16,32,640]{2,1,0:T(8,128)(2,1)}, u32[]{:S(2)}, u32[]{:S(2)}) %collective-permute-start.22) | collective-permute-done | bytes 655392 | tf_op jit(solution)/shard_map/ppermute | solution.py:398
  206.0 3.9 %attend.3 = (bf16[32,64,576]{2,1,0:T(8,128)(2,1)}, bf16[32,32,512]{2,1,0:T(8,128)(2,1)}, f32[1]{0:T(128)}) custom-call(f32[1]{0:T(128)} %get-tuple-element.30.late_ref, s32[1]{0:T(128)} %bitcast.7.half_ref.tp_ref, s32[32]{0:T(128)S(1)} %get-tuple-element.38.length_ref, ...), custom_call_target="tpu_custom_call", output_to_operand_aliasing={{0}: (7, {}), {1}: (8, {})} | custom-call | flops 100000000 | bytes 4000000 | tf_op jit(solution)/shard_map/attend/pallas_call | solution.py:351
  (74 shorter events, 1.9 us)
Async XLA Ops:
  0.6 8.9 %copy-start = (s32[32,4]{0,1:T(4,128)S(1)}, s32[32,4]{0,1:T(4,128)}, u32[]{:S(2)}) copy-start(s32[32,4]{0,1:T(4,128)} %param.18) | copy-start | bytes 1540
  0.6 8.9 %copy-start.14 = (s32[64]{0:T(128)S(1)}, s32[64]{0:T(128)}, u32[]{:S(2)}) copy-start(s32[64]{0:T(128)} %constant.94.clone) | copy-start | bytes 772
  0.7 8.8 %copy-start.16 = (s32[32]{0:T(128)S(1)}, s32[32]{0:T(128)}, u32[]{:S(2)}) copy-start(s32[32]{0:T(128)} %param.20) | copy-start | bytes 388
  0.7 9.0 %copy-start.15 = (s32[32]{0:T(128)S(1)}, s32[32]{0:T(128)}, u32[]{:S(2)}) copy-start(s32[32]{0:T(128)} %param.19) | copy-start | bytes 388
  3.1 12.0 %collective-permute-start = (bf16[32,3712]{1,0:T(8,128)(2,1)}, bf16[32,3712]{1,0:T(8,128)(2,1)}, u32[]{:S(2)}, u32[]{:S(2)}) collective-permute-start(bf16[32,3712]{1,0:T(8,128)(2,1)} %fusion.1.refs_0_), channel_id=1, source_target_pairs={{0,8},{8,16},{16,24},{24,32},{32,40},{40,48},{48,56},{56,0},{1,9},... | collective-permute-start | bytes 712712 | tf_op jit(solution)/shard_map/ppermute | solution.py:402
  5.1 10.1 %collective-permute-start.4 = (bf16[32,3712]{1,0:T(8,128)(2,1)}, bf16[32,3712]{1,0:T(8,128)(2,1)}, u32[]{:S(2)}, u32[]{:S(2)}) collective-permute-start(bf16[32,3712]{1,0:T(8,128)(2,1)} %fusion.1.refs_0_), channel_id=1, source_target_pairs={{0,56},{8,0},{16,8},{24,16},{32,24},{40,32},{48,40},{56,48},{1,57}... | collective-permute-start | bytes 712712 | tf_op jit(solution)/shard_map/ppermute | solution.py:402
  8.3 29.4 %collective-permute-start.14 = (bf16[256,1792]{1,0:T(8,128)(2,1)}, bf16[256,1792]{1,0:T(8,128)(2,1)S(1)}, u32[]{:S(2)}, u32[]{:S(2)}) collective-permute-start(bf16[256,1792]{1,0:T(8,128)(2,1)} %scale_down.2), channel_id=1, source_target_pairs={{0,1},{1,0},{2,3},{3,2},{4,5},{5,4},{6,7},{7,6},{8,9},{9,8},{10,11... | collective-permute-start | bytes 2752520 | tf_op jit(solution)/shard_map/ppermute | solution.py:398
  19.6 10.6 %copy-start.17 = (bf16[1,28,2]{1,2,0:T(2,128)(2,1)S(1)}, bf16[1,28,2]{1,2,0:T(2,128)(2,1)}, u32[]{:S(2)}) copy-start(bf16[1,28,2]{1,2,0:T(2,128)(2,1)} %param.27) | copy-start | bytes 340
  19.6 10.6 %copy-start.18 = (bf16[1,28,2]{1,2,0:T(2,128)(2,1)S(1)}, bf16[1,28,2]{1,2,0:T(2,128)(2,1)}, u32[]{:S(2)}) copy-start(bf16[1,28,2]{1,2,0:T(2,128)(2,1)} %param.29) | copy-start | bytes 340
  19.6 42.9 %all-to-all-start = ((bf16[8,8,32,640]{3,2,1,0:T(8,128)(2,1)}), bf16[8,8,32,640]{3,2,1,0:T(8,128)(2,1)}, u32[]{:S(2)}, u32[]{:S(2)}) async-start(bf16[8,8,32,640]{3,2,1,0:T(8,128)(2,1)} %bitcast.28), calls=%async_computation | async-start | bytes 5242880 | tf_op jit(solution)/shard_map/all_to_all | solution.py:452
  27.2 7.3 %collective-permute-start.1 = (bf16[32,3712]{1,0:T(8,128)(2,1)}, bf16[32,3712]{1,0:T(8,128)(2,1)S(1)}, u32[]{:S(2)}, u32[]{:S(2)}) collective-permute-start(bf16[32,3712]{1,0:T(8,128)(2,1)} %collective-permute-done.refs_1_.refs_0_), channel_id=1, source_target_pairs={{0,8},{8,16},{16,24},{24,32},{32,40},{40,48},{48,56},{56,0},{1,9},... | collective-permute-start | bytes 712712 | tf_op jit(solution)/shard_map/ppermute | solution.py:402
  30.2 7.5 %collective-permute-start.5 = (bf16[32,3712]{1,0:T(8,128)(2,1)}, bf16[32,3712]{1,0:T(8,128)(2,1)S(1)}, u32[]{:S(2)}, u32[]{:S(2)}) collective-permute-start(bf16[32,3712]{1,0:T(8,128)(2,1)} %collective-permute-done.4.refs_5_.refs_1_), channel_id=1, source_target_pairs={{0,56},{8,0},{16,8},{24,16},{32,24},{40,32},{48,40},{56,48},{1,57}... | collective-permute-start | bytes 712712 | tf_op jit(solution)/shard_map/ppermute | solution.py:402
  32.8 25.9 %collective-permute-start.15 = (bf16[3584,256]{1,0:T(8,128)(2,1)S(1)}, bf16[3584,256]{1,0:T(8,128)(2,1)S(1)}, u32[]{:S(2)}, u32[]{:S(2)}) collective-permute-start(bf16[3584,256]{1,0:T(8,128)(2,1)S(1)} %scale_wide.2.refs_8_), channel_id=1, source_target_pairs={{0,128},{128,0},{1,129},{129,1},{2,130},{130,2},{3,131},{131,3},{4... | collective-permute-start | bytes 5505032 | tf_op jit(solution)/shard_map/ppermute | solution.py:398
  40.8 17.8 %collective-permute-start.16 = (bf16[3584,256]{1,0:T(8,128)(2,1)S(1)}, bf16[3584,256]{1,0:T(8,128)(2,1)S(1)}, u32[]{:S(2)}, u32[]{:S(2)}) collective-permute-start(bf16[3584,256]{1,0:T(8,128)(2,1)S(1)} %scale_wide.3.refs_9_), channel_id=1, source_target_pairs={{0,128},{128,0},{1,129},{129,1},{2,130},{130,2},{3,131},{131,3},{4... | collective-permute-start | bytes 5505032 | tf_op jit(solution)/shard_map/ppermute | solution.py:398
  40.9 1.3 copy-start.1
  42.2 8.9 %collective-permute-start.2 = (bf16[32,3712]{1,0:T(8,128)(2,1)S(1)}, bf16[32,3712]{1,0:T(8,128)(2,1)S(1)}, u32[]{:S(2)}, u32[]{:S(2)}) collective-permute-start(bf16[32,3712]{1,0:T(8,128)(2,1)S(1)} %collective-permute-done.1.refs_2_.refs_0_), channel_id=1, source_target_pairs={{0,8},{8,16},{16,24},{24,32},{32,40},{40,48},{48,56},{56,0},{1,9},... | collective-permute-start | bytes 712712 | tf_op jit(solution)/shard_map/ppermute | solution.py:402
  45.5 8.9 %collective-permute-start.6 = (bf16[32,3712]{1,0:T(8,128)(2,1)S(1)}, bf16[32,3712]{1,0:T(8,128)(2,1)S(1)}, u32[]{:S(2)}, u32[]{:S(2)}) collective-permute-start(bf16[32,3712]{1,0:T(8,128)(2,1)S(1)} %collective-permute-done.5.refs_6_.refs_1_), channel_id=1, source_target_pairs={{0,56},{8,0},{16,8},{24,16},{32,24},{40,32},{48,40},{56,48},{1,57}... | collective-permute-start | bytes 712712 | tf_op jit(solution)/shard_map/ppermute | solution.py:402
  51.2 7.5 %collective-permute-start.3 = (bf16[32,3712]{1,0:T(8,128)(2,1)S(1)}, bf16[32,3712]{1,0:T(8,128)(2,1)S(1)}, u32[]{:S(2)}, u32[]{:S(2)}) collective-permute-start(bf16[32,3712]{1,0:T(8,128)(2,1)S(1)} %collective-permute-done.2.refs_3_), channel_id=1, source_target_pairs={{0,8},{8,16},{16,24},{24,32},{32,40},{40,48},{48,56},{56,0},{1,9},... | collective-permute-start | bytes 712712 | tf_op jit(solution)/shard_map/ppermute | solution.py:402
  53.6 0.7 copy-start.9
  59.2 1.3 copy-start.3
  60.5 1.3 copy-start.5
  61.8 0.7 copy-start.7
  66.0 79.1 %all-to-all-start.1 = ((bf16[8,8,32,640]{3,2,1,0:T(8,128)(2,1)}), bf16[8,8,32,640]{3,2,1,0:T(8,128)(2,1)}, u32[]{:S(2)}, u32[]{:S(2)}) async-start(bf16[8,8,32,640]{3,2,1,0:T(8,128)(2,1)} %regroup.1), calls=%async_computation.1 | async-start | bytes 5242880 | tf_op jit(solution)/shard_map/all_to_all | solution.py:474
  74.6 0.9 copy-start.8
  75.5 0.9 copy-start.10
  80.3 47.9 %copy-start.2 = (bf16[3584,256]{1,0:T(8,128)(2,1)S(1)}, bf16[3584,256]{1,0:T(8,128)(2,1)}, u32[]{:S(2)}) copy-start(bf16[3584,256]{1,0:T(8,128)(2,1)} %copy-done.1) | copy-start | bytes 5505028
  80.3 15.0 %collective-permute-start.7 = (bf16[64,3584]{1,0:T(8,128)(2,1)S(1)}, bf16[64,3584]{1,0:T(8,128)(2,1)S(1)}, u32[]{:S(2)}, u32[]{:S(2)}) collective-permute-start(bf16[64,3584]{1,0:T(8,128)(2,1)S(1)} %get-tuple-element.20), channel_id=1, source_target_pairs={{0,64},{2,66},{4,68},{6,70},{64,0},{66,2},{68,4},{70,6},{1,65},{3,... | collective-permute-start | bytes 1376264 | tf_op jit(solution)/shard_map/ppermute | solution.py:406
  80.4 21.4 %collective-permute-start.8 = (bf16[64,3584]{1,0:T(8,128)(2,1)S(1)}, bf16[64,3584]{1,0:T(8,128)(2,1)S(1)}, u32[]{:S(2)}, u32[]{:S(2)}) collective-permute-start(bf16[64,3584]{1,0:T(8,128)(2,1)S(1)} %get-tuple-element.21), channel_id=1, source_target_pairs={{0,2},{2,4},{4,6},{6,0},{64,66},{66,68},{68,70},{70,64},{1,3},{3,5... | collective-permute-start | bytes 1376264 | tf_op jit(solution)/shard_map/ppermute | solution.py:406
  82.5 26.9 %collective-permute-start.9 = (bf16[64,3584]{1,0:T(8,128)(2,1)S(1)}, bf16[64,3584]{1,0:T(8,128)(2,1)S(1)}, u32[]{:S(2)}, u32[]{:S(2)}) collective-permute-start(bf16[64,3584]{1,0:T(8,128)(2,1)S(1)} %get-tuple-element.22.refs_0_), channel_id=1, source_target_pairs={{0,66},{2,68},{4,70},{6,64},{64,2},{66,4},{68,6},{70,0},{1,67},{3,... | collective-permute-start | bytes 1376264 | tf_op jit(solution)/shard_map/ppermute | solution.py:406
  86.3 28.2 %collective-permute-start.10 = (bf16[64,3584]{1,0:T(8,128)(2,1)S(1)}, bf16[64,3584]{1,0:T(8,128)(2,1)S(1)}, u32[]{:S(2)}, u32[]{:S(2)}) collective-permute-start(bf16[64,3584]{1,0:T(8,128)(2,1)S(1)} %get-tuple-element.23), channel_id=1, source_target_pairs={{0,4},{2,6},{4,0},{6,2},{64,68},{66,70},{68,64},{70,66},{1,5},{3,7... | collective-permute-start | bytes 1376264 | tf_op jit(solution)/shard_map/ppermute | solution.py:406
  88.1 28.0 %collective-permute-start.11 = (bf16[64,3584]{1,0:T(8,128)(2,1)S(1)}, bf16[64,3584]{1,0:T(8,128)(2,1)S(1)}, u32[]{:S(2)}, u32[]{:S(2)}) collective-permute-start(bf16[64,3584]{1,0:T(8,128)(2,1)S(1)} %get-tuple-element.24), channel_id=1, source_target_pairs={{0,70},{2,64},{4,66},{6,68},{64,6},{66,0},{68,2},{70,4},{1,71},{3,... | collective-permute-start | bytes 1376264 | tf_op jit(solution)/shard_map/ppermute | solution.py:406
  95.4 29.6 %collective-permute-start.12 = (bf16[64,3584]{1,0:T(8,128)(2,1)S(1)}, bf16[64,3584]{1,0:T(8,128)(2,1)S(1)}, u32[]{:S(2)}, u32[]{:S(2)}) collective-permute-start(bf16[64,3584]{1,0:T(8,128)(2,1)S(1)} %get-tuple-element.25), channel_id=1, source_target_pairs={{0,68},{2,70},{4,64},{6,66},{64,4},{66,6},{68,0},{70,2},{1,69},{3,... | collective-permute-start | bytes 1376264 | tf_op jit(solution)/shard_map/ppermute | solution.py:406
  101.8 26.4 %collective-permute-start.13 = (bf16[64,3584]{1,0:T(8,128)(2,1)S(1)}, bf16[64,3584]{1,0:T(8,128)(2,1)S(1)}, u32[]{:S(2)}, u32[]{:S(2)}) collective-permute-start(bf16[64,3584]{1,0:T(8,128)(2,1)S(1)} %get-tuple-element.26), channel_id=1, source_target_pairs={{0,6},{2,0},{4,2},{6,4},{64,70},{66,64},{68,66},{70,68},{1,7},{3,1... | collective-permute-start | bytes 1376264 | tf_op jit(solution)/shard_map/ppermute | solution.py:406
  109.3 27.5 %collective-permute-start.20 = (bf16[256,1792]{1,0:T(8,128)(2,1)S(1)}, bf16[256,1792]{1,0:T(8,128)(2,1)}, u32[]{:S(2)}, u32[]{:S(2)}) collective-permute-start(bf16[256,1792]{1,0:T(8,128)(2,1)S(1)} %collective-permute-done.14.refs_2_.w2), channel_id=1, source_target_pairs={{0,128},{128,0},{1,129},{129,1},{2,130},{130,2},{3,131},{131,3},{4... | collective-permute-start | bytes 2752520 | tf_op jit(solution)/shard_map/ppermute | solution.py:398
  114.5 22.3 %collective-permute-start.19 = (bf16[256,1792]{1,0:T(8,128)(2,1)}, bf16[256,1792]{1,0:T(8,128)(2,1)}, u32[]{:S(2)}, u32[]{:S(2)}) collective-permute-start(bf16[256,1792]{1,0:T(8,128)(2,1)} %scale_down.3.w0), channel_id=1, source_target_pairs={{0,128},{128,0},{1,129},{129,1},{2,130},{130,2},{3,131},{131,3},{4... | collective-permute-start | bytes 2752520 | tf_op jit(solution)/shard_map/ppermute | solution.py:398
  128.3 3.1 %copy-start.4 = (bf16[3584,256]{1,0:T(8,128)(2,1)S(1)}, bf16[3584,256]{1,0:T(8,128)(2,1)}, u32[]{:S(2)}) copy-start(bf16[3584,256]{1,0:T(8,128)(2,1)} %copy-done.3) | copy-start | bytes 5505028
  128.3 3.1 %copy-start.6 = (bf16[3584,256]{1,0:T(8,128)(2,1)S(1)}, bf16[3584,256]{1,0:T(8,128)(2,1)}, u32[]{:S(2)}) copy-start(bf16[3584,256]{1,0:T(8,128)(2,1)} %copy-done.5) | copy-start | bytes 5505028
  130.3 4.3 %copy-start.19 = (s32[8]{0:T(128)S(1)}, s32[8]{0:T(128)}, u32[]{:S(2)}) copy-start(s32[8]{0:T(128)} %constant.112) | copy-start | bytes 100
  130.4 6.5 %collective-permute-start.17 = (bf16[512,256]{1,0:T(8,128)(2,1)S(1)}, bf16[512,256]{1,0:T(8,128)(2,1)S(1)}, u32[]{:S(2)}, u32[]{:S(2)}) collective-permute-start(bf16[512,256]{1,0:T(8,128)(2,1)S(1)} %hidden_units.2.h0), channel_id=1, source_target_pairs={{0,1},{1,0},{2,3},{3,2},{4,5},{5,4},{6,7},{7,6},{8,9},{9,8},{10,11... | collective-permute-start | bytes 786440 | tf_op jit(solution)/shard_map/ppermute | solution.py:398
  133.5 6.5 %collective-permute-start.18 = (bf16[512,256]{1,0:T(8,128)(2,1)S(1)}, bf16[512,256]{1,0:T(8,128)(2,1)S(1)}, u32[]{:S(2)}, u32[]{:S(2)}) collective-permute-start(bf16[512,256]{1,0:T(8,128)(2,1)S(1)} %hidden_units.3.h1), channel_id=1, source_target_pairs={{0,1},{1,0},{2,3},{3,2},{4,5},{5,4},{6,7},{7,6},{8,9},{9,8},{10,11... | collective-permute-start | bytes 786440 | tf_op jit(solution)/shard_map/ppermute | solution.py:398
  145.1 52.8 %all-to-all-start.2 = ((bf16[64,8,1792]{2,1,0:T(8,128)(2,1)}), bf16[64,8,1792]{2,1,0:T(8,128)(2,1)S(1)}, u32[]{:S(2)}, u32[]{:S(2)}) async-start(bf16[64,8,1792]{2,1,0:T(8,128)(2,1)} %down_rows.1.refs_0_), calls=%async_computation.2 | async-start | bytes 3670016 | tf_op jit(solution)/shard_map/all_to_all | solution.py:487
  157.6 7.2 %copy-start.12 = (s32[32,8]{0,1:T(8,128)S(1)}, s32[32,8]{0,1:T(8,128)}, u32[]{:S(2)}) copy-start(s32[32,8]{0,1:T(8,128)} %param.24) | copy-start | bytes 3076
  158.1 6.7 %copy-start.11 = (bf16[32,576]{1,0:T(8,128)(2,1)S(1)}, bf16[32,576]{1,0:T(8,128)(2,1)}, u32[]{:S(2)}) copy-start(bf16[32,576]{1,0:T(8,128)(2,1)} %param.22) | copy-start | bytes 110596
  158.2 6.8 %copy-start.13 = (f32[32,8]{0,1:T(8,128)S(1)}, f32[32,8]{0,1:T(8,128)}, u32[]{:S(2)}) copy-start(f32[32,8]{0,1:T(8,128)} %param.25) | copy-start | bytes 3076
  162.8 31.3 %collective-permute-start.21 = (bf16[16,32,640]{2,1,0:T(8,128)(2,1)S(1)}, bf16[16,32,640]{2,1,0:T(8,128)(2,1)S(1)}, u32[]{:S(2)}, u32[]{:S(2)}) collective-permute-start(bf16[16,32,640]{2,1,0:T(8,128)(2,1)S(1)} %get-tuple-element.28.mine), channel_id=1, source_target_pairs={{0,1},{1,0},{2,3},{3,2},{4,5},{5,4},{6,7},{7,6},{8,9},{9,8},{10,11... | collective-permute-start | bytes 1966088 | tf_op jit(solution)/shard_map/ppermute | solution.py:398
  163.9 42.1 %collective-permute-start.22 = (bf16[16,32,640]{2,1,0:T(8,128)(2,1)}, bf16[16,32,640]{2,1,0:T(8,128)(2,1)}, u32[]{:S(2)}, u32[]{:S(2)}) collective-permute-start(bf16[16,32,640]{2,1,0:T(8,128)(2,1)} %get-tuple-element.31.mine), channel_id=1, source_target_pairs={{0,1},{1,0},{2,3},{3,2},{4,5},{5,4},{6,7},{7,6},{8,9},{9,8},{10,11... | collective-permute-start | bytes 1966088 | tf_op jit(solution)/shard_map/ppermute | solution.py:398
